TPU v7x, 32 devices: a whole 2x2x4 slice. The times are simulated.
32 devices in a mesh: dp: 16 (over z, x, core), tensor: 2 (over y).
Axes of the slice: x: 2, y: 2, z: 4, core: 2. Of those that a mesh axis runs over, the one named last changes fastest.
Arguments:
- hidden: bfloat16 [2048, 4096], P('dp', 'tensor'), may hold values from -6 to 6
- norm_gain: float32 [4096], replicated, may hold values from 0.1 to 1.9
- w_query: bfloat16 [4096, 4096], P('dp', 'tensor'), may hold values from -0.09375 to 0.09375
- w_key: bfloat16 [4096, 1024], P('dp', 'tensor'), may hold values from -0.09375 to 0.09375
- w_value: bfloat16 [4096, 1024], P('dp', 'tensor'), may hold values from -0.09375 to 0.09375
- upstream: bfloat16 [2048, 4096], P('dp', 'tensor'), may hold values from -6 to 6
- cached: float32 [16, 4096], P(None, 'tensor'), may hold values from -192 to 192
- lengths: int32 [16], replicated, may hold values from 1 to 512, 2048 in all
Outputs:
- grad_hidden: bfloat16 [2048, 4096], P('dp', 'tensor')
- grad_wkey: float32 [4096, 1024], P('dp', 'tensor')
Inputs may be any that keep to these rules, and one draw needn't show every extreme that they name: The 16 documents are laid end to end and fill the stream; their lengths sum to 2048 and the longest has exactly 512 tokens.
All inputs are finite; a program needn't handle non-finite values.
Results may differ from a plain program's by a relative error of at most 0.015.
Values may be sent and summed in bfloat16 or wider, within the bound.
No kernel may reach another device: no remote copies, remote signals or barrier semaphores. Data moves between devices by JAX's collectives and lax.ppermute only.
A program may use at most 128 MiB of HBM per device.

v0:
```python
import jax
import jax.numpy as jnp
from jax import lax
from jax.sharding import PartitionSpec as P

D = 4096
HD = 128
HOPS = 4


EPSILON = 1e-05
ROPE_BASE = 500000.0


def from_behind(block, axis, distance):
    devices = range(lax.axis_size(axis))
    route = [(i - distance, i) for i in devices if i - distance in devices]
    return lax.ppermute(block, axis, route)


def document_info(lengths, positions_global):
    doc_ends = jnp.cumsum(lengths)
    documents = jnp.sum((positions_global[:, None] >= doc_ends[None, :]).astype(jnp.int32), axis=1)
    doc_slots = jnp.arange(lengths.shape[0], dtype=jnp.int32)
    onehot = documents[:, None] == doc_slots[None, :]
    doc_len = jnp.sum(jnp.where(onehot, lengths[None, :], 0), axis=1)
    doc_end = jnp.sum(jnp.where(onehot, doc_ends[None, :], 0), axis=1)
    return (documents, doc_len, positions_global - doc_end + doc_len, onehot)


def block_mask(lengths, query_positions, key_positions):
    query_docs = document_info(lengths, query_positions)[0]
    key_docs = document_info(lengths, key_positions)[0]
    return (
        (key_positions[None, :] >= 0)
        & (key_docs[None, :] == query_docs[:, None])
        & (key_positions[None, :] <= query_positions[:, None])
    )


def rope_tables(positions):
    half_width = HD // 2
    frequency = ROPE_BASE ** (-(jnp.arange(half_width, dtype=jnp.float32) * 2.0 / HD))
    angles = positions.astype(jnp.float32)[:, None] * frequency[None, :]
    angles = jnp.concatenate([angles, angles], axis=1)
    return (jnp.cos(angles), jnp.sin(angles))


def rotate(values, cosine_table, sine_table):
    half_width = values.shape[-1] // 2
    turned = jnp.concatenate([-values[..., half_width:], values[..., :half_width]], axis=-1)
    return values * cosine_table[:, None, :] + turned * sine_table[:, None, :]


def unrotate(gradient, cosine_table, sine_table):
    half_width = gradient.shape[-1] // 2
    scaled = gradient * sine_table[:, None, :]
    back_part = jnp.concatenate([scaled[..., half_width:], -scaled[..., :half_width]], axis=-1)
    return gradient * cosine_table[:, None, :] + back_part


def contract(left, right):
    return lax.dot_general(
        left, right, (((1,), (1,)), ((), ())), preferred_element_type=jnp.float32
    )


def attend_head(queries, key_rows, value_rows, out_grad, allowed):
    score_scale = HD ** (-0.5)
    scores = contract(queries, key_rows) * score_scale
    weights = jnp.where(allowed, jnp.exp(scores), 0.0)
    totals = jnp.sum(weights, axis=1, keepdims=True)
    softmax = weights / totals
    prob_grad = contract(out_grad, value_rows)
    row_delta = jnp.sum(softmax * prob_grad, axis=1, keepdims=True)
    score_grad = (softmax * (prob_grad - row_delta)).astype(jnp.bfloat16)
    query_grad = jnp.dot(score_grad, key_rows, preferred_element_type=jnp.float32) * score_scale
    key_grad = (
        lax.dot_general(
            score_grad, queries, (((0,), (0,)), ((), ())), preferred_element_type=jnp.float32
        )
        * score_scale
    )
    value_grad = lax.dot_general(
        softmax.astype(jnp.bfloat16),
        out_grad,
        (((0,), (0,)), ((), ())),
        preferred_element_type=jnp.float32,
    )
    return (query_grad, key_grad, value_grad, totals, row_delta)


def fold_heads(per_head, kv_count, group_size):
    summed = per_head.reshape(kv_count, group_size, per_head.shape[1], HD).sum(axis=1)
    return jnp.transpose(summed, (1, 0, 2))


def per_device(hidden, norm_gain, w_query, w_key, w_value, upstream, cached, lengths):
    gathered = lax.all_gather(hidden, "tensor", axis=1, tiled=True)
    row_count = gathered.shape[0]
    query_cols = w_query.shape[1]
    key_cols = w_key.shape[1]
    head_count = query_cols // HD
    kv_count = key_cols // HD
    group_size = head_count // kv_count
    hidden_wide = gathered.astype(jnp.float32)
    inverse_scale = lax.rsqrt(jnp.mean(hidden_wide * hidden_wide, axis=1, keepdims=True) + EPSILON)
    normed = (hidden_wide * inverse_scale * norm_gain[None, :]).astype(jnp.bfloat16)
    dp_index = lax.axis_index("dp")
    own_positions = dp_index * row_count + jnp.arange(row_count, dtype=jnp.int32)
    documents, doc_len, positions, onehot = document_info(lengths, own_positions)
    cosine_table, sine_table = rope_tables(positions)
    full_query, full_key, full_value = (
        lax.all_gather(w_query, "dp", axis=0, tiled=True),
        lax.all_gather(w_key, "dp", axis=0, tiled=True),
        lax.all_gather(w_value, "dp", axis=0, tiled=True),
    )
    query_proj = jnp.dot(normed, full_query, preferred_element_type=jnp.float32)
    key_proj = jnp.dot(normed, full_key, preferred_element_type=jnp.float32)
    value_proj = jnp.dot(normed, full_value, preferred_element_type=jnp.float32)
    queries = rotate(
        query_proj.reshape(row_count, head_count, HD), cosine_table, sine_table
    ).astype(jnp.bfloat16)
    key_rows = rotate(key_proj.reshape(row_count, kv_count, HD), cosine_table, sine_table).astype(
        jnp.bfloat16
    )
    value_rows = value_proj.astype(jnp.bfloat16).reshape(row_count, kv_count, HD)
    pooled = (
        jnp.dot(onehot.astype(jnp.float32), cached, precision=lax.Precision.HIGHEST)
        / doc_len.astype(jnp.float32)[:, None]
    )
    out_grad = (
        (upstream.astype(jnp.float32) + pooled)
        .astype(jnp.bfloat16)
        .reshape(row_count, head_count, HD)
    )
    key_list = []
    value_list = []
    for distance in range(HOPS, 0, -1):
        earlier_key, earlier_value = from_behind((key_rows, value_rows), "dp", distance)
        key_list.append(earlier_key)
        value_list.append(earlier_value)
    key_window = jnp.concatenate(key_list + [key_rows], axis=0)
    value_window = jnp.concatenate(value_list + [value_rows], axis=0)
    window = key_window.shape[0]
    window_positions = dp_index * row_count - HOPS * row_count + jnp.arange(window, dtype=jnp.int32)
    allowed = block_mask(lengths, own_positions, window_positions)
    head_queries = jnp.transpose(queries, (1, 0, 2))
    head_grads = jnp.transpose(out_grad, (1, 0, 2))
    head_keys = jnp.transpose(jnp.repeat(key_window, group_size, axis=1), (1, 0, 2))
    head_values = jnp.transpose(jnp.repeat(value_window, group_size, axis=1), (1, 0, 2))

    def one_head(operands):
        return attend_head(operands[0], operands[1], operands[2], operands[3], allowed)

    query_grad, key_grad, value_grad, totals, row_delta = lax.map(
        one_head, (head_queries, head_keys, head_values, head_grads)
    )
    key_sum = fold_heads(key_grad, kv_count, group_size)
    value_sum = fold_heads(value_grad, kv_count, group_size)
    own_key = key_sum[HOPS * row_count :]
    own_value = value_sum[HOPS * row_count :]
    for distance in range(1, HOPS + 1):
        lower = (HOPS - distance) * row_count
        back_key, back_value = (
            from_behind(
                key_sum[lower : lower + row_count].astype(jnp.bfloat16), "dp", -distance
            ).astype(jnp.float32),
            from_behind(
                value_sum[lower : lower + row_count].astype(jnp.bfloat16), "dp", -distance
            ).astype(jnp.float32),
        )
        own_key = own_key + back_key
        own_value = own_value + back_value
    query_done = (
        unrotate(jnp.transpose(query_grad, (1, 0, 2)), cosine_table, sine_table)
        .astype(jnp.bfloat16)
        .reshape(row_count, query_cols)
    )
    key_done = (
        unrotate(own_key, cosine_table, sine_table)
        .astype(jnp.bfloat16)
        .reshape(row_count, key_cols)
    )
    value_done = own_value.astype(jnp.bfloat16).reshape(row_count, key_cols)
    portion = (
        contract(query_done, full_query)
        + contract(key_done, full_key)
        + contract(value_done, full_value)
    )
    own_hidden = hidden.astype(jnp.float32)
    own_cols = hidden.shape[1]
    gain_offset = lax.axis_index("tensor") * own_cols
    own_gain = lax.dynamic_slice_in_dim(norm_gain, gain_offset, own_cols, 0)
    normed_grad = lax.psum_scatter(
        portion.astype(jnp.bfloat16), "tensor", scatter_dimension=1, tiled=True
    ).astype(jnp.float32)
    projection = lax.psum(
        jnp.sum(normed_grad * own_gain[None, :] * own_hidden, axis=1, keepdims=True), "tensor"
    )
    grad_hidden = (
        inverse_scale * own_gain[None, :] * normed_grad
        - own_hidden * (inverse_scale * inverse_scale * inverse_scale) * projection / D
    ).astype(jnp.bfloat16)
    grad_wkey = lax.psum_scatter(
        lax.dot_general(
            normed, key_done, (((0,), (0,)), ((), ())), preferred_element_type=jnp.float32
        ),
        "dp",
        scatter_dimension=0,
        tiled=True,
    )
    return (grad_hidden, grad_wkey)


def solution(mesh):
    placed = (
        P("dp", "tensor"),
        P(),
        P("dp", "tensor"),
        P("dp", "tensor"),
        P("dp", "tensor"),
        P("dp", "tensor"),
        P(None, "tensor"),
        P(),
    )
    return jax.shard_map(
        per_device,
        mesh=mesh,
        in_specs=placed,
        out_specs=(P("dp", "tensor"), P("dp", "tensor")),
        check_vma=False,
    )
```

profile of v0, /device:TPU:0, one launch (start us, length us, event | category | flops | bytes accessed | tf_op | source)
XLA Modules:
  0.0 597.0 jit_solution(3399508541606752690)
XLA Ops:
  11.8 1.7 fusion.35
  16.4 17.2 %all-gather.5.cloned.1.call-done = bf16[128,4096]{1,0:T(8,128)(2,1)} async-done(((bf16[128,2048]{1,0:T(8,128)(2,1)}), bf16[128,4096]{1,0:T(8,128)(2,1)}) %all-gather.5.cloned.1.call-update) | async-done | bytes 1048592 | tf_op jit(solution)/shard_map/all_gather | solution.py:99
  35.6 50.5 %all-gather.11.cloned.1.call-done = bf16[4096,512]{1,0:T(8,128)(2,1)} async-done(((bf16[256,512]{1,0:T(8,128)(2,1)}), bf16[4096,512]{1,0:T(8,128)(2,1)}) %all-gather.11.cloned.1.call-update) | async-done | bytes 4194320 | tf_op jit(solution)/shard_map/all_gather | solution.py:116
  86.2 3.3 convolution_convert_fusion
  89.5 4.1 collective-permute-start.4
  93.6 2.7 collective-permute-start.5
  96.3 41.4 %all-gather.9.cloned.1.call-done = bf16[4096,512]{1,0:T(8,128)(2,1)} async-done(((bf16[256,512]{1,0:T(8,128)(2,1)}), bf16[4096,512]{1,0:T(8,128)(2,1)}) %all-gather.9.cloned.1.call-update) | async-done | bytes 4194320 | tf_op jit(solution)/shard_map/all_gather | solution.py:115
  137.7 2.9 convolution_bitcast_fusion.2
  141.0 3.4 collective-permute-start
  144.4 2.0 collective-permute-start.1
  146.5 3.7 collective-permute-start.2
  150.2 2.5 collective-permute-start.6
  153.6 1.9 collective-permute-start.7
  156.5 6.8 %collective-permute-done.6 = bf16[128,4,128]{2,1,0:T(4,128)(2,1)S(1)} collective-permute-done((bf16[128,4,128]{2,1,0:T(4,128)(2,1)S(1)}, bf16[128,4,128]{2,1,0:T(4,128)(2,1)S(1)}, u32[]{:S(2)}, u32[]{:S(2)}) %collective-permute-start.6) | collective-permute-done | bytes 131104 | tf_op jit(solution)/shard_map/ppermute | solution.py:18
  168.4 105.6 %all-gather.7.cloned.1.call-done = bf16[4096,2048]{1,0:T(8,128)(2,1)} async-done(((bf16[256,2048]{1,0:T(8,128)(2,1)}), bf16[4096,2048]{1,0:T(8,128)(2,1)}) %all-gather.7.cloned.1.call-update) | async-done | bytes 16777232 | tf_op jit(solution)/shard_map/all_gather | solution.py:114
  274.1 8.1 %convolution_bitcast_fusion.1 = f32[16,16,8,128]{3,2,1,0:T(8,128)S(1)} fusion(bf16[4096,2048]{1,0:T(8,128)(2,1)} %all-gather.7.cloned.1.call-done, bf16[128,4096]{1,0:T(8,128)(2,1)S(1)} %copy-done.2, f32[4096]{0:T(1024)S(1)} %copy-done.7, f32[128]{0:T(128)} %copy-done.10), kind=kOutput, calls=%fused_computation.49 | convolution fusion | flops 2149580800 | bytes 18891264 | tf_op jit(solution)/shard_map/dot_general | solution.py:118
  283.9 3.2 broadcast_in_dim.41
  287.1 2.0 broadcast_in_dim.45
  289.1 118.9 %while.15 = (s32[]{:T(128)}, f32[16,128,128]{1,2,0:T(8,128)S(1)}, f32[16,640,128]{2,1,0:T(8,128)}, f32[16,640,128]{2,1,0:T(8,128)}, bf16[16,128,128]{2,1,0:T(8,1...) while((s32[]{:T(128)}, f32[16,128,128]{1,2,0:T(8,128)S(1)}, ...), condition=%wide.region_9.10_spmd.clone, body=%wide.region_6.9_spmd.clone.sunk | while | flops 106266368 | bytes 4077833 | solution.py:156
  291.8 1.7 fusion.101
  293.5 1.8 fusion.102
  299.2 1.7 fusion.101
  301.0 1.8 fusion.102
  306.6 1.7 fusion.101
  308.4 1.8 fusion.102
  314.1 1.7 fusion.101
  315.8 1.8 fusion.102
  321.5 1.7 fusion.101
  323.2 1.8 fusion.102
  328.9 1.7 fusion.101
  330.7 1.8 fusion.102
  336.3 1.7 fusion.101
  338.1 1.8 fusion.102
  343.8 1.7 fusion.101
  345.5 1.8 fusion.102
  351.2 1.7 fusion.101
  352.9 1.9 fusion.102
  358.7 1.7 fusion.101
  360.4 1.8 fusion.102
  366.1 1.7 fusion.101
  367.8 1.8 fusion.102
  373.5 1.7 fusion.101
  375.3 1.8 fusion.102
  381.0 1.7 fusion.101
  382.7 1.8 fusion.102
  388.4 1.7 fusion.101
  390.1 1.8 fusion.102
  395.8 1.8 fusion.101
  397.5 1.8 fusion.102
  403.2 1.7 fusion.101
  404.9 1.8 fusion.102
  408.0 5.0 bitcast_reduce_fusion
  422.8 11.7 %fusion.69 = f32[128,4096]{1,0:T(8,128)S(1)} fusion(bf16[128,2048]{0,1:T(8,128)(2,1)} %bitcast.126, bf16[4096,2048]{1,0:T(8,128)(2,1)} %all-gather.7.cloned.1.call-done), kind=kOutput, calls=%fused_computation.127 | convolution fusion | flops 2147483648 | bytes 19398656 | tf_op jit(solution)/shard_map/dot_general | solution.py:63
  439.7 1.9 fusion.54
  442.6 2.0 collective-permute-done.13
  444.6 1.6 collective-permute-done.14
  446.2 6.0 collective-permute-done.15
  453.6 3.8 convolution_add_fusion.1
  457.4 2.5 fusion.29
  460.1 4.6 fusion.58
  464.7 17.5 %reduce-scatter.3.cloned.1.call-done = bf16[128,2048]{1,0:T(8,128)(2,1)} async-done(((bf16[128,4096]{1,0:T(8,128)(2,1)}), bf16[128,2048]{1,0:T(8,128)(2,1)}) %reduce-scatter.3.cloned.1.call-update) | async-done | bytes 524304 | tf_op jit(solution)/shard_map/reduce_scatter | solution.py:195
  483.5 4.9 psum.7
  488.4 2.3 fusion.37
  490.7 99.4 %reduce-scatter.5.cloned.1.call-done = f32[256,512]{1,0:T(8,128)} async-done(((f32[4096,512]{1,0:T(8,128)}), f32[256,512]{1,0:T(8,128)}) %reduce-scatter.5.cloned.1.call-update) | async-done | bytes 524304 | tf_op jit(solution)/shard_map/reduce_scatter | solution.py:205
  (220 shorter events, 98.4 us)
Async XLA Ops:
  7.2 4.7 copy-start
  7.2 26.4 %all-gather.5.cloned.1.call-start = ((), (), s32[]{:S(2)}) async-start(), calls=%async_computation.2 | async-start | bytes 1572864 | tf_op jit(solution)/shard_map/all_gather | solution.py:99
  7.9 78.2 %all-gather.11.cloned.1.call-start = ((), (), s32[]{:S(2)}) async-start(), calls=%async_computation.5 | async-start | bytes 4456448 | tf_op jit(solution)/shard_map/all_gather | solution.py:116
  8.7 129.1 %all-gather.9.cloned.1.call-start = ((), (), s32[]{:S(2)}) async-start(), calls=%async_computation.4 | async-start | bytes 4456448 | tf_op jit(solution)/shard_map/all_gather | solution.py:115
  9.4 264.7 %all-gather.7.cloned.1.call-start = ((), (), s32[]{:S(2)}) async-start(), calls=%async_computation.3 | async-start | bytes 17825792 | tf_op jit(solution)/shard_map/all_gather | solution.py:114
  10.0 472.2 %reduce-scatter.3.cloned.1.call-start = ((), (), s32[]{:S(2)}) async-start(), calls=%async_computation.6 | async-start | bytes 1572864 | tf_op jit(solution)/shard_map/reduce_scatter | solution.py:195
  11.0 0.8 copy-start.17
  11.1 3.8 copy-start.14
  11.8 74.3 %copy-start.7 = (f32[4096]{0:T(1024)S(1)}, f32[4096]{0:T(1024)}, u32[]{:S(2)}) copy-start(f32[4096]{0:T(1024)} %param.11) | copy-start | bytes 49156
  15.7 70.4 %copy-start.8 = (s32[640]{0:T(1024)}, s32[640]{0:T(1024)S(1)}, u32[]{:S(2)}) copy-start(s32[640]{0:T(1024)S(1)} %iota_add_fusion) | copy-start | bytes 7684
  35.6 102.1 %copy-start.10 = (f32[128]{0:T(128)}, f32[128]{0:T(128)S(1)}, u32[]{:S(2)}) copy-start(f32[128]{0:T(128)S(1)} %get-tuple-element.138) | copy-start | bytes 1540
  86.1 51.6 %copy-start.2 = (bf16[128,4096]{1,0:T(8,128)(2,1)S(1)}, bf16[128,4096]{1,0:T(8,128)(2,1)}, u32[]{:S(2)}) copy-start(bf16[128,4096]{1,0:T(8,128)(2,1)} %all-gather.5.cloned.1.call-done) | copy-start | bytes 3145732
  89.5 60.6 %collective-permute-start.4 = (bf16[128,4,128]{2,1,0:T(4,128)(2,1)S(1)}, bf16[128,4,128]{2,1,0:T(4,128)(2,1)}, u32[]{:S(2)}, u32[]{:S(2)}) collective-permute-start(bf16[128,4,128]{2,1,0:T(4,128)(2,1)S(1)} %reshape.172), channel_id=1, source_target_pairs={{0,8},{2,10},{4,12},{6,14},{8,16},{10,18},{12,20},{14,22},{16,24},... | collective-permute-start | bytes 393224 | tf_op jit(solution)/shard_map/ppermute | solution.py:18
  93.6 60.0 %collective-permute-start.5 = (bf16[128,4,128]{2,1,0:T(4,128)(2,1)S(1)}, bf16[128,4,128]{2,1,0:T(4,128)(2,1)}, u32[]{:S(2)}, u32[]{:S(2)}) collective-permute-start(bf16[128,4,128]{2,1,0:T(4,128)(2,1)S(1)} %reshape.172), channel_id=1, source_target_pairs={{0,6},{2,8},{4,10},{6,12},{8,14},{10,16},{12,18},{14,20},{16,22},{... | collective-permute-start | bytes 393224 | tf_op jit(solution)/shard_map/ppermute | solution.py:18
  141.0 23.9 %collective-permute-start = (bf16[128,4,128]{2,0,1:T(8,128)(2,1)S(1)}, bf16[128,4,128]{2,0,1:T(8,128)(2,1)S(1)}, u32[]{:S(2)}, u32[]{:S(2)}) collective-permute-start(bf16[128,4,128]{2,0,1:T(8,128)(2,1)S(1)} %fusion.53), channel_id=1, source_target_pairs={{0,8},{2,10},{4,12},{6,14},{8,16},{10,18},{12,20},{14,22},{16,24},... | collective-permute-start | bytes 393224 | tf_op jit(solution)/shard_map/ppermute | solution.py:18
  144.4 21.1 %collective-permute-start.1 = (bf16[128,4,128]{2,0,1:T(8,128)(2,1)S(1)}, bf16[128,4,128]{2,0,1:T(8,128)(2,1)S(1)}, u32[]{:S(2)}, u32[]{:S(2)}) collective-permute-start(bf16[128,4,128]{2,0,1:T(8,128)(2,1)S(1)} %fusion.53), channel_id=1, source_target_pairs={{0,6},{2,8},{4,10},{6,12},{8,14},{10,16},{12,18},{14,20},{16,22},{... | collective-permute-start | bytes 393224 | tf_op jit(solution)/shard_map/ppermute | solution.py:18
  146.5 19.9 %collective-permute-start.2 = (bf16[128,4,128]{2,0,1:T(8,128)(2,1)S(1)}, bf16[128,4,128]{2,0,1:T(8,128)(2,1)S(1)}, u32[]{:S(2)}, u32[]{:S(2)}) collective-permute-start(bf16[128,4,128]{2,0,1:T(8,128)(2,1)S(1)} %fusion.53), channel_id=1, source_target_pairs={{0,4},{2,6},{4,8},{6,10},{8,12},{10,14},{12,16},{14,18},{16,20},{1... | collective-permute-start | bytes 393224 | tf_op jit(solution)/shard_map/ppermute | solution.py:18
  150.2 13.2 %collective-permute-start.6 = (bf16[128,4,128]{2,1,0:T(4,128)(2,1)S(1)}, bf16[128,4,128]{2,1,0:T(4,128)(2,1)S(1)}, u32[]{:S(2)}, u32[]{:S(2)}) collective-permute-start(bf16[128,4,128]{2,1,0:T(4,128)(2,1)S(1)} %reshape.172), channel_id=1, source_target_pairs={{0,4},{2,6},{4,8},{6,10},{8,12},{10,14},{12,16},{14,18},{16,20},{1... | collective-permute-start | bytes 393224 | tf_op jit(solution)/shard_map/ppermute | solution.py:18
  153.6 11.1 %collective-permute-start.7 = (bf16[128,4,128]{2,1,0:T(4,128)(2,1)S(1)}, bf16[128,4,128]{2,1,0:T(4,128)(2,1)S(1)}, u32[]{:S(2)}, u32[]{:S(2)}) collective-permute-start(bf16[128,4,128]{2,1,0:T(4,128)(2,1)S(1)} %reshape.172), channel_id=1, source_target_pairs={{0,2},{2,4},{4,6},{6,8},{8,10},{10,12},{12,14},{14,16},{16,18},{18... | collective-permute-start | bytes 393224 | tf_op jit(solution)/shard_map/ppermute | solution.py:18
  163.3 3.7 collective-permute-start.3
  283.9 5.2 copy-start.9
  283.9 5.2 copy-start.12
  283.9 5.2 copy-start.15
  283.9 5.2 copy-start.16
  283.9 5.2 copy-start.18
  413.0 7.2 %copy-start.3 = (f32[4,640,128]{2,1,0:T(8,128)}, f32[4,640,128]{2,1,0:T(8,128)S(1)}, u32[]{:S(2)}) copy-start(f32[4,640,128]{2,1,0:T(8,128)S(1)} %get-tuple-element.142) | copy-start | bytes 3932164
  413.0 7.2 %copy-start.4 = (f32[4,640,128]{2,1,0:T(8,128)}, f32[4,640,128]{2,1,0:T(8,128)S(1)}, u32[]{:S(2)}) copy-start(f32[4,640,128]{2,1,0:T(8,128)S(1)} %get-tuple-element.141) | copy-start | bytes 3932164
  414.1 20.4 %collective-permute-start.10 = (bf16[128,4,128]{2,0,1:T(8,128)(2,1)}, bf16[128,4,128]{2,0,1:T(8,128)(2,1)S(1)}, u32[]{:S(2)}, u32[]{:S(2)}) collective-permute-start(bf16[128,4,128]{2,0,1:T(8,128)(2,1)} %get-tuple-element.129), channel_id=1, source_target_pairs={{6,0},{8,2},{10,4},{12,6},{14,8},{16,10},{18,12},{20,14},{22,16},{... | collective-permute-start | bytes 393224 | tf_op jit(solution)/shard_map/ppermute | solution.py:18
  415.4 20.4 %collective-permute-start.11 = (bf16[128,4,128]{2,0,1:T(8,128)(2,1)}, bf16[128,4,128]{2,0,1:T(8,128)(2,1)S(1)}, u32[]{:S(2)}, u32[]{:S(2)}) collective-permute-start(bf16[128,4,128]{2,0,1:T(8,128)(2,1)} %get-tuple-element.128), channel_id=1, source_target_pairs={{8,0},{10,2},{12,4},{14,6},{16,8},{18,10},{20,12},{22,14},{24,16},... | collective-permute-start | bytes 393224 | tf_op jit(solution)/shard_map/ppermute | solution.py:18
  416.7 20.4 %collective-permute-start.8 = (bf16[128,4,128]{2,0,1:T(8,128)(2,1)}, bf16[128,4,128]{2,0,1:T(8,128)(2,1)}, u32[]{:S(2)}, u32[]{:S(2)}) collective-permute-start(bf16[128,4,128]{2,0,1:T(8,128)(2,1)} %get-tuple-element.127), channel_id=1, source_target_pairs={{2,0},{4,2},{6,4},{8,6},{10,8},{12,10},{14,12},{16,14},{18,16},{20... | collective-permute-start | bytes 393224 | tf_op jit(solution)/shard_map/ppermute | solution.py:18
  418.0 20.4 %collective-permute-start.9 = (bf16[128,4,128]{2,0,1:T(8,128)(2,1)}, bf16[128,4,128]{2,0,1:T(8,128)(2,1)}, u32[]{:S(2)}, u32[]{:S(2)}) collective-permute-start(bf16[128,4,128]{2,0,1:T(8,128)(2,1)} %get-tuple-element.130), channel_id=1, source_target_pairs={{4,0},{6,2},{8,4},{10,6},{12,8},{14,10},{16,12},{18,14},{20,16},{2... | collective-permute-start | bytes 393224 | tf_op jit(solution)/shard_map/ppermute | solution.py:18
  420.2 22.5 %collective-permute-start.12 = (bf16[128,4,128]{2,0,1:T(8,128)(2,1)}, bf16[128,4,128]{2,0,1:T(8,128)(2,1)}, u32[]{:S(2)}, u32[]{:S(2)}) collective-permute-start(bf16[128,4,128]{2,0,1:T(8,128)(2,1)} %get-tuple-element.123), channel_id=1, source_target_pairs={{2,0},{4,2},{6,4},{8,6},{10,8},{12,10},{14,12},{16,14},{18,16},{20... | collective-permute-start | bytes 393224 | tf_op jit(solution)/shard_map/ppermute | solution.py:18
  434.5 10.1 %collective-permute-start.13 = (bf16[128,4,128]{2,0,1:T(8,128)(2,1)}, bf16[128,4,128]{2,0,1:T(8,128)(2,1)}, u32[]{:S(2)}, u32[]{:S(2)}) collective-permute-start(bf16[128,4,128]{2,0,1:T(8,128)(2,1)} %get-tuple-element.126), channel_id=1, source_target_pairs={{4,0},{6,2},{8,4},{10,6},{12,8},{14,10},{16,12},{18,14},{20,16},{2... | collective-permute-start | bytes 393224 | tf_op jit(solution)/shard_map/ppermute | solution.py:18
  435.8 10.4 %collective-permute-start.14 = (bf16[128,4,128]{2,0,1:T(8,128)(2,1)}, bf16[128,4,128]{2,0,1:T(8,128)(2,1)}, u32[]{:S(2)}, u32[]{:S(2)}) collective-permute-start(bf16[128,4,128]{2,0,1:T(8,128)(2,1)} %get-tuple-element.125), channel_id=1, source_target_pairs={{6,0},{8,2},{10,4},{12,6},{14,8},{16,10},{18,12},{20,14},{22,16},{... | collective-permute-start | bytes 393224 | tf_op jit(solution)/shard_map/ppermute | solution.py:18
  437.1 15.1 %collective-permute-start.15 = (bf16[128,4,128]{2,0,1:T(8,128)(2,1)}, bf16[128,4,128]{2,0,1:T(8,128)(2,1)}, u32[]{:S(2)}, u32[]{:S(2)}) collective-permute-start(bf16[128,4,128]{2,0,1:T(8,128)(2,1)} %get-tuple-element.124), channel_id=1, source_target_pairs={{8,0},{10,2},{12,4},{14,6},{16,8},{18,10},{20,12},{22,14},{24,16},... | collective-permute-start | bytes 393224 | tf_op jit(solution)/shard_map/ppermute | solution.py:18
  453.5 3.9 copy-start.6
  457.4 2.6 copy-start.11
  460.0 130.2 %reduce-scatter.5.cloned.1.call-start = ((), (), s32[]{:S(2)}) async-start(), calls=%async_computation.7 | async-start | bytes 8912896 | tf_op jit(solution)/shard_map/reduce_scatter | solution.py:205
  464.7 17.5 %copy-start.5 = (bf16[128,2048]{1,0:T(8,128)(2,1)S(1)}, bf16[128,2048]{1,0:T(8,128)(2,1)}, u32[]{:S(2)}) copy-start(bf16[128,2048]{1,0:T(8,128)(2,1)} %param.10) | copy-start | bytes 1572868
  464.7 23.8 %copy-start.13 = (f32[128]{0:T(128)S(1)}, f32[128]{0:T(128)}, u32[]{:S(2)}) copy-start(f32[128]{0:T(128)} %get-tuple-element.137) | copy-start | bytes 1540
  464.7 125.5 %copy-start.1 = (f32[16,2048]{1,0:T(8,128)S(1)}, f32[16,2048]{1,0:T(8,128)}, u32[]{:S(2)}) copy-start(f32[16,2048]{1,0:T(8,128)} %param.16) | copy-start | bytes 393220
Sparse Core Ops, SparseCore 0:
  9.5 23.9 all-gather.4
  35.7 50.3 all-gather.10
  88.3 49.3 all-gather.8
  139.7 134.3 all-gather.6
  460.1 22.0 reduce-scatter.2
  486.7 103.4 reduce-scatter.4
where the time goes:
time: 601 us; the launch traced here: 597 us
  waiting for transfers between devices  351 us (58%)
  matrix products  153 us (25%)
  starting transfers between devices  32.3 us (5%)
  other arithmetic  22.8 us (4%)
  local copies, waits for them, and re-layouts  17.6 us (3%)
  between operations  14.7 us (2%)
    all_gather x1, waiting for transfers between devices, per_device(): lax.all_gather(w_query, 'dp', axis=0, tiled=True)  106 us
    reduce_scatter x1, waiting for transfers between devices, per_device(): lax.psum_scatter(lax.dot_general(normed, key_done, (((0,), (0,)), ((), ()...  99.4 us
    dot_general x35, matrix products, contract(): lax.dot_general(left, right, (((1,), (1,)), ((), ())), preferred_element_...  58.1 us
    all_gather x1, waiting for transfers between devices, per_device(): lax.all_gather(w_value, 'dp', axis=0, tiled=True)  50.5 us
    all_gather x1, waiting for transfers between devices, per_device(): lax.all_gather(w_key, 'dp', axis=0, tiled=True)  41.4 us
    ppermute x16, starting transfers between devices, from_behind(): return lax.ppermute(block, axis, route)  32.1 us
    dot_general x16, matrix products, attend_head(): lax.dot_general(softmax.astype(jnp.bfloat16), out_grad, (((0,), (0,)), ((...  29 us
    dot_general x16, matrix products, attend_head(): lax.dot_general(score_grad, queries, (((0,), (0,)), ((), ())), preferred_...  27.7 us
  transfers between devices with their start and end apart: 22, of which 10 were waited for; matrix products, arithmetic and copies ran while one was open for 8% of the time, Pallas kernels for 0%

commit v1 on v0

--- a/solution.py
+++ b/solution.py
@@ -1,11 +1,16 @@
+from functools import partial
+
 import jax
 import jax.numpy as jnp
 from jax import lax
+from jax.experimental import pallas as pl
+from jax.experimental.pallas import tpu as pltpu
 from jax.sharding import PartitionSpec as P
 
 D = 4096
 HD = 128
 HOPS = 4
+LONGEST = 512
 
 
 EPSILON = 1e-05
@@ -95,7 +100,7 @@
     return jnp.transpose(summed, (1, 0, 2))
 
 
-def per_device(hidden, norm_gain, w_query, w_key, w_value, upstream, cached, lengths):
+def plain_device(hidden, norm_gain, w_query, w_key, w_value, upstream, cached, lengths):
     gathered = lax.all_gather(hidden, "tensor", axis=1, tiled=True)
     row_count = gathered.shape[0]
     query_cols = w_query.shape[1]
@@ -213,6 +218,376 @@
     return (grad_hidden, grad_wkey)
 
 
+def norm_kernel(where, near_ref, far_ref, gain_ref, *outs):
+    pieces, inv_ref = outs[:-1], outs[-1]
+    ring, group, tensor = where[0], where[1], where[2]
+    ring_size = len(pieces)
+    members = where.shape[0] - 3
+    step = pieces[0].shape[1] // members
+
+    def write(ref):
+        total = jnp.zeros((ref.shape[2], 1), jnp.float32)
+        for half in range(2):
+            wide = ref[0, half].astype(jnp.float32)
+            total = total + jnp.sum(wide * wide, axis=1, keepdims=True)
+        inverse = lax.rsqrt(total / D + EPSILON)
+        inv_ref[...] = jnp.broadcast_to(inverse, inv_ref.shape)
+        planes_per_half = ring_size // 2
+        for s in range(ring_size):
+            plane = lax.rem(ring - s + ring_size, ring_size)
+            half = lax.rem(plane // planes_per_half + tensor, 2)
+            for d in range(members):
+                inner = lax.rem(plane, planes_per_half) * (members * step) + where[3 + d] * step
+                inner = pl.multiple_of(inner, step)
+                outer = pl.multiple_of((plane * members + where[3 + d]) * step, step)
+                wide = ref[0, half, :, pl.ds(inner, step)].astype(jnp.float32)
+                scaled = wide * inverse * gain_ref[:, pl.ds(outer, step)]
+                pieces[s][:, d * step : (d + 1) * step] = scaled.astype(jnp.bfloat16)
+
+    @pl.when(pl.program_id(1) == 0)
+    def _():
+        write(near_ref)
+
+    @pl.when(pl.program_id(1) == 1)
+    def _():
+        write(far_ref)
+
+
+def norm_pieces(where, near, far, gain, ring_size):
+    rows, half = near.shape[2], near.shape[3]
+    members = where.shape[0] - 3
+    tokens = members * rows
+    width = 2 * half // ring_size
+    spec = pl.BlockSpec((1, 2, rows, half), lambda u, v, w: (u, 0, 0, 0))
+
+    def out_row(u, v, w):
+        return (w[3 + 2 * u + v], 0)
+
+    return pl.pallas_call(
+        norm_kernel,
+        grid_spec=pltpu.PrefetchScalarGridSpec(
+            num_scalar_prefetch=1,
+            grid=(2, 2),
+            in_specs=[spec, spec, pl.BlockSpec((1, 2 * half), lambda u, v, w: (0, 0))],
+            out_specs=[pl.BlockSpec((rows, width), out_row)] * ring_size
+            + [pl.BlockSpec((rows, 128), out_row)],
+        ),
+        out_shape=[jax.ShapeDtypeStruct((tokens, width), jnp.bfloat16)] * ring_size
+        + [jax.ShapeDtypeStruct((tokens, 128), jnp.float32)],
+        cost_estimate=pl.CostEstimate(
+            flops=8 * tokens * 2 * half, bytes_accessed=8 * tokens * half, transcendentals=tokens
+        ),
+    )(where, near, far, gain)
+
+
+def attend_kernel(heads, rows, q_ref, g_ref, k_ref, kt_ref, v_ref, cos_ref, sin_ref, low_ref,
+                  dq_ref, dkv_ref, qs, gs, ps, ds):
+    scale = HD ** (-0.5)
+    window = ps.shape[0]
+
+    @pl.when(pl.program_id(0) == 0)
+    def _():
+        dkv_ref[...] = jnp.zeros_like(dkv_ref)
+
+    base = pl.multiple_of(pl.program_id(0) * rows, rows)
+    cosine, sine = cos_ref[...], sin_ref[...]
+    for h in range(heads):
+        lanes = slice(h * HD, (h + 1) * HD)
+        there = slice(h * rows, (h + 1) * rows)
+        u = q_ref[:, lanes]
+        qs[there, :] = (u * cosine + pltpu.roll(u, HD // 2, 1) * sine).astype(jnp.bfloat16)
+        gs[there, :] = g_ref[:, lanes]
+    keys = k_ref[pl.ds(base, window), :]
+    values = v_ref[pl.ds(base, window), :]
+    scores = contract(keys, qs[...]) * scale
+    prob_grads = contract(values, gs[...])
+    key_at = lax.broadcasted_iota(jnp.int32, (window, rows), 0)
+    query_at = lax.broadcasted_iota(jnp.int32, (window, rows), 1) + (window - rows)
+    allowed = (key_at >= low_ref[...] - base) & (key_at <= query_at)
+    for h in range(heads):
+        there = slice(h * rows, (h + 1) * rows)
+        weights = jnp.where(allowed, jnp.exp(scores[:, there]), 0.0)
+        softmax = weights * (1.0 / jnp.sum(weights, axis=0, keepdims=True))
+        prob_grad = prob_grads[:, there]
+        row_delta = jnp.sum(softmax * prob_grad, axis=0, keepdims=True)
+        ps[:, there] = softmax.astype(jnp.bfloat16)
+        ds[:, there] = (softmax * (prob_grad - row_delta)).astype(jnp.bfloat16)
+    dkv_ref[pl.ds(base, window), :HD] += (
+        jnp.dot(ds[...], qs[...], preferred_element_type=jnp.float32) * scale
+    )
+    dkv_ref[pl.ds(base, window), HD:] += jnp.dot(
+        ps[...], gs[...], preferred_element_type=jnp.float32
+    )
+    turned = jnp.dot(
+        kt_ref[:, pl.ds(base, window)], ds[...], preferred_element_type=jnp.float32
+    )
+    for h in range(heads):
+        there = slice(h * rows, (h + 1) * rows)
+        grad = turned[:, there].T * scale
+        back = grad * cosine - pltpu.roll(grad, HD // 2, 1) * sine
+        dq_ref[:, h * HD : (h + 1) * HD] = back.astype(jnp.bfloat16)
+
+
+def attend(q_proj, grads, keys, keys_turned, values, cosine, sine, low):
+    tokens, width = q_proj.shape
+    heads, rows = width // HD, 128
+    total = keys.shape[0]
+    window = total - tokens + rows
+    whole = lambda a: pl.BlockSpec(a.shape, lambda i: (0, 0))
+    by_rows = lambda w: pl.BlockSpec((rows, w), lambda i: (i, 0))
+    return pl.pallas_call(
+        partial(attend_kernel, heads, rows),
+        grid=(tokens // rows,),
+        in_specs=[by_rows(width), by_rows(width), whole(keys), whole(keys_turned), whole(values),
+                  by_rows(HD), by_rows(HD), pl.BlockSpec((1, rows), lambda i: (0, i))],
+        out_specs=[by_rows(width), pl.BlockSpec((total, 2 * HD), lambda i: (0, 0))],
+        out_shape=[jax.ShapeDtypeStruct((tokens, width), jnp.bfloat16),
+                   jax.ShapeDtypeStruct((total, 2 * HD), jnp.float32)],
+        scratch_shapes=[pltpu.VMEM((heads * rows, HD), jnp.bfloat16)] * 2
+        + [pltpu.VMEM((window, heads * rows), jnp.bfloat16)] * 2,
+        cost_estimate=pl.CostEstimate(
+            flops=10 * tokens * window * width, bytes_accessed=12 * tokens * width,
+            transcendentals=tokens * window * heads,
+        ),
+    )(q_proj, grads, keys, keys_turned, values, cosine, sine, low)
+
+
+def spread_kernel(chunks, ring_size, where, *refs):
+    grads = refs[:chunks]
+    weights = refs[chunks : chunks + chunks * ring_size]
+    out_ref = refs[-1]
+    ring, tensor = where[0], where[2]
+    members = where.shape[0] - 3
+    step = weights[0].shape[0] // members
+    rows = out_ref.shape[3]
+    planes_per_half = ring_size // 2
+    s = pl.program_id(0)
+    plane = lax.rem(ring - s + ring_size, ring_size)
+    half = lax.rem(plane // planes_per_half + tensor, 2)
+    for piece in range(ring_size):
+
+        @pl.when(s == piece)
+        def _():
+            for d in range(members):
+                inner = lax.rem(plane, planes_per_half) * (members * step) + where[3 + d] * step
+                inner = pl.multiple_of(inner, step)
+                total = None
+                for c in range(chunks):
+                    term = contract(
+                        grads[c][...], weights[c * ring_size + piece][d * step : (d + 1) * step, :]
+                    )
+                    total = term if total is None else total + term
+                total = total.astype(jnp.bfloat16)
+                for owner in range(members):
+                    for v in range(2):
+                        for u in range(members // 2):
+
+                            @pl.when(where[3 + owner] == 2 * u + v)
+                            def _():
+                                out_ref[v, u, half, :, pl.ds(inner, step)] = total[
+                                    owner * rows : (owner + 1) * rows, :
+                                ]
+
+
+def spread(where, grads, weights, ring_size):
+    tokens = grads[0].shape[0]
+    members = where.shape[0] - 3
+    rows = tokens // members
+    width = weights[0].shape[0] * ring_size
+    whole = lambda a: pl.BlockSpec(a.shape, lambda i, w: (0, 0))
+    shape = (2, members // 2, 2, rows, width // 2)
+    return pl.pallas_call(
+        partial(spread_kernel, len(grads), ring_size),
+        grid_spec=pltpu.PrefetchScalarGridSpec(
+            num_scalar_prefetch=1,
+            grid=(ring_size,),
+            in_specs=[whole(a) for a in grads] + [whole(a) for a in weights],
+            out_specs=pl.BlockSpec(shape, lambda i, w: (0, 0, 0, 0, 0)),
+        ),
+        out_shape=jax.ShapeDtypeStruct(shape, jnp.bfloat16),
+        cost_estimate=pl.CostEstimate(
+            flops=2 * tokens * width * sum(a.shape[1] for a in grads),
+            bytes_accessed=4 * tokens * width,
+            transcendentals=0,
+        ),
+    )(where, *grads, *weights)
+
+
+def grouped_device(hidden, norm_gain, w_query, w_key, w_value, upstream, cached, lengths):
+    rows, half = hidden.shape
+    kv_count = w_key.shape[1] // HD
+    query_width = w_query.shape[1] // kv_count
+    members = kv_count
+    devices, tensors = lax.axis_size("dp"), lax.axis_size("tensor")
+    ring_size = devices // members
+    tokens = members * rows
+    weight_rows = w_key.shape[0]
+    me, tensor = lax.axis_index("dp"), lax.axis_index("tensor")
+    ring, group = me // members, me % members
+    partners = [jnp.bitwise_xor(group, d) for d in range(members)]
+    where = jnp.stack([ring, group, tensor] + partners).astype(jnp.int32)
+
+    def to_partner(block, d):
+        return lax.ppermute(block, "dp", [(i, i ^ d) for i in range(devices)])
+
+    def to_side(block):
+        return lax.ppermute(block, "tensor", [(i, i ^ 1) for i in range(tensors)])
+
+    def to_corner(block, d):
+        route = [(i * 2 + t, (i ^ d) * 2 + (t ^ 1)) for i in range(devices) for t in range(2)]
+        return lax.ppermute(block, ("dp", "tensor"), route)
+
+    def along(block, distance):
+        return lax.ppermute(
+            block, "dp", [(i, (i + distance * members) % devices) for i in range(devices)]
+        )
+
+    def columns(array, owner, width):
+        return lax.dynamic_slice_in_dim(array, owner * width, width, 1)
+
+    def pack_kv(owner):
+        return jnp.concatenate([columns(w_key, owner, HD), columns(w_value, owner, HD)], axis=1)
+
+    def pack_q(owner):
+        return jnp.concatenate(
+            [columns(w_query, owner, query_width), columns(upstream, owner, query_width)], axis=0
+        )
+
+    kv_parts = [pack_kv(group)] + [to_partner(pack_kv(partners[d]), d) for d in range(1, members)]
+    q_parts = [pack_q(group)] + [to_partner(pack_q(partners[d]), d) for d in range(1, members)]
+    kv_own = jnp.concatenate(kv_parts, axis=0)
+    q_own = jnp.concatenate([p[:weight_rows] for p in q_parts], axis=0)
+    chunk_width = 2 * HD
+    q_chunks = query_width // chunk_width
+
+    across = to_partner(hidden, 2)
+    near = jnp.stack(
+        [jnp.stack([hidden, to_side(hidden)]), jnp.stack([across, to_corner(hidden, 2)])]
+    )
+    far = to_partner(near, 1)
+    *normed, inverse = norm_pieces(where, near, far, norm_gain[None, :], ring_size)
+
+    def circulate(own):
+        pieces = [own]
+        for _ in range(ring_size - 1):
+            pieces.append(along(pieces[-1], 1))
+        return pieces
+
+    def project(pieces):
+        total = None
+        for s in range(ring_size):
+            term = jnp.dot(normed[s], pieces[s], preferred_element_type=jnp.float32)
+            total = term if total is None else total + term
+        return total
+
+    first = ring * tokens
+    token_positions = first + jnp.arange(tokens, dtype=jnp.int32)
+    _, doc_len, positions, onehot = document_info(lengths, token_positions)
+    cosine, sine = rope_tables(positions)
+    sign = jnp.where(jnp.arange(HD) < HD // 2, -1.0, 1.0).astype(jnp.float32)
+    sine = sine * sign[None, :]
+    low = (token_positions - positions - first + LONGEST)[None, :]
+
+    def place(parts):
+        stacked = jnp.stack(parts)
+        return [
+            lax.dynamic_index_in_dim(stacked, jnp.bitwise_xor(group, o), 0, keepdims=False)
+            for o in range(members)
+        ]
+
+    up_own = jnp.concatenate(place([p[weight_rows:] for p in q_parts]), axis=0)
+    pooled = (
+        jnp.dot(
+            onehot.astype(jnp.float32),
+            columns(cached, group, query_width),
+            precision=lax.Precision.HIGHEST,
+        )
+        / doc_len.astype(jnp.float32)[:, None]
+    )
+    out_grad = (up_own.astype(jnp.float32) + pooled).astype(jnp.bfloat16)
+
+    kv_pieces = circulate(kv_own)
+    q_pieces = [
+        circulate(q_own[:, c * chunk_width : (c + 1) * chunk_width]) for c in range(q_chunks)
+    ]
+    kv_proj = project(kv_pieces)
+    key_proj = kv_proj[:, :HD]
+    key_own = key_proj * cosine + jnp.roll(key_proj, HD // 2, axis=1) * sine
+    kv_rows = jnp.concatenate([key_own, kv_proj[:, HD:]], axis=1).astype(jnp.bfloat16)
+    halo = lax.ppermute(kv_rows, "dp", [(i, i + members) for i in range(devices - members)])
+    kv_all = jnp.concatenate([halo, kv_rows], axis=0)
+    keys, values = kv_all[:, :HD], kv_all[:, HD:]
+    keys_turned = keys.T
+    query_dones, kv_sum = [], None
+    for c in range(q_chunks):
+        query_done, kv_grad = attend(
+            project(q_pieces[c]),
+            out_grad[:, c * chunk_width : (c + 1) * chunk_width],
+            keys, keys_turned, values, cosine, sine, low,
+        )
+        query_dones.append(query_done)
+        kv_sum = kv_grad if kv_sum is None else kv_sum + kv_grad
+    back = lax.ppermute(
+        kv_sum[:LONGEST].astype(jnp.bfloat16),
+        "dp",
+        [(i + members, i) for i in range(devices - members)],
+    )
+    kv_total = kv_sum[LONGEST:] + back.astype(jnp.float32)
+    key_grad = kv_total[:, :HD]
+    key_done = (key_grad * cosine - jnp.roll(key_grad, HD // 2, axis=1) * sine).astype(jnp.bfloat16)
+    kv_done = jnp.concatenate([key_done, kv_total[:, HD:].astype(jnp.bfloat16)], axis=1)
+
+    key_dones = jnp.concatenate(
+        place([key_done] + [to_partner(key_done, d) for d in range(1, members)]), axis=1
+    )
+    grad_wkey = None
+    for s in range(ring_size):
+        term = lax.dot_general(
+            normed[s][:, :weight_rows],
+            key_dones,
+            (((0,), (0,)), ((), ())),
+            preferred_element_type=jnp.float32,
+        )
+        if s:
+            term = along(term.astype(jnp.bfloat16), -s).astype(jnp.float32)
+        grad_wkey = term if grad_wkey is None else grad_wkey + term
+
+    weights = [piece for pieces in q_pieces + [kv_pieces] for piece in pieces]
+    owned = spread(where, query_dones + [kv_done], weights, ring_size)
+    wide = lambda a: a.astype(jnp.float32)
+    narrow = lambda a: a.astype(jnp.bfloat16)
+    both = narrow(wide(owned[0]) + wide(to_partner(owned[1], 1)))
+    cut = half // 2
+    left = wide(both[0, :, :, :cut]) + wide(to_partner(both[1, :, :, :cut], 2))
+    right = wide(both[:, 0, :, cut:]) + wide(to_side(both[:, 1, :, cut:]))
+    left_sum = left[0] + wide(to_side(narrow(left[1])))
+    right_sum = right[0] + wide(to_partner(narrow(right[1]), 2))
+    normed_grad = jnp.concatenate([left_sum, right_sum], axis=1)
+    own_hidden = wide(hidden)
+    own_gain = lax.dynamic_slice_in_dim(norm_gain, tensor * half, half, 0)
+    own_inverse = lax.dynamic_slice_in_dim(inverse, group * rows, rows, 0)[:, :1]
+    part = jnp.sum(normed_grad * own_gain[None, :] * own_hidden, axis=1)[None, :]
+    projection = (part + to_side(part)).reshape(rows, 1)
+    grad_hidden = (
+        own_inverse * own_gain[None, :] * normed_grad
+        - own_hidden * (own_inverse * own_inverse * own_inverse) * projection / D
+    ).astype(jnp.bfloat16)
+    return (grad_hidden, grad_wkey)
+
+
+def per_device(hidden, norm_gain, w_query, w_key, w_value, upstream, cached, lengths):
+    members = w_key.shape[1] // HD
+    devices = lax.axis_size("dp")
+    grouped = (
+        lax.axis_size("tensor") == 2
+        and members == 4
+        and devices == 4 * members
+        and members * hidden.shape[0] == LONGEST
+    )
+    run = grouped_device if grouped else plain_device
+    return run(hidden, norm_gain, w_query, w_key, w_value, upstream, cached, lengths)
+
+
 def solution(mesh):
     placed = (
         P("dp", "tensor"),

time: 601 us -> 270 us (0.45)
  waiting for transfers between devices: 351 us -> 146 us
  matrix products: 153 us -> 20.4 us
  Pallas kernels: 0 us -> 39 us
  between operations: 14.7 us -> 1.45 us
  other arithmetic: 22.8 us -> 15.6 us
    all_gather x4 -> x0, waiting for transfers between devices: 215 us -> none  [the longest x1 106 us: per_device(): lax.all_gather(w_query, 'dp', axis=0, tiled=True)]
    dot_general x88 -> x17, matrix products: 153 us -> 20.4 us  [the longest x12 15.7 us: project(): term = jnp.dot(normed[s], pieces[s], preferred_element_type=jnp.float32)]
    ppermute x16 -> x33, waiting for transfers between devices: 16.4 us -> 146 us  [the longest x12 82.9 us: along(): lax.ppermute(block, 'dp', [(i, (i + distance * members) % devices) for i...]
    reduce_scatter x2 -> x0, waiting for transfers between devices: 117 us -> none  [the longest x1 99.4 us: per_device(): lax.psum_scatter(lax.dot_general(normed, key_done, (((0,), (0,)), ((), ()...]
    pallas_call x0 -> x4, Pallas kernels: none -> 39 us  [the longest x1 17.4 us: spread(): pl.pallas_call(partial(spread_kernel, len(grads), ring_size), grid_spec=p...]
    reduce_sum x3 -> x1, other arithmetic: 7.78 us -> 0.23 us  [grouped_device(): jnp.sum(normed_grad * own_gain[None, :] * own_hidden, axis=1)[None, :]]
    ppermute x16 -> x33, starting transfers between devices: 32.1 us -> 30.3 us  [the longest x12 9.67 us: along(): lax.ppermute(block, 'dp', [(i, (i + distance * members) % devices) for i...]
  transfers between devices with their start and end apart: 22 -> 33, of which waited for: 10 -> 20; matrix products, arithmetic and copies ran while one was open for 8% -> 14% of each run, Pallas kernels for 0% -> 3%
where the time goes in v1:
time: 270 us; the launch traced here: 269 us
  waiting for transfers between devices  146 us (54%)
  Pallas kernels  39 us (14%)
  starting transfers between devices  30.3 us (11%)
  matrix products  20.4 us (8%)
  local copies, waits for them, and re-layouts  16.4 us (6%)
  other arithmetic  15.6 us (6%)
    ppermute x12, waiting for transfers between devices, along(): lax.ppermute(block, 'dp', [(i, (i + distance * members) % devices) for i...  82.9 us
    ppermute x14, waiting for transfers between devices, to_partner(): return lax.ppermute(block, 'dp', [(i, i ^ d) for i in range(devices)])  44.9 us
    pallas_call x1, Pallas kernels, spread(): pl.pallas_call(partial(spread_kernel, len(grads), ring_size), grid_spec=p...  17.4 us
    dot_general x12, matrix products, project(): term = jnp.dot(normed[s], pieces[s], preferred_element_type=jnp.float32)  15.7 us
    pallas_call x2, Pallas kernels, attend(): pl.pallas_call(partial(attend_kernel, heads, rows), grid=(tokens // rows,...  14.2 us
    ppermute x12, starting transfers between devices, along(): lax.ppermute(block, 'dp', [(i, (i + distance * members) % devices) for i...  9.67 us
    ppermute x1, waiting for transfers between devices, grouped_device(): lax.ppermute(kv_sum[:LONGEST].astype(jnp.bfloat16), 'dp', [(i + members,...  9.2 us
    ppermute x14, starting transfers between devices, to_partner(): return lax.ppermute(block, 'dp', [(i, i ^ d) for i in range(devices)])  8.96 us
  transfers between devices with their start and end apart: 33, of which 20 were waited for; matrix products, arithmetic and copies ran while one was open for 14% of the time, Pallas kernels for 3%

profile of v1, /device:TPU:0, one launch (start us, length us, event | category | flops | bytes accessed | tf_op | source)
XLA Modules:
  0.0 269.3 jit_solution(3094649551097915882)
XLA Ops:
  0.7 4.0 %collective-permute-start.2 = (bf16[128,2048]{1,0:T(8,128)(2,1)}, bf16[128,2048]{1,0:T(8,128)(2,1)S(1)}, u32[]{:S(2)}, u32[]{:S(2)}) collective-permute-start(bf16[128,2048]{1,0:T(8,128)(2,1)} %param.8), channel_id=1, source_target_pairs={{0,5},{1,4},{2,7},{3,6},{4,1},{5,0},{6,3},{7,2},{8,13},{9,12},{10,... | collective-permute-start | bytes 1572872 | tf_op jit(solution)/shard_map/ppermute | solution.py:438
  5.3 2.0 constant_dynamic-slice_fusion.14
  8.1 2.0 collective-permute-start.5
  11.7 6.0 %collective-permute-done.2 = bf16[128,2048]{1,0:T(8,128)(2,1)S(1)} collective-permute-done((bf16[128,2048]{1,0:T(8,128)(2,1)}, bf16[128,2048]{1,0:T(8,128)(2,1)S(1)}, u32[]{:S(2)}, u32[]{:S(2)}) %collective-permute-start.2) | collective-permute-done | bytes 524320 | tf_op jit(solution)/shard_map/ppermute | solution.py:438
  17.7 11.8 %collective-permute-done.1 = bf16[128,2048]{1,0:T(8,128)(2,1)S(1)} collective-permute-done((bf16[128,2048]{1,0:T(8,128)(2,1)}, bf16[128,2048]{1,0:T(8,128)(2,1)S(1)}, u32[]{:S(2)}, u32[]{:S(2)}) %collective-permute-start.1) | collective-permute-done | bytes 524320 | tf_op jit(solution)/shard_map/ppermute | solution.py:431
  29.6 1.6 collective-permute-start.11
  32.2 16.9 %collective-permute-done.11 = bf16[256,256]{1,0:T(8,128)(2,1)S(1)} collective-permute-done((bf16[256,256]{1,0:T(8,128)(2,1)S(1)}, bf16[256,256]{1,0:T(8,128)(2,1)S(1)}, u32[]{:S(2)}, u32[]{:S(2)}) %collective-permute-start.11) | collective-permute-done | bytes 131104 | tf_op jit(solution)/shard_map/ppermute | solution.py:431
  51.0 1.1 pad_maximum_fusion.4.refs_11_
  52.1 1.6 collective-permute-start.13
  53.7 1.0 slice.159
  54.7 1.0 slice.160
  55.7 1.0 slice.161
  56.6 1.1 pad_maximum_fusion.1
  57.8 1.6 collective-permute-start.17
  59.5 1.6 collective-permute-start.7
  61.0 0.9 slice_bitcast_fusion.10
  61.9 0.9 slice_bitcast_fusion.8
  62.9 0.9 slice_bitcast_fusion.9
  63.9 4.8 %collective-permute-done.13.refs_12_ = bf16[1024,256]{1,0:T(8,128)(2,1)S(1)} collective-permute-done((bf16[1024,256]{1,0:T(8,128)(2,1)S(1)}, bf16[1024,256]{1,0:T(8,128)(2,1)S(1)}, u32[]{:S(2)}, u32[]{:S(2)}) %collective-permute-start.13) | collective-permute-done | bytes 524320 | tf_op jit(solution)/shard_map/ppermute | solution.py:441
  68.7 11.2 %collective-permute-done.17.refs_8_ = bf16[1024,256]{1,0:T(8,128)(2,1)S(1)} collective-permute-done((bf16[1024,256]{1,0:T(8,128)(2,1)S(1)}, bf16[1024,256]{1,0:T(8,128)(2,1)S(1)}, u32[]{:S(2)}, u32[]{:S(2)}) %collective-permute-start.17) | collective-permute-done | bytes 524320 | tf_op jit(solution)/shard_map/ppermute | solution.py:441
  80.0 11.2 %collective-permute-done.7.refs_4_ = bf16[1024,256]{1,0:T(8,128)(2,1)S(1)} collective-permute-done((bf16[1024,256]{1,0:T(8,128)(2,1)S(1)}, bf16[1024,256]{1,0:T(8,128)(2,1)S(1)}, u32[]{:S(2)}, u32[]{:S(2)}) %collective-permute-start.7) | collective-permute-done | bytes 524320 | tf_op jit(solution)/shard_map/ppermute | solution.py:441
  92.8 9.7 %collective-permute-done.14.refs_13_ = bf16[1024,256]{1,0:T(8,128)(2,1)} collective-permute-done((bf16[1024,256]{1,0:T(8,128)(2,1)S(1)}, bf16[1024,256]{1,0:T(8,128)(2,1)}, u32[]{:S(2)}, u32[]{:S(2)}) %collective-permute-start.14) | collective-permute-done | bytes 524320 | tf_op jit(solution)/shard_map/ppermute | solution.py:441
  102.5 11.2 %collective-permute-done.18.refs_9_ = bf16[1024,256]{1,0:T(8,128)(2,1)} collective-permute-done((bf16[1024,256]{1,0:T(8,128)(2,1)S(1)}, bf16[1024,256]{1,0:T(8,128)(2,1)}, u32[]{:S(2)}, u32[]{:S(2)}) %collective-permute-start.18) | collective-permute-done | bytes 524320 | tf_op jit(solution)/shard_map/ppermute | solution.py:441
  113.8 11.2 %collective-permute-done.8.refs_5_ = bf16[1024,256]{1,0:T(8,128)(2,1)} collective-permute-done((bf16[1024,256]{1,0:T(8,128)(2,1)S(1)}, bf16[1024,256]{1,0:T(8,128)(2,1)}, u32[]{:S(2)}, u32[]{:S(2)}) %collective-permute-start.8) | collective-permute-done | bytes 524320 | tf_op jit(solution)/shard_map/ppermute | solution.py:441
  125.0 7.4 %shard_map.95 = (bf16[512,1024]{1,0:T(8,128)(2,1)}, bf16[512,1024]{1,0:T(8,128)(2,1)}, bf16[512,1024]{1,0:T(8,128)(2,1)}, bf16[512,1024]{1,0:T(8,128)(2,1)}, f32[512,128]{1,0:T(8,128)}) custom-call(s32[7]{0:T(128)} %stack.85.where, bf16[2,2,128,2048]{3,2,1,0:T(8,128)(2,1)} %copy-done.5, bf16[2,2,128,2048]{3,2,1,0:T(8,128)(2,1)} %collective-permute-done.3.far_ref, ...), custom_call_target="tpu_custom_call" | custom-call | flops 16777216 | bytes 8388608 | tf_op jit(solution)/shard_map/pallas_call | solution.py:266
  132.4 1.8 fusion.35
  134.3 1.5 convolution_add_fusion.5
  135.8 1.6 convolution_add_fusion.4
  137.4 1.6 convolution_add_fusion.3
  140.1 1.9 fusion.17
  142.1 3.4 %collective-permute-start.16 = (bf16[512,256]{1,0:T(8,128)(2,1)S(1)}, bf16[512,256]{1,0:T(8,128)(2,1)S(1)}, u32[]{:S(2)}, u32[]{:S(2)}) collective-permute-start(bf16[512,256]{1,0:T(8,128)(2,1)S(1)} %pad_maximum_fusion.11), channel_id=1, source_target_pairs={{0,8},{2,10},{4,12},{6,14},{8,16},{10,18},{12,20},{14,22},{16,24},... | collective-permute-start | bytes 786440 | tf_op jit(solution)/shard_map/ppermute | solution.py:517
  146.4 1.5 convolution_add_fusion.1
  147.9 1.5 convolution_add_fusion.7
  149.4 2.3 convolution_add_fusion.q_ref
  151.7 6.6 %collective-permute-done.9.refs_6_ = bf16[1024,256]{1,0:T(8,128)(2,1)} collective-permute-done((bf16[1024,256]{1,0:T(8,128)(2,1)}, bf16[1024,256]{1,0:T(8,128)(2,1)}, u32[]{:S(2)}, u32[]{:S(2)}) %collective-permute-start.9) | collective-permute-done | bytes 524320 | tf_op jit(solution)/shard_map/ppermute | solution.py:441
  158.3 2.3 convolution_add_fusion.6.q_ref
  161.1 0.9 fusion.32
  162.0 0.8 copy.31.kt_ref
  162.9 7.1 %shard_map.97 = (bf16[512,256]{1,0:T(8,128)(2,1)}, f32[1024,256]{1,0:T(8,128)}) custom-call(f32[512,256]{1,0:T(8,128)} %convolution_add_fusion.q_ref, bf16[512,256]{1,0:T(8,128)(2,1)} %get-tuple-element.40.g_ref, bf16[1024,128]{1,0:T(8,128)(2,1)} %get-tuple-element.44.k_ref, bf16[128,1024]{1,0:T(8,128)(2,1)} %copy.31.kt_ref, ...), custom_call_target="tpu_custom_call" | custom-call | flops 838860800 | bytes 1572864 | tf_op jit(solution)/shard_map/pallas_call | solution.py:338
  169.9 7.1 %shard_map.96 = (bf16[512,256]{1,0:T(8,128)(2,1)}, f32[1024,256]{1,0:T(8,128)}) custom-call(f32[512,256]{1,0:T(8,128)} %convolution_add_fusion.6.q_ref, bf16[512,256]{1,0:T(8,128)(2,1)} %get-tuple-element.41.g_ref, bf16[1024,128]{1,0:T(8,128)(2,1)} %get-tuple-element.44.k_ref, bf16[128,1024]{1,0:T(8,128)(2,1)} %copy.31.kt_ref, ...), custom_call_target="tpu_custom_call" | custom-call | flops 838860800 | bytes 1572864 | tf_op jit(solution)/shard_map/pallas_call | solution.py:338
  177.1 1.4 add.212
  178.5 1.4 collective-permute-start.20
  179.9 9.2 %collective-permute-done.20 = bf16[512,256]{1,0:T(8,128)(2,1)S(1)} collective-permute-done((bf16[512,256]{1,0:T(8,128)(2,1)S(1)}, bf16[512,256]{1,0:T(8,128)(2,1)S(1)}, u32[]{:S(2)}, u32[]{:S(2)}) %collective-permute-start.20) | collective-permute-done | bytes 262176 | tf_op jit(solution)/shard_map/ppermute | solution.py:530
  189.3 1.0 fusion.15
  191.1 17.4 %shard_map.98 = bf16[2,2,2,128,2048]{4,3,2,1,0:T(8,128)(2,1)} custom-call(s32[7]{0:T(128)} %stack.85.where, bf16[512,256]{1,0:T(8,128)(2,1)} %get-tuple-element.16.refs_0_, bf16[512,256]{1,0:T(8,128)(2,1)} %get-tuple-element.17.refs_1_, bf16[512,256]{1,0:T(8,128)(2,1)} %pad_maximum_fusion.12.refs_2_, bf16[1024,256]{1,0:T(8,128)(2,1)} %copy-done.16, ...), custom_call_target="tpu_custom_call" | custom-call | flops 3221225472 | bytes 8388608 | tf_op jit(solution)/shard_map/pallas_call | solution.py:399
  208.5 3.2 %slice_bitcast_fusion = bf16[2,2,128,2048]{3,2,1,0:T(8,128)(2,1)} fusion(bf16[2,2,2,128,2048]{4,3,2,1,0:T(8,128)(2,1)} %shard_map.98), kind=kLoop, calls=%fused_computation.2 | loop fusion | bytes 4194304 | tf_op jit(solution)/shard_map/squeeze | solution.py:559
  212.2 1.4 collective-permute-start.28
  213.7 0.9 dynamic-slice_reduce_fusion
  214.6 1.7 collective-permute-done.27
  216.3 2.3 collective-permute-done.28
  218.6 0.9 collective-permute-done.29
  219.5 3.0 %fusion = bf16[2,2,128,2048]{3,2,1,0:T(8,128)(2,1)S(1)} fusion(bf16[2,2,128,2048]{3,2,1,0:T(8,128)(2,1)} %collective-permute-done.21, bf16[2,2,2,128,2048]{4,3,2,1,0:T(8,128)(2,1)} %shard_map.98), kind=kLoop, calls=%fused_computation.1 | loop fusion | flops 4194304 | bytes 6291456 | tf_op jit(solution)/shard_map/convert_element_type | solution.py:558
  222.7 1.5 collective-permute-start.22
  224.7 1.3 convolution_convert_fusion.2
  226.3 11.0 %collective-permute-done.22 = bf16[2,128,1024]{2,1,0:T(8,128)(2,1)S(1)} collective-permute-done((bf16[2,128,1024]{2,1,0:T(8,128)(2,1)S(1)}, bf16[2,128,1024]{2,1,0:T(8,128)(2,1)S(1)}, u32[]{:S(2)}, u32[]{:S(2)}) %collective-permute-start.22) | collective-permute-done | bytes 524320 | tf_op jit(solution)/shard_map/ppermute | solution.py:431
  237.3 1.2 collective-permute-done.24
  240.5 1.8 collective-permute-start.30
  242.3 1.5 collective-permute-start.31
  243.8 1.6 collective-permute-start.32
  245.4 1.5 collective-permute-done.23
  247.5 1.6 collective-permute-start.26
  249.1 16.8 %collective-permute-done.31 = bf16[256,512]{1,0:T(8,128)(2,1)S(1)} collective-permute-done((bf16[256,512]{1,0:T(8,128)(2,1)S(1)}, bf16[256,512]{1,0:T(8,128)(2,1)S(1)}, u32[]{:S(2)}, u32[]{:S(2)}) %collective-permute-start.31) | collective-permute-done | bytes 262176 | tf_op jit(solution)/shard_map/ppermute | solution.py:441
  265.9 2.1 fusion.4
  268.1 1.2 fusion.8
  (153 shorter events, 15.4 us)
Async XLA Ops:
  0.6 90.6 %copy-start = (f32[16,2048]{1,0:T(8,128)S(1)}, f32[16,2048]{1,0:T(8,128)}, u32[]{:S(2)}) copy-start(f32[16,2048]{1,0:T(8,128)} %param.14) | copy-start | bytes 393220
  0.6 6.6 %copy-start.11 = (bf16[128,2048]{1,0:T(8,128)(2,1)S(1)}, bf16[128,2048]{1,0:T(8,128)(2,1)}, u32[]{:S(2)}) copy-start(bf16[128,2048]{1,0:T(8,128)(2,1)} %param.13) | copy-start | bytes 1572868
  0.7 17.0 %collective-permute-start.2 = (bf16[128,2048]{1,0:T(8,128)(2,1)}, bf16[128,2048]{1,0:T(8,128)(2,1)S(1)}, u32[]{:S(2)}, u32[]{:S(2)}) collective-permute-start(bf16[128,2048]{1,0:T(8,128)(2,1)} %param.8), channel_id=1, source_target_pairs={{0,5},{1,4},{2,7},{3,6},{4,1},{5,0},{6,3},{7,2},{8,13},{9,12},{10,... | collective-permute-start | bytes 1572872 | tf_op jit(solution)/shard_map/ppermute | solution.py:438
  4.6 24.8 %collective-permute-start.1 = (bf16[128,2048]{1,0:T(8,128)(2,1)}, bf16[128,2048]{1,0:T(8,128)(2,1)S(1)}, u32[]{:S(2)}, u32[]{:S(2)}) collective-permute-start(bf16[128,2048]{1,0:T(8,128)(2,1)} %param.8), channel_id=1, source_target_pairs={{0,4},{2,6},{4,0},{6,2},{8,12},{10,14},{12,8},{14,10},{16,20},{18,... | collective-permute-start | bytes 1572872 | tf_op jit(solution)/shard_map/ppermute | solution.py:431
  5.2 24.4 %collective-permute-start = (bf16[128,2048]{1,0:T(8,128)(2,1)}, bf16[128,2048]{1,0:T(8,128)(2,1)S(1)}, u32[]{:S(2)}, u32[]{:S(2)}) collective-permute-start(bf16[128,2048]{1,0:T(8,128)(2,1)} %param.8), channel_id=1, source_target_pairs={{0,1},{1,0},{2,3},{3,2},{4,5},{5,4},{6,7},{7,6},{8,9},{9,8},{10,11... | collective-permute-start | bytes 1572872 | tf_op jit(solution)/shard_map/ppermute | solution.py:434
  5.3 4.8 %copy-start.31 = (s32[16]{0:T(128)S(1)}, s32[16]{0:T(128)}, u32[]{:S(2)}) copy-start(s32[16]{0:T(128)} %param.15) | copy-start | bytes 196
  8.0 3.3 %copy-start.26 = (bf16[256,512]{1,0:T(8,128)(2,1)S(1)}, bf16[256,512]{1,0:T(8,128)(2,1)}, u32[]{:S(2)}) copy-start(bf16[256,512]{1,0:T(8,128)(2,1)} %param.12) | copy-start | bytes 786436
  8.0 3.3 %copy-start.27 = (bf16[256,512]{1,0:T(8,128)(2,1)S(1)}, bf16[256,512]{1,0:T(8,128)(2,1)}, u32[]{:S(2)}) copy-start(bf16[256,512]{1,0:T(8,128)(2,1)} %param.11) | copy-start | bytes 786436
  8.0 45.7 %collective-permute-start.4 = (bf16[384,512]{1,0:T(8,128)(2,1)S(1)}, bf16[384,512]{1,0:T(8,128)(2,1)}, u32[]{:S(2)}, u32[]{:S(2)}) collective-permute-start(bf16[384,512]{1,0:T(8,128)(2,1)S(1)} %pad_maximum_fusion.7), channel_id=1, source_target_pairs={{0,2},{2,0},{4,6},{6,4},{8,10},{10,8},{12,14},{14,12},{16,18},{18,... | collective-permute-start | bytes 1179656 | tf_op jit(solution)/shard_map/ppermute | solution.py:431
  8.1 46.5 %collective-permute-start.5 = (bf16[384,512]{1,0:T(8,128)(2,1)S(1)}, bf16[384,512]{1,0:T(8,128)(2,1)}, u32[]{:S(2)}, u32[]{:S(2)}) collective-permute-start(bf16[384,512]{1,0:T(8,128)(2,1)S(1)} %pad_maximum_fusion.8), channel_id=1, source_target_pairs={{0,4},{2,6},{4,0},{6,2},{8,12},{10,14},{12,8},{14,10},{16,20},{18,... | collective-permute-start | bytes 1179656 | tf_op jit(solution)/shard_map/ppermute | solution.py:431
  11.3 19.8 %copy-start.6 = (bf16[128,2048]{1,0:T(8,128)(2,1)S(1)}, bf16[128,2048]{1,0:T(8,128)(2,1)}, u32[]{:S(2)}) copy-start(bf16[128,2048]{1,0:T(8,128)(2,1)} %param.8) | copy-start | bytes 1572868
  11.4 39.6 %copy-start.22 = (bf16[256,128]{1,0:T(8,128)(2,1)}, bf16[256,128]{1,0:T(8,128)(2,1)S(1)}, u32[]{:S(2)}) copy-start(bf16[256,128]{1,0:T(8,128)(2,1)S(1)} %get-tuple-element.60) | copy-start | bytes 196612
  11.4 39.6 %copy-start.24 = (bf16[256,128]{1,0:T(8,128)(2,1)}, bf16[256,128]{1,0:T(8,128)(2,1)S(1)}, u32[]{:S(2)}) copy-start(bf16[256,128]{1,0:T(8,128)(2,1)S(1)} %get-tuple-element.69) | copy-start | bytes 196612
  17.7 38.0 %collective-permute-start.6 = (bf16[384,512]{1,0:T(8,128)(2,1)}, bf16[384,512]{1,0:T(8,128)(2,1)}, u32[]{:S(2)}, u32[]{:S(2)}) collective-permute-start(bf16[384,512]{1,0:T(8,128)(2,1)} %pad_maximum_fusion.9), channel_id=1, source_target_pairs={{0,6},{2,4},{4,2},{6,0},{8,14},{10,12},{12,10},{14,8},{16,22},{18,... | collective-permute-start | bytes 1179656 | tf_op jit(solution)/shard_map/ppermute | solution.py:431
  29.4 2.0 collective-permute-start.10
  29.6 19.5 %collective-permute-start.11 = (bf16[256,256]{1,0:T(8,128)(2,1)S(1)}, bf16[256,256]{1,0:T(8,128)(2,1)S(1)}, u32[]{:S(2)}, u32[]{:S(2)}) collective-permute-start(bf16[256,256]{1,0:T(8,128)(2,1)S(1)} %pad_maximum_fusion.14), channel_id=1, source_target_pairs={{0,4},{2,6},{4,0},{6,2},{8,12},{10,14},{12,8},{14,10},{16,20},{18,... | collective-permute-start | bytes 393224 | tf_op jit(solution)/shard_map/ppermute | solution.py:431
  31.4 26.3 %copy-start.5 = (bf16[2,2,128,2048]{3,2,1,0:T(8,128)(2,1)}, bf16[2,2,128,2048]{3,2,1,0:T(8,128)(2,1)S(1)}, u32[]{:S(2)}) copy-start(bf16[2,2,128,2048]{3,2,1,0:T(8,128)(2,1)S(1)} %pad_maximum_fusion.near_ref) | copy-start | bytes 6291460
  31.4 19.5 %collective-permute-start.12 = (bf16[256,256]{1,0:T(8,128)(2,1)S(1)}, bf16[256,256]{1,0:T(8,128)(2,1)}, u32[]{:S(2)}, u32[]{:S(2)}) collective-permute-start(bf16[256,256]{1,0:T(8,128)(2,1)S(1)} %pad_maximum_fusion.15), channel_id=1, source_target_pairs={{0,6},{2,4},{4,2},{6,0},{8,14},{10,12},{12,10},{14,8},{16,22},{18,... | collective-permute-start | bytes 393224 | tf_op jit(solution)/shard_map/ppermute | solution.py:431
  49.8 75.2 %collective-permute-start.3 = (bf16[2,2,128,2048]{3,2,1,0:T(8,128)(2,1)S(1)}, bf16[2,2,128,2048]{3,2,1,0:T(8,128)(2,1)}, u32[]{:S(2)}, u32[]{:S(2)}) collective-permute-start(bf16[2,2,128,2048]{3,2,1,0:T(8,128)(2,1)S(1)} %pad_maximum_fusion.near_ref), channel_id=1, source_target_pairs={{0,2},{2,0},{4,6},{6,4},{8,10},{10,8},{12,14},{14,12},{16,18},{18,... | collective-permute-start | bytes 6291464 | tf_op jit(solution)/shard_map/ppermute | solution.py:431
  52.1 5.7 %copy-start.12 = (bf16[1024,256]{1,0:T(8,128)(2,1)}, bf16[1024,256]{1,0:T(8,128)(2,1)S(1)}, u32[]{:S(2)}) copy-start(bf16[1024,256]{1,0:T(8,128)(2,1)S(1)} %pad_maximum_fusion.4.refs_11_) | copy-start | bytes 1572868
  52.1 16.6 %collective-permute-start.13 = (bf16[1024,256]{1,0:T(8,128)(2,1)S(1)}, bf16[1024,256]{1,0:T(8,128)(2,1)S(1)}, u32[]{:S(2)}, u32[]{:S(2)}) collective-permute-start(bf16[1024,256]{1,0:T(8,128)(2,1)S(1)} %pad_maximum_fusion.4.refs_11_), channel_id=1, source_target_pairs={{0,8},{2,10},{4,12},{6,14},{8,16},{10,18},{12,20},{14,22},{16,24},... | collective-permute-start | bytes 1572872 | tf_op jit(solution)/shard_map/ppermute | solution.py:441
  56.6 7.1 %copy-start.21 = (bf16[1,128,512]{2,1,0:T(8,128)(2,1)S(1)}, bf16[1,128,512]{2,1,0:T(8,128)(2,1)}, u32[]{:S(2)}) copy-start(bf16[1,128,512]{2,1,0:T(8,128)(2,1)} %get-tuple-element.51) | copy-start | bytes 393220
  57.8 34.1 %copy-start.15 = (bf16[1024,256]{1,0:T(8,128)(2,1)}, bf16[1024,256]{1,0:T(8,128)(2,1)S(1)}, u32[]{:S(2)}) copy-start(bf16[1024,256]{1,0:T(8,128)(2,1)S(1)} %get-tuple-element.28.refs_7_) | copy-start | bytes 1572868
  57.8 34.1 %copy-start.16 = (bf16[1024,256]{1,0:T(8,128)(2,1)}, bf16[1024,256]{1,0:T(8,128)(2,1)S(1)}, u32[]{:S(2)}) copy-start(bf16[1024,256]{1,0:T(8,128)(2,1)S(1)} %get-tuple-element.29.refs_3_) | copy-start | bytes 1572868
  57.8 22.1 %collective-permute-start.17 = (bf16[1024,256]{1,0:T(8,128)(2,1)S(1)}, bf16[1024,256]{1,0:T(8,128)(2,1)S(1)}, u32[]{:S(2)}, u32[]{:S(2)}) collective-permute-start(bf16[1024,256]{1,0:T(8,128)(2,1)S(1)} %get-tuple-element.28.refs_7_), channel_id=1, source_target_pairs={{0,8},{2,10},{4,12},{6,14},{8,16},{10,18},{12,20},{14,22},{16,24},... | collective-permute-start | bytes 1572872 | tf_op jit(solution)/shard_map/ppermute | solution.py:441
  59.5 31.7 %collective-permute-start.7 = (bf16[1024,256]{1,0:T(8,128)(2,1)S(1)}, bf16[1024,256]{1,0:T(8,128)(2,1)S(1)}, u32[]{:S(2)}, u32[]{:S(2)}) collective-permute-start(bf16[1024,256]{1,0:T(8,128)(2,1)S(1)} %get-tuple-element.29.refs_3_), channel_id=1, source_target_pairs={{0,8},{2,10},{4,12},{6,14},{8,16},{10,18},{12,20},{14,22},{16,24},... | collective-permute-start | bytes 1572872 | tf_op jit(solution)/shard_map/ppermute | solution.py:441
  68.7 23.2 %copy-start.13 = (bf16[1024,256]{1,0:T(8,128)(2,1)}, bf16[1024,256]{1,0:T(8,128)(2,1)S(1)}, u32[]{:S(2)}) copy-start(bf16[1024,256]{1,0:T(8,128)(2,1)S(1)} %collective-permute-done.13.refs_12_) | copy-start | bytes 1572868
  68.7 33.8 %collective-permute-start.14 = (bf16[1024,256]{1,0:T(8,128)(2,1)S(1)}, bf16[1024,256]{1,0:T(8,128)(2,1)}, u32[]{:S(2)}, u32[]{:S(2)}) collective-permute-start(bf16[1024,256]{1,0:T(8,128)(2,1)S(1)} %collective-permute-done.13.refs_12_), channel_id=1, source_target_pairs={{0,8},{2,10},{4,12},{6,14},{8,16},{10,18},{12,20},{14,22},{16,24},... | collective-permute-start | bytes 1572872 | tf_op jit(solution)/shard_map/ppermute | solution.py:441
  79.9 12.0 %copy-start.17 = (bf16[1024,256]{1,0:T(8,128)(2,1)}, bf16[1024,256]{1,0:T(8,128)(2,1)S(1)}, u32[]{:S(2)}) copy-start(bf16[1024,256]{1,0:T(8,128)(2,1)S(1)} %collective-permute-done.17.refs_8_) | copy-start | bytes 1572868
  79.9 33.8 %collective-permute-start.18 = (bf16[1024,256]{1,0:T(8,128)(2,1)S(1)}, bf16[1024,256]{1,0:T(8,128)(2,1)}, u32[]{:S(2)}, u32[]{:S(2)}) collective-permute-start(bf16[1024,256]{1,0:T(8,128)(2,1)S(1)} %collective-permute-done.17.refs_8_), channel_id=1, source_target_pairs={{0,8},{2,10},{4,12},{6,14},{8,16},{10,18},{12,20},{14,22},{16,24},... | collective-permute-start | bytes 1572872 | tf_op jit(solution)/shard_map/ppermute | solution.py:441
  91.2 0.8 copy-start.19
  91.2 33.8 %collective-permute-start.8 = (bf16[1024,256]{1,0:T(8,128)(2,1)S(1)}, bf16[1024,256]{1,0:T(8,128)(2,1)}, u32[]{:S(2)}, u32[]{:S(2)}) collective-permute-start(bf16[1024,256]{1,0:T(8,128)(2,1)S(1)} %collective-permute-done.7.refs_4_), channel_id=1, source_target_pairs={{0,8},{2,10},{4,12},{6,14},{8,16},{10,18},{12,20},{14,22},{16,24},... | collective-permute-start | bytes 1572872 | tf_op jit(solution)/shard_map/ppermute | solution.py:441
  102.5 34.9 %collective-permute-start.15 = (bf16[1024,256]{1,0:T(8,128)(2,1)}, bf16[1024,256]{1,0:T(8,128)(2,1)}, u32[]{:S(2)}, u32[]{:S(2)}) collective-permute-start(bf16[1024,256]{1,0:T(8,128)(2,1)} %collective-permute-done.14.refs_13_), channel_id=1, source_target_pairs={{0,8},{2,10},{4,12},{6,14},{8,16},{10,18},{12,20},{14,22},{16,24},... | collective-permute-start | bytes 1572872 | tf_op jit(solution)/shard_map/ppermute | solution.py:441
  113.8 35.7 %collective-permute-start.19 = (bf16[1024,256]{1,0:T(8,128)(2,1)}, bf16[1024,256]{1,0:T(8,128)(2,1)}, u32[]{:S(2)}, u32[]{:S(2)}) collective-permute-start(bf16[1024,256]{1,0:T(8,128)(2,1)} %collective-permute-done.18.refs_9_), channel_id=1, source_target_pairs={{0,8},{2,10},{4,12},{6,14},{8,16},{10,18},{12,20},{14,22},{16,24},... | collective-permute-start | bytes 1572872 | tf_op jit(solution)/shard_map/ppermute | solution.py:441
  125.0 33.3 %collective-permute-start.9 = (bf16[1024,256]{1,0:T(8,128)(2,1)}, bf16[1024,256]{1,0:T(8,128)(2,1)}, u32[]{:S(2)}, u32[]{:S(2)}) collective-permute-start(bf16[1024,256]{1,0:T(8,128)(2,1)} %collective-permute-done.8.refs_5_), channel_id=1, source_target_pairs={{0,8},{2,10},{4,12},{6,14},{8,16},{10,18},{12,20},{14,22},{16,24},... | collective-permute-start | bytes 1572872 | tf_op jit(solution)/shard_map/ppermute | solution.py:441
  125.0 7.4 %copy-start.14 = (bf16[1024,256]{1,0:T(8,128)(2,1)S(1)}, bf16[1024,256]{1,0:T(8,128)(2,1)}, u32[]{:S(2)}) copy-start(bf16[1024,256]{1,0:T(8,128)(2,1)} %copy-done.13) | copy-start | bytes 1572868
  132.4 1.8 copy-start.8
  132.4 1.8 copy-start.23
  132.4 1.8 copy-start.25
  132.4 1.8 copy-start.29
  134.2 1.5 copy-start.3
  135.8 1.6 copy-start.2
  137.4 1.8 copy-start.4
  137.4 1.8 copy-start.18
  139.6 5.9 %copy-start.20 = (bf16[1024,256]{1,0:T(8,128)(2,1)S(1)}, bf16[1024,256]{1,0:T(8,128)(2,1)}, u32[]{:S(2)}) copy-start(bf16[1024,256]{1,0:T(8,128)(2,1)} %copy-done.19) | copy-start | bytes 1572868
  142.1 19.0 %collective-permute-start.16 = (bf16[512,256]{1,0:T(8,128)(2,1)S(1)}, bf16[512,256]{1,0:T(8,128)(2,1)S(1)}, u32[]{:S(2)}, u32[]{:S(2)}) collective-permute-start(bf16[512,256]{1,0:T(8,128)(2,1)S(1)} %pad_maximum_fusion.11), channel_id=1, source_target_pairs={{0,8},{2,10},{4,12},{6,14},{8,16},{10,18},{12,20},{14,22},{16,24},... | collective-permute-start | bytes 786440 | tf_op jit(solution)/shard_map/ppermute | solution.py:517
  169.9 7.1 %copy-start.9 = (f32[1024,256]{1,0:T(8,128)S(1)}, f32[1024,256]{1,0:T(8,128)}, u32[]{:S(2)}) copy-start(f32[1024,256]{1,0:T(8,128)} %get-tuple-element.19) | copy-start | bytes 3145732
  178.4 10.9 %copy-start.10 = (f32[512,128]{1,0:T(8,128)S(1)}, f32[512,128]{1,0:T(8,128)}, u32[]{:S(2)}) copy-start(f32[512,128]{1,0:T(8,128)} %get-tuple-element.25.sin_ref) | copy-start | bytes 786436
  178.5 10.6 %collective-permute-start.20 = (bf16[512,256]{1,0:T(8,128)(2,1)S(1)}, bf16[512,256]{1,0:T(8,128)(2,1)S(1)}, u32[]{:S(2)}, u32[]{:S(2)}) collective-permute-start(bf16[512,256]{1,0:T(8,128)(2,1)S(1)} %slice.245), channel_id=1, source_target_pairs={{8,0},{10,2},{12,4},{14,6},{16,8},{18,10},{20,12},{22,14},{24,16},... | collective-permute-start | bytes 786440 | tf_op jit(solution)/shard_map/ppermute | solution.py:530
  208.5 5.2 %copy-start.30 = (f32[4096]{0:T(1024)S(1)}, f32[4096]{0:T(1024)}, u32[]{:S(2)}) copy-start(f32[4096]{0:T(1024)} %param.9) | copy-start | bytes 49156
  211.7 7.8 %collective-permute-start.21 = (bf16[2,2,128,2048]{3,2,1,0:T(8,128)(2,1)}, bf16[2,2,128,2048]{3,2,1,0:T(8,128)(2,1)}, u32[]{:S(2)}, u32[]{:S(2)}) collective-permute-start(bf16[2,2,128,2048]{3,2,1,0:T(8,128)(2,1)} %slice_bitcast_fusion), channel_id=1, source_target_pairs={{0,2},{2,0},{4,6},{6,4},{8,10},{10,8},{12,14},{14,12},{16,18},{18,... | collective-permute-start | bytes 6291464 | tf_op jit(solution)/shard_map/ppermute | solution.py:431
  211.7 4.6 %collective-permute-start.27 = (bf16[512,128]{1,0:T(8,128)(2,1)S(1)}, bf16[512,128]{1,0:T(8,128)(2,1)S(1)}, u32[]{:S(2)}, u32[]{:S(2)}) collective-permute-start(bf16[512,128]{1,0:T(8,128)(2,1)S(1)} %fusion.15), channel_id=1, source_target_pairs={{0,2},{2,0},{4,6},{6,4},{8,10},{10,8},{12,14},{14,12},{16,18},{18,... | collective-permute-start | bytes 393224 | tf_op jit(solution)/shard_map/ppermute | solution.py:431
  212.2 6.4 %collective-permute-start.28 = (bf16[512,128]{1,0:T(8,128)(2,1)S(1)}, bf16[512,128]{1,0:T(8,128)(2,1)S(1)}, u32[]{:S(2)}, u32[]{:S(2)}) collective-permute-start(bf16[512,128]{1,0:T(8,128)(2,1)S(1)} %fusion.15), channel_id=1, source_target_pairs={{0,4},{2,6},{4,0},{6,2},{8,12},{10,14},{12,8},{14,10},{16,20},{18,... | collective-permute-start | bytes 393224 | tf_op jit(solution)/shard_map/ppermute | solution.py:431
  213.7 5.8 %collective-permute-start.29 = (bf16[512,128]{1,0:T(8,128)(2,1)S(1)}, bf16[512,128]{1,0:T(8,128)(2,1)S(1)}, u32[]{:S(2)}, u32[]{:S(2)}) collective-permute-start(bf16[512,128]{1,0:T(8,128)(2,1)S(1)} %fusion.15), channel_id=1, source_target_pairs={{0,6},{2,4},{4,2},{6,0},{8,14},{10,12},{12,10},{14,8},{16,22},{18,... | collective-permute-start | bytes 393224 | tf_op jit(solution)/shard_map/ppermute | solution.py:431
  222.7 14.7 %collective-permute-start.22 = (bf16[2,128,1024]{2,1,0:T(8,128)(2,1)S(1)}, bf16[2,128,1024]{2,1,0:T(8,128)(2,1)S(1)}, u32[]{:S(2)}, u32[]{:S(2)}) collective-permute-start(bf16[2,128,1024]{2,1,0:T(8,128)(2,1)S(1)} %slice_bitcast_fusion.6), channel_id=1, source_target_pairs={{0,4},{2,6},{4,0},{6,2},{8,12},{10,14},{12,8},{14,10},{16,20},{18,... | collective-permute-start | bytes 1572872 | tf_op jit(solution)/shard_map/ppermute | solution.py:431
  224.2 14.3 %collective-permute-start.24 = (bf16[2,128,1024]{2,1,0:T(8,128)(2,1)S(1)}, bf16[2,128,1024]{2,1,0:T(8,128)(2,1)S(1)}, u32[]{:S(2)}, u32[]{:S(2)}) collective-permute-start(bf16[2,128,1024]{2,1,0:T(8,128)(2,1)S(1)} %slice_bitcast_fusion.3), channel_id=1, source_target_pairs={{0,1},{1,0},{2,3},{3,2},{4,5},{5,4},{6,7},{7,6},{8,9},{9,8},{10,11... | collective-permute-start | bytes 1572872 | tf_op jit(solution)/shard_map/ppermute | solution.py:434
  238.9 7.9 %collective-permute-start.23 = (bf16[128,1024]{1,0:T(8,128)(2,1)S(1)}, bf16[128,1024]{1,0:T(8,128)(2,1)S(1)}, u32[]{:S(2)}, u32[]{:S(2)}) collective-permute-start(bf16[128,1024]{1,0:T(8,128)(2,1)S(1)} %fusion.12), channel_id=1, source_target_pairs={{0,1},{1,0},{2,3},{3,2},{4,5},{5,4},{6,7},{7,6},{8,9},{9,8},{10,11... | collective-permute-start | bytes 786440 | tf_op jit(solution)/shard_map/ppermute | solution.py:434
  239.5 7.7 %copy-start.7 = (bf16[128,2048]{1,0:T(8,128)(2,1)S(1)}, bf16[128,2048]{1,0:T(8,128)(2,1)}, u32[]{:S(2)}) copy-start(bf16[128,2048]{1,0:T(8,128)(2,1)} %param.8) | copy-start | bytes 1572868
  239.5 7.7 %collective-permute-start.25 = (bf16[128,1024]{1,0:T(8,128)(2,1)S(1)}, bf16[128,1024]{1,0:T(8,128)(2,1)S(1)}, u32[]{:S(2)}, u32[]{:S(2)}) collective-permute-start(bf16[128,1024]{1,0:T(8,128)(2,1)S(1)} %fusion.13), channel_id=1, source_target_pairs={{0,4},{2,6},{4,0},{6,2},{8,12},{10,14},{12,8},{14,10},{16,20},{18,... | collective-permute-start | bytes 786440 | tf_op jit(solution)/shard_map/ppermute | solution.py:431
  240.5 8.6 %collective-permute-start.30 = (bf16[256,512]{1,0:T(8,128)(2,1)S(1)}, bf16[256,512]{1,0:T(8,128)(2,1)S(1)}, u32[]{:S(2)}, u32[]{:S(2)}) collective-permute-start(bf16[256,512]{1,0:T(8,128)(2,1)S(1)} %convolution_convert_fusion.2), channel_id=1, source_target_pairs={{0,24},{2,26},{4,28},{6,30},{8,0},{10,2},{12,4},{14,6},{16,8},{18,... | collective-permute-start | bytes 786440 | tf_op jit(solution)/shard_map/ppermute | solution.py:441
  242.3 23.6 %collective-permute-start.31 = (bf16[256,512]{1,0:T(8,128)(2,1)S(1)}, bf16[256,512]{1,0:T(8,128)(2,1)S(1)}, u32[]{:S(2)}, u32[]{:S(2)}) collective-permute-start(bf16[256,512]{1,0:T(8,128)(2,1)S(1)} %convolution_convert_fusion.1), channel_id=1, source_target_pairs={{0,16},{2,18},{4,20},{6,22},{8,24},{10,26},{12,28},{14,30},{16,0},... | collective-permute-start | bytes 786440 | tf_op jit(solution)/shard_map/ppermute | solution.py:441
  243.8 22.1 %collective-permute-start.32 = (bf16[256,512]{1,0:T(8,128)(2,1)S(1)}, bf16[256,512]{1,0:T(8,128)(2,1)S(1)}, u32[]{:S(2)}, u32[]{:S(2)}) collective-permute-start(bf16[256,512]{1,0:T(8,128)(2,1)S(1)} %convolution_convert_fusion), channel_id=1, source_target_pairs={{0,8},{2,10},{4,12},{6,14},{8,16},{10,18},{12,20},{14,22},{16,24},... | collective-permute-start | bytes 786440 | tf_op jit(solution)/shard_map/ppermute | solution.py:441
  247.5 21.8 %copy-start.1 = (f32[16,2048]{1,0:T(8,128)S(1)}, f32[16,2048]{1,0:T(8,128)}, u32[]{:S(2)}) copy-start(f32[16,2048]{1,0:T(8,128)} %param.14) | copy-start | bytes 393220
  247.5 20.5 %collective-permute-start.26 = (f32[1,128]{1,0:T(1,128)S(1)}, f32[1,128]{1,0:T(1,128)S(1)}, u32[]{:S(2)}, u32[]{:S(2)}) collective-permute-start(f32[1,128]{1,0:T(1,128)S(1)} %bitcast.120), channel_id=1, source_target_pairs={{0,1},{1,0},{2,3},{3,2},{4,5},{5,4},{6,7},{7,6},{8,9},{9,8},{10,11... | collective-permute-start | bytes 1544 | tf_op jit(solution)/shard_map/ppermute | solution.py:434
  (1 other events, 0.7 us)

commit v2 on v1

--- a/solution.py
+++ b/solution.py
@@ -6,6 +6,7 @@
 from jax.experimental import pallas as pl
 from jax.experimental.pallas import tpu as pltpu
 from jax.sharding import PartitionSpec as P
+
 
 D = 4096
 HD = 128
@@ -113,7 +114,7 @@
     normed = (hidden_wide * inverse_scale * norm_gain[None, :]).astype(jnp.bfloat16)
     dp_index = lax.axis_index("dp")
     own_positions = dp_index * row_count + jnp.arange(row_count, dtype=jnp.int32)
-    documents, doc_len, positions, onehot = document_info(lengths, own_positions)
+    _, doc_len, positions, onehot = document_info(lengths, own_positions)
     cosine_table, sine_table = rope_tables(positions)
     full_query, full_key, full_value = (
         lax.all_gather(w_query, "dp", axis=0, tiled=True),
@@ -158,7 +159,7 @@
     def one_head(operands):
         return attend_head(operands[0], operands[1], operands[2], operands[3], allowed)
 
-    query_grad, key_grad, value_grad, totals, row_delta = lax.map(
+    query_grad, key_grad, value_grad, _, _ = lax.map(
         one_head, (head_queries, head_keys, head_values, head_grads)
     )
     key_sum = fold_heads(key_grad, kv_count, group_size)
@@ -218,9 +219,13 @@
     return (grad_hidden, grad_wkey)
 
 
+def after(array, *others):
+    return lax.optimization_barrier((array, *others))[0]
+
+
 def norm_kernel(where, near_ref, far_ref, gain_ref, *outs):
     pieces, inv_ref = outs[:-1], outs[-1]
-    ring, group, tensor = where[0], where[1], where[2]
+    ring, tensor = where[0], where[2]
     ring_size = len(pieces)
     members = where.shape[0] - 3
     step = pieces[0].shape[1] // members
@@ -280,14 +285,16 @@
     )(where, near, far, gain)
 
 
-def attend_kernel(heads, rows, q_ref, g_ref, k_ref, kt_ref, v_ref, cos_ref, sin_ref, low_ref,
-                  dq_ref, dkv_ref, qs, gs, ps, ds):
+def attend_kernel(heads, rows, first, q_ref, g_ref, k_ref, kt_ref, v_ref, cos_ref, sin_ref, low_ref,
+                  *refs):
+    before = None if first else refs[0]
+    dq_ref, halo_ref, dkv_ref, qs, gs, ps, ds = refs[0 if first else 1 :]
     scale = HD ** (-0.5)
     window = ps.shape[0]
 
     @pl.when(pl.program_id(0) == 0)
     def _():
-        dkv_ref[...] = jnp.zeros_like(dkv_ref)
+        dkv_ref[...] = jnp.zeros_like(dkv_ref) if first else before[...]
 
     base = pl.multiple_of(pl.program_id(0) * rows, rows)
     cosine, sine = cos_ref[...], sin_ref[...]
@@ -327,21 +334,29 @@
         back = grad * cosine - pltpu.roll(grad, HD // 2, 1) * sine
         dq_ref[:, h * HD : (h + 1) * HD] = back.astype(jnp.bfloat16)
 
-
-def attend(q_proj, grads, keys, keys_turned, values, cosine, sine, low):
+    @pl.when(pl.program_id(0) == pl.num_programs(0) - 1)
+    def _():
+        halo_ref[...] = dkv_ref[: halo_ref.shape[0], :].astype(jnp.bfloat16)
+
+
+def attend(q_proj, grads, keys, keys_turned, values, cosine, sine, low, before=None):
     tokens, width = q_proj.shape
     heads, rows = width // HD, 128
     total = keys.shape[0]
     window = total - tokens + rows
     whole = lambda a: pl.BlockSpec(a.shape, lambda i: (0, 0))
     by_rows = lambda w: pl.BlockSpec((rows, w), lambda i: (i, 0))
+    fixed = lambda n: pl.BlockSpec((n, 2 * HD), lambda i: (0, 0))
+    extra = [] if before is None else [before]
     return pl.pallas_call(
-        partial(attend_kernel, heads, rows),
+        partial(attend_kernel, heads, rows, before is None),
         grid=(tokens // rows,),
         in_specs=[by_rows(width), by_rows(width), whole(keys), whole(keys_turned), whole(values),
-                  by_rows(HD), by_rows(HD), pl.BlockSpec((1, rows), lambda i: (0, i))],
-        out_specs=[by_rows(width), pl.BlockSpec((total, 2 * HD), lambda i: (0, 0))],
+                  by_rows(HD), by_rows(HD), pl.BlockSpec((1, rows), lambda i: (0, i))]
+        + [fixed(total) for _ in extra],
+        out_specs=[by_rows(width), fixed(total - tokens), fixed(total)],
         out_shape=[jax.ShapeDtypeStruct((tokens, width), jnp.bfloat16),
+                   jax.ShapeDtypeStruct((total - tokens, 2 * HD), jnp.bfloat16),
                    jax.ShapeDtypeStruct((total, 2 * HD), jnp.float32)],
         scratch_shapes=[pltpu.VMEM((heads * rows, HD), jnp.bfloat16)] * 2
         + [pltpu.VMEM((window, heads * rows), jnp.bfloat16)] * 2,
@@ -349,64 +364,82 @@
             flops=10 * tokens * window * width, bytes_accessed=12 * tokens * width,
             transcendentals=tokens * window * heads,
         ),
-    )(q_proj, grads, keys, keys_turned, values, cosine, sine, low)
-
-
-def spread_kernel(chunks, ring_size, where, *refs):
-    grads = refs[:chunks]
-    weights = refs[chunks : chunks + chunks * ring_size]
-    out_ref = refs[-1]
-    ring, tensor = where[0], where[2]
+    )(q_proj, grads, keys, keys_turned, values, cosine, sine, low, *extra)
+
+
+def spread_kernel(counts, ring_size, where, *refs):
+    grads, weights = refs[: counts[0]], refs[counts[0] : counts[0] + counts[1] * ring_size]
+    keep_ref, send_ref, wide, held, arrived = refs[counts[0] + counts[1] * ring_size :]
     members = where.shape[0] - 3
-    step = weights[0].shape[0] // members
-    rows = out_ref.shape[3]
-    planes_per_half = ring_size // 2
+    step = held.shape[1] // members
+    rows = keep_ref.shape[2]
     s = pl.program_id(0)
-    plane = lax.rem(ring - s + ring_size, ring_size)
-    half = lax.rem(plane // planes_per_half + tensor, 2)
-    for piece in range(ring_size):
-
-        @pl.when(s == piece)
-        def _():
-            for d in range(members):
-                inner = lax.rem(plane, planes_per_half) * (members * step) + where[3 + d] * step
-                inner = pl.multiple_of(inner, step)
-                total = None
-                for c in range(chunks):
-                    term = contract(
-                        grads[c][...], weights[c * ring_size + piece][d * step : (d + 1) * step, :]
-                    )
-                    total = term if total is None else total + term
-                total = total.astype(jnp.bfloat16)
-                for owner in range(members):
-                    for v in range(2):
-                        for u in range(members // 2):
-
-                            @pl.when(where[3 + owner] == 2 * u + v)
-                            def _():
-                                out_ref[v, u, half, :, pl.ds(inner, step)] = total[
-                                    owner * rows : (owner + 1) * rows, :
-                                ]
+
+    def copy(source, piece, c):
+        width = source.shape[1]
+        return pltpu.make_async_copy(
+            source, held.at[piece, :, pl.ds(c * width, width)], arrived.at[piece, c]
+        )
+
+    @pl.when(s == 0)
+    def _():
+        for piece in range(ring_size):
+            for c in range(counts[1]):
+                copy(weights[c * ring_size + piece], piece, c).start()
+        for block in range(members):
+            partner = (block % (members // 2)) * 2 + block // (members // 2)
+            source = pl.multiple_of(where[3 + partner] * rows, rows)
+            at = 0
+            for grad in grads:
+                wide[block * rows : (block + 1) * rows, at : at + grad.shape[1]] = grad[
+                    pl.ds(source, rows), :
+                ]
+                at += grad.shape[1]
+
+    for c in range(counts[1]):
+        copy(weights[c * ring_size], s, c).wait()
+    for owner in range(members):
+        source = pl.multiple_of(where[3 + owner] * step, step)
+        total = contract(wide[...], held[s, pl.ds(source, step), :]).astype(jnp.bfloat16)
+        columns = slice(owner * step, (owner + 1) * step)
+        for u in range(members // 2):
+            keep_ref[u, 0, :, columns] = total[u * rows : (u + 1) * rows, :]
+            lower = (members // 2 + u) * rows
+            send_ref[u, 0, :, columns] = total[lower : lower + rows, :]
 
 
 def spread(where, grads, weights, ring_size):
     tokens = grads[0].shape[0]
     members = where.shape[0] - 3
     rows = tokens // members
+    depth = sum(a.shape[1] for a in grads)
     width = weights[0].shape[0] * ring_size
+    planes_per_half = ring_size // 2
     whole = lambda a: pl.BlockSpec(a.shape, lambda i, w: (0, 0))
-    shape = (2, members // 2, 2, rows, width // 2)
+
+    def out_at(s, w):
+        plane = lax.rem(w[0] - s + ring_size, ring_size)
+        half = lax.rem(plane // planes_per_half + w[2], 2)
+        return (0, half, 0, lax.rem(plane, planes_per_half))
+
+    shape = (members // 2, 2, rows, width // 2)
     return pl.pallas_call(
-        partial(spread_kernel, len(grads), ring_size),
+        partial(spread_kernel, (len(grads), len(weights) // ring_size), ring_size),
         grid_spec=pltpu.PrefetchScalarGridSpec(
             num_scalar_prefetch=1,
             grid=(ring_size,),
-            in_specs=[whole(a) for a in grads] + [whole(a) for a in weights],
-            out_specs=pl.BlockSpec(shape, lambda i, w: (0, 0, 0, 0, 0)),
+            in_specs=[whole(a) for a in grads]
+            + [pl.BlockSpec(memory_space=pl.ANY) for _ in weights],
+            out_specs=[pl.BlockSpec((members // 2, 1, rows, width // ring_size), out_at)] * 2,
+            scratch_shapes=[
+                pltpu.VMEM((tokens, depth), jnp.bfloat16),
+                pltpu.VMEM((ring_size, width // ring_size, depth), jnp.bfloat16),
+                pltpu.SemaphoreType.DMA((ring_size, len(weights) // ring_size)),
+            ],
         ),
-        out_shape=jax.ShapeDtypeStruct(shape, jnp.bfloat16),
+        out_shape=[jax.ShapeDtypeStruct(shape, jnp.bfloat16)] * 2,
         cost_estimate=pl.CostEstimate(
-            flops=2 * tokens * width * sum(a.shape[1] for a in grads),
+            flops=2 * tokens * width * depth,
             bytes_accessed=4 * tokens * width,
             transcendentals=0,
         ),
@@ -438,40 +471,53 @@
         return lax.ppermute(block, ("dp", "tensor"), route)
 
     def along(block, distance):
-        return lax.ppermute(
-            block, "dp", [(i, (i + distance * members) % devices) for i in range(devices)]
-        )
+        route = [(i, (i + distance * members) % devices) for i in range(devices)]
+        return lax.ppermute(block, "dp", route)
 
     def columns(array, owner, width):
         return lax.dynamic_slice_in_dim(array, owner * width, width, 1)
 
-    def pack_kv(owner):
-        return jnp.concatenate([columns(w_key, owner, HD), columns(w_value, owner, HD)], axis=1)
+    def circulate(own, gate=None):
+        pieces = [own]
+        for hop in range(1, ring_size):
+            block = pieces[-1] if gate is None else gate(hop, pieces[-1])
+            pieces.append(along(block, 1))
+        return pieces
+
+    k_ring, v_ring = circulate(w_key), circulate(w_value)
 
     def pack_q(owner):
         return jnp.concatenate(
             [columns(w_query, owner, query_width), columns(upstream, owner, query_width)], axis=0
         )
 
-    kv_parts = [pack_kv(group)] + [to_partner(pack_kv(partners[d]), d) for d in range(1, members)]
     q_parts = [pack_q(group)] + [to_partner(pack_q(partners[d]), d) for d in range(1, members)]
-    kv_own = jnp.concatenate(kv_parts, axis=0)
     q_own = jnp.concatenate([p[:weight_rows] for p in q_parts], axis=0)
     chunk_width = 2 * HD
     q_chunks = query_width // chunk_width
+    q_chunk = [q_own[:, c * chunk_width : (c + 1) * chunk_width] for c in range(q_chunks)]
+
+    def pack_kv(owner):
+        pairs = []
+        for k, v in zip(k_ring, v_ring):
+            cut = [columns(k, owner, HD), columns(v, owner, HD)]
+            pairs.append(lax.optimization_barrier(jnp.concatenate(cut, axis=1)))
+        return jnp.concatenate(pairs, axis=0)
 
     across = to_partner(hidden, 2)
-    near = jnp.stack(
-        [jnp.stack([hidden, to_side(hidden)]), jnp.stack([across, to_corner(hidden, 2)])]
-    )
+    beside, corner = to_side(hidden), to_corner(hidden, 2)
+    near = jnp.stack([hidden, beside, across, corner]).reshape(2, 2, rows, half)
     far = to_partner(near, 1)
     *normed, inverse = norm_pieces(where, near, far, norm_gain[None, :], ring_size)
 
-    def circulate(own):
-        pieces = [own]
-        for _ in range(ring_size - 1):
-            pieces.append(along(pieces[-1], 1))
-        return pieces
+    kv_parts = [pack_kv(group)] + [
+        after(to_partner(pack_kv(partners[d]), d), normed[0])
+        for d in range(1, members)
+    ]
+    kv_pieces = [
+        jnp.concatenate([p[s * weight_rows : (s + 1) * weight_rows] for p in kv_parts], axis=0)
+        for s in range(ring_size)
+    ]
 
     def project(pieces):
         total = None
@@ -506,39 +552,41 @@
     )
     out_grad = (up_own.astype(jnp.float32) + pooled).astype(jnp.bfloat16)
 
-    kv_pieces = circulate(kv_own)
-    q_pieces = [
-        circulate(q_own[:, c * chunk_width : (c + 1) * chunk_width]) for c in range(q_chunks)
-    ]
     kv_proj = project(kv_pieces)
     key_proj = kv_proj[:, :HD]
     key_own = key_proj * cosine + jnp.roll(key_proj, HD // 2, axis=1) * sine
     kv_rows = jnp.concatenate([key_own, kv_proj[:, HD:]], axis=1).astype(jnp.bfloat16)
+
+    q_pieces = []
+    for c in range(q_chunks):
+        gate = lambda hop, block, c=c: (
+            after(block, q_pieces[c - 1][-1] if c else kv_rows) if hop == ring_size - 1 else block
+        )
+        q_pieces.append(circulate(q_chunk[c], gate))
     halo = lax.ppermute(kv_rows, "dp", [(i, i + members) for i in range(devices - members)])
     kv_all = jnp.concatenate([halo, kv_rows], axis=0)
     keys, values = kv_all[:, :HD], kv_all[:, HD:]
     keys_turned = keys.T
     query_dones, kv_sum = [], None
     for c in range(q_chunks):
-        query_done, kv_grad = attend(
-            project(q_pieces[c]),
+        pieces = q_pieces[c]
+        if c:
+            pieces = pieces[:-1] + [after(pieces[-1], query_dones[-1])]
+        query_done, halo_grad, kv_sum = attend(
+            project(pieces),
             out_grad[:, c * chunk_width : (c + 1) * chunk_width],
-            keys, keys_turned, values, cosine, sine, low,
+            keys, keys_turned, values, cosine, sine, low, kv_sum,
         )
         query_dones.append(query_done)
-        kv_sum = kv_grad if kv_sum is None else kv_sum + kv_grad
-    back = lax.ppermute(
-        kv_sum[:LONGEST].astype(jnp.bfloat16),
-        "dp",
-        [(i + members, i) for i in range(devices - members)],
-    )
+    back = lax.ppermute(halo_grad, "dp", [(i + members, i) for i in range(devices - members)])
     kv_total = kv_sum[LONGEST:] + back.astype(jnp.float32)
     key_grad = kv_total[:, :HD]
     key_done = (key_grad * cosine - jnp.roll(key_grad, HD // 2, axis=1) * sine).astype(jnp.bfloat16)
-    kv_done = jnp.concatenate([key_done, kv_total[:, HD:].astype(jnp.bfloat16)], axis=1)
+    value_done = kv_total[:, HD:].astype(jnp.bfloat16)
 
     key_dones = jnp.concatenate(
-        place([key_done] + [to_partner(key_done, d) for d in range(1, members)]), axis=1
+        place([key_done] + [to_partner(key_done, d) for d in range(1, members)]),
+        axis=1,
     )
     grad_wkey = None
     for s in range(ring_size):
@@ -553,13 +601,17 @@
         grad_wkey = term if grad_wkey is None else grad_wkey + term
 
     weights = [piece for pieces in q_pieces + [kv_pieces] for piece in pieces]
-    owned = spread(where, query_dones + [kv_done], weights, ring_size)
+    keep, send = spread(where, query_dones + [key_done, value_done], weights, ring_size)
     wide = lambda a: a.astype(jnp.float32)
     narrow = lambda a: a.astype(jnp.bfloat16)
-    both = narrow(wide(owned[0]) + wide(to_partner(owned[1], 1)))
+    other = to_partner(send, 1)
+    both = lambda *at: wide(keep[at]) + wide(other[at])
     cut = half // 2
-    left = wide(both[0, :, :, :cut]) + wide(to_partner(both[1, :, :, :cut], 2))
-    right = wide(both[:, 0, :, cut:]) + wide(to_side(both[:, 1, :, cut:]))
+    low_cut, high_cut, every = slice(0, cut), slice(cut, half), slice(None)
+    left_half = to_partner(narrow(both(1, every, every, low_cut)), 2)
+    right_half = to_side(narrow(both(every, 1, every, high_cut)))
+    left = both(0, every, every, low_cut) + wide(left_half)
+    right = both(every, 0, every, high_cut) + wide(right_half)
     left_sum = left[0] + wide(to_side(narrow(left[1])))
     right_sum = right[0] + wide(to_partner(narrow(right[1]), 2))
     normed_grad = jnp.concatenate([left_sum, right_sum], axis=1)
@@ -575,17 +627,22 @@
     return (grad_hidden, grad_wkey)
 
 
+def is_grouped(mesh_shape, rows, key_columns):
+    members = key_columns // HD
+    return (
+        mesh_shape["tensor"] == 2
+        and members == 4
+        and mesh_shape["dp"] == 4 * members
+        and members * rows == LONGEST
+    )
+
+
 def per_device(hidden, norm_gain, w_query, w_key, w_value, upstream, cached, lengths):
-    members = w_key.shape[1] // HD
-    devices = lax.axis_size("dp")
-    grouped = (
-        lax.axis_size("tensor") == 2
-        and members == 4
-        and devices == 4 * members
-        and members * hidden.shape[0] == LONGEST
-    )
-    run = grouped_device if grouped else plain_device
-    return run(hidden, norm_gain, w_query, w_key, w_value, upstream, cached, lengths)
+    arrays = (hidden, norm_gain, w_query, w_key, w_value, upstream, cached, lengths)
+    sizes = {axis: lax.axis_size(axis) for axis in ("dp", "tensor")}
+    if not is_grouped(sizes, hidden.shape[0], w_key.shape[1]):
+        return plain_device(*arrays)
+    return grouped_device(*arrays)
 
 
 def solution(mesh):

time: 270 us -> 252 us (0.933); the launches traced: 269 us -> 248 us
  waiting for transfers between devices: 146 us -> 117 us
  other arithmetic: 15.6 us -> 25.1 us
  Pallas kernels: 39 us -> 31.3 us
  starting transfers between devices: 30.3 us -> 37.7 us
    ppermute x13 -> x16, waiting for transfers between devices: 92.1 us -> 71.9 us  [the longest x15 68.6 us: along(): return lax.ppermute(block, 'dp', route)]
    concatenate x5 -> x19, other arithmetic: 1.86 us -> 9.95 us  [the longest x4 5.52 us: grouped_device(): jnp.concatenate([p[s * weight_rows:(s + 1) * weight_rows] for p in kv_par...]
    pallas_call x3, Pallas kernels: 31.6 us -> 24.1 us  [the longest x2 15.2 us: attend(): pl.pallas_call(partial(attend_kernel, heads, rows, before is None), grid=...]
    ppermute x13 -> x16, starting transfers between devices: 11.1 us -> 17.8 us  [the longest x15 16.4 us: along(): return lax.ppermute(block, 'dp', route)]
    ppermute x1, waiting for transfers between devices: 6.02 us -> 0.01 us  [to_corner(): return lax.ppermute(block, ('dp', 'tensor'), route)]
    ppermute x1, starting transfers between devices: 3.99 us -> 0.02 us  [to_corner(): return lax.ppermute(block, ('dp', 'tensor'), route)]
    ppermute x4, starting transfers between devices: 2.77 us -> 6.69 us  [to_side(): return lax.ppermute(block, 'tensor', [(i, i ^ 1) for i in range(tensors)])]
    squeeze x3 -> x0, local copies, waits for them, and re-layouts: 3.3 us -> none  [the longest x1 3.22 us: grouped_device(): both = narrow(wide(owned[0]) + wide(to_partner(owned[1], 1)))]
  transfers between devices with their start and end apart: 33 -> 36, of which waited for: 20 -> 20; matrix products, arithmetic and copies ran while one was open for 14% -> 19% of each run, Pallas kernels for 3% -> 6%
where the time goes in v2:
time: 252 us; the launch traced here: 248 us
  waiting for transfers between devices  117 us (46%)
  starting transfers between devices  37.7 us (15%)
  Pallas kernels  31.3 us (12%)
  other arithmetic  25.1 us (10%)
  matrix products  19.5 us (8%)
  local copies, waits for them, and re-layouts  15.7 us (6%)
    ppermute x15, waiting for transfers between devices, along(): return lax.ppermute(block, 'dp', route)  68.6 us
    ppermute x14, waiting for transfers between devices, to_partner(): return lax.ppermute(block, 'dp', [(i, i ^ d) for i in range(devices)])  42.6 us
    ppermute x15, starting transfers between devices, along(): return lax.ppermute(block, 'dp', route)  16.4 us
    dot_general x12, matrix products, project(): term = jnp.dot(normed[s], pieces[s], preferred_element_type=jnp.float32)  15.7 us
    pallas_call x2, Pallas kernels, attend(): pl.pallas_call(partial(attend_kernel, heads, rows, before is None), grid=...  15.2 us
    ppermute x14, starting transfers between devices, to_partner(): return lax.ppermute(block, 'dp', [(i, i ^ d) for i in range(devices)])  11.5 us
    pallas_call x1, Pallas kernels, spread(): pl.pallas_call(partial(spread_kernel, (len(grads), len(weights) // ring_s...  8.85 us
    pallas_call x1, Pallas kernels, norm_pieces(): pl.pallas_call(norm_kernel, grid_spec=pltpu.PrefetchScalarGridSpec(num_sc...  7.24 us
  transfers between devices with their start and end apart: 36, of which 20 were waited for; matrix products, arithmetic and copies ran while one was open for 19% of the time, Pallas kernels for 6%

profile of v2, /device:TPU:0, one launch (start us, length us, event | category | flops | bytes accessed | tf_op | source)
XLA Modules:
  0.0 248.4 jit_solution(1942088411010309206)
XLA Ops:
  0.7 3.0 %collective-permute-start.1 = (bf16[128,2048]{1,0:T(8,128)(2,1)}, bf16[128,2048]{1,0:T(8,128)(2,1)S(1)}, u32[]{:S(2)}, u32[]{:S(2)}) collective-permute-start(bf16[128,2048]{1,0:T(8,128)(2,1)} %param.8), channel_id=1, source_target_pairs={{0,4},{2,6},{4,0},{6,2},{8,12},{10,14},{12,8},{14,10},{16,20},{18,... | collective-permute-start | bytes 1572872 | tf_op jit(solution)/shard_map/ppermute | solution.py:464
  3.7 1.5 collective-permute-start
  5.2 2.0 collective-permute-start.9
  7.3 1.6 collective-permute-start.10
  12.6 1.1 dynamic-slice_bitcast_fusion.8
  16.8 1.7 collective-permute-start.5
  19.4 1.2 collective-permute-done.10
  22.4 14.0 %collective-permute-done.5 = bf16[384,512]{1,0:T(8,128)(2,1)S(1)} collective-permute-done((bf16[384,512]{1,0:T(8,128)(2,1)S(1)}, bf16[384,512]{1,0:T(8,128)(2,1)S(1)}, u32[]{:S(2)}, u32[]{:S(2)}) %collective-permute-start.5) | collective-permute-done | bytes 393248 | tf_op jit(solution)/shard_map/ppermute | solution.py:464
  36.4 6.8 %collective-permute-done.6 = bf16[384,512]{1,0:T(8,128)(2,1)S(1)} collective-permute-done((bf16[384,512]{1,0:T(8,128)(2,1)S(1)}, bf16[384,512]{1,0:T(8,128)(2,1)S(1)}, u32[]{:S(2)}, u32[]{:S(2)}) %collective-permute-start.6) | collective-permute-done | bytes 393248 | tf_op jit(solution)/shard_map/ppermute | solution.py:464
  43.2 1.6 collective-permute-start.11
  44.9 1.6 collective-permute-start.12
  46.8 1.6 collective-permute-start.20
  48.7 1.5 pad_maximum_fusion
  51.5 3.0 %collective-permute-done.11 = bf16[256,512]{1,0:T(8,128)(2,1)S(1)} collective-permute-done((bf16[256,512]{1,0:T(8,128)(2,1)}, bf16[256,512]{1,0:T(8,128)(2,1)S(1)}, u32[]{:S(2)}, u32[]{:S(2)}) %collective-permute-start.11) | collective-permute-done | bytes 262176 | tf_op jit(solution)/shard_map/ppermute | solution.py:475
  54.5 5.6 %collective-permute-done.12 = bf16[256,512]{1,0:T(8,128)(2,1)S(1)} collective-permute-done((bf16[256,512]{1,0:T(8,128)(2,1)}, bf16[256,512]{1,0:T(8,128)(2,1)S(1)}, u32[]{:S(2)}, u32[]{:S(2)}) %collective-permute-start.12) | collective-permute-done | bytes 262176 | tf_op jit(solution)/shard_map/ppermute | solution.py:475
  60.2 27.9 %collective-permute-done.13 = bf16[256,512]{1,0:T(8,128)(2,1)S(1)} collective-permute-done((bf16[256,512]{1,0:T(8,128)(2,1)S(1)}, bf16[256,512]{1,0:T(8,128)(2,1)S(1)}, u32[]{:S(2)}, u32[]{:S(2)}) %collective-permute-start.13) | collective-permute-done | bytes 262176 | tf_op jit(solution)/shard_map/ppermute | solution.py:475
  88.2 5.5 %collective-permute-done.14 = bf16[256,512]{1,0:T(8,128)(2,1)S(1)} collective-permute-done((bf16[256,512]{1,0:T(8,128)(2,1)S(1)}, bf16[256,512]{1,0:T(8,128)(2,1)S(1)}, u32[]{:S(2)}, u32[]{:S(2)}) %collective-permute-start.14) | collective-permute-done | bytes 262176 | tf_op jit(solution)/shard_map/ppermute | solution.py:475
  93.8 1.5 collective-permute-start.16
  99.1 1.3 copy-done.12
  100.5 1.3 collective-permute-start.8
  101.8 7.2 %shard_map.95 = (bf16[512,1024]{1,0:T(8,128)(2,1)}, bf16[512,1024]{1,0:T(8,128)(2,1)}, bf16[512,1024]{1,0:T(8,128)(2,1)}, bf16[512,1024]{1,0:T(8,128)(2,1)}, f32[512,128]{1,0:T(8,128)}) custom-call(s32[7]{0:T(128)} %stack.73.where, bf16[2,2,128,2048]{3,2,1,0:T(8,128)(2,1)} %bitcast.92, bf16[2,2,128,2048]{3,2,1,0:T(8,128)(2,1)} %copy-done.12, f32[1,4096]{1,0:T(1,128)} %bitcast.98), custom_call_target="tpu_custom_call" | custom-call | flops 16777216 | bytes 8388608 | tf_op jit(solution)/shard_map/pallas_call | solution.py:271
  109.0 9.0 %collective-permute-done.17 = bf16[1024,256]{1,0:T(8,128)(2,1)S(1)} collective-permute-done((bf16[1024,256]{1,0:T(8,128)(2,1)S(1)}, bf16[1024,256]{1,0:T(8,128)(2,1)S(1)}, u32[]{:S(2)}, u32[]{:S(2)}) %collective-permute-start.17) | collective-permute-done | bytes 524320 | tf_op jit(solution)/shard_map/ppermute | solution.py:464
  118.2 1.3 fusion.42
  119.6 1.5 fusion.34
  123.5 1.9 fusion.22
  125.4 1.7 collective-permute-start.19
  127.1 1.5 fusion.48
  128.6 1.2 convolution_add_fusion.1
  129.9 1.6 collective-permute-start.18
  131.4 1.5 fusion.46
  132.9 1.2 convolution_add_fusion.4
  136.0 1.8 copy.33.kt_ref
  137.8 8.8 %collective-permute-done.18.refs_7_ = bf16[1024,256]{1,0:T(8,128)(2,1)} collective-permute-done((bf16[1024,256]{1,0:T(8,128)(2,1)}, bf16[1024,256]{1,0:T(8,128)(2,1)}, u32[]{:S(2)}, u32[]{:S(2)}) %collective-permute-start.18) | collective-permute-done | bytes 524320 | tf_op jit(solution)/shard_map/ppermute | solution.py:475
  147.5 1.5 fusion.47
  149.0 2.3 fusion.2.q_ref
  151.3 7.4 %shard_map.96 = (bf16[512,256]{1,0:T(8,128)(2,1)}, bf16[512,256]{1,0:T(8,128)(2,1)}, f32[1024,256]{1,0:T(8,128)}) custom-call(f32[512,256]{1,0:T(8,128)} %fusion.2.q_ref, bf16[512,256]{1,0:T(8,128)(2,1)} %get-tuple-element.59.g_ref, bf16[1024,128]{1,0:T(8,128)(2,1)} %get-tuple-element.62.k_ref, bf16[128,1024]{1,0:T(8,128)(2,1)} %copy.33.kt_ref, ...), custom_call_target="tpu_custom_call" | custom-call | flops 838860800 | bytes 1572864 | tf_op jit(solution)/shard_map/pallas_call | solution.py:351
  158.7 3.8 %collective-permute-done.22.refs_11_ = bf16[1024,256]{1,0:T(8,128)(2,1)} collective-permute-done((bf16[1024,256]{1,0:T(8,128)(2,1)}, bf16[1024,256]{1,0:T(8,128)(2,1)}, u32[]{:S(2)}, u32[]{:S(2)}) %collective-permute-start.22) | collective-permute-done | bytes 524320 | tf_op jit(solution)/shard_map/ppermute | solution.py:475
  162.5 1.5 fusion.49
  164.0 2.3 fusion.4.q_ref
  166.2 7.8 %shard_map.97 = (bf16[512,256]{1,0:T(8,128)(2,1)}, bf16[512,256]{1,0:T(8,128)(2,1)}, f32[1024,256]{1,0:T(8,128)}) custom-call(f32[512,256]{1,0:T(8,128)} %fusion.4.q_ref, bf16[512,256]{1,0:T(8,128)(2,1)} %get-tuple-element.58.g_ref, bf16[1024,128]{1,0:T(8,128)(2,1)} %get-tuple-element.62.k_ref, bf16[128,1024]{1,0:T(8,128)(2,1)} %copy.33.kt_ref, ...), custom_call_target="tpu_custom_call" | custom-call | flops 838860800 | bytes 1572864 | tf_op jit(solution)/shard_map/pallas_call | solution.py:351
  174.1 1.4 collective-permute-start.23
  175.5 1.9 pad_maximum_fusion.9.refs_15_
  177.5 1.9 pad_maximum_fusion.8.refs_14_
  180.3 3.4 %collective-permute-done.23 = bf16[512,256]{1,0:T(8,128)(2,1)S(1)} collective-permute-done((bf16[512,256]{1,0:T(8,128)(2,1)}, bf16[512,256]{1,0:T(8,128)(2,1)S(1)}, u32[]{:S(2)}, u32[]{:S(2)}) %collective-permute-start.23) | collective-permute-done | bytes 262176 | tf_op jit(solution)/shard_map/ppermute | solution.py:581
  184.5 1.7 fusion.20.refs_2_
  186.2 8.9 %shard_map.98 = (bf16[2,2,128,2048]{3,2,1,0:T(8,128)(2,1)}, bf16[2,2,128,2048]{3,2,1,0:T(8,128)(2,1)}) custom-call(s32[7]{0:T(128)} %stack.73.where, bf16[512,256]{1,0:T(8,128)(2,1)} %get-tuple-element.29.refs_0_, bf16[512,256]{1,0:T(8,128)(2,1)} %get-tuple-element.33.refs_1_, bf16[512,128]{1,0:T(8,128)(2,1)} %fusion.20.refs_2_, ...), custom_call_target="tpu_custom_call" | custom-call | flops 3221225472 | bytes 8388608 | tf_op jit(solution)/shard_map/pallas_call | solution.py:426
  195.1 1.8 collective-permute-start.32
  198.4 2.4 collective-permute-done.32
  200.8 3.0 %collective-permute-done.31 = bf16[512,128]{1,0:T(8,128)(2,1)S(1)} collective-permute-done((bf16[512,128]{1,0:T(8,128)(2,1)S(1)}, bf16[512,128]{1,0:T(8,128)(2,1)S(1)}, u32[]{:S(2)}, u32[]{:S(2)}) %collective-permute-start.31) | collective-permute-done | bytes 131104 | tf_op jit(solution)/shard_map/ppermute | solution.py:464
  204.8 1.4 fusion.13
  206.2 1.7 collective-permute-start.25
  207.9 1.2 fusion.14
  209.2 1.6 collective-permute-start.27
  210.8 1.3 convolution_convert_fusion.2
  212.4 7.2 %collective-permute-done.25 = bf16[2,128,1024]{2,1,0:T(8,128)(2,1)S(1)} collective-permute-done((bf16[2,128,1024]{2,1,0:T(8,128)(2,1)S(1)}, bf16[2,128,1024]{2,1,0:T(8,128)(2,1)S(1)}, u32[]{:S(2)}, u32[]{:S(2)}) %collective-permute-start.25) | collective-permute-done | bytes 524320 | tf_op jit(solution)/shard_map/ppermute | solution.py:464
  219.6 2.7 %collective-permute-done.27 = bf16[2,128,1024]{2,1,0:T(8,128)(2,1)S(1)} collective-permute-done((bf16[2,128,1024]{2,1,0:T(8,128)(2,1)S(1)}, bf16[2,128,1024]{2,1,0:T(8,128)(2,1)S(1)}, u32[]{:S(2)}, u32[]{:S(2)}) %collective-permute-start.27) | collective-permute-done | bytes 524320 | tf_op jit(solution)/shard_map/ppermute | solution.py:467
  222.3 1.8 bitcast_add_fusion.1
  224.6 1.8 collective-permute-start.26
  227.0 3.6 %collective-permute-start.33 = (bf16[256,512]{1,0:T(8,128)(2,1)S(1)}, bf16[256,512]{1,0:T(8,128)(2,1)S(1)}, u32[]{:S(2)}, u32[]{:S(2)}) collective-permute-start(bf16[256,512]{1,0:T(8,128)(2,1)S(1)} %convolution_convert_fusion.2), channel_id=1, source_target_pairs={{0,24},{2,26},{4,28},{6,30},{8,0},{10,2},{12,4},{14,6},{16,8},{18,... | collective-permute-start | bytes 786440 | tf_op jit(solution)/shard_map/ppermute | solution.py:475
  231.4 1.8 collective-permute-start.29
  233.2 4.6 %collective-permute-done.35 = bf16[256,512]{1,0:T(8,128)(2,1)S(1)} collective-permute-done((bf16[256,512]{1,0:T(8,128)(2,1)S(1)}, bf16[256,512]{1,0:T(8,128)(2,1)S(1)}, u32[]{:S(2)}, u32[]{:S(2)}) %collective-permute-start.35) | collective-permute-done | bytes 262176 | tf_op jit(solution)/shard_map/ppermute | solution.py:475
  237.8 8.2 %collective-permute-done.34 = bf16[256,512]{1,0:T(8,128)(2,1)S(1)} collective-permute-done((bf16[256,512]{1,0:T(8,128)(2,1)S(1)}, bf16[256,512]{1,0:T(8,128)(2,1)S(1)}, u32[]{:S(2)}, u32[]{:S(2)}) %collective-permute-start.34) | collective-permute-done | bytes 262176 | tf_op jit(solution)/shard_map/ppermute | solution.py:475
  246.0 1.2 fusion.7
  247.2 1.2 fusion.11
  (189 shorter events, 26.9 us)
Async XLA Ops:
  0.6 49.7 %copy-start = (f32[16,2048]{1,0:T(8,128)S(1)}, f32[16,2048]{1,0:T(8,128)}, u32[]{:S(2)}) copy-start(f32[16,2048]{1,0:T(8,128)} %param.14) | copy-start | bytes 393220
  0.6 13.1 %copy-start.15 = (bf16[256,2048]{1,0:T(8,128)(2,1)S(1)}, bf16[256,2048]{1,0:T(8,128)(2,1)}, u32[]{:S(2)}) copy-start(bf16[256,2048]{1,0:T(8,128)(2,1)} %param.10) | copy-start | bytes 3145732
  0.7 46.1 %collective-permute-start.1 = (bf16[128,2048]{1,0:T(8,128)(2,1)}, bf16[128,2048]{1,0:T(8,128)(2,1)S(1)}, u32[]{:S(2)}, u32[]{:S(2)}) collective-permute-start(bf16[128,2048]{1,0:T(8,128)(2,1)} %param.8), channel_id=1, source_target_pairs={{0,4},{2,6},{4,0},{6,2},{8,12},{10,14},{12,8},{14,10},{16,20},{18,... | collective-permute-start | bytes 1572872 | tf_op jit(solution)/shard_map/ppermute | solution.py:464
  3.7 44.8 %collective-permute-start = (bf16[128,2048]{1,0:T(8,128)(2,1)}, bf16[128,2048]{1,0:T(8,128)(2,1)}, u32[]{:S(2)}, u32[]{:S(2)}) collective-permute-start(bf16[128,2048]{1,0:T(8,128)(2,1)} %param.8), channel_id=1, source_target_pairs={{0,1},{1,0},{2,3},{3,2},{4,5},{5,4},{6,7},{7,6},{8,9},{9,8},{10,11... | collective-permute-start | bytes 1572872 | tf_op jit(solution)/shard_map/ppermute | solution.py:467
  5.2 43.5 %collective-permute-start.2 = (bf16[128,2048]{1,0:T(8,128)(2,1)}, bf16[128,2048]{1,0:T(8,128)(2,1)}, u32[]{:S(2)}, u32[]{:S(2)}) collective-permute-start(bf16[128,2048]{1,0:T(8,128)(2,1)} %param.8), channel_id=1, source_target_pairs={{0,5},{1,4},{2,7},{3,6},{4,1},{5,0},{6,3},{7,2},{8,13},{9,12},{10,... | collective-permute-start | bytes 1572872 | tf_op jit(solution)/shard_map/ppermute | solution.py:471
  5.2 11.5 %collective-permute-start.9 = (bf16[256,512]{1,0:T(8,128)(2,1)}, bf16[256,512]{1,0:T(8,128)(2,1)}, u32[]{:S(2)}, u32[]{:S(2)}) collective-permute-start(bf16[256,512]{1,0:T(8,128)(2,1)} %param.11), channel_id=1, source_target_pairs={{0,8},{2,10},{4,12},{6,14},{8,16},{10,18},{12,20},{14,22},{16,24},... | collective-permute-start | bytes 786440 | tf_op jit(solution)/shard_map/ppermute | solution.py:475
  7.3 13.4 %collective-permute-start.10 = (bf16[256,512]{1,0:T(8,128)(2,1)}, bf16[256,512]{1,0:T(8,128)(2,1)}, u32[]{:S(2)}, u32[]{:S(2)}) collective-permute-start(bf16[256,512]{1,0:T(8,128)(2,1)} %param.12), channel_id=1, source_target_pairs={{0,8},{2,10},{4,12},{6,14},{8,16},{10,18},{12,20},{14,22},{16,24},... | collective-permute-start | bytes 786440 | tf_op jit(solution)/shard_map/ppermute | solution.py:475
  16.8 19.6 %collective-permute-start.5 = (bf16[384,512]{1,0:T(8,128)(2,1)S(1)}, bf16[384,512]{1,0:T(8,128)(2,1)S(1)}, u32[]{:S(2)}, u32[]{:S(2)}) collective-permute-start(bf16[384,512]{1,0:T(8,128)(2,1)S(1)} %pad_maximum_fusion.14), channel_id=1, source_target_pairs={{0,4},{2,6},{4,0},{6,2},{8,12},{10,14},{12,8},{14,10},{16,20},{18,... | collective-permute-start | bytes 1179656 | tf_op jit(solution)/shard_map/ppermute | solution.py:464
  20.7 22.5 %collective-permute-start.6 = (bf16[384,512]{1,0:T(8,128)(2,1)S(1)}, bf16[384,512]{1,0:T(8,128)(2,1)S(1)}, u32[]{:S(2)}, u32[]{:S(2)}) collective-permute-start(bf16[384,512]{1,0:T(8,128)(2,1)S(1)} %pad_maximum_fusion.15), channel_id=1, source_target_pairs={{0,6},{2,4},{4,2},{6,0},{8,14},{10,12},{12,10},{14,8},{16,22},{18,... | collective-permute-start | bytes 1179656 | tf_op jit(solution)/shard_map/ppermute | solution.py:464
  36.4 8.5 %collective-permute-start.4 = (bf16[384,512]{1,0:T(8,128)(2,1)S(1)}, bf16[384,512]{1,0:T(8,128)(2,1)S(1)}, u32[]{:S(2)}, u32[]{:S(2)}) collective-permute-start(bf16[384,512]{1,0:T(8,128)(2,1)S(1)} %pad_maximum_fusion.13), channel_id=1, source_target_pairs={{0,2},{2,0},{4,6},{6,4},{8,10},{10,8},{12,14},{14,12},{16,18},{18,... | collective-permute-start | bytes 1179656 | tf_op jit(solution)/shard_map/ppermute | solution.py:464
  43.2 11.2 %collective-permute-start.11 = (bf16[256,512]{1,0:T(8,128)(2,1)}, bf16[256,512]{1,0:T(8,128)(2,1)S(1)}, u32[]{:S(2)}, u32[]{:S(2)}) collective-permute-start(bf16[256,512]{1,0:T(8,128)(2,1)} %collective-permute-done.9), channel_id=1, source_target_pairs={{0,8},{2,10},{4,12},{6,14},{8,16},{10,18},{12,20},{14,22},{16,24},... | collective-permute-start | bytes 786440 | tf_op jit(solution)/shard_map/ppermute | solution.py:475
  44.9 15.2 %collective-permute-start.12 = (bf16[256,512]{1,0:T(8,128)(2,1)}, bf16[256,512]{1,0:T(8,128)(2,1)S(1)}, u32[]{:S(2)}, u32[]{:S(2)}) collective-permute-start(bf16[256,512]{1,0:T(8,128)(2,1)} %collective-permute-done.10), channel_id=1, source_target_pairs={{0,8},{2,10},{4,12},{6,14},{8,16},{10,18},{12,20},{14,22},{16,24},... | collective-permute-start | bytes 786440 | tf_op jit(solution)/shard_map/ppermute | solution.py:475
  46.8 3.4 %copy-start.16 = (bf16[1024,256]{1,0:T(8,128)(2,1)}, bf16[1024,256]{1,0:T(8,128)(2,1)S(1)}, u32[]{:S(2)}) copy-start(bf16[1024,256]{1,0:T(8,128)(2,1)S(1)} %get-tuple-element.46.refs_8_) | copy-start | bytes 1572868
  46.8 3.4 %copy-start.17 = (bf16[1024,256]{1,0:T(8,128)(2,1)}, bf16[1024,256]{1,0:T(8,128)(2,1)S(1)}, u32[]{:S(2)}) copy-start(bf16[1024,256]{1,0:T(8,128)(2,1)S(1)} %get-tuple-element.47.refs_4_) | copy-start | bytes 1572868
  46.8 50.9 %collective-permute-start.20 = (bf16[1024,256]{1,0:T(8,128)(2,1)S(1)}, bf16[1024,256]{1,0:T(8,128)(2,1)}, u32[]{:S(2)}, u32[]{:S(2)}) collective-permute-start(bf16[1024,256]{1,0:T(8,128)(2,1)S(1)} %get-tuple-element.46.refs_8_), channel_id=1, source_target_pairs={{0,8},{2,10},{4,12},{6,14},{8,16},{10,18},{12,20},{14,22},{16,24},... | collective-permute-start | bytes 1572872 | tf_op jit(solution)/shard_map/ppermute | solution.py:475
  48.4 50.7 %collective-permute-start.7 = (bf16[1024,256]{1,0:T(8,128)(2,1)S(1)}, bf16[1024,256]{1,0:T(8,128)(2,1)}, u32[]{:S(2)}, u32[]{:S(2)}) collective-permute-start(bf16[1024,256]{1,0:T(8,128)(2,1)S(1)} %get-tuple-element.47.refs_4_), channel_id=1, source_target_pairs={{0,8},{2,10},{4,12},{6,14},{8,16},{10,18},{12,20},{14,22},{16,24},... | collective-permute-start | bytes 1572872 | tf_op jit(solution)/shard_map/ppermute | solution.py:475
  50.2 48.9 %collective-permute-start.3 = (bf16[2,2,128,2048]{3,2,1,0:T(8,128)(2,1)S(1)}, bf16[2,2,128,2048]{3,2,1,0:T(8,128)(2,1)S(1)}, u32[]{:S(2)}, u32[]{:S(2)}) collective-permute-start(bf16[2,2,128,2048]{3,2,1,0:T(8,128)(2,1)S(1)} %bitcast.91), channel_id=1, source_target_pairs={{0,2},{2,0},{4,6},{6,4},{8,10},{10,8},{12,14},{14,12},{16,18},{18,... | collective-permute-start | bytes 6291464 | tf_op jit(solution)/shard_map/ppermute | solution.py:464
  54.4 33.7 %collective-permute-start.13 = (bf16[256,512]{1,0:T(8,128)(2,1)S(1)}, bf16[256,512]{1,0:T(8,128)(2,1)S(1)}, u32[]{:S(2)}, u32[]{:S(2)}) collective-permute-start(bf16[256,512]{1,0:T(8,128)(2,1)S(1)} %collective-permute-done.11), channel_id=1, source_target_pairs={{0,8},{2,10},{4,12},{6,14},{8,16},{10,18},{12,20},{14,22},{16,24},... | collective-permute-start | bytes 786440 | tf_op jit(solution)/shard_map/ppermute | solution.py:475
  60.1 33.6 %collective-permute-start.14 = (bf16[256,512]{1,0:T(8,128)(2,1)S(1)}, bf16[256,512]{1,0:T(8,128)(2,1)S(1)}, u32[]{:S(2)}, u32[]{:S(2)}) collective-permute-start(bf16[256,512]{1,0:T(8,128)(2,1)S(1)} %collective-permute-done.12), channel_id=1, source_target_pairs={{0,8},{2,10},{4,12},{6,14},{8,16},{10,18},{12,20},{14,22},{16,24},... | collective-permute-start | bytes 786440 | tf_op jit(solution)/shard_map/ppermute | solution.py:475
  93.7 3.2 %copy-start.22 = (bf16[256,256]{1,0:T(8,128)(2,1)S(1)}, bf16[256,256]{1,0:T(8,128)(2,1)}, u32[]{:S(2)}) copy-start(bf16[256,256]{1,0:T(8,128)(2,1)} %get-tuple-element.126) | copy-start | bytes 393220
  93.8 24.2 %collective-permute-start.16 = (bf16[1024,256]{1,0:T(8,128)(2,1)S(1)}, bf16[1024,256]{1,0:T(8,128)(2,1)S(1)}, u32[]{:S(2)}, u32[]{:S(2)}) collective-permute-start(bf16[1024,256]{1,0:T(8,128)(2,1)S(1)} %pad_maximum_fusion.4), channel_id=1, source_target_pairs={{0,4},{2,6},{4,0},{6,2},{8,12},{10,14},{12,8},{14,10},{16,20},{18,... | collective-permute-start | bytes 1572872 | tf_op jit(solution)/shard_map/ppermute | solution.py:464
  95.3 22.7 %collective-permute-start.17 = (bf16[1024,256]{1,0:T(8,128)(2,1)S(1)}, bf16[1024,256]{1,0:T(8,128)(2,1)S(1)}, u32[]{:S(2)}, u32[]{:S(2)}) collective-permute-start(bf16[1024,256]{1,0:T(8,128)(2,1)S(1)} %pad_maximum_fusion.5), channel_id=1, source_target_pairs={{0,6},{2,4},{4,2},{6,0},{8,14},{10,12},{12,10},{14,8},{16,22},{18,... | collective-permute-start | bytes 1572872 | tf_op jit(solution)/shard_map/ppermute | solution.py:464
  97.7 20.5 %collective-permute-start.15 = (bf16[1024,256]{1,0:T(8,128)(2,1)}, bf16[1024,256]{1,0:T(8,128)(2,1)}, u32[]{:S(2)}, u32[]{:S(2)}) collective-permute-start(bf16[1024,256]{1,0:T(8,128)(2,1)} %pad_maximum_fusion.3), channel_id=1, source_target_pairs={{0,2},{2,0},{4,6},{6,4},{8,10},{10,8},{12,14},{14,12},{16,18},{18,... | collective-permute-start | bytes 1572872 | tf_op jit(solution)/shard_map/ppermute | solution.py:464
  99.1 38.7 %collective-permute-start.21 = (bf16[1024,256]{1,0:T(8,128)(2,1)}, bf16[1024,256]{1,0:T(8,128)(2,1)}, u32[]{:S(2)}, u32[]{:S(2)}) collective-permute-start(bf16[1024,256]{1,0:T(8,128)(2,1)} %collective-permute-done.20.refs_9_), channel_id=1, source_target_pairs={{0,8},{2,10},{4,12},{6,14},{8,16},{10,18},{12,20},{14,22},{16,24},... | collective-permute-start | bytes 1572872 | tf_op jit(solution)/shard_map/ppermute | solution.py:475
  100.5 29.4 %collective-permute-start.8 = (bf16[1024,256]{1,0:T(8,128)(2,1)}, bf16[1024,256]{1,0:T(8,128)(2,1)}, u32[]{:S(2)}, u32[]{:S(2)}) collective-permute-start(bf16[1024,256]{1,0:T(8,128)(2,1)} %collective-permute-done.7.refs_5_), channel_id=1, source_target_pairs={{0,8},{2,10},{4,12},{6,14},{8,16},{10,18},{12,20},{14,22},{16,24},... | collective-permute-start | bytes 1572872 | tf_op jit(solution)/shard_map/ppermute | solution.py:475
  109.0 10.5 %copy-start.7 = (bf16[512,1024]{1,0:T(8,128)(2,1)S(1)}, bf16[512,1024]{1,0:T(8,128)(2,1)}, u32[]{:S(2)}) copy-start(bf16[512,1024]{1,0:T(8,128)(2,1)} %get-tuple-element.24) | copy-start | bytes 3145732
  118.0 3.0 %copy-start.25 = (bf16[256,256]{1,0:T(8,128)(2,1)}, bf16[256,256]{1,0:T(8,128)(2,1)S(1)}, u32[]{:S(2)}) copy-start(bf16[256,256]{1,0:T(8,128)(2,1)S(1)} %get-tuple-element.83) | copy-start | bytes 393220
  118.0 3.5 %copy-start.23 = (bf16[256,256]{1,0:T(8,128)(2,1)}, bf16[256,256]{1,0:T(8,128)(2,1)S(1)}, u32[]{:S(2)}) copy-start(bf16[256,256]{1,0:T(8,128)(2,1)S(1)} %get-tuple-element.84) | copy-start | bytes 393220
  118.1 2.9 %copy-start.30 = (bf16[256,256]{1,0:T(8,128)(2,1)}, bf16[256,256]{1,0:T(8,128)(2,1)S(1)}, u32[]{:S(2)}) copy-start(bf16[256,256]{1,0:T(8,128)(2,1)S(1)} %get-tuple-element.78) | copy-start | bytes 393220
  118.1 2.9 %copy-start.29 = (bf16[256,256]{1,0:T(8,128)(2,1)}, bf16[256,256]{1,0:T(8,128)(2,1)S(1)}, u32[]{:S(2)}) copy-start(bf16[256,256]{1,0:T(8,128)(2,1)S(1)} %get-tuple-element.79) | copy-start | bytes 393220
  118.1 3.5 %copy-start.26 = (bf16[256,256]{1,0:T(8,128)(2,1)}, bf16[256,256]{1,0:T(8,128)(2,1)S(1)}, u32[]{:S(2)}) copy-start(bf16[256,256]{1,0:T(8,128)(2,1)S(1)} %get-tuple-element.80) | copy-start | bytes 393220
  118.1 3.0 %copy-start.5 = (bf16[512,1024]{1,0:T(8,128)(2,1)S(1)}, bf16[512,1024]{1,0:T(8,128)(2,1)}, u32[]{:S(2)}) copy-start(bf16[512,1024]{1,0:T(8,128)(2,1)} %get-tuple-element.23) | copy-start | bytes 3145732
  118.1 3.0 %copy-start.21 = (bf16[256,256]{1,0:T(8,128)(2,1)S(1)}, bf16[256,256]{1,0:T(8,128)(2,1)}, u32[]{:S(2)}) copy-start(bf16[256,256]{1,0:T(8,128)(2,1)} %pad_maximum_fusion.32) | copy-start | bytes 393220
  119.5 2.1 copy-start.31
  125.4 9.6 %collective-permute-start.19 = (bf16[512,256]{1,0:T(8,128)(2,1)S(1)}, bf16[512,256]{1,0:T(8,128)(2,1)S(1)}, u32[]{:S(2)}, u32[]{:S(2)}) collective-permute-start(bf16[512,256]{1,0:T(8,128)(2,1)S(1)} %pad_maximum_fusion.17), channel_id=1, source_target_pairs={{0,8},{2,10},{4,12},{6,14},{8,16},{10,18},{12,20},{14,22},{16,24},... | collective-permute-start | bytes 786440 | tf_op jit(solution)/shard_map/ppermute | solution.py:566
  129.9 16.7 %collective-permute-start.18 = (bf16[1024,256]{1,0:T(8,128)(2,1)}, bf16[1024,256]{1,0:T(8,128)(2,1)}, u32[]{:S(2)}, u32[]{:S(2)}) collective-permute-start(bf16[1024,256]{1,0:T(8,128)(2,1)} %collective-permute-done.8.refs_6_), channel_id=1, source_target_pairs={{0,8},{2,10},{4,12},{6,14},{8,16},{10,18},{12,20},{14,22},{16,24},... | collective-permute-start | bytes 1572872 | tf_op jit(solution)/shard_map/ppermute | solution.py:475
  134.1 13.4 %copy-start.8 = (bf16[512,1024]{1,0:T(8,128)(2,1)S(1)}, bf16[512,1024]{1,0:T(8,128)(2,1)}, u32[]{:S(2)}) copy-start(bf16[512,1024]{1,0:T(8,128)(2,1)} %get-tuple-element.24) | copy-start | bytes 3145732
  137.8 11.2 %copy-start.14 = (f32[512,256]{1,0:T(8,128)S(1)}, f32[512,256]{1,0:T(8,128)}, u32[]{:S(2)}) copy-start(f32[512,256]{1,0:T(8,128)} %convolution_add_fusion.4) | copy-start | bytes 1572868
  146.6 15.9 %collective-permute-start.22 = (bf16[1024,256]{1,0:T(8,128)(2,1)}, bf16[1024,256]{1,0:T(8,128)(2,1)}, u32[]{:S(2)}, u32[]{:S(2)}) collective-permute-start(bf16[1024,256]{1,0:T(8,128)(2,1)} %collective-permute-done.21.refs_10_), channel_id=1, source_target_pairs={{0,8},{2,10},{4,12},{6,14},{8,16},{10,18},{12,20},{14,22},{16,24},... | collective-permute-start | bytes 1572872 | tf_op jit(solution)/shard_map/ppermute | solution.py:475
  158.7 5.3 %copy-start.13 = (f32[512,256]{1,0:T(8,128)S(1)}, f32[512,256]{1,0:T(8,128)}, u32[]{:S(2)}) copy-start(f32[512,256]{1,0:T(8,128)} %convolution_add_fusion.1) | copy-start | bytes 1572868
  166.2 13.2 %copy-start.20 = (bf16[256,256]{1,0:T(8,128)(2,1)S(1)}, bf16[256,256]{1,0:T(8,128)(2,1)}, u32[]{:S(2)}) copy-start(bf16[256,256]{1,0:T(8,128)(2,1)} %pad_maximum_fusion.31) | copy-start | bytes 393220
  174.1 5.3 %copy-start.24 = (bf16[256,256]{1,0:T(8,128)(2,1)S(1)}, bf16[256,256]{1,0:T(8,128)(2,1)}, u32[]{:S(2)}) copy-start(bf16[256,256]{1,0:T(8,128)(2,1)} %copy-done.23) | copy-start | bytes 393220
  174.1 5.3 %copy-start.27 = (bf16[256,256]{1,0:T(8,128)(2,1)S(1)}, bf16[256,256]{1,0:T(8,128)(2,1)}, u32[]{:S(2)}) copy-start(bf16[256,256]{1,0:T(8,128)(2,1)} %copy-done.26) | copy-start | bytes 393220
  174.1 5.3 %copy-start.32 = (bf16[256,256]{1,0:T(8,128)(2,1)S(1)}, bf16[256,256]{1,0:T(8,128)(2,1)}, u32[]{:S(2)}) copy-start(bf16[256,256]{1,0:T(8,128)(2,1)} %copy-done.31) | copy-start | bytes 393220
  174.1 9.5 %copy-start.36 = (f32[1024,256]{1,0:T(8,128)S(1)}, f32[1024,256]{1,0:T(8,128)}, u32[]{:S(2)}) copy-start(f32[1024,256]{1,0:T(8,128)} %get-tuple-element.34) | copy-start | bytes 3145732
  174.1 9.5 %collective-permute-start.23 = (bf16[512,256]{1,0:T(8,128)(2,1)}, bf16[512,256]{1,0:T(8,128)(2,1)S(1)}, u32[]{:S(2)}, u32[]{:S(2)}) collective-permute-start(bf16[512,256]{1,0:T(8,128)(2,1)} %get-tuple-element.35), channel_id=1, source_target_pairs={{8,0},{10,2},{12,4},{14,6},{16,8},{18,10},{20,12},{22,14},{24,16},... | collective-permute-start | bytes 786440 | tf_op jit(solution)/shard_map/ppermute | solution.py:581
  179.4 5.1 %copy-start.10 = (f32[512,128]{1,0:T(8,128)S(1)}, f32[512,128]{1,0:T(8,128)}, u32[]{:S(2)}) copy-start(f32[512,128]{1,0:T(8,128)} %get-tuple-element.43.sin_ref) | copy-start | bytes 786436
  186.2 8.9 %copy-start.35 = (bf16[512,128]{1,0:T(8,128)(2,1)S(1)}, bf16[512,128]{1,0:T(8,128)(2,1)}, u32[]{:S(2)}) copy-start(bf16[512,128]{1,0:T(8,128)(2,1)} %fusion.20.refs_2_) | copy-start | bytes 393220
  186.2 11.1 %copy-start.37 = (f32[4096]{0:T(1024)S(1)}, f32[4096]{0:T(1024)}, u32[]{:S(2)}) copy-start(f32[4096]{0:T(1024)} %param.9) | copy-start | bytes 49156
  195.0 9.7 %collective-permute-start.24 = (bf16[2,2,128,2048]{3,2,1,0:T(8,128)(2,1)}, bf16[2,2,128,2048]{3,2,1,0:T(8,128)(2,1)}, u32[]{:S(2)}, u32[]{:S(2)}) collective-permute-start(bf16[2,2,128,2048]{3,2,1,0:T(8,128)(2,1)} %get-tuple-element.37), channel_id=1, source_target_pairs={{0,2},{2,0},{4,6},{6,4},{8,10},{10,8},{12,14},{14,12},{16,18},{18,... | collective-permute-start | bytes 6291464 | tf_op jit(solution)/shard_map/ppermute | solution.py:464
  195.1 5.7 %collective-permute-start.32 = (bf16[512,128]{1,0:T(8,128)(2,1)S(1)}, bf16[512,128]{1,0:T(8,128)(2,1)S(1)}, u32[]{:S(2)}, u32[]{:S(2)}) collective-permute-start(bf16[512,128]{1,0:T(8,128)(2,1)S(1)} %copy-done.35), channel_id=1, source_target_pairs={{0,6},{2,4},{4,2},{6,0},{8,14},{10,12},{12,10},{14,8},{16,22},{18,... | collective-permute-start | bytes 393224 | tf_op jit(solution)/shard_map/ppermute | solution.py:464
  196.9 6.9 %collective-permute-start.31 = (bf16[512,128]{1,0:T(8,128)(2,1)S(1)}, bf16[512,128]{1,0:T(8,128)(2,1)S(1)}, u32[]{:S(2)}, u32[]{:S(2)}) collective-permute-start(bf16[512,128]{1,0:T(8,128)(2,1)S(1)} %copy-done.35), channel_id=1, source_target_pairs={{0,4},{2,6},{4,0},{6,2},{8,12},{10,14},{12,8},{14,10},{16,20},{18,... | collective-permute-start | bytes 393224 | tf_op jit(solution)/shard_map/ppermute | solution.py:464
  197.2 6.6 %collective-permute-start.30 = (bf16[512,128]{1,0:T(8,128)(2,1)S(1)}, bf16[512,128]{1,0:T(8,128)(2,1)}, u32[]{:S(2)}, u32[]{:S(2)}) collective-permute-start(bf16[512,128]{1,0:T(8,128)(2,1)S(1)} %copy-done.35), channel_id=1, source_target_pairs={{0,2},{2,0},{4,6},{6,4},{8,10},{10,8},{12,14},{14,12},{16,18},{18,... | collective-permute-start | bytes 393224 | tf_op jit(solution)/shard_map/ppermute | solution.py:464
  197.2 10.7 %copy-start.11 = (bf16[2,2,128,2048]{3,2,1,0:T(8,128)(2,1)S(1)}, bf16[2,2,128,2048]{3,2,1,0:T(8,128)(2,1)}, u32[]{:S(2)}) copy-start(bf16[2,2,128,2048]{3,2,1,0:T(8,128)(2,1)} %get-tuple-element.36) | copy-start | bytes 6291460
  206.2 13.4 %collective-permute-start.25 = (bf16[2,128,1024]{2,1,0:T(8,128)(2,1)S(1)}, bf16[2,128,1024]{2,1,0:T(8,128)(2,1)S(1)}, u32[]{:S(2)}, u32[]{:S(2)}) collective-permute-start(bf16[2,128,1024]{2,1,0:T(8,128)(2,1)S(1)} %fusion.13), channel_id=1, source_target_pairs={{0,4},{2,6},{4,0},{6,2},{8,12},{10,14},{12,8},{14,10},{16,20},{18,... | collective-permute-start | bytes 1572872 | tf_op jit(solution)/shard_map/ppermute | solution.py:464
  209.2 13.1 %collective-permute-start.27 = (bf16[2,128,1024]{2,1,0:T(8,128)(2,1)S(1)}, bf16[2,128,1024]{2,1,0:T(8,128)(2,1)S(1)}, u32[]{:S(2)}, u32[]{:S(2)}) collective-permute-start(bf16[2,128,1024]{2,1,0:T(8,128)(2,1)S(1)} %fusion.14), channel_id=1, source_target_pairs={{0,1},{1,0},{2,3},{3,2},{4,5},{5,4},{6,7},{7,6},{8,9},{9,8},{10,11... | collective-permute-start | bytes 1572872 | tf_op jit(solution)/shard_map/ppermute | solution.py:467
  224.1 6.7 %collective-permute-start.28 = (bf16[128,1024]{1,0:T(8,128)(2,1)S(1)}, bf16[128,1024]{1,0:T(8,128)(2,1)S(1)}, u32[]{:S(2)}, u32[]{:S(2)}) collective-permute-start(bf16[128,1024]{1,0:T(8,128)(2,1)S(1)} %fusion.18), channel_id=1, source_target_pairs={{0,4},{2,6},{4,0},{6,2},{8,12},{10,14},{12,8},{14,10},{16,20},{18,... | collective-permute-start | bytes 786440 | tf_op jit(solution)/shard_map/ppermute | solution.py:464
  224.6 6.5 %copy-start.4 = (bf16[128,2048]{1,0:T(8,128)(2,1)S(1)}, bf16[128,2048]{1,0:T(8,128)(2,1)}, u32[]{:S(2)}) copy-start(bf16[128,2048]{1,0:T(8,128)(2,1)} %param.8) | copy-start | bytes 1572868
  224.6 6.4 %collective-permute-start.26 = (bf16[128,1024]{1,0:T(8,128)(2,1)S(1)}, bf16[128,1024]{1,0:T(8,128)(2,1)S(1)}, u32[]{:S(2)}, u32[]{:S(2)}) collective-permute-start(bf16[128,1024]{1,0:T(8,128)(2,1)S(1)} %fusion.17), channel_id=1, source_target_pairs={{0,1},{1,0},{2,3},{3,2},{4,5},{5,4},{6,7},{7,6},{8,9},{9,8},{10,11... | collective-permute-start | bytes 786440 | tf_op jit(solution)/shard_map/ppermute | solution.py:467
  226.8 11.0 %collective-permute-start.35 = (bf16[256,512]{1,0:T(8,128)(2,1)S(1)}, bf16[256,512]{1,0:T(8,128)(2,1)S(1)}, u32[]{:S(2)}, u32[]{:S(2)}) collective-permute-start(bf16[256,512]{1,0:T(8,128)(2,1)S(1)} %convolution_convert_fusion), channel_id=1, source_target_pairs={{0,8},{2,10},{4,12},{6,14},{8,16},{10,18},{12,20},{14,22},{16,24},... | collective-permute-start | bytes 786440 | tf_op jit(solution)/shard_map/ppermute | solution.py:475
  226.8 19.2 %collective-permute-start.34 = (bf16[256,512]{1,0:T(8,128)(2,1)S(1)}, bf16[256,512]{1,0:T(8,128)(2,1)S(1)}, u32[]{:S(2)}, u32[]{:S(2)}) collective-permute-start(bf16[256,512]{1,0:T(8,128)(2,1)S(1)} %convolution_convert_fusion.1), channel_id=1, source_target_pairs={{0,16},{2,18},{4,20},{6,22},{8,24},{10,26},{12,28},{14,30},{16,0},... | collective-permute-start | bytes 786440 | tf_op jit(solution)/shard_map/ppermute | solution.py:475
  227.0 19.0 %collective-permute-start.33 = (bf16[256,512]{1,0:T(8,128)(2,1)S(1)}, bf16[256,512]{1,0:T(8,128)(2,1)S(1)}, u32[]{:S(2)}, u32[]{:S(2)}) collective-permute-start(bf16[256,512]{1,0:T(8,128)(2,1)S(1)} %convolution_convert_fusion.2), channel_id=1, source_target_pairs={{0,24},{2,26},{4,28},{6,30},{8,0},{10,2},{12,4},{14,6},{16,8},{18,... | collective-permute-start | bytes 786440 | tf_op jit(solution)/shard_map/ppermute | solution.py:475
  231.4 17.0 %copy-start.1 = (f32[16,2048]{1,0:T(8,128)S(1)}, f32[16,2048]{1,0:T(8,128)}, u32[]{:S(2)}) copy-start(f32[16,2048]{1,0:T(8,128)} %param.14) | copy-start | bytes 393220
  231.4 15.8 %collective-permute-start.29 = (f32[1,128]{1,0:T(1,128)S(1)}, f32[1,128]{1,0:T(1,128)S(1)}, u32[]{:S(2)}, u32[]{:S(2)}) collective-permute-start(f32[1,128]{1,0:T(1,128)S(1)} %bitcast.102), channel_id=1, source_target_pairs={{0,1},{1,0},{2,3},{3,2},{4,5},{5,4},{6,7},{7,6},{8,9},{9,8},{10,11... | collective-permute-start | bytes 1544 | tf_op jit(solution)/shard_map/ppermute | solution.py:467
  (10 other events, 14.4 us)

commit v3 on v2

--- a/solution.py
+++ b/solution.py
@@ -15,6 +15,7 @@
 
 
 EPSILON = 1e-05
+LOG2_E = 1.4426950408889634
 ROPE_BASE = 500000.0
 
 
@@ -279,100 +280,139 @@
         ),
         out_shape=[jax.ShapeDtypeStruct((tokens, width), jnp.bfloat16)] * ring_size
         + [jax.ShapeDtypeStruct((tokens, 128), jnp.float32)],
+        compiler_params=pltpu.CompilerParams(vmem_limit_bytes=24 << 20),
         cost_estimate=pl.CostEstimate(
             flops=8 * tokens * 2 * half, bytes_accessed=8 * tokens * half, transcendentals=tokens
         ),
     )(where, near, far, gain)
 
 
-def attend_kernel(heads, rows, first, q_ref, g_ref, k_ref, kt_ref, v_ref, cos_ref, sin_ref, low_ref,
-                  *refs):
-    before = None if first else refs[0]
-    dq_ref, halo_ref, dkv_ref, qs, gs, ps, ds = refs[0 if first else 1 :]
+def attend_kernel(heads, rows, terms, first, q_ref, *refs):
+    n_refs, w_refs, refs = refs[:terms], refs[terms : 2 * terms], refs[2 * terms :]
+    g_ref, k_ref, kt_ref, v_ref, cos_ref, sin_ref, low_ref = refs[:7]
+    before = None if first else refs[7]
+    dq_ref, key_halo_ref, value_halo_ref, dkv_ref = refs[7 if first else 8 :]
     scale = HD ** (-0.5)
-    window = ps.shape[0]
+    halo = key_halo_ref.shape[0]
+    window = halo + rows
+    blocks = q_ref.shape[0] // rows
 
     @pl.when(pl.program_id(0) == 0)
     def _():
         dkv_ref[...] = jnp.zeros_like(dkv_ref) if first else before[...]
 
-    base = pl.multiple_of(pl.program_id(0) * rows, rows)
-    cosine, sine = cos_ref[...], sin_ref[...]
-    for h in range(heads):
-        lanes = slice(h * HD, (h + 1) * HD)
-        there = slice(h * rows, (h + 1) * rows)
-        u = q_ref[:, lanes]
-        qs[there, :] = (u * cosine + pltpu.roll(u, HD // 2, 1) * sine).astype(jnp.bfloat16)
-        gs[there, :] = g_ref[:, lanes]
-    keys = k_ref[pl.ds(base, window), :]
-    values = v_ref[pl.ds(base, window), :]
-    scores = contract(keys, qs[...]) * scale
-    prob_grads = contract(values, gs[...])
+    projected = q_ref[...]
+    for n_ref, w_ref in zip(n_refs, w_refs):
+        projected += jnp.dot(n_ref[...], w_ref[...], preferred_element_type=jnp.float32)
     key_at = lax.broadcasted_iota(jnp.int32, (window, rows), 0)
-    query_at = lax.broadcasted_iota(jnp.int32, (window, rows), 1) + (window - rows)
-    allowed = (key_at >= low_ref[...] - base) & (key_at <= query_at)
-    for h in range(heads):
-        there = slice(h * rows, (h + 1) * rows)
-        weights = jnp.where(allowed, jnp.exp(scores[:, there]), 0.0)
-        softmax = weights * (1.0 / jnp.sum(weights, axis=0, keepdims=True))
-        prob_grad = prob_grads[:, there]
-        row_delta = jnp.sum(softmax * prob_grad, axis=0, keepdims=True)
-        ps[:, there] = softmax.astype(jnp.bfloat16)
-        ds[:, there] = (softmax * (prob_grad - row_delta)).astype(jnp.bfloat16)
-    dkv_ref[pl.ds(base, window), :HD] += (
-        jnp.dot(ds[...], qs[...], preferred_element_type=jnp.float32) * scale
-    )
-    dkv_ref[pl.ds(base, window), HD:] += jnp.dot(
-        ps[...], gs[...], preferred_element_type=jnp.float32
-    )
-    turned = jnp.dot(
-        kt_ref[:, pl.ds(base, window)], ds[...], preferred_element_type=jnp.float32
-    )
-    for h in range(heads):
-        there = slice(h * rows, (h + 1) * rows)
-        grad = turned[:, there].T * scale
-        back = grad * cosine - pltpu.roll(grad, HD // 2, 1) * sine
-        dq_ref[:, h * HD : (h + 1) * HD] = back.astype(jnp.bfloat16)
+    query_at = lax.broadcasted_iota(jnp.int32, (rows, rows), 1)
+    causal = key_at[:rows] <= query_at
+    staged = []
+    for block in range(blocks):
+        here = slice(block * rows, (block + 1) * rows)
+        base = pl.multiple_of((pl.program_id(0) * blocks + block) * rows, rows)
+        cosine, sine = cos_ref[here, :], sin_ref[here, :]
+        turned = []
+        for h in range(heads):
+            u = projected[here, h * HD : (h + 1) * HD]
+            turned.append((u * cosine + pltpu.roll(u, HD // 2, 1) * sine).astype(jnp.bfloat16))
+        queries = jnp.concatenate(turned, axis=0)
+        grads = jnp.concatenate([g_ref[here, h * HD : (h + 1) * HD] for h in range(heads)], axis=0)
+        scores = contract(k_ref[pl.ds(base, window), :], queries)
+        prob_grads = contract(v_ref[pl.ds(base, window), :], grads)
+        staged.append((here, base, cosine, sine, queries, grads, scores, prob_grads))
+    for here, base, cosine, sine, queries, grads, scores, prob_grads in staged:
+        low = low_ref[:, here] - base
+        inside = key_at >= low
+        allowed = (inside[:halo], inside[halo:] & causal)
+        probs, score_grads = [], []
+        for h in range(heads):
+            there = slice(h * rows, (h + 1) * rows)
+            grown = jnp.exp2(scores[:, there] * (scale * LOG2_E))
+            weights = jnp.concatenate(
+                [
+                    jnp.where(allowed[0], grown[:halo], 0.0),
+                    jnp.where(allowed[1], grown[halo:], 0.0),
+                ],
+                axis=0,
+            )
+            prob_grad = prob_grads[:, there]
+            share = 1.0 / jnp.sum(weights, axis=0, keepdims=True)
+            row_delta = jnp.sum(weights * prob_grad, axis=0, keepdims=True) * share
+            softmax = weights * share
+            probs.append(softmax.astype(jnp.bfloat16))
+            score_grads.append((softmax * (prob_grad - row_delta)).astype(jnp.bfloat16))
+        probs = jnp.concatenate(probs, axis=1)
+        score_grads = jnp.concatenate(score_grads, axis=1)
+        dkv_ref[pl.ds(base, window), :HD] += (
+            jnp.dot(score_grads, queries, preferred_element_type=jnp.float32) * scale
+        )
+        dkv_ref[pl.ds(base, window), HD:] += jnp.dot(
+            probs, grads, preferred_element_type=jnp.float32
+        )
+        query_grads = jnp.dot(
+            kt_ref[:, pl.ds(base, window)], score_grads, preferred_element_type=jnp.float32
+        )
+        for h in range(heads):
+            grad = query_grads[:, h * rows : (h + 1) * rows].T * scale
+            back = grad * cosine - pltpu.roll(grad, HD // 2, 1) * sine
+            dq_ref[here, h * HD : (h + 1) * HD] = back.astype(jnp.bfloat16)
 
     @pl.when(pl.program_id(0) == pl.num_programs(0) - 1)
     def _():
-        halo_ref[...] = dkv_ref[: halo_ref.shape[0], :].astype(jnp.bfloat16)
-
-
-def attend(q_proj, grads, keys, keys_turned, values, cosine, sine, low, before=None):
+        key_halo_ref[...] = dkv_ref[:halo, :HD].astype(jnp.bfloat16)
+        value_halo_ref[...] = dkv_ref[:halo, HD:].astype(jnp.bfloat16)
+
+
+def attend(q_proj, normed, weights, grads, keys, keys_turned, values, cosine, sine, low, before=None):
     tokens, width = q_proj.shape
     heads, rows = width // HD, 128
+    step = 2 * rows
     total = keys.shape[0]
     window = total - tokens + rows
     whole = lambda a: pl.BlockSpec(a.shape, lambda i: (0, 0))
-    by_rows = lambda w: pl.BlockSpec((rows, w), lambda i: (i, 0))
-    fixed = lambda n: pl.BlockSpec((n, 2 * HD), lambda i: (0, 0))
+    by_rows = lambda w: pl.BlockSpec((step, w), lambda i: (i, 0))
+    fixed = lambda n, w: pl.BlockSpec((n, w), lambda i: (0, 0))
     extra = [] if before is None else [before]
     return pl.pallas_call(
-        partial(attend_kernel, heads, rows, before is None),
-        grid=(tokens // rows,),
-        in_specs=[by_rows(width), by_rows(width), whole(keys), whole(keys_turned), whole(values),
-                  by_rows(HD), by_rows(HD), pl.BlockSpec((1, rows), lambda i: (0, i))]
-        + [fixed(total) for _ in extra],
-        out_specs=[by_rows(width), fixed(total - tokens), fixed(total)],
+        partial(attend_kernel, heads, rows, len(normed), before is None),
+        grid=(tokens // step,),
+        in_specs=[by_rows(width)]
+        + [by_rows(n.shape[1]) for n in normed]
+        + [whole(w) for w in weights]
+        + [by_rows(width), whole(keys), whole(keys_turned), whole(values)]
+        + [by_rows(HD), by_rows(HD), pl.BlockSpec((1, step), lambda i: (0, i))]
+        + [fixed(total, 2 * HD) for _ in extra],
+        out_specs=[by_rows(width)] + [fixed(total - tokens, HD)] * 2 + [fixed(total, 2 * HD)],
         out_shape=[jax.ShapeDtypeStruct((tokens, width), jnp.bfloat16),
-                   jax.ShapeDtypeStruct((total - tokens, 2 * HD), jnp.bfloat16),
+                   jax.ShapeDtypeStruct((total - tokens, HD), jnp.bfloat16),
+                   jax.ShapeDtypeStruct((total - tokens, HD), jnp.bfloat16),
                    jax.ShapeDtypeStruct((total, 2 * HD), jnp.float32)],
-        scratch_shapes=[pltpu.VMEM((heads * rows, HD), jnp.bfloat16)] * 2
-        + [pltpu.VMEM((window, heads * rows), jnp.bfloat16)] * 2,
         cost_estimate=pl.CostEstimate(
             flops=10 * tokens * window * width, bytes_accessed=12 * tokens * width,
             transcendentals=tokens * window * heads,
         ),
-    )(q_proj, grads, keys, keys_turned, values, cosine, sine, low, *extra)
-
-
-def spread_kernel(counts, ring_size, where, *refs):
+    )(q_proj, *normed, *weights, grads, keys, keys_turned, values, cosine, sine, low, *extra)
+
+
+def spread_blocks(where, wide, grads, rows):
+    members = where.shape[0] - 3
+    for block in range(members):
+        partner = (block % (members // 2)) * 2 + block // (members // 2)
+        source = pl.multiple_of(where[3 + partner] * rows, rows)
+        at = 0
+        for grad in grads:
+            wide[block * rows : (block + 1) * rows, at : at + grad.shape[1]] = grad[
+                pl.ds(source, rows), :
+            ]
+            at += grad.shape[1]
+
+
+def spread_first_kernel(counts, ring_size, where, *refs):
     grads, weights = refs[: counts[0]], refs[counts[0] : counts[0] + counts[1] * ring_size]
-    keep_ref, send_ref, wide, held, arrived = refs[counts[0] + counts[1] * ring_size :]
+    out_ref, wide, held, arrived = refs[counts[0] + counts[1] * ring_size :]
     members = where.shape[0] - 3
     step = held.shape[1] // members
-    rows = keep_ref.shape[2]
     s = pl.program_id(0)
 
     def copy(source, piece, c):
@@ -386,34 +426,79 @@
         for piece in range(ring_size):
             for c in range(counts[1]):
                 copy(weights[c * ring_size + piece], piece, c).start()
-        for block in range(members):
-            partner = (block % (members // 2)) * 2 + block // (members // 2)
-            source = pl.multiple_of(where[3 + partner] * rows, rows)
-            at = 0
-            for grad in grads:
-                wide[block * rows : (block + 1) * rows, at : at + grad.shape[1]] = grad[
-                    pl.ds(source, rows), :
-                ]
-                at += grad.shape[1]
+        spread_blocks(where, wide, grads, wide.shape[0] // members)
 
     for c in range(counts[1]):
         copy(weights[c * ring_size], s, c).wait()
     for owner in range(members):
         source = pl.multiple_of(where[3 + owner] * step, step)
-        total = contract(wide[...], held[s, pl.ds(source, step), :]).astype(jnp.bfloat16)
-        columns = slice(owner * step, (owner + 1) * step)
-        for u in range(members // 2):
-            keep_ref[u, 0, :, columns] = total[u * rows : (u + 1) * rows, :]
-            lower = (members // 2 + u) * rows
-            send_ref[u, 0, :, columns] = total[lower : lower + rows, :]
-
-
-def spread(where, grads, weights, ring_size):
+        out_ref[0, :, owner * step : (owner + 1) * step] = contract(
+            wide[...], held[s, pl.ds(source, step), :]
+        )
+
+
+def spread_first(where, grads, weights, ring_size):
+    tokens = grads[0].shape[0]
+    depth = sum(a.shape[1] for a in grads)
+    width = weights[0].shape[0]
+    chunks = len(weights) // ring_size
+    return pl.pallas_call(
+        partial(spread_first_kernel, (len(grads), chunks), ring_size),
+        grid_spec=pltpu.PrefetchScalarGridSpec(
+            num_scalar_prefetch=1,
+            grid=(ring_size,),
+            in_specs=[pl.BlockSpec(a.shape, lambda i, w: (0, 0)) for a in grads]
+            + [pl.BlockSpec(memory_space=pltpu.HBM) for _ in weights],
+            out_specs=pl.BlockSpec((1, tokens, width), lambda i, w: (i, 0, 0)),
+            scratch_shapes=[
+                pltpu.VMEM((tokens, depth), jnp.bfloat16),
+                pltpu.VMEM((ring_size, width, depth), jnp.bfloat16),
+                pltpu.SemaphoreType.DMA((ring_size, chunks)),
+            ],
+        ),
+        out_shape=jax.ShapeDtypeStruct((ring_size, tokens, width), jnp.float32),
+        compiler_params=pltpu.CompilerParams(vmem_limit_bytes=24 << 20),
+        cost_estimate=pl.CostEstimate(
+            flops=2 * tokens * width * ring_size * depth,
+            bytes_accessed=4 * tokens * width * ring_size,
+            transcendentals=0,
+        ),
+    )(where, *grads, *weights)
+
+
+def spread_last_kernel(count, where, so_far, *refs):
+    grads, weights = refs[:count], refs[count:-3]
+    keep_ref, send_ref, wide = refs[-3:]
+    members = where.shape[0] - 3
+    step = weights[0].shape[0] // members
+    rows = keep_ref.shape[2]
+    s = pl.program_id(0)
+
+    @pl.when(s == 0)
+    def _():
+        spread_blocks(where, wide, grads, rows)
+
+    for piece, weight in enumerate(weights):
+
+        @pl.when(s == piece)
+        def _():
+            for owner in range(members):
+                source = pl.multiple_of(where[3 + owner] * step, step)
+                lanes = slice(owner * step, (owner + 1) * step)
+                total = so_far[0, :, lanes] + contract(wide[...], weight[pl.ds(source, step), :])
+                total = total.astype(jnp.bfloat16)
+                for u in range(members // 2):
+                    keep_ref[u, 0, :, lanes] = total[u * rows : (u + 1) * rows, :]
+                    lower = (members // 2 + u) * rows
+                    send_ref[u, 0, :, lanes] = total[lower : lower + rows, :]
+
+
+def spread_last(where, so_far, grads, weights, ring_size):
     tokens = grads[0].shape[0]
     members = where.shape[0] - 3
     rows = tokens // members
     depth = sum(a.shape[1] for a in grads)
-    width = weights[0].shape[0] * ring_size
+    width = weights[0].shape[0]
     planes_per_half = ring_size // 2
     whole = lambda a: pl.BlockSpec(a.shape, lambda i, w: (0, 0))
 
@@ -422,28 +507,69 @@
         half = lax.rem(plane // planes_per_half + w[2], 2)
         return (0, half, 0, lax.rem(plane, planes_per_half))
 
-    shape = (members // 2, 2, rows, width // 2)
+    shape = (members // 2, 2, rows, width * planes_per_half)
     return pl.pallas_call(
-        partial(spread_kernel, (len(grads), len(weights) // ring_size), ring_size),
+        partial(spread_last_kernel, len(grads)),
         grid_spec=pltpu.PrefetchScalarGridSpec(
             num_scalar_prefetch=1,
             grid=(ring_size,),
-            in_specs=[whole(a) for a in grads]
-            + [pl.BlockSpec(memory_space=pl.ANY) for _ in weights],
-            out_specs=[pl.BlockSpec((members // 2, 1, rows, width // ring_size), out_at)] * 2,
-            scratch_shapes=[
-                pltpu.VMEM((tokens, depth), jnp.bfloat16),
-                pltpu.VMEM((ring_size, width // ring_size, depth), jnp.bfloat16),
-                pltpu.SemaphoreType.DMA((ring_size, len(weights) // ring_size)),
-            ],
+            in_specs=[pl.BlockSpec((1, tokens, width), lambda i, w: (i, 0, 0))]
+            + [whole(a) for a in grads]
+            + [pl.BlockSpec(memory_space=pltpu.VMEM) for a in weights],
+            out_specs=[pl.BlockSpec((members // 2, 1, rows, width), out_at)] * 2,
+            scratch_shapes=[pltpu.VMEM((tokens, depth), jnp.bfloat16)],
         ),
         out_shape=[jax.ShapeDtypeStruct(shape, jnp.bfloat16)] * 2,
+        compiler_params=pltpu.CompilerParams(vmem_limit_bytes=24 << 20),
         cost_estimate=pl.CostEstimate(
-            flops=2 * tokens * width * depth,
-            bytes_accessed=4 * tokens * width,
+            flops=2 * tokens * width * ring_size * depth,
+            bytes_accessed=4 * tokens * width * ring_size,
             transcendentals=0,
         ),
-    )(where, *grads, *weights)
+    )(where, so_far, *grads, *weights)
+
+
+def key_weights_kernel(ring_size, where, *refs):
+    members = where.shape[0] - 3
+    normed, grads = refs[:ring_size], refs[ring_size : ring_size + members]
+    out_refs, wide = refs[ring_size + members : -1], refs[-1]
+    width = grads[0].shape[1]
+    for owner in range(members):
+        for d in range(members):
+
+            @pl.when(where[3 + owner] == d)
+            def _():
+                wide[:, owner * width : (owner + 1) * width] = grads[d][...]
+
+    for n_ref, out_ref in zip(normed, out_refs):
+        out_ref[...] = lax.dot_general(
+            n_ref[...], wide[...], (((0,), (0,)), ((), ())), preferred_element_type=jnp.float32
+        ).astype(out_ref.dtype)
+
+
+def key_weights(where, normed, grads, rows):
+    tokens, members = grads[0].shape[0], len(grads)
+    width = members * grads[0].shape[1]
+    shape = (rows, width)
+    return pl.pallas_call(
+        partial(key_weights_kernel, len(normed)),
+        grid_spec=pltpu.PrefetchScalarGridSpec(
+            num_scalar_prefetch=1,
+            grid=(1,),
+            in_specs=[pl.BlockSpec((tokens, rows), lambda i, w: (0, 0)) for _ in normed]
+            + [pl.BlockSpec(g.shape, lambda i, w: (0, 0)) for g in grads],
+            out_specs=[pl.BlockSpec(shape, lambda i, w: (0, 0))] * len(normed),
+            scratch_shapes=[pltpu.VMEM((tokens, width), jnp.bfloat16)],
+        ),
+        out_shape=[jax.ShapeDtypeStruct(shape, jnp.float32)]
+        + [jax.ShapeDtypeStruct(shape, jnp.bfloat16)] * (len(normed) - 1),
+        compiler_params=pltpu.CompilerParams(vmem_limit_bytes=16 << 20),
+        cost_estimate=pl.CostEstimate(
+            flops=2 * tokens * width * rows * len(normed),
+            bytes_accessed=2 * tokens * (width + rows * len(normed)),
+            transcendentals=0,
+        ),
+    )(where, *normed, *grads)
 
 
 def grouped_device(hidden, norm_gain, w_query, w_key, w_value, upstream, cached, lengths):
@@ -521,8 +647,8 @@
 
     def project(pieces):
         total = None
-        for s in range(ring_size):
-            term = jnp.dot(normed[s], pieces[s], preferred_element_type=jnp.float32)
+        for s, piece in enumerate(pieces):
+            term = jnp.dot(normed[s], piece, preferred_element_type=jnp.float32)
             total = term if total is None else total + term
         return total
 
@@ -559,9 +685,7 @@
 
     q_pieces = []
     for c in range(q_chunks):
-        gate = lambda hop, block, c=c: (
-            after(block, q_pieces[c - 1][-1] if c else kv_rows) if hop == ring_size - 1 else block
-        )
+        gate = lambda hop, block, c=c: after(block, kv_rows) if c and hop == ring_size - 1 else block
         q_pieces.append(circulate(q_chunk[c], gate))
     halo = lax.ppermute(kv_rows, "dp", [(i, i + members) for i in range(devices - members)])
     kv_all = jnp.concatenate([halo, kv_rows], axis=0)
@@ -569,47 +693,45 @@
     keys_turned = keys.T
     query_dones, kv_sum = [], None
     for c in range(q_chunks):
-        pieces = q_pieces[c]
-        if c:
-            pieces = pieces[:-1] + [after(pieces[-1], query_dones[-1])]
-        query_done, halo_grad, kv_sum = attend(
-            project(pieces),
+        early = lax.optimization_barrier(project(q_pieces[c][:-1]))
+        query_done, key_halo, value_halo, kv_sum = attend(
+            early, normed[-1:], q_pieces[c][-1:],
             out_grad[:, c * chunk_width : (c + 1) * chunk_width],
             keys, keys_turned, values, cosine, sine, low, kv_sum,
         )
         query_dones.append(query_done)
-    back = lax.ppermute(halo_grad, "dp", [(i + members, i) for i in range(devices - members)])
-    kv_total = kv_sum[LONGEST:] + back.astype(jnp.float32)
-    key_grad = kv_total[:, :HD]
-    key_done = (key_grad * cosine - jnp.roll(key_grad, HD // 2, axis=1) * sine).astype(jnp.bfloat16)
-    value_done = kv_total[:, HD:].astype(jnp.bfloat16)
-
-    key_dones = jnp.concatenate(
-        place([key_done] + [to_partner(key_done, d) for d in range(1, members)]),
-        axis=1,
-    )
-    grad_wkey = None
-    for s in range(ring_size):
-        term = lax.dot_general(
-            normed[s][:, :weight_rows],
-            key_dones,
-            (((0,), (0,)), ((), ())),
-            preferred_element_type=jnp.float32,
-        )
-        if s:
-            term = along(term.astype(jnp.bfloat16), -s).astype(jnp.float32)
-        grad_wkey = term if grad_wkey is None else grad_wkey + term
-
-    weights = [piece for pieces in q_pieces + [kv_pieces] for piece in pieces]
-    keep, send = spread(where, query_dones + [key_done, value_done], weights, ring_size)
+    later = [(i + members, i) for i in range(devices - members)]
+    key_back = lax.ppermute(key_halo, "dp", later)
+    value_back = lax.ppermute(value_halo, "dp", later)
+    key_grad = kv_sum[LONGEST:, :HD] + key_back.astype(jnp.float32)
+    turned = jnp.roll(key_grad, HD // 2, axis=1)
+    key_done = (key_grad * cosine - turned * sine).astype(jnp.bfloat16)
+    value_grad = after(kv_sum[LONGEST:, HD:], key_done) + value_back.astype(jnp.float32)
+    value_done = value_grad.astype(jnp.bfloat16)
+
+    key_dones = [key_done] + [to_partner(key_done, d) for d in range(1, members)]
+    grad_wkey, *others = key_weights(where, normed, key_dones, weight_rows)
+    for s in range(1, ring_size):
+        term = along(others[s - 1], -s)
+        grad_wkey = grad_wkey + term.astype(jnp.float32)
+
+    weights = [
+        pltpu.with_memory_space_constraint(piece, pltpu.HBM)
+        for pieces in q_pieces
+        for piece in pieces
+    ]
+    so_far = spread_first(where, query_dones, weights, ring_size)
+    keep, send = spread_last(where, so_far, [key_done, value_done], kv_pieces, ring_size)
     wide = lambda a: a.astype(jnp.float32)
     narrow = lambda a: a.astype(jnp.bfloat16)
     other = to_partner(send, 1)
     both = lambda *at: wide(keep[at]) + wide(other[at])
     cut = half // 2
     low_cut, high_cut, every = slice(0, cut), slice(cut, half), slice(None)
-    left_half = to_partner(narrow(both(1, every, every, low_cut)), 2)
-    right_half = to_side(narrow(both(every, 1, every, high_cut)))
+    left_half = narrow(both(1, every, every, low_cut))
+    right_half = narrow(both(every, 1, every, high_cut))
+    left_half = to_partner(left_half, 2)
+    right_half = to_side(right_half)
     left = both(0, every, every, low_cut) + wide(left_half)
     right = both(every, 0, every, high_cut) + wide(right_half)
     left_sum = left[0] + wide(to_side(narrow(left[1])))

time: 252 us -> 232 us (0.921)
  matrix products: 19.5 us -> 8.77 us
  waiting for transfers between devices: 117 us -> 124 us
  Pallas kernels: 31.3 us -> 26.1 us
  other arithmetic: 25.1 us -> 20.4 us
  local copies, waits for them, and re-layouts: 15.7 us -> 12 us
    dot_general x16 -> x10, matrix products: 18.9 us -> 8.12 us  [project(): term = jnp.dot(normed[s], piece, preferred_element_type=jnp.float32)]
    ppermute x15, waiting for transfers between devices: 68.6 us -> 77.7 us  [along(): return lax.ppermute(block, 'dp', route)]
    ppermute x14, waiting for transfers between devices: 42.6 us -> 34 us  [to_partner(): return lax.ppermute(block, 'dp', [(i, i ^ d) for i in range(devices)])]
    ppermute x4, waiting for transfers between devices: 2.93 us -> 8.58 us  [to_side(): return lax.ppermute(block, 'tensor', [(i, i ^ 1) for i in range(tensors)])]
    pallas_call x1, Pallas kernels: 7.24 us -> 2.69 us  [norm_pieces(): pl.pallas_call(norm_kernel, grid_spec=pltpu.PrefetchScalarGridSpec(num_sc...]
    ppermute x1, waiting for transfers between devices: 0.01 us -> 3.5 us  [grouped_device(): lax.ppermute(kv_rows, 'dp', [(i, i + members) for i in range(devices - me...]
    ppermute x1 -> x2, waiting for transfers between devices: 3.36 us -> 0.4 us  [the longest x1 0.4 us: grouped_device(): key_back = lax.ppermute(key_halo, 'dp', later)]
    concatenate x12, other arithmetic: 3.53 us -> 0.92 us  [pack_kv(): pairs.append(lax.optimization_barrier(jnp.concatenate(cut, axis=1)))]
  transfers between devices with their start and end apart: 36 -> 37, of which waited for: 20 -> 16; matrix products, arithmetic and copies ran while one was open for 19% -> 16% of each run, Pallas kernels for 6% -> 7%
where the time goes in v3:
time: 232 us; the launch traced here: 231 us
  waiting for transfers between devices  124 us (53%)
  starting transfers between devices  37.5 us (16%)
  Pallas kernels  26.1 us (11%)
  other arithmetic  20.4 us (9%)
  local copies, waits for them, and re-layouts  12 us (5%)
  matrix products  8.77 us (4%)
    ppermute x15, waiting for transfers between devices, along(): return lax.ppermute(block, 'dp', route)  77.7 us
    ppermute x14, waiting for transfers between devices, to_partner(): return lax.ppermute(block, 'dp', [(i, i ^ d) for i in range(devices)])  34 us
    ppermute x15, starting transfers between devices, along(): return lax.ppermute(block, 'dp', route)  17.6 us
    pallas_call x2, Pallas kernels, attend(): pl.pallas_call(partial(attend_kernel, heads, rows, len(normed), before is...  13.8 us
    ppermute x14, starting transfers between devices, to_partner(): return lax.ppermute(block, 'dp', [(i, i ^ d) for i in range(devices)])  9.95 us
    ppermute x4, waiting for transfers between devices, to_side(): return lax.ppermute(block, 'tensor', [(i, i ^ 1) for i in range(tensors)])  8.58 us
    dot_general x10, matrix products, project(): term = jnp.dot(normed[s], piece, preferred_element_type=jnp.float32)  8.12 us
    dynamic_slice x9, local copies, waits for them, and re-layouts, columns(): return lax.dynamic_slice_in_dim(array, owner * width, width, 1)  5.72 us
  transfers between devices with their start and end apart: 37, of which 16 were waited for; matrix products, arithmetic and copies ran while one was open for 16% of the time, Pallas kernels for 7%

profile of v3, /device:TPU:0, one launch (start us, length us, event | category | flops | bytes accessed | tf_op | source)
XLA Modules:
  0.0 230.6 jit_solution(4686369840088767191)
XLA Ops:
  0.7 3.1 %collective-permute-start = (bf16[128,2048]{1,0:T(8,128)(2,1)}, bf16[128,2048]{1,0:T(8,128)(2,1)S(1)}, u32[]{:S(2)}, u32[]{:S(2)}) collective-permute-start(bf16[128,2048]{1,0:T(8,128)(2,1)} %param.8), channel_id=1, source_target_pairs={{0,1},{1,0},{2,3},{3,2},{4,5},{5,4},{6,7},{7,6},{8,9},{9,8},{10,11... | collective-permute-start | bytes 1572872 | tf_op jit(solution)/shard_map/ppermute | solution.py:593
  3.7 1.5 collective-permute-start.1
  5.3 2.0 collective-permute-start.10
  7.3 1.6 collective-permute-start.11
  8.8 1.6 constant_dynamic-slice_fusion.31
  10.5 1.6 constant_dynamic-slice_fusion.30
  14.4 1.3 constant_dynamic-slice_fusion.38
  16.6 0.8 pad_maximum_fusion.11
  17.4 0.8 pad_maximum_fusion.12
  19.6 1.6 collective-permute-start.5
  21.2 1.0 constant_dynamic-slice_fusion.5
  22.4 16.0 %collective-permute-done.5 = bf16[384,512]{1,0:T(8,128)(2,1)S(1)} collective-permute-done((bf16[384,512]{1,0:T(8,128)(2,1)}, bf16[384,512]{1,0:T(8,128)(2,1)S(1)}, u32[]{:S(2)}, u32[]{:S(2)}) %collective-permute-start.5) | collective-permute-done | bytes 393248 | tf_op jit(solution)/shard_map/ppermute | solution.py:590
  38.4 6.0 %collective-permute-done.6 = bf16[384,512]{1,0:T(8,128)(2,1)S(1)} collective-permute-done((bf16[384,512]{1,0:T(8,128)(2,1)S(1)}, bf16[384,512]{1,0:T(8,128)(2,1)S(1)}, u32[]{:S(2)}, u32[]{:S(2)}) %collective-permute-start.6) | collective-permute-done | bytes 393248 | tf_op jit(solution)/shard_map/ppermute | solution.py:590
  44.4 1.6 collective-permute-start.12
  46.1 1.6 collective-permute-start.13
  48.0 1.6 collective-permute-start.20
  51.2 0.8 fusion.31
  52.0 3.6 %collective-permute-done.12 = bf16[256,512]{1,0:T(8,128)(2,1)S(1)} collective-permute-done((bf16[256,512]{1,0:T(8,128)(2,1)}, bf16[256,512]{1,0:T(8,128)(2,1)S(1)}, u32[]{:S(2)}, u32[]{:S(2)}) %collective-permute-start.12) | collective-permute-done | bytes 262176 | tf_op jit(solution)/shard_map/ppermute | solution.py:601
  55.6 5.6 %collective-permute-done.13 = bf16[256,512]{1,0:T(8,128)(2,1)S(1)} collective-permute-done((bf16[256,512]{1,0:T(8,128)(2,1)S(1)}, bf16[256,512]{1,0:T(8,128)(2,1)S(1)}, u32[]{:S(2)}, u32[]{:S(2)}) %collective-permute-start.13) | collective-permute-done | bytes 262176 | tf_op jit(solution)/shard_map/ppermute | solution.py:601
  61.3 28.0 %collective-permute-done.14 = bf16[256,512]{1,0:T(8,128)(2,1)S(1)} collective-permute-done((bf16[256,512]{1,0:T(8,128)(2,1)S(1)}, bf16[256,512]{1,0:T(8,128)(2,1)S(1)}, u32[]{:S(2)}, u32[]{:S(2)}) %collective-permute-start.14) | collective-permute-done | bytes 262176 | tf_op jit(solution)/shard_map/ppermute | solution.py:601
  89.4 5.5 %collective-permute-done.15 = bf16[256,512]{1,0:T(8,128)(2,1)S(1)} collective-permute-done((bf16[256,512]{1,0:T(8,128)(2,1)S(1)}, bf16[256,512]{1,0:T(8,128)(2,1)S(1)}, u32[]{:S(2)}, u32[]{:S(2)}) %collective-permute-start.15) | collective-permute-done | bytes 262176 | tf_op jit(solution)/shard_map/ppermute | solution.py:601
  95.1 1.0 collective-permute-start.17
  96.3 0.9 collective-permute-start.18
  97.2 14.7 %collective-permute-done.8.refs_4_ = bf16[1024,256]{1,0:T(8,128)(2,1)} collective-permute-done((bf16[1024,256]{1,0:T(8,128)(2,1)S(1)}, bf16[1024,256]{1,0:T(8,128)(2,1)}, u32[]{:S(2)}, u32[]{:S(2)}) %collective-permute-start.8) | collective-permute-done | bytes 524320 | tf_op jit(solution)/shard_map/ppermute | solution.py:601
  112.0 2.7 %shard_map.95 = (bf16[512,1024]{1,0:T(8,128)(2,1)S(1)}, bf16[512,1024]{1,0:T(8,128)(2,1)S(1)}, bf16[512,1024]{1,0:T(8,128)(2,1)S(1)}, bf16[512,1024]{1,0:T(8,128)(2,1)S(1)}, f32[512,128]{1,0:T(8,128)S(1)}) custom-call(s32[7]{0:T(128)S(1)} %stack.58.where, bf16[2,2,128,2048]{3,2,1,0:T(8,128)(2,1)S(1)} %bitcast.76, ...), custom_call_target="tpu_custom_call" | custom-call | flops 16777216 | bytes 8388608 | tf_op jit(solution)/shard_map/pallas_call | solution.py:272
  114.8 5.4 %collective-permute-done.18 = bf16[1024,256]{1,0:T(8,128)(2,1)S(1)} collective-permute-done((bf16[1024,256]{1,0:T(8,128)(2,1)S(1)}, bf16[1024,256]{1,0:T(8,128)(2,1)S(1)}, u32[]{:S(2)}, u32[]{:S(2)}) %collective-permute-start.18) | collective-permute-done | bytes 524320 | tf_op jit(solution)/shard_map/ppermute | solution.py:590
  122.7 1.9 fusion.16
  124.6 1.6 collective-permute-start.19
  126.3 0.8 pad_maximum_fusion.10.refs_5_
  127.1 0.8 pad_maximum_fusion.9.refs_4_
  128.0 0.8 pad_maximum_fusion.8.refs_3_
  128.8 1.6 collective-permute-start.22
  132.2 2.3 convolution_add_fusion.q_ref
  134.5 2.3 convolution_add_fusion.3.q_ref
  136.8 0.8 pad_maximum_fusion.7.refs_2_
  137.6 3.5 %collective-permute-done.19 = bf16[512,256]{1,0:T(8,128)(2,1)S(1)} collective-permute-done((bf16[512,256]{1,0:T(8,128)(2,1)S(1)}, bf16[512,256]{1,0:T(8,128)(2,1)S(1)}, u32[]{:S(2)}, u32[]{:S(2)}) %collective-permute-start.19) | collective-permute-done | bytes 262176 | tf_op jit(solution)/shard_map/ppermute | solution.py:690
  141.2 0.9 fusion.32
  142.1 0.9 copy.33.refs_4_
  143.0 6.7 %shard_map.96 = (bf16[512,256]{1,0:T(8,128)(2,1)}, bf16[512,128]{1,0:T(8,128)(2,1)}, bf16[512,128]{1,0:T(8,128)(2,1)}, f32[1024,256]{1,0:T(8,128)}) custom-call(f32[512,256]{1,0:T(8,128)} %convolution_add_fusion.3.q_ref, bf16[512,1024]{1,0:T(8,128)(2,1)} %copy-done.2, bf16[1024,256]{1,0:T(8,128)(2,1)} %collective-permute-done.9.refs_1_.refs_5_, ...), custom_call_target="tpu_custom_call" | custom-call | flops 838860800 | bytes 1572864 | tf_op jit(solution)/shard_map/pallas_call | solution.py:377
  149.7 1.3 collective-permute-done.22.refs_1_.refs_9_
  151.0 7.1 %shard_map.97 = (bf16[512,256]{1,0:T(8,128)(2,1)}, bf16[512,128]{1,0:T(8,128)(2,1)}, bf16[512,128]{1,0:T(8,128)(2,1)}, f32[1024,256]{1,0:T(8,128)}) custom-call(f32[512,256]{1,0:T(8,128)} %convolution_add_fusion.q_ref, bf16[512,1024]{1,0:T(8,128)(2,1)} %copy-done.2, bf16[1024,256]{1,0:T(8,128)(2,1)} %collective-permute-done.22.refs_1_.refs_9_, ...), custom_call_target="tpu_custom_call" | custom-call | flops 838860800 | bytes 1572864 | tf_op jit(solution)/shard_map/pallas_call | solution.py:377
  158.1 1.3 collective-permute-start.23
  159.4 1.3 collective-permute-start.24
  160.8 0.9 copy-done.10
  161.7 4.8 %shard_map.98.so_far = f32[4,512,1024]{2,1,0:T(8,128)S(1)} custom-call(s32[7]{0:T(128)S(1)} %stack.58.where, bf16[512,256]{1,0:T(8,128)(2,1)S(1)} %copy-done.9, bf16[512,256]{1,0:T(8,128)(2,1)S(1)} %copy-done.10, bf16[1024,256]{1,0:T(8,128)(2,1)} %copy-done.20, bf16[1024,256]{1,0:T(8,128)(2,1)} %copy-done.22, ...), custom_call_target="tpu_custom_call" | custom-call | flops 2147483648 | bytes 8388608 | tf_op jit(solution)/shard_map/pallas_call | solution.py:445
  167.6 1.0 fusion.18.refs_0_.refs_4_
  168.7 3.2 %shard_map.99 = (bf16[2,2,128,2048]{3,2,1,0:T(8,128)(2,1)S(1)}, bf16[2,2,128,2048]{3,2,1,0:T(8,128)(2,1)S(1)}) custom-call(s32[7]{0:T(128)S(1)} %stack.58.where, f32[4,512,1024]{2,1,0:T(8,128)S(1)} %shard_map.98.so_far, bf16[512,128]{1,0:T(8,128)(2,1)S(1)} %fusion.18.refs_0_.refs_4_, bf16[512,128]{1,0:T(8,128)(2,1)S(1)} %add_convert_fusion.2.refs_1_, ...), custom_call_target="tpu_custom_call" | custom-call | flops 1073741824 | bytes 8388608 | tf_op jit(solution)/shard_map/pallas_call | solution.py:511
  171.9 4.1 %collective-permute-done.25 = bf16[2,2,128,2048]{3,2,1,0:T(8,128)(2,1)S(1)} collective-permute-done((bf16[2,2,128,2048]{3,2,1,0:T(8,128)(2,1)S(1)}, bf16[2,2,128,2048]{3,2,1,0:T(8,128)(2,1)S(1)}, u32[]{:S(2)}, u32[]{:S(2)}) %collective-permute-start.25) | collective-permute-done | bytes 2097184 | tf_op jit(solution)/shard_map/ppermute | solution.py:590
  176.1 1.2 fusion.10
  177.8 1.0 fusion.9
  178.8 1.3 collective-permute-start.26
  180.1 0.9 dynamic-slice_reduce_fusion
  181.9 1.1 collective-permute-start.33
  183.0 8.6 %collective-permute-done.28 = bf16[2,128,1024]{2,1,0:T(8,128)(2,1)} collective-permute-done((bf16[2,128,1024]{2,1,0:T(8,128)(2,1)}, bf16[2,128,1024]{2,1,0:T(8,128)(2,1)}, u32[]{:S(2)}, u32[]{:S(2)}) %collective-permute-start.28) | collective-permute-done | bytes 524320 | tf_op jit(solution)/shard_map/ppermute | solution.py:593
  191.6 2.3 %collective-permute-done.26 = bf16[2,128,1024]{2,1,0:T(8,128)(2,1)} collective-permute-done((bf16[2,128,1024]{2,1,0:T(8,128)(2,1)}, bf16[2,128,1024]{2,1,0:T(8,128)(2,1)}, u32[]{:S(2)}, u32[]{:S(2)}) %collective-permute-start.26) | collective-permute-done | bytes 524320 | tf_op jit(solution)/shard_map/ppermute | solution.py:590
  193.9 2.4 %bitcast_add_fusion.1 = (f32[2,128,1024]{2,1,0:T(8,128)S(1)}, f32[2,128,1024]{2,1,0:T(8,128)S(1)}) fusion(bf16[2,128,1024]{2,1,0:T(8,128)(2,1)} %collective-permute-done.26, bf16[2,2,128,2048]{3,2,1,0:T(8,128)(2,1)} %copy-done.18, bf16[2,2,128,2048]{3,2,1,0:T(8,128)(2,1)} %copy-done.4, bf16[2,128,1024]{2,1,0:T(8,128)(2,1)} %collective-permute-done.28), kind=kLoop, calls=%fused_computation.21 | loop fusion | flops 2621440 | bytes 5242880 | tf_op jit(solution)/shard_map/add | solution.py:735
  196.4 1.6 collective-permute-start.27
  198.0 1.4 collective-permute-start.29
  199.4 1.6 shard_map.100
  201.1 6.7 %collective-permute-start.34 = (bf16[256,512]{1,0:T(8,128)(2,1)S(1)}, bf16[256,512]{1,0:T(8,128)(2,1)S(1)}, u32[]{:S(2)}, u32[]{:S(2)}) collective-permute-start(bf16[256,512]{1,0:T(8,128)(2,1)S(1)} %get-tuple-element.43), channel_id=1, source_target_pairs={{0,24},{2,26},{4,28},{6,30},{8,0},{10,2},{12,4},{14,6},{16,8},{18,... | collective-permute-start | bytes 786440 | tf_op jit(solution)/shard_map/ppermute | solution.py:601
  209.4 5.1 %collective-permute-done.34 = bf16[256,512]{1,0:T(8,128)(2,1)S(1)} collective-permute-done((bf16[256,512]{1,0:T(8,128)(2,1)S(1)}, bf16[256,512]{1,0:T(8,128)(2,1)S(1)}, u32[]{:S(2)}, u32[]{:S(2)}) %collective-permute-start.34) | collective-permute-done | bytes 262176 | tf_op jit(solution)/shard_map/ppermute | solution.py:601
  214.5 13.9 %collective-permute-done.35 = bf16[256,512]{1,0:T(8,128)(2,1)S(1)} collective-permute-done((bf16[256,512]{1,0:T(8,128)(2,1)S(1)}, bf16[256,512]{1,0:T(8,128)(2,1)S(1)}, u32[]{:S(2)}, u32[]{:S(2)}) %collective-permute-start.35) | collective-permute-done | bytes 262176 | tf_op jit(solution)/shard_map/ppermute | solution.py:601
  228.4 0.9 convert_add_fusion
  229.3 1.2 fusion.7
  (178 shorter events, 15.6 us)
Async XLA Ops:
  0.6 49.7 %copy-start = (f32[16,2048]{1,0:T(8,128)S(1)}, f32[16,2048]{1,0:T(8,128)}, u32[]{:S(2)}) copy-start(f32[16,2048]{1,0:T(8,128)} %param.14) | copy-start | bytes 393220
  0.6 15.0 %copy-start.23 = (bf16[128,2048]{1,0:T(8,128)(2,1)S(1)}, bf16[128,2048]{1,0:T(8,128)(2,1)}, u32[]{:S(2)}) copy-start(bf16[128,2048]{1,0:T(8,128)(2,1)} %param.13) | copy-start | bytes 1572868
  0.7 47.3 %collective-permute-start = (bf16[128,2048]{1,0:T(8,128)(2,1)}, bf16[128,2048]{1,0:T(8,128)(2,1)S(1)}, u32[]{:S(2)}, u32[]{:S(2)}) collective-permute-start(bf16[128,2048]{1,0:T(8,128)(2,1)} %param.8), channel_id=1, source_target_pairs={{0,1},{1,0},{2,3},{3,2},{4,5},{5,4},{6,7},{7,6},{8,9},{9,8},{10,11... | collective-permute-start | bytes 1572872 | tf_op jit(solution)/shard_map/ppermute | solution.py:593
  3.7 45.9 %collective-permute-start.1 = (bf16[128,2048]{1,0:T(8,128)(2,1)}, bf16[128,2048]{1,0:T(8,128)(2,1)S(1)}, u32[]{:S(2)}, u32[]{:S(2)}) collective-permute-start(bf16[128,2048]{1,0:T(8,128)(2,1)} %param.8), channel_id=1, source_target_pairs={{0,4},{2,6},{4,0},{6,2},{8,12},{10,14},{12,8},{14,10},{16,20},{18,... | collective-permute-start | bytes 1572872 | tf_op jit(solution)/shard_map/ppermute | solution.py:590
  5.2 44.7 %collective-permute-start.2 = (bf16[128,2048]{1,0:T(8,128)(2,1)}, bf16[128,2048]{1,0:T(8,128)(2,1)S(1)}, u32[]{:S(2)}, u32[]{:S(2)}) collective-permute-start(bf16[128,2048]{1,0:T(8,128)(2,1)} %param.8), channel_id=1, source_target_pairs={{0,5},{1,4},{2,7},{3,6},{4,1},{5,0},{6,3},{7,2},{8,13},{9,12},{10,... | collective-permute-start | bytes 1572872 | tf_op jit(solution)/shard_map/ppermute | solution.py:597
  5.3 14.3 %collective-permute-start.10 = (bf16[256,512]{1,0:T(8,128)(2,1)}, bf16[256,512]{1,0:T(8,128)(2,1)}, u32[]{:S(2)}, u32[]{:S(2)}) collective-permute-start(bf16[256,512]{1,0:T(8,128)(2,1)} %param.11), channel_id=1, source_target_pairs={{0,8},{2,10},{4,12},{6,14},{8,16},{10,18},{12,20},{14,22},{16,24},... | collective-permute-start | bytes 786440 | tf_op jit(solution)/shard_map/ppermute | solution.py:601
  7.3 14.9 %collective-permute-start.11 = (bf16[256,512]{1,0:T(8,128)(2,1)}, bf16[256,512]{1,0:T(8,128)(2,1)S(1)}, u32[]{:S(2)}, u32[]{:S(2)}) collective-permute-start(bf16[256,512]{1,0:T(8,128)(2,1)} %param.12), channel_id=1, source_target_pairs={{0,8},{2,10},{4,12},{6,14},{8,16},{10,18},{12,20},{14,22},{16,24},... | collective-permute-start | bytes 786440 | tf_op jit(solution)/shard_map/ppermute | solution.py:601
  14.4 2.0 copy-start.33
  15.7 3.1 %copy-start.28 = (bf16[256,128]{1,0:T(8,128)(2,1)S(1)}, bf16[256,128]{1,0:T(8,128)(2,1)}, u32[]{:S(2)}) copy-start(bf16[256,128]{1,0:T(8,128)(2,1)} %get-tuple-element.93) | copy-start | bytes 196612
  15.7 3.1 %copy-start.29 = (bf16[256,128]{1,0:T(8,128)(2,1)S(1)}, bf16[256,128]{1,0:T(8,128)(2,1)}, u32[]{:S(2)}) copy-start(bf16[256,128]{1,0:T(8,128)(2,1)} %get-tuple-element.95) | copy-start | bytes 196612
  15.7 3.1 %copy-start.30 = (bf16[256,128]{1,0:T(8,128)(2,1)S(1)}, bf16[256,128]{1,0:T(8,128)(2,1)}, u32[]{:S(2)}) copy-start(bf16[256,128]{1,0:T(8,128)(2,1)} %get-tuple-element.97) | copy-start | bytes 196612
  15.7 3.1 %copy-start.31 = (bf16[256,128]{1,0:T(8,128)(2,1)S(1)}, bf16[256,128]{1,0:T(8,128)(2,1)}, u32[]{:S(2)}) copy-start(bf16[256,128]{1,0:T(8,128)(2,1)} %get-tuple-element.99) | copy-start | bytes 196612
  15.7 3.1 %copy-start.26 = (bf16[256,128]{1,0:T(8,128)(2,1)S(1)}, bf16[256,128]{1,0:T(8,128)(2,1)}, u32[]{:S(2)}) copy-start(bf16[256,128]{1,0:T(8,128)(2,1)} %get-tuple-element.92) | copy-start | bytes 196612
  15.7 3.1 %copy-start.27 = (bf16[256,128]{1,0:T(8,128)(2,1)S(1)}, bf16[256,128]{1,0:T(8,128)(2,1)}, u32[]{:S(2)}) copy-start(bf16[256,128]{1,0:T(8,128)(2,1)} %get-tuple-element.96) | copy-start | bytes 196612
  16.5 106.1 %copy-start.16 = (f32[512,64]{1,0:T(8,128)}, f32[512,64]{1,0:T(8,128)S(1)}, u32[]{:S(2)}) copy-start(f32[512,64]{1,0:T(8,128)S(1)} %broadcast_multiply_fusion) | copy-start | bytes 393220
  19.6 18.8 %collective-permute-start.5 = (bf16[384,512]{1,0:T(8,128)(2,1)}, bf16[384,512]{1,0:T(8,128)(2,1)S(1)}, u32[]{:S(2)}, u32[]{:S(2)}) collective-permute-start(bf16[384,512]{1,0:T(8,128)(2,1)} %pad_maximum_fusion.12), channel_id=1, source_target_pairs={{0,4},{2,6},{4,0},{6,2},{8,12},{10,14},{12,8},{14,10},{16,20},{18,... | collective-permute-start | bytes 1179656 | tf_op jit(solution)/shard_map/ppermute | solution.py:590
  22.1 22.3 %collective-permute-start.6 = (bf16[384,512]{1,0:T(8,128)(2,1)S(1)}, bf16[384,512]{1,0:T(8,128)(2,1)S(1)}, u32[]{:S(2)}, u32[]{:S(2)}) collective-permute-start(bf16[384,512]{1,0:T(8,128)(2,1)S(1)} %pad_maximum_fusion.13), channel_id=1, source_target_pairs={{0,6},{2,4},{4,2},{6,0},{8,14},{10,12},{12,10},{14,8},{16,22},{18,... | collective-permute-start | bytes 1179656 | tf_op jit(solution)/shard_map/ppermute | solution.py:590
  38.4 7.7 %collective-permute-start.4 = (bf16[384,512]{1,0:T(8,128)(2,1)}, bf16[384,512]{1,0:T(8,128)(2,1)S(1)}, u32[]{:S(2)}, u32[]{:S(2)}) collective-permute-start(bf16[384,512]{1,0:T(8,128)(2,1)} %pad_maximum_fusion.11), channel_id=1, source_target_pairs={{0,2},{2,0},{4,6},{6,4},{8,10},{10,8},{12,14},{14,12},{16,18},{18,... | collective-permute-start | bytes 1179656 | tf_op jit(solution)/shard_map/ppermute | solution.py:590
  44.4 11.2 %collective-permute-start.12 = (bf16[256,512]{1,0:T(8,128)(2,1)}, bf16[256,512]{1,0:T(8,128)(2,1)S(1)}, u32[]{:S(2)}, u32[]{:S(2)}) collective-permute-start(bf16[256,512]{1,0:T(8,128)(2,1)} %collective-permute-done.10), channel_id=1, source_target_pairs={{0,8},{2,10},{4,12},{6,14},{8,16},{10,18},{12,20},{14,22},{16,24},... | collective-permute-start | bytes 786440 | tf_op jit(solution)/shard_map/ppermute | solution.py:601
  46.1 15.2 %collective-permute-start.13 = (bf16[256,512]{1,0:T(8,128)(2,1)S(1)}, bf16[256,512]{1,0:T(8,128)(2,1)S(1)}, u32[]{:S(2)}, u32[]{:S(2)}) collective-permute-start(bf16[256,512]{1,0:T(8,128)(2,1)S(1)} %collective-permute-done.11), channel_id=1, source_target_pairs={{0,8},{2,10},{4,12},{6,14},{8,16},{10,18},{12,20},{14,22},{16,24},... | collective-permute-start | bytes 786440 | tf_op jit(solution)/shard_map/ppermute | solution.py:601
  47.8 2.1 copy-start.13
  48.0 2.2 copy-start.19
  48.0 2.2 copy-start.20
  48.0 48.3 %collective-permute-start.20 = (bf16[1024,256]{1,0:T(8,128)(2,1)S(1)}, bf16[1024,256]{1,0:T(8,128)(2,1)S(1)}, u32[]{:S(2)}, u32[]{:S(2)}) collective-permute-start(bf16[1024,256]{1,0:T(8,128)(2,1)S(1)} %get-tuple-element.56.refs_6_), channel_id=1, source_target_pairs={{0,8},{2,10},{4,12},{6,14},{8,16},{10,18},{12,20},{14,22},{16,24},... | collective-permute-start | bytes 1572872 | tf_op jit(solution)/shard_map/ppermute | solution.py:601
  49.6 46.5 %collective-permute-start.7 = (bf16[1024,256]{1,0:T(8,128)(2,1)S(1)}, bf16[1024,256]{1,0:T(8,128)(2,1)S(1)}, u32[]{:S(2)}, u32[]{:S(2)}) collective-permute-start(bf16[1024,256]{1,0:T(8,128)(2,1)S(1)} %get-tuple-element.57.refs_2_), channel_id=1, source_target_pairs={{0,8},{2,10},{4,12},{6,14},{8,16},{10,18},{12,20},{14,22},{16,24},... | collective-permute-start | bytes 1572872 | tf_op jit(solution)/shard_map/ppermute | solution.py:601
  50.2 61.8 %collective-permute-start.3 = (bf16[2,2,128,2048]{3,2,1,0:T(8,128)(2,1)S(1)}, bf16[2,2,128,2048]{3,2,1,0:T(8,128)(2,1)S(1)}, u32[]{:S(2)}, u32[]{:S(2)}) collective-permute-start(bf16[2,2,128,2048]{3,2,1,0:T(8,128)(2,1)S(1)} %bitcast.75), channel_id=1, source_target_pairs={{0,2},{2,0},{4,6},{6,4},{8,10},{10,8},{12,14},{14,12},{16,18},{18,... | collective-permute-start | bytes 6291464 | tf_op jit(solution)/shard_map/ppermute | solution.py:590
  55.6 33.7 %collective-permute-start.14 = (bf16[256,512]{1,0:T(8,128)(2,1)S(1)}, bf16[256,512]{1,0:T(8,128)(2,1)S(1)}, u32[]{:S(2)}, u32[]{:S(2)}) collective-permute-start(bf16[256,512]{1,0:T(8,128)(2,1)S(1)} %collective-permute-done.12), channel_id=1, source_target_pairs={{0,8},{2,10},{4,12},{6,14},{8,16},{10,18},{12,20},{14,22},{16,24},... | collective-permute-start | bytes 786440 | tf_op jit(solution)/shard_map/ppermute | solution.py:601
  61.2 33.6 %collective-permute-start.15 = (bf16[256,512]{1,0:T(8,128)(2,1)S(1)}, bf16[256,512]{1,0:T(8,128)(2,1)S(1)}, u32[]{:S(2)}, u32[]{:S(2)}) collective-permute-start(bf16[256,512]{1,0:T(8,128)(2,1)S(1)} %collective-permute-done.13), channel_id=1, source_target_pairs={{0,8},{2,10},{4,12},{6,14},{8,16},{10,18},{12,20},{14,22},{16,24},... | collective-permute-start | bytes 786440 | tf_op jit(solution)/shard_map/ppermute | solution.py:601
  94.9 17.0 %copy-start.11 = (f32[4096]{0:T(1024)S(1)}, f32[4096]{0:T(1024)}, u32[]{:S(2)}) copy-start(f32[4096]{0:T(1024)} %param.9) | copy-start | bytes 49156
  95.0 19.7 %collective-permute-start.16 = (bf16[1024,256]{1,0:T(8,128)(2,1)S(1)}, bf16[1024,256]{1,0:T(8,128)(2,1)S(1)}, u32[]{:S(2)}, u32[]{:S(2)}) collective-permute-start(bf16[1024,256]{1,0:T(8,128)(2,1)S(1)} %pad_maximum_fusion.4), channel_id=1, source_target_pairs={{0,2},{2,0},{4,6},{6,4},{8,10},{10,8},{12,14},{14,12},{16,18},{18,... | collective-permute-start | bytes 1572872 | tf_op jit(solution)/shard_map/ppermute | solution.py:590
  95.1 19.6 %collective-permute-start.17 = (bf16[1024,256]{1,0:T(8,128)(2,1)S(1)}, bf16[1024,256]{1,0:T(8,128)(2,1)S(1)}, u32[]{:S(2)}, u32[]{:S(2)}) collective-permute-start(bf16[1024,256]{1,0:T(8,128)(2,1)S(1)} %pad_maximum_fusion.5), channel_id=1, source_target_pairs={{0,4},{2,6},{4,0},{6,2},{8,12},{10,14},{12,8},{14,10},{16,20},{18,... | collective-permute-start | bytes 1572872 | tf_op jit(solution)/shard_map/ppermute | solution.py:590
  96.1 35.2 %copy-start.22 = (bf16[1024,256]{1,0:T(8,128)(2,1)}, bf16[1024,256]{1,0:T(8,128)(2,1)S(1)}, u32[]{:S(2)}) copy-start(bf16[1024,256]{1,0:T(8,128)(2,1)S(1)} %collective-permute-done.7.refs_3_) | copy-start | bytes 1572868
  96.1 15.8 %collective-permute-start.8 = (bf16[1024,256]{1,0:T(8,128)(2,1)S(1)}, bf16[1024,256]{1,0:T(8,128)(2,1)}, u32[]{:S(2)}, u32[]{:S(2)}) collective-permute-start(bf16[1024,256]{1,0:T(8,128)(2,1)S(1)} %collective-permute-done.7.refs_3_), channel_id=1, source_target_pairs={{0,8},{2,10},{4,12},{6,14},{8,16},{10,18},{12,20},{14,22},{16,24},... | collective-permute-start | bytes 1572872 | tf_op jit(solution)/shard_map/ppermute | solution.py:601
  96.3 34.1 %copy-start.21 = (bf16[1024,256]{1,0:T(8,128)(2,1)}, bf16[1024,256]{1,0:T(8,128)(2,1)S(1)}, u32[]{:S(2)}) copy-start(bf16[1024,256]{1,0:T(8,128)(2,1)S(1)} %collective-permute-done.20.refs_7_) | copy-start | bytes 1572868
  96.3 24.0 %collective-permute-start.18 = (bf16[1024,256]{1,0:T(8,128)(2,1)S(1)}, bf16[1024,256]{1,0:T(8,128)(2,1)S(1)}, u32[]{:S(2)}, u32[]{:S(2)}) collective-permute-start(bf16[1024,256]{1,0:T(8,128)(2,1)S(1)} %pad_maximum_fusion.6), channel_id=1, source_target_pairs={{0,6},{2,4},{4,2},{6,0},{8,14},{10,12},{12,10},{14,8},{16,22},{18,... | collective-permute-start | bytes 1572872 | tf_op jit(solution)/shard_map/ppermute | solution.py:590
  111.9 16.9 %collective-permute-start.21 = (bf16[1024,256]{1,0:T(8,128)(2,1)S(1)}, bf16[1024,256]{1,0:T(8,128)(2,1)}, u32[]{:S(2)}, u32[]{:S(2)}) collective-permute-start(bf16[1024,256]{1,0:T(8,128)(2,1)S(1)} %collective-permute-done.20.refs_7_), channel_id=1, source_target_pairs={{0,8},{2,10},{4,12},{6,14},{8,16},{10,18},{12,20},{14,22},{16,24},... | collective-permute-start | bytes 1572872 | tf_op jit(solution)/shard_map/ppermute | solution.py:601
  112.0 31.0 %collective-permute-start.9 = (bf16[1024,256]{1,0:T(8,128)(2,1)}, bf16[1024,256]{1,0:T(8,128)(2,1)}, u32[]{:S(2)}, u32[]{:S(2)}) collective-permute-start(bf16[1024,256]{1,0:T(8,128)(2,1)} %collective-permute-done.8.refs_4_), channel_id=1, source_target_pairs={{0,8},{2,10},{4,12},{6,14},{8,16},{10,18},{12,20},{14,22},{16,24},... | collective-permute-start | bytes 1572872 | tf_op jit(solution)/shard_map/ppermute | solution.py:601
  114.7 6.1 %copy-start.12 = (f32[512,128]{1,0:T(8,128)}, f32[512,128]{1,0:T(8,128)S(1)}, u32[]{:S(2)}) copy-start(f32[512,128]{1,0:T(8,128)S(1)} %get-tuple-element.24) | copy-start | bytes 786436
  114.7 6.5 %copy-start.2 = (bf16[512,1024]{1,0:T(8,128)(2,1)}, bf16[512,1024]{1,0:T(8,128)(2,1)S(1)}, u32[]{:S(2)}) copy-start(bf16[512,1024]{1,0:T(8,128)(2,1)S(1)} %get-tuple-element.28.refs_0_.refs_3_) | copy-start | bytes 3145732
  124.6 16.5 %collective-permute-start.19 = (bf16[512,256]{1,0:T(8,128)(2,1)S(1)}, bf16[512,256]{1,0:T(8,128)(2,1)S(1)}, u32[]{:S(2)}, u32[]{:S(2)}) collective-permute-start(bf16[512,256]{1,0:T(8,128)(2,1)S(1)} %pad_maximum_fusion.15), channel_id=1, source_target_pairs={{0,8},{2,10},{4,12},{6,14},{8,16},{10,18},{12,20},{14,22},{16,24},... | collective-permute-start | bytes 786440 | tf_op jit(solution)/shard_map/ppermute | solution.py:690
  128.8 22.2 %collective-permute-start.22 = (bf16[1024,256]{1,0:T(8,128)(2,1)}, bf16[1024,256]{1,0:T(8,128)(2,1)}, u32[]{:S(2)}, u32[]{:S(2)}) collective-permute-start(bf16[1024,256]{1,0:T(8,128)(2,1)} %collective-permute-done.21.refs_8_), channel_id=1, source_target_pairs={{0,8},{2,10},{4,12},{6,14},{8,16},{10,18},{12,20},{14,22},{16,24},... | collective-permute-start | bytes 1572872 | tf_op jit(solution)/shard_map/ppermute | solution.py:601
  151.0 9.7 %copy-start.9 = (bf16[512,256]{1,0:T(8,128)(2,1)S(1)}, bf16[512,256]{1,0:T(8,128)(2,1)}, u32[]{:S(2)}) copy-start(bf16[512,256]{1,0:T(8,128)(2,1)} %get-tuple-element.32.refs_0_) | copy-start | bytes 786436
  158.1 8.8 %collective-permute-start.23 = (bf16[512,128]{1,0:T(8,128)(2,1)}, bf16[512,128]{1,0:T(8,128)(2,1)S(1)}, u32[]{:S(2)}, u32[]{:S(2)}) collective-permute-start(bf16[512,128]{1,0:T(8,128)(2,1)} %get-tuple-element.37), channel_id=1, source_target_pairs={{8,0},{10,2},{12,4},{14,6},{16,8},{18,10},{20,12},{22,14},{24,16},... | collective-permute-start | bytes 393224 | tf_op jit(solution)/shard_map/ppermute | solution.py:704
  159.4 9.2 %collective-permute-start.24 = (bf16[512,128]{1,0:T(8,128)(2,1)}, bf16[512,128]{1,0:T(8,128)(2,1)S(1)}, u32[]{:S(2)}, u32[]{:S(2)}) collective-permute-start(bf16[512,128]{1,0:T(8,128)(2,1)} %get-tuple-element.39), channel_id=1, source_target_pairs={{8,0},{10,2},{12,4},{14,6},{16,8},{18,10},{20,12},{22,14},{24,16},... | collective-permute-start | bytes 393224 | tf_op jit(solution)/shard_map/ppermute | solution.py:705
  161.7 5.3 %copy-start.25 = (f32[1024,256]{1,0:T(8,128)S(1)}, f32[1024,256]{1,0:T(8,128)}, u32[]{:S(2)}) copy-start(f32[1024,256]{1,0:T(8,128)} %get-tuple-element.36) | copy-start | bytes 3145732
  167.0 1.7 copy-start.7
  167.0 1.7 copy-start.8
  171.9 6.0 %copy-start.4 = (bf16[2,2,128,2048]{3,2,1,0:T(8,128)(2,1)}, bf16[2,2,128,2048]{3,2,1,0:T(8,128)(2,1)S(1)}, u32[]{:S(2)}) copy-start(bf16[2,2,128,2048]{3,2,1,0:T(8,128)(2,1)S(1)} %get-tuple-element.40) | copy-start | bytes 6291460
  171.9 4.2 %collective-permute-start.25 = (bf16[2,2,128,2048]{3,2,1,0:T(8,128)(2,1)S(1)}, bf16[2,2,128,2048]{3,2,1,0:T(8,128)(2,1)S(1)}, u32[]{:S(2)}, u32[]{:S(2)}) collective-permute-start(bf16[2,2,128,2048]{3,2,1,0:T(8,128)(2,1)S(1)} %get-tuple-element.41), channel_id=1, source_target_pairs={{0,2},{2,0},{4,6},{6,4},{8,10},{10,8},{12,14},{14,12},{16,18},{18,... | collective-permute-start | bytes 6291464 | tf_op jit(solution)/shard_map/ppermute | solution.py:590
  176.1 2.7 %copy-start.18 = (bf16[2,2,128,2048]{3,2,1,0:T(8,128)(2,1)}, bf16[2,2,128,2048]{3,2,1,0:T(8,128)(2,1)S(1)}, u32[]{:S(2)}) copy-start(bf16[2,2,128,2048]{3,2,1,0:T(8,128)(2,1)S(1)} %collective-permute-done.25) | copy-start | bytes 6291460
  177.3 14.3 %collective-permute-start.28 = (bf16[2,128,1024]{2,1,0:T(8,128)(2,1)}, bf16[2,128,1024]{2,1,0:T(8,128)(2,1)}, u32[]{:S(2)}, u32[]{:S(2)}) collective-permute-start(bf16[2,128,1024]{2,1,0:T(8,128)(2,1)} %fusion.10), channel_id=1, source_target_pairs={{0,1},{1,0},{2,3},{3,2},{4,5},{5,4},{6,7},{7,6},{8,9},{9,8},{10,11... | collective-permute-start | bytes 1572872 | tf_op jit(solution)/shard_map/ppermute | solution.py:593
  178.8 15.1 %collective-permute-start.26 = (bf16[2,128,1024]{2,1,0:T(8,128)(2,1)}, bf16[2,128,1024]{2,1,0:T(8,128)(2,1)}, u32[]{:S(2)}, u32[]{:S(2)}) collective-permute-start(bf16[2,128,1024]{2,1,0:T(8,128)(2,1)} %fusion.9), channel_id=1, source_target_pairs={{0,4},{2,6},{4,0},{6,2},{8,12},{10,14},{12,8},{14,10},{16,20},{18,... | collective-permute-start | bytes 1572872 | tf_op jit(solution)/shard_map/ppermute | solution.py:590
  181.1 18.3 %copy-start.3 = (bf16[512,1024]{1,0:T(8,128)(2,1)S(1)}, bf16[512,1024]{1,0:T(8,128)(2,1)}, u32[]{:S(2)}) copy-start(bf16[512,1024]{1,0:T(8,128)(2,1)} %copy-done.2) | copy-start | bytes 3145732
  181.1 18.3 %collective-permute-start.31 = (bf16[512,128]{1,0:T(8,128)(2,1)S(1)}, bf16[512,128]{1,0:T(8,128)(2,1)S(1)}, u32[]{:S(2)}, u32[]{:S(2)}) collective-permute-start(bf16[512,128]{1,0:T(8,128)(2,1)S(1)} %fusion.18.refs_0_.refs_4_), channel_id=1, source_target_pairs={{0,2},{2,0},{4,6},{6,4},{8,10},{10,8},{12,14},{14,12},{16,18},{18,... | collective-permute-start | bytes 393224 | tf_op jit(solution)/shard_map/ppermute | solution.py:590
  181.2 18.2 %collective-permute-start.32 = (bf16[512,128]{1,0:T(8,128)(2,1)S(1)}, bf16[512,128]{1,0:T(8,128)(2,1)S(1)}, u32[]{:S(2)}, u32[]{:S(2)}) collective-permute-start(bf16[512,128]{1,0:T(8,128)(2,1)S(1)} %fusion.18.refs_0_.refs_4_), channel_id=1, source_target_pairs={{0,4},{2,6},{4,0},{6,2},{8,12},{10,14},{12,8},{14,10},{16,20},{18,... | collective-permute-start | bytes 393224 | tf_op jit(solution)/shard_map/ppermute | solution.py:590
  181.9 17.5 %collective-permute-start.33 = (bf16[512,128]{1,0:T(8,128)(2,1)S(1)}, bf16[512,128]{1,0:T(8,128)(2,1)S(1)}, u32[]{:S(2)}, u32[]{:S(2)}) collective-permute-start(bf16[512,128]{1,0:T(8,128)(2,1)S(1)} %fusion.18.refs_0_.refs_4_), channel_id=1, source_target_pairs={{0,6},{2,4},{4,2},{6,0},{8,14},{10,12},{12,10},{14,8},{16,22},{18,... | collective-permute-start | bytes 393224 | tf_op jit(solution)/shard_map/ppermute | solution.py:590
  196.4 12.0 %collective-permute-start.27 = (bf16[128,1024]{1,0:T(8,128)(2,1)S(1)}, bf16[128,1024]{1,0:T(8,128)(2,1)S(1)}, u32[]{:S(2)}, u32[]{:S(2)}) collective-permute-start(bf16[128,1024]{1,0:T(8,128)(2,1)S(1)} %fusion.13), channel_id=1, source_target_pairs={{0,1},{1,0},{2,3},{3,2},{4,5},{5,4},{6,7},{7,6},{8,9},{9,8},{10,11... | collective-permute-start | bytes 786440 | tf_op jit(solution)/shard_map/ppermute | solution.py:593
  198.0 10.5 %collective-permute-start.29 = (bf16[128,1024]{1,0:T(8,128)(2,1)S(1)}, bf16[128,1024]{1,0:T(8,128)(2,1)S(1)}, u32[]{:S(2)}, u32[]{:S(2)}) collective-permute-start(bf16[128,1024]{1,0:T(8,128)(2,1)S(1)} %fusion.14), channel_id=1, source_target_pairs={{0,4},{2,6},{4,0},{6,2},{8,12},{10,14},{12,8},{14,10},{16,20},{18,... | collective-permute-start | bytes 786440 | tf_op jit(solution)/shard_map/ppermute | solution.py:590
  201.0 7.5 %copy-start.14 = (bf16[128,2048]{1,0:T(8,128)(2,1)S(1)}, bf16[128,2048]{1,0:T(8,128)(2,1)}, u32[]{:S(2)}) copy-start(bf16[128,2048]{1,0:T(8,128)(2,1)} %param.8) | copy-start | bytes 1572868
  201.1 13.4 %collective-permute-start.34 = (bf16[256,512]{1,0:T(8,128)(2,1)S(1)}, bf16[256,512]{1,0:T(8,128)(2,1)S(1)}, u32[]{:S(2)}, u32[]{:S(2)}) collective-permute-start(bf16[256,512]{1,0:T(8,128)(2,1)S(1)} %get-tuple-element.43), channel_id=1, source_target_pairs={{0,24},{2,26},{4,28},{6,30},{8,0},{10,2},{12,4},{14,6},{16,8},{18,... | collective-permute-start | bytes 786440 | tf_op jit(solution)/shard_map/ppermute | solution.py:601
  207.7 20.6 %collective-permute-start.35 = (bf16[256,512]{1,0:T(8,128)(2,1)S(1)}, bf16[256,512]{1,0:T(8,128)(2,1)S(1)}, u32[]{:S(2)}, u32[]{:S(2)}) collective-permute-start(bf16[256,512]{1,0:T(8,128)(2,1)S(1)} %get-tuple-element.44), channel_id=1, source_target_pairs={{0,16},{2,18},{4,20},{6,22},{8,24},{10,26},{12,28},{14,30},{16,0},... | collective-permute-start | bytes 786440 | tf_op jit(solution)/shard_map/ppermute | solution.py:601
  207.8 20.6 %collective-permute-start.36 = (bf16[256,512]{1,0:T(8,128)(2,1)S(1)}, bf16[256,512]{1,0:T(8,128)(2,1)S(1)}, u32[]{:S(2)}, u32[]{:S(2)}) collective-permute-start(bf16[256,512]{1,0:T(8,128)(2,1)S(1)} %get-tuple-element.45), channel_id=1, source_target_pairs={{0,8},{2,10},{4,12},{6,14},{8,16},{10,18},{12,20},{14,22},{16,24},... | collective-permute-start | bytes 786440 | tf_op jit(solution)/shard_map/ppermute | solution.py:601
  208.6 22.0 %copy-start.1 = (f32[16,2048]{1,0:T(8,128)S(1)}, f32[16,2048]{1,0:T(8,128)}, u32[]{:S(2)}) copy-start(f32[16,2048]{1,0:T(8,128)} %param.14) | copy-start | bytes 393220
  208.8 20.5 %collective-permute-start.30 = (f32[1,128]{1,0:T(1,128)S(1)}, f32[1,128]{1,0:T(1,128)S(1)}, u32[]{:S(2)}, u32[]{:S(2)}) collective-permute-start(f32[1,128]{1,0:T(1,128)S(1)} %bitcast.85), channel_id=1, source_target_pairs={{0,1},{1,0},{2,3},{3,2},{4,5},{5,4},{6,7},{7,6},{8,9},{9,8},{10,11... | collective-permute-start | bytes 1544 | tf_op jit(solution)/shard_map/ppermute | solution.py:593
  (7 other events, 7.9 us)

commit v4 on v3

--- a/solution.py
+++ b/solution.py
@@ -12,6 +12,7 @@
 HD = 128
 HOPS = 4
 LONGEST = 512
+CHUNKS = (2, 2)
 
 
 EPSILON = 1e-05
@@ -291,15 +292,15 @@
     n_refs, w_refs, refs = refs[:terms], refs[terms : 2 * terms], refs[2 * terms :]
     g_ref, k_ref, kt_ref, v_ref, cos_ref, sin_ref, low_ref = refs[:7]
     before = None if first else refs[7]
-    dq_ref, key_halo_ref, value_halo_ref, dkv_ref = refs[7 if first else 8 :]
+    dq_ref, halo_ref, own_ref, dkv_ref = refs[7 if first else 8 :]
     scale = HD ** (-0.5)
-    halo = key_halo_ref.shape[0]
+    halo = halo_ref.shape[0]
     window = halo + rows
     blocks = q_ref.shape[0] // rows
 
     @pl.when(pl.program_id(0) == 0)
     def _():
-        dkv_ref[...] = jnp.zeros_like(dkv_ref) if first else before[...]
+        dkv_ref[...] = jnp.zeros_like(dkv_ref)
 
     projected = q_ref[...]
     for n_ref, w_ref in zip(n_refs, w_refs):
@@ -337,9 +338,8 @@
                 axis=0,
             )
             prob_grad = prob_grads[:, there]
-            share = 1.0 / jnp.sum(weights, axis=0, keepdims=True)
-            row_delta = jnp.sum(weights * prob_grad, axis=0, keepdims=True) * share
-            softmax = weights * share
+            softmax = weights / jnp.sum(weights, axis=0, keepdims=True)
+            row_delta = jnp.sum(softmax * prob_grad, axis=0, keepdims=True)
             probs.append(softmax.astype(jnp.bfloat16))
             score_grads.append((softmax * (prob_grad - row_delta)).astype(jnp.bfloat16))
         probs = jnp.concatenate(probs, axis=1)
@@ -360,8 +360,9 @@
 
     @pl.when(pl.program_id(0) == pl.num_programs(0) - 1)
     def _():
-        key_halo_ref[...] = dkv_ref[:halo, :HD].astype(jnp.bfloat16)
-        value_halo_ref[...] = dkv_ref[:halo, HD:].astype(jnp.bfloat16)
+        halo_sum = dkv_ref[:halo, :]
+        halo_ref[...] = halo_sum if first else (halo_sum + before[...]).astype(jnp.bfloat16)
+        own_ref[...] = dkv_ref[halo:, :]
 
 
 def attend(q_proj, normed, weights, grads, keys, keys_turned, values, cosine, sine, low, before=None):
@@ -382,12 +383,14 @@
         + [whole(w) for w in weights]
         + [by_rows(width), whole(keys), whole(keys_turned), whole(values)]
         + [by_rows(HD), by_rows(HD), pl.BlockSpec((1, step), lambda i: (0, i))]
-        + [fixed(total, 2 * HD) for _ in extra],
-        out_specs=[by_rows(width)] + [fixed(total - tokens, HD)] * 2 + [fixed(total, 2 * HD)],
+        + [fixed(total - tokens, 2 * HD) for _ in extra],
+        out_specs=[by_rows(width), fixed(total - tokens, 2 * HD), fixed(tokens, 2 * HD)],
         out_shape=[jax.ShapeDtypeStruct((tokens, width), jnp.bfloat16),
-                   jax.ShapeDtypeStruct((total - tokens, HD), jnp.bfloat16),
-                   jax.ShapeDtypeStruct((total - tokens, HD), jnp.bfloat16),
-                   jax.ShapeDtypeStruct((total, 2 * HD), jnp.float32)],
+                   jax.ShapeDtypeStruct(
+                       (total - tokens, 2 * HD), jnp.float32 if before is None else jnp.bfloat16
+                   ),
+                   jax.ShapeDtypeStruct((tokens, 2 * HD), jnp.float32)],
+        scratch_shapes=[pltpu.VMEM((total, 2 * HD), jnp.float32)],
         cost_estimate=pl.CostEstimate(
             flops=10 * tokens * window * width, bytes_accessed=12 * tokens * width,
             transcendentals=tokens * window * heads,
@@ -466,9 +469,10 @@
     )(where, *grads, *weights)
 
 
-def spread_last_kernel(count, where, so_far, *refs):
-    grads, weights = refs[:count], refs[count:-3]
-    keep_ref, send_ref, wide = refs[-3:]
+def spread_last_kernel(parts, where, so_far, *refs):
+    owns, (back_ref, cos_ref, sin_ref) = refs[:parts], refs[parts : parts + 3]
+    weights = refs[parts + 3 : -4]
+    key_ref, keep_ref, send_ref, wide = refs[-4:]
     members = where.shape[0] - 3
     step = weights[0].shape[0] // members
     rows = keep_ref.shape[2]
@@ -476,7 +480,19 @@
 
     @pl.when(s == 0)
     def _():
-        spread_blocks(where, wide, grads, rows)
+        for block in range(members):
+            partner = (block % (members // 2)) * 2 + block // (members // 2)
+            lines = pl.ds(pl.multiple_of(where[3 + partner] * rows, rows), rows)
+            grad = back_ref[lines, :].astype(jnp.float32)
+            for own in owns:
+                grad += own[lines, :]
+            key_grad = grad[:, :HD]
+            turned = pltpu.roll(key_grad, HD // 2, 1)
+            key_done = key_grad * cos_ref[lines, :] - turned * sin_ref[lines, :]
+            key_ref[lines, :] = key_done.astype(jnp.bfloat16)
+            here = slice(block * rows, (block + 1) * rows)
+            wide[here, :HD] = key_done.astype(jnp.bfloat16)
+            wide[here, HD:] = grad[:, HD:].astype(jnp.bfloat16)
 
     for piece, weight in enumerate(weights):
 
@@ -493,11 +509,10 @@
                     send_ref[u, 0, :, lanes] = total[lower : lower + rows, :]
 
 
-def spread_last(where, so_far, grads, weights, ring_size):
-    tokens = grads[0].shape[0]
+def spread_last(where, so_far, owns, back, cosine, sine, weights, ring_size):
+    tokens = back.shape[0]
     members = where.shape[0] - 3
     rows = tokens // members
-    depth = sum(a.shape[1] for a in grads)
     width = weights[0].shape[0]
     planes_per_half = ring_size // 2
     whole = lambda a: pl.BlockSpec(a.shape, lambda i, w: (0, 0))
@@ -508,25 +523,28 @@
         return (0, half, 0, lax.rem(plane, planes_per_half))
 
     shape = (members // 2, 2, rows, width * planes_per_half)
+    small = [*owns, back, cosine, sine]
     return pl.pallas_call(
-        partial(spread_last_kernel, len(grads)),
+        partial(spread_last_kernel, len(owns)),
         grid_spec=pltpu.PrefetchScalarGridSpec(
             num_scalar_prefetch=1,
             grid=(ring_size,),
             in_specs=[pl.BlockSpec((1, tokens, width), lambda i, w: (i, 0, 0))]
-            + [whole(a) for a in grads]
+            + [whole(a) for a in small]
             + [pl.BlockSpec(memory_space=pltpu.VMEM) for a in weights],
-            out_specs=[pl.BlockSpec((members // 2, 1, rows, width), out_at)] * 2,
-            scratch_shapes=[pltpu.VMEM((tokens, depth), jnp.bfloat16)],
-        ),
-        out_shape=[jax.ShapeDtypeStruct(shape, jnp.bfloat16)] * 2,
-        compiler_params=pltpu.CompilerParams(vmem_limit_bytes=24 << 20),
+            out_specs=[pl.BlockSpec((tokens, HD), lambda i, w: (0, 0))]
+            + [pl.BlockSpec((members // 2, 1, rows, width), out_at)] * 2,
+            scratch_shapes=[pltpu.VMEM((tokens, 2 * HD), jnp.bfloat16)],
+        ),
+        out_shape=[jax.ShapeDtypeStruct((tokens, HD), jnp.bfloat16)]
+        + [jax.ShapeDtypeStruct(shape, jnp.bfloat16)] * 2,
+        compiler_params=pltpu.CompilerParams(vmem_limit_bytes=28 << 20),
         cost_estimate=pl.CostEstimate(
-            flops=2 * tokens * width * ring_size * depth,
+            flops=4 * tokens * width * ring_size * HD,
             bytes_accessed=4 * tokens * width * ring_size,
             transcendentals=0,
         ),
-    )(where, so_far, *grads, *weights)
+    )(where, so_far, *small, *weights)
 
 
 def key_weights_kernel(ring_size, where, *refs):
@@ -592,10 +610,6 @@
     def to_side(block):
         return lax.ppermute(block, "tensor", [(i, i ^ 1) for i in range(tensors)])
 
-    def to_corner(block, d):
-        route = [(i * 2 + t, (i ^ d) * 2 + (t ^ 1)) for i in range(devices) for t in range(2)]
-        return lax.ppermute(block, ("dp", "tensor"), route)
-
     def along(block, distance):
         route = [(i, (i + distance * members) % devices) for i in range(devices)]
         return lax.ppermute(block, "dp", route)
@@ -619,9 +633,9 @@
 
     q_parts = [pack_q(group)] + [to_partner(pack_q(partners[d]), d) for d in range(1, members)]
     q_own = jnp.concatenate([p[:weight_rows] for p in q_parts], axis=0)
-    chunk_width = 2 * HD
-    q_chunks = query_width // chunk_width
-    q_chunk = [q_own[:, c * chunk_width : (c + 1) * chunk_width] for c in range(q_chunks)]
+    ends = [sum(CHUNKS[: c + 1]) * HD for c in range(len(CHUNKS))]
+    spans = [slice(end - count * HD, end) for end, count in zip(ends, CHUNKS)]
+    q_chunk = [q_own[:, span] for span in spans]
 
     def pack_kv(owner):
         pairs = []
@@ -631,7 +645,8 @@
         return jnp.concatenate(pairs, axis=0)
 
     across = to_partner(hidden, 2)
-    beside, corner = to_side(hidden), to_corner(hidden, 2)
+    beside = to_side(hidden)
+    corner = to_side(across)
     near = jnp.stack([hidden, beside, across, corner]).reshape(2, 2, rows, half)
     far = to_partner(near, 1)
     *normed, inverse = norm_pieces(where, near, far, norm_gain[None, :], ring_size)
@@ -684,36 +699,25 @@
     kv_rows = jnp.concatenate([key_own, kv_proj[:, HD:]], axis=1).astype(jnp.bfloat16)
 
     q_pieces = []
-    for c in range(q_chunks):
+    for c in range(len(CHUNKS)):
         gate = lambda hop, block, c=c: after(block, kv_rows) if c and hop == ring_size - 1 else block
         q_pieces.append(circulate(q_chunk[c], gate))
     halo = lax.ppermute(kv_rows, "dp", [(i, i + members) for i in range(devices - members)])
     kv_all = jnp.concatenate([halo, kv_rows], axis=0)
     keys, values = kv_all[:, :HD], kv_all[:, HD:]
     keys_turned = keys.T
-    query_dones, kv_sum = [], None
-    for c in range(q_chunks):
+    query_dones, owns, halo_grad = [], [], None
+    for c in range(len(CHUNKS)):
         early = lax.optimization_barrier(project(q_pieces[c][:-1]))
-        query_done, key_halo, value_halo, kv_sum = attend(
+        query_done, halo_grad, own_grad = attend(
             early, normed[-1:], q_pieces[c][-1:],
-            out_grad[:, c * chunk_width : (c + 1) * chunk_width],
-            keys, keys_turned, values, cosine, sine, low, kv_sum,
+            out_grad[:, spans[c]],
+            keys, keys_turned, values, cosine, sine, low, halo_grad,
         )
         query_dones.append(query_done)
+        owns.append(own_grad)
     later = [(i + members, i) for i in range(devices - members)]
-    key_back = lax.ppermute(key_halo, "dp", later)
-    value_back = lax.ppermute(value_halo, "dp", later)
-    key_grad = kv_sum[LONGEST:, :HD] + key_back.astype(jnp.float32)
-    turned = jnp.roll(key_grad, HD // 2, axis=1)
-    key_done = (key_grad * cosine - turned * sine).astype(jnp.bfloat16)
-    value_grad = after(kv_sum[LONGEST:, HD:], key_done) + value_back.astype(jnp.float32)
-    value_done = value_grad.astype(jnp.bfloat16)
-
-    key_dones = [key_done] + [to_partner(key_done, d) for d in range(1, members)]
-    grad_wkey, *others = key_weights(where, normed, key_dones, weight_rows)
-    for s in range(1, ring_size):
-        term = along(others[s - 1], -s)
-        grad_wkey = grad_wkey + term.astype(jnp.float32)
+    back = lax.ppermute(halo_grad, "dp", later)
 
     weights = [
         pltpu.with_memory_space_constraint(piece, pltpu.HBM)
@@ -721,7 +725,17 @@
         for piece in pieces
     ]
     so_far = spread_first(where, query_dones, weights, ring_size)
-    keep, send = spread_last(where, so_far, [key_done, value_done], kv_pieces, ring_size)
+    in_hbm = [pltpu.with_memory_space_constraint(a, pltpu.HBM) for a in (*owns, cosine, sine)]
+    key_done, keep, send = spread_last(
+        where, so_far, in_hbm[:-2], back, *in_hbm[-2:], kv_pieces, ring_size
+    )
+
+    key_dones = [key_done] + [to_partner(key_done, d) for d in range(1, members)]
+    grad_wkey, *others = key_weights(where, normed, key_dones, weight_rows)
+    for s in range(1, ring_size):
+        term = along(others[s - 1], -s)
+        grad_wkey = grad_wkey + term.astype(jnp.float32)
+
     wide = lambda a: a.astype(jnp.float32)
     narrow = lambda a: a.astype(jnp.bfloat16)
     other = to_partner(send, 1)

time: 232 us -> 213 us (0.918)
  waiting for transfers between devices: 124 us -> 108 us
  other arithmetic: 20.4 us -> 17.3 us
    ppermute x15, waiting for transfers between devices: 77.7 us -> 61.7 us  [along(): return lax.ppermute(block, 'dp', route)]
    ppermute x14, waiting for transfers between devices: 34 us -> 27.1 us  [to_partner(): return lax.ppermute(block, 'dp', [(i, i ^ d) for i in range(devices)])]
    ppermute x4 -> x5, waiting for transfers between devices: 8.58 us -> 12 us  [to_side(): return lax.ppermute(block, 'tensor', [(i, i ^ 1) for i in range(tensors)])]
    ppermute x4 -> x5, starting transfers between devices: 5.71 us -> 6.36 us  [to_side(): return lax.ppermute(block, 'tensor', [(i, i ^ 1) for i in range(tensors)])]
  transfers between devices with their start and end apart: 37 -> 36, of which waited for: 16 -> 18; matrix products, arithmetic and copies ran while one was open for 16% -> 16% of each run, Pallas kernels for 7% -> 7%
where the time goes in v4:
time: 213 us; the launch traced here: 212 us
  waiting for transfers between devices  108 us (51%)
  starting transfers between devices  36.2 us (17%)
  Pallas kernels  27.3 us (13%)
  other arithmetic  17.3 us (8%)
  local copies, waits for them, and re-layouts  12.6 us (6%)
  matrix products  8.83 us (4%)
    ppermute x15, waiting for transfers between devices, along(): return lax.ppermute(block, 'dp', route)  61.7 us
    ppermute x14, waiting for transfers between devices, to_partner(): return lax.ppermute(block, 'dp', [(i, i ^ d) for i in range(devices)])  27.1 us
    ppermute x15, starting transfers between devices, along(): return lax.ppermute(block, 'dp', route)  18.5 us
    pallas_call x2, Pallas kernels, attend(): pl.pallas_call(partial(attend_kernel, heads, rows, len(normed), before is...  13.6 us
    ppermute x5, waiting for transfers between devices, to_side(): return lax.ppermute(block, 'tensor', [(i, i ^ 1) for i in range(tensors)])  12 us
    ppermute x14, starting transfers between devices, to_partner(): return lax.ppermute(block, 'dp', [(i, i ^ d) for i in range(devices)])  8.68 us
    dot_general x10, matrix products, project(): term = jnp.dot(normed[s], piece, preferred_element_type=jnp.float32)  8.16 us
    ppermute x5, starting transfers between devices, to_side(): return lax.ppermute(block, 'tensor', [(i, i ^ 1) for i in range(tensors)])  6.36 us
  transfers between devices with their start and end apart: 36, of which 18 were waited for; matrix products, arithmetic and copies ran while one was open for 16% of the time, Pallas kernels for 7%

profile of v4, /device:TPU:0, one launch (start us, length us, event | category | flops | bytes accessed | tf_op | source)
XLA Modules:
  0.0 212.2 jit_solution(4508035317336438102)
XLA Ops:
  0.7 3.1 %collective-permute-start = (bf16[128,2048]{1,0:T(8,128)(2,1)}, bf16[128,2048]{1,0:T(8,128)(2,1)S(1)}, u32[]{:S(2)}, u32[]{:S(2)}) collective-permute-start(bf16[128,2048]{1,0:T(8,128)(2,1)} %param.8), channel_id=1, source_target_pairs={{0,1},{1,0},{2,3},{3,2},{4,5},{5,4},{6,7},{7,6},{8,9},{9,8},{10,11... | collective-permute-start | bytes 1572872 | tf_op jit(solution)/shard_map/ppermute | solution.py:611
  3.7 1.5 collective-permute-start.1
  5.2 1.6 collective-permute-start.10
  6.8 1.6 collective-permute-start.11
  8.4 1.2 dynamic-slice_bitcast_fusion.4
  9.6 1.3 constant_dynamic-slice_fusion.38
  14.7 1.0 pad_maximum_fusion.17
  16.5 1.0 constant_dynamic-slice_fusion.5
  17.5 3.0 %collective-permute-done.11 = bf16[256,512]{1,0:T(8,128)(2,1)} collective-permute-done((bf16[256,512]{1,0:T(8,128)(2,1)}, bf16[256,512]{1,0:T(8,128)(2,1)}, u32[]{:S(2)}, u32[]{:S(2)}) %collective-permute-start.11) | collective-permute-done | bytes 262176 | tf_op jit(solution)/shard_map/ppermute | solution.py:615
  20.5 1.0 constant_dynamic-slice_fusion.4
  21.6 5.7 %collective-permute-done.5 = bf16[384,512]{1,0:T(8,128)(2,1)} collective-permute-done((bf16[384,512]{1,0:T(8,128)(2,1)S(1)}, bf16[384,512]{1,0:T(8,128)(2,1)}, u32[]{:S(2)}, u32[]{:S(2)}) %collective-permute-start.5) | collective-permute-done | bytes 393248 | tf_op jit(solution)/shard_map/ppermute | solution.py:608
  27.3 1.6 collective-permute-start.12
  28.8 1.0 slice.172
  29.8 3.4 %collective-permute-done.6 = bf16[384,512]{1,0:T(8,128)(2,1)S(1)} collective-permute-done((bf16[384,512]{1,0:T(8,128)(2,1)S(1)}, bf16[384,512]{1,0:T(8,128)(2,1)S(1)}, u32[]{:S(2)}, u32[]{:S(2)}) %collective-permute-start.6) | collective-permute-done | bytes 393248 | tf_op jit(solution)/shard_map/ppermute | solution.py:608
  33.2 1.6 collective-permute-start.13
  35.0 1.6 collective-permute-start.20
  36.6 0.9 slice_bitcast_fusion.4
  38.2 1.6 collective-permute-start.7
  39.9 11.8 %collective-permute-done.2 = bf16[128,2048]{1,0:T(8,128)(2,1)S(1)} collective-permute-done((bf16[128,2048]{1,0:T(8,128)(2,1)S(1)}, bf16[128,2048]{1,0:T(8,128)(2,1)S(1)}, u32[]{:S(2)}, u32[]{:S(2)}) %collective-permute-start.2) | collective-permute-done | bytes 524320 | tf_op jit(solution)/shard_map/ppermute | solution.py:611
  52.8 1.6 collective-permute-start.14
  55.3 17.0 %collective-permute-done.14 = bf16[256,512]{1,0:T(8,128)(2,1)S(1)} collective-permute-done((bf16[256,512]{1,0:T(8,128)(2,1)S(1)}, bf16[256,512]{1,0:T(8,128)(2,1)S(1)}, u32[]{:S(2)}, u32[]{:S(2)}) %collective-permute-start.14) | collective-permute-done | bytes 262176 | tf_op jit(solution)/shard_map/ppermute | solution.py:615
  72.4 5.6 %collective-permute-done.15 = bf16[256,512]{1,0:T(8,128)(2,1)S(1)} collective-permute-done((bf16[256,512]{1,0:T(8,128)(2,1)S(1)}, bf16[256,512]{1,0:T(8,128)(2,1)S(1)}, u32[]{:S(2)}, u32[]{:S(2)}) %collective-permute-start.15) | collective-permute-done | bytes 262176 | tf_op jit(solution)/shard_map/ppermute | solution.py:615
  78.8 0.9 collective-permute-start.18
  79.8 0.9 fusion.28
  81.5 14.7 %collective-permute-done.8.refs_4_ = bf16[1024,256]{1,0:T(8,128)(2,1)} collective-permute-done((bf16[1024,256]{1,0:T(8,128)(2,1)S(1)}, bf16[1024,256]{1,0:T(8,128)(2,1)}, u32[]{:S(2)}, u32[]{:S(2)}) %collective-permute-start.8) | collective-permute-done | bytes 524320 | tf_op jit(solution)/shard_map/ppermute | solution.py:615
  96.2 2.7 %shard_map.95 = (bf16[512,1024]{1,0:T(8,128)(2,1)S(1)}, bf16[512,1024]{1,0:T(8,128)(2,1)S(1)}, bf16[512,1024]{1,0:T(8,128)(2,1)S(1)}, bf16[512,1024]{1,0:T(8,128)(2,1)S(1)}, f32[512,128]{1,0:T(8,128)S(1)}) custom-call(s32[7]{0:T(128)S(1)} %stack.58.where, bf16[2,2,128,2048]{3,2,1,0:T(8,128)(2,1)S(1)} %bitcast.76, ...), custom_call_target="tpu_custom_call" | custom-call | flops 16777216 | bytes 8388608 | tf_op jit(solution)/shard_map/pallas_call | solution.py:273
  98.9 3.6 %collective-permute-done.18 = bf16[1024,256]{1,0:T(8,128)(2,1)S(1)} collective-permute-done((bf16[1024,256]{1,0:T(8,128)(2,1)S(1)}, bf16[1024,256]{1,0:T(8,128)(2,1)S(1)}, u32[]{:S(2)}, u32[]{:S(2)}) %collective-permute-start.18) | collective-permute-done | bytes 524320 | tf_op jit(solution)/shard_map/ppermute | solution.py:608
  106.0 1.9 fusion.16
  108.0 1.3 collective-permute-start.19
  110.3 2.3 %convolution_add_fusion.3.q_ref = f32[512,256]{1,0:T(8,128)} fusion(f32[512,256]{1,0:T(8,128)S(1)} %convolution_add_fusion.4, bf16[512,1024]{1,0:T(8,128)(2,1)S(1)} %get-tuple-element.27.refs_2_, bf16[1024,256]{1,0:T(8,128)(2,1)} %collective-permute-done.8.refs_4_), kind=kOutput, calls=%fused_computation.9 | convolution fusion | flops 268566528 | bytes 2621440 | tf_op jit(solution)/shard_map/dot_general | solution.py:666
  112.9 2.3 %convolution_add_fusion.q_ref = f32[512,256]{1,0:T(8,128)} fusion(f32[512,256]{1,0:T(8,128)S(1)} %convolution_add_fusion.1, bf16[512,1024]{1,0:T(8,128)(2,1)S(1)} %get-tuple-element.27.refs_2_, bf16[1024,256]{1,0:T(8,128)(2,1)} %collective-permute-done.21.refs_8_), kind=kOutput, calls=%fused_computation.6 | convolution fusion | flops 268566528 | bytes 2621440 | tf_op jit(solution)/shard_map/dot_general | solution.py:666
  115.2 0.8 pad_maximum_fusion.7.refs_5_
  116.0 0.8 pad_maximum_fusion.10.refs_8_
  116.9 2.0 collective-permute-start.22
  119.7 5.6 %collective-permute-done.19 = bf16[512,256]{1,0:T(8,128)(2,1)S(1)} collective-permute-done((bf16[512,256]{1,0:T(8,128)(2,1)S(1)}, bf16[512,256]{1,0:T(8,128)(2,1)S(1)}, u32[]{:S(2)}, u32[]{:S(2)}) %collective-permute-start.19) | collective-permute-done | bytes 262176 | tf_op jit(solution)/shard_map/ppermute | solution.py:705
  125.4 0.9 fusion.29
  126.3 0.9 copy.33.refs_4_
  127.1 6.7 %shard_map.96 = (bf16[512,256]{1,0:T(8,128)(2,1)}, f32[512,256]{1,0:T(8,128)}, f32[512,256]{1,0:T(8,128)}) custom-call(f32[512,256]{1,0:T(8,128)} %convolution_add_fusion.3.q_ref, bf16[512,1024]{1,0:T(8,128)(2,1)} %copy-done.2, bf16[1024,256]{1,0:T(8,128)(2,1)} %collective-permute-done.9.refs_1_.refs_5_, bf16[512,256]{1,0:T(8,128)(2,1)} %get-tuple-element.61.refs_2_, ...), custom_call_target="tpu_custom_call" | custom-call | flops 838860800 | bytes 1572864 | tf_op jit(solution)/shard_map/pallas_call | solution.py:378
  133.9 1.9 collective-permute-done.22.refs_1_.refs_9_
  135.8 6.9 %shard_map.97 = (bf16[512,256]{1,0:T(8,128)(2,1)}, bf16[512,256]{1,0:T(8,128)(2,1)}, f32[512,256]{1,0:T(8,128)}) custom-call(f32[512,256]{1,0:T(8,128)} %convolution_add_fusion.q_ref, bf16[512,1024]{1,0:T(8,128)(2,1)} %copy-done.2, bf16[1024,256]{1,0:T(8,128)(2,1)} %collective-permute-done.22.refs_1_.refs_9_, bf16[512,256]{1,0:T(8,128)(2,1)} %get-tuple-element.60.refs_2_, ...), custom_call_target="tpu_custom_call" | custom-call | flops 838860800 | bytes 1572864 | tf_op jit(solution)/shard_map/pallas_call | solution.py:378
  142.7 1.3 collective-permute-start.23
  144.0 1.1 pad_maximum_fusion.8.refs_6_
  145.1 0.9 copy-done.9
  146.1 4.8 %shard_map.98.so_far = f32[4,512,1024]{2,1,0:T(8,128)S(1)} custom-call(s32[7]{0:T(128)S(1)} %stack.58.where, bf16[512,256]{1,0:T(8,128)(2,1)S(1)} %copy-done.8, bf16[512,256]{1,0:T(8,128)(2,1)S(1)} %copy-done.9, bf16[1024,256]{1,0:T(8,128)(2,1)} %copy-done.16, bf16[1024,256]{1,0:T(8,128)(2,1)} %copy-done.18, ...), custom_call_target="tpu_custom_call" | custom-call | flops 2147483648 | bytes 8388608 | tf_op jit(solution)/shard_map/pallas_call | solution.py:448
  150.9 2.1 collective-permute-done.23.refs_2_
  153.0 4.6 %shard_map.99 = (bf16[512,128]{1,0:T(8,128)(2,1)S(1)}, bf16[2,2,128,2048]{3,2,1,0:T(8,128)(2,1)S(1)}, bf16[2,2,128,2048]{3,2,1,0:T(8,128)(2,1)S(1)}) custom-call(s32[7]{0:T(128)S(1)} %stack.58.where, f32[4,512,1024]{2,1,0:T(8,128)S(1)} %shard_map.98.so_far, f32[512,256]{1,0:T(8,128)} %get-tuple-element.36.refs_0_, f32[512,256]{1,0:T(8,128)} %get-tuple-element.37.refs_1_, ...), custom_call_target="tpu_custom_call" | custom-call | flops 1073741824 | bytes 8388608 | tf_op jit(solution)/shard_map/pallas_call | solution.py:527
  157.7 4.1 %collective-permute-done.24 = bf16[2,2,128,2048]{3,2,1,0:T(8,128)(2,1)S(1)} collective-permute-done((bf16[2,2,128,2048]{3,2,1,0:T(8,128)(2,1)S(1)}, bf16[2,2,128,2048]{3,2,1,0:T(8,128)(2,1)S(1)}, u32[]{:S(2)}, u32[]{:S(2)}) %collective-permute-start.24) | collective-permute-done | bytes 2097184 | tf_op jit(solution)/shard_map/ppermute | solution.py:608
  161.8 1.2 fusion.9
  163.1 1.0 fusion.10
  164.7 0.9 dynamic-slice_reduce_fusion
  165.6 1.3 collective-permute-start.32
  166.9 0.9 collective-permute-start.31
  167.8 10.3 %collective-permute-done.25 = bf16[2,128,1024]{2,1,0:T(8,128)(2,1)} collective-permute-done((bf16[2,128,1024]{2,1,0:T(8,128)(2,1)}, bf16[2,128,1024]{2,1,0:T(8,128)(2,1)}, u32[]{:S(2)}, u32[]{:S(2)}) %collective-permute-start.25) | collective-permute-done | bytes 524320 | tf_op jit(solution)/shard_map/ppermute | solution.py:608
  178.3 2.4 %bitcast_add_fusion.1 = (f32[2,128,1024]{2,1,0:T(8,128)S(1)}, f32[2,128,1024]{2,1,0:T(8,128)S(1)}) fusion(bf16[2,128,1024]{2,1,0:T(8,128)(2,1)} %collective-permute-done.25, bf16[2,2,128,2048]{3,2,1,0:T(8,128)(2,1)} %copy-done.14, bf16[2,2,128,2048]{3,2,1,0:T(8,128)(2,1)} %copy-done.4, bf16[2,128,1024]{2,1,0:T(8,128)(2,1)} %collective-permute-done.27), kind=kLoop, calls=%fused_computation.21 | loop fusion | flops 2621440 | bytes 5242880 | tf_op jit(solution)/shard_map/add | solution.py:749
  180.8 1.8 collective-permute-start.28
  183.4 1.6 shard_map.100
  185.0 1.3 collective-permute-start.33
  186.3 1.9 collective-permute-start.34
  188.2 1.4 collective-permute-start.35
  190.0 1.4 collective-permute-start.29
  191.5 1.6 collective-permute-done.33
  193.1 16.9 %collective-permute-done.34 = bf16[256,512]{1,0:T(8,128)(2,1)S(1)} collective-permute-done((bf16[256,512]{1,0:T(8,128)(2,1)S(1)}, bf16[256,512]{1,0:T(8,128)(2,1)S(1)}, u32[]{:S(2)}, u32[]{:S(2)}) %collective-permute-start.34) | collective-permute-done | bytes 262176 | tf_op jit(solution)/shard_map/ppermute | solution.py:615
  210.0 0.9 convert_add_fusion
  211.0 1.2 fusion.7
  (158 shorter events, 16.9 us)
Async XLA Ops:
  0.6 51.5 %copy-start = (f32[16,2048]{1,0:T(8,128)S(1)}, f32[16,2048]{1,0:T(8,128)}, u32[]{:S(2)}) copy-start(f32[16,2048]{1,0:T(8,128)} %param.14) | copy-start | bytes 393220
  0.6 10.8 %copy-start.24 = (bf16[256,512]{1,0:T(8,128)(2,1)S(1)}, bf16[256,512]{1,0:T(8,128)(2,1)}, u32[]{:S(2)}) copy-start(bf16[256,512]{1,0:T(8,128)(2,1)} %param.11) | copy-start | bytes 786436
  0.7 37.6 %collective-permute-start = (bf16[128,2048]{1,0:T(8,128)(2,1)}, bf16[128,2048]{1,0:T(8,128)(2,1)S(1)}, u32[]{:S(2)}, u32[]{:S(2)}) collective-permute-start(bf16[128,2048]{1,0:T(8,128)(2,1)} %param.8), channel_id=1, source_target_pairs={{0,1},{1,0},{2,3},{3,2},{4,5},{5,4},{6,7},{7,6},{8,9},{9,8},{10,11... | collective-permute-start | bytes 1572872 | tf_op jit(solution)/shard_map/ppermute | solution.py:611
  3.7 33.8 %collective-permute-start.1 = (bf16[128,2048]{1,0:T(8,128)(2,1)}, bf16[128,2048]{1,0:T(8,128)(2,1)S(1)}, u32[]{:S(2)}, u32[]{:S(2)}) collective-permute-start(bf16[128,2048]{1,0:T(8,128)(2,1)} %param.8), channel_id=1, source_target_pairs={{0,4},{2,6},{4,0},{6,2},{8,12},{10,14},{12,8},{14,10},{16,20},{18,... | collective-permute-start | bytes 1572872 | tf_op jit(solution)/shard_map/ppermute | solution.py:608
  5.2 11.3 %collective-permute-start.10 = (bf16[256,512]{1,0:T(8,128)(2,1)}, bf16[256,512]{1,0:T(8,128)(2,1)}, u32[]{:S(2)}, u32[]{:S(2)}) collective-permute-start(bf16[256,512]{1,0:T(8,128)(2,1)} %param.11), channel_id=1, source_target_pairs={{0,8},{2,10},{4,12},{6,14},{8,16},{10,18},{12,20},{14,22},{16,24},... | collective-permute-start | bytes 786440 | tf_op jit(solution)/shard_map/ppermute | solution.py:615
  6.8 13.7 %collective-permute-start.11 = (bf16[256,512]{1,0:T(8,128)(2,1)}, bf16[256,512]{1,0:T(8,128)(2,1)}, u32[]{:S(2)}, u32[]{:S(2)}) collective-permute-start(bf16[256,512]{1,0:T(8,128)(2,1)} %param.12), channel_id=1, source_target_pairs={{0,8},{2,10},{4,12},{6,14},{8,16},{10,18},{12,20},{14,22},{16,24},... | collective-permute-start | bytes 786440 | tf_op jit(solution)/shard_map/ppermute | solution.py:615
  8.4 3.8 %copy-start.25 = (bf16[256,512]{1,0:T(8,128)(2,1)S(1)}, bf16[256,512]{1,0:T(8,128)(2,1)}, u32[]{:S(2)}) copy-start(bf16[256,512]{1,0:T(8,128)(2,1)} %param.12) | copy-start | bytes 786436
  9.5 3.3 %copy-start.26 = (s32[16]{0:T(128)S(1)}, s32[16]{0:T(128)}, u32[]{:S(2)}) copy-start(s32[16]{0:T(128)} %param.15) | copy-start | bytes 196
  10.9 16.4 %collective-permute-start.5 = (bf16[384,512]{1,0:T(8,128)(2,1)S(1)}, bf16[384,512]{1,0:T(8,128)(2,1)}, u32[]{:S(2)}, u32[]{:S(2)}) collective-permute-start(bf16[384,512]{1,0:T(8,128)(2,1)S(1)} %pad_maximum_fusion.12), channel_id=1, source_target_pairs={{0,4},{2,6},{4,0},{6,2},{8,12},{10,14},{12,8},{14,10},{16,20},{18,... | collective-permute-start | bytes 1179656 | tf_op jit(solution)/shard_map/ppermute | solution.py:608
  16.5 16.7 %collective-permute-start.6 = (bf16[384,512]{1,0:T(8,128)(2,1)S(1)}, bf16[384,512]{1,0:T(8,128)(2,1)S(1)}, u32[]{:S(2)}, u32[]{:S(2)}) collective-permute-start(bf16[384,512]{1,0:T(8,128)(2,1)S(1)} %pad_maximum_fusion.13), channel_id=1, source_target_pairs={{0,6},{2,4},{4,2},{6,0},{8,14},{10,12},{12,10},{14,8},{16,22},{18,... | collective-permute-start | bytes 1179656 | tf_op jit(solution)/shard_map/ppermute | solution.py:608
  20.5 14.3 %collective-permute-start.4 = (bf16[384,512]{1,0:T(8,128)(2,1)S(1)}, bf16[384,512]{1,0:T(8,128)(2,1)S(1)}, u32[]{:S(2)}, u32[]{:S(2)}) collective-permute-start(bf16[384,512]{1,0:T(8,128)(2,1)S(1)} %pad_maximum_fusion.11), channel_id=1, source_target_pairs={{0,2},{2,0},{4,6},{6,4},{8,10},{10,8},{12,14},{14,12},{16,18},{18,... | collective-permute-start | bytes 1179656 | tf_op jit(solution)/shard_map/ppermute | solution.py:608
  21.5 82.1 %copy-start.20 = (bf16[256,256]{1,0:T(8,128)(2,1)}, bf16[256,256]{1,0:T(8,128)(2,1)S(1)}, u32[]{:S(2)}) copy-start(bf16[256,256]{1,0:T(8,128)(2,1)S(1)} %pad_maximum_fusion.29) | copy-start | bytes 393220
  27.3 25.6 %collective-permute-start.12 = (bf16[256,512]{1,0:T(8,128)(2,1)}, bf16[256,512]{1,0:T(8,128)(2,1)S(1)}, u32[]{:S(2)}, u32[]{:S(2)}) collective-permute-start(bf16[256,512]{1,0:T(8,128)(2,1)} %collective-permute-done.10), channel_id=1, source_target_pairs={{0,8},{2,10},{4,12},{6,14},{8,16},{10,18},{12,20},{14,22},{16,24},... | collective-permute-start | bytes 786440 | tf_op jit(solution)/shard_map/ppermute | solution.py:615
  33.2 21.3 %collective-permute-start.13 = (bf16[256,512]{1,0:T(8,128)(2,1)}, bf16[256,512]{1,0:T(8,128)(2,1)S(1)}, u32[]{:S(2)}, u32[]{:S(2)}) collective-permute-start(bf16[256,512]{1,0:T(8,128)(2,1)} %collective-permute-done.11), channel_id=1, source_target_pairs={{0,8},{2,10},{4,12},{6,14},{8,16},{10,18},{12,20},{14,22},{16,24},... | collective-permute-start | bytes 786440 | tf_op jit(solution)/shard_map/ppermute | solution.py:615
  34.9 16.8 %copy-start.12 = (bf16[128,2048]{1,0:T(8,128)(2,1)S(1)}, bf16[128,2048]{1,0:T(8,128)(2,1)}, u32[]{:S(2)}) copy-start(bf16[128,2048]{1,0:T(8,128)(2,1)} %param.8) | copy-start | bytes 1572868
  35.0 17.0 %copy-start.15 = (bf16[1024,256]{1,0:T(8,128)(2,1)}, bf16[1024,256]{1,0:T(8,128)(2,1)S(1)}, u32[]{:S(2)}) copy-start(bf16[1024,256]{1,0:T(8,128)(2,1)S(1)} %get-tuple-element.54.refs_6_) | copy-start | bytes 1572868
  35.0 17.0 %copy-start.16 = (bf16[1024,256]{1,0:T(8,128)(2,1)}, bf16[1024,256]{1,0:T(8,128)(2,1)S(1)}, u32[]{:S(2)}) copy-start(bf16[1024,256]{1,0:T(8,128)(2,1)S(1)} %get-tuple-element.55.refs_2_) | copy-start | bytes 1572868
  35.0 45.7 %collective-permute-start.20 = (bf16[1024,256]{1,0:T(8,128)(2,1)S(1)}, bf16[1024,256]{1,0:T(8,128)(2,1)S(1)}, u32[]{:S(2)}, u32[]{:S(2)}) collective-permute-start(bf16[1024,256]{1,0:T(8,128)(2,1)S(1)} %get-tuple-element.54.refs_6_), channel_id=1, source_target_pairs={{0,8},{2,10},{4,12},{6,14},{8,16},{10,18},{12,20},{14,22},{16,24},... | collective-permute-start | bytes 1572872 | tf_op jit(solution)/shard_map/ppermute | solution.py:615
  37.6 14.1 %collective-permute-start.2 = (bf16[128,2048]{1,0:T(8,128)(2,1)S(1)}, bf16[128,2048]{1,0:T(8,128)(2,1)S(1)}, u32[]{:S(2)}, u32[]{:S(2)}) collective-permute-start(bf16[128,2048]{1,0:T(8,128)(2,1)S(1)} %collective-permute-done.1), channel_id=1, source_target_pairs={{0,1},{1,0},{2,3},{3,2},{4,5},{5,4},{6,7},{7,6},{8,9},{9,8},{10,11... | collective-permute-start | bytes 1572872 | tf_op jit(solution)/shard_map/ppermute | solution.py:611
  38.2 41.5 %collective-permute-start.7 = (bf16[1024,256]{1,0:T(8,128)(2,1)S(1)}, bf16[1024,256]{1,0:T(8,128)(2,1)S(1)}, u32[]{:S(2)}, u32[]{:S(2)}) collective-permute-start(bf16[1024,256]{1,0:T(8,128)(2,1)S(1)} %get-tuple-element.55.refs_2_), channel_id=1, source_target_pairs={{0,8},{2,10},{4,12},{6,14},{8,16},{10,18},{12,20},{14,22},{16,24},... | collective-permute-start | bytes 1572872 | tf_op jit(solution)/shard_map/ppermute | solution.py:615
  52.0 44.2 %collective-permute-start.3 = (bf16[2,2,128,2048]{3,2,1,0:T(8,128)(2,1)S(1)}, bf16[2,2,128,2048]{3,2,1,0:T(8,128)(2,1)S(1)}, u32[]{:S(2)}, u32[]{:S(2)}) collective-permute-start(bf16[2,2,128,2048]{3,2,1,0:T(8,128)(2,1)S(1)} %bitcast.75), channel_id=1, source_target_pairs={{0,2},{2,0},{4,6},{6,4},{8,10},{10,8},{12,14},{14,12},{16,18},{18,... | collective-permute-start | bytes 6291464 | tf_op jit(solution)/shard_map/ppermute | solution.py:608
  52.8 19.5 %collective-permute-start.14 = (bf16[256,512]{1,0:T(8,128)(2,1)S(1)}, bf16[256,512]{1,0:T(8,128)(2,1)S(1)}, u32[]{:S(2)}, u32[]{:S(2)}) collective-permute-start(bf16[256,512]{1,0:T(8,128)(2,1)S(1)} %collective-permute-done.12), channel_id=1, source_target_pairs={{0,8},{2,10},{4,12},{6,14},{8,16},{10,18},{12,20},{14,22},{16,24},... | collective-permute-start | bytes 786440 | tf_op jit(solution)/shard_map/ppermute | solution.py:615
  54.6 23.4 %collective-permute-start.15 = (bf16[256,512]{1,0:T(8,128)(2,1)S(1)}, bf16[256,512]{1,0:T(8,128)(2,1)S(1)}, u32[]{:S(2)}, u32[]{:S(2)}) collective-permute-start(bf16[256,512]{1,0:T(8,128)(2,1)S(1)} %collective-permute-done.13), channel_id=1, source_target_pairs={{0,8},{2,10},{4,12},{6,14},{8,16},{10,18},{12,20},{14,22},{16,24},... | collective-permute-start | bytes 786440 | tf_op jit(solution)/shard_map/ppermute | solution.py:615
  78.1 18.1 %copy-start.10 = (f32[4096]{0:T(1024)S(1)}, f32[4096]{0:T(1024)}, u32[]{:S(2)}) copy-start(f32[4096]{0:T(1024)} %param.9) | copy-start | bytes 49156
  78.1 24.4 %collective-permute-start.17 = (bf16[1024,256]{1,0:T(8,128)(2,1)S(1)}, bf16[1024,256]{1,0:T(8,128)(2,1)S(1)}, u32[]{:S(2)}, u32[]{:S(2)}) collective-permute-start(bf16[1024,256]{1,0:T(8,128)(2,1)S(1)} %pad_maximum_fusion.5), channel_id=1, source_target_pairs={{0,4},{2,6},{4,0},{6,2},{8,12},{10,14},{12,8},{14,10},{16,20},{18,... | collective-permute-start | bytes 1572872 | tf_op jit(solution)/shard_map/ppermute | solution.py:608
  78.8 23.6 %collective-permute-start.18 = (bf16[1024,256]{1,0:T(8,128)(2,1)S(1)}, bf16[1024,256]{1,0:T(8,128)(2,1)S(1)}, u32[]{:S(2)}, u32[]{:S(2)}) collective-permute-start(bf16[1024,256]{1,0:T(8,128)(2,1)S(1)} %pad_maximum_fusion.6), channel_id=1, source_target_pairs={{0,6},{2,4},{4,2},{6,0},{8,14},{10,12},{12,10},{14,8},{16,22},{18,... | collective-permute-start | bytes 1572872 | tf_op jit(solution)/shard_map/ppermute | solution.py:608
  79.7 29.6 %copy-start.18 = (bf16[1024,256]{1,0:T(8,128)(2,1)}, bf16[1024,256]{1,0:T(8,128)(2,1)S(1)}, u32[]{:S(2)}) copy-start(bf16[1024,256]{1,0:T(8,128)(2,1)S(1)} %collective-permute-done.7.refs_3_) | copy-start | bytes 1572868
  79.7 16.4 %collective-permute-start.8 = (bf16[1024,256]{1,0:T(8,128)(2,1)S(1)}, bf16[1024,256]{1,0:T(8,128)(2,1)}, u32[]{:S(2)}, u32[]{:S(2)}) collective-permute-start(bf16[1024,256]{1,0:T(8,128)(2,1)S(1)} %collective-permute-done.7.refs_3_), channel_id=1, source_target_pairs={{0,8},{2,10},{4,12},{6,14},{8,16},{10,18},{12,20},{14,22},{16,24},... | collective-permute-start | bytes 1572872 | tf_op jit(solution)/shard_map/ppermute | solution.py:615
  80.7 24.4 %copy-start.17 = (bf16[1024,256]{1,0:T(8,128)(2,1)}, bf16[1024,256]{1,0:T(8,128)(2,1)S(1)}, u32[]{:S(2)}) copy-start(bf16[1024,256]{1,0:T(8,128)(2,1)S(1)} %collective-permute-done.20.refs_7_) | copy-start | bytes 1572868
  80.7 21.9 %collective-permute-start.16 = (bf16[1024,256]{1,0:T(8,128)(2,1)S(1)}, bf16[1024,256]{1,0:T(8,128)(2,1)S(1)}, u32[]{:S(2)}, u32[]{:S(2)}) collective-permute-start(bf16[1024,256]{1,0:T(8,128)(2,1)S(1)} %pad_maximum_fusion.4), channel_id=1, source_target_pairs={{0,2},{2,0},{4,6},{6,4},{8,10},{10,8},{12,14},{14,12},{16,18},{18,... | collective-permute-start | bytes 1572872 | tf_op jit(solution)/shard_map/ppermute | solution.py:608
  96.2 16.7 %collective-permute-start.21 = (bf16[1024,256]{1,0:T(8,128)(2,1)S(1)}, bf16[1024,256]{1,0:T(8,128)(2,1)}, u32[]{:S(2)}, u32[]{:S(2)}) collective-permute-start(bf16[1024,256]{1,0:T(8,128)(2,1)S(1)} %collective-permute-done.20.refs_7_), channel_id=1, source_target_pairs={{0,8},{2,10},{4,12},{6,14},{8,16},{10,18},{12,20},{14,22},{16,24},... | collective-permute-start | bytes 1572872 | tf_op jit(solution)/shard_map/ppermute | solution.py:615
  96.2 31.0 %collective-permute-start.9 = (bf16[1024,256]{1,0:T(8,128)(2,1)}, bf16[1024,256]{1,0:T(8,128)(2,1)}, u32[]{:S(2)}, u32[]{:S(2)}) collective-permute-start(bf16[1024,256]{1,0:T(8,128)(2,1)} %collective-permute-done.8.refs_4_), channel_id=1, source_target_pairs={{0,8},{2,10},{4,12},{6,14},{8,16},{10,18},{12,20},{14,22},{16,24},... | collective-permute-start | bytes 1572872 | tf_op jit(solution)/shard_map/ppermute | solution.py:615
  98.9 4.2 %copy-start.2 = (bf16[512,1024]{1,0:T(8,128)(2,1)}, bf16[512,1024]{1,0:T(8,128)(2,1)S(1)}, u32[]{:S(2)}) copy-start(bf16[512,1024]{1,0:T(8,128)(2,1)S(1)} %get-tuple-element.28.refs_0_.refs_3_) | copy-start | bytes 3145732
  98.9 4.2 %copy-start.11 = (f32[512,128]{1,0:T(8,128)}, f32[512,128]{1,0:T(8,128)S(1)}, u32[]{:S(2)}) copy-start(f32[512,128]{1,0:T(8,128)S(1)} %get-tuple-element.24) | copy-start | bytes 786436
  102.5 1.1 copy-start.21
  102.6 1.0 copy-start.22
  102.7 1.0 copy-start.23
  103.6 0.9 copy-start.19
  108.0 17.3 %collective-permute-start.19 = (bf16[512,256]{1,0:T(8,128)(2,1)S(1)}, bf16[512,256]{1,0:T(8,128)(2,1)S(1)}, u32[]{:S(2)}, u32[]{:S(2)}) collective-permute-start(bf16[512,256]{1,0:T(8,128)(2,1)S(1)} %pad_maximum_fusion.15), channel_id=1, source_target_pairs={{0,8},{2,10},{4,12},{6,14},{8,16},{10,18},{12,20},{14,22},{16,24},... | collective-permute-start | bytes 786440 | tf_op jit(solution)/shard_map/ppermute | solution.py:705
  116.9 18.9 %collective-permute-start.22 = (bf16[1024,256]{1,0:T(8,128)(2,1)}, bf16[1024,256]{1,0:T(8,128)(2,1)}, u32[]{:S(2)}, u32[]{:S(2)}) collective-permute-start(bf16[1024,256]{1,0:T(8,128)(2,1)} %collective-permute-done.21.refs_8_), channel_id=1, source_target_pairs={{0,8},{2,10},{4,12},{6,14},{8,16},{10,18},{12,20},{14,22},{16,24},... | collective-permute-start | bytes 1572872 | tf_op jit(solution)/shard_map/ppermute | solution.py:615
  135.8 9.3 %copy-start.8 = (bf16[512,256]{1,0:T(8,128)(2,1)S(1)}, bf16[512,256]{1,0:T(8,128)(2,1)}, u32[]{:S(2)}) copy-start(bf16[512,256]{1,0:T(8,128)(2,1)} %get-tuple-element.32.refs_0_) | copy-start | bytes 786436
  142.7 10.3 %collective-permute-start.23 = (bf16[512,256]{1,0:T(8,128)(2,1)}, bf16[512,256]{1,0:T(8,128)(2,1)S(1)}, u32[]{:S(2)}, u32[]{:S(2)}) collective-permute-start(bf16[512,256]{1,0:T(8,128)(2,1)} %get-tuple-element.38), channel_id=1, source_target_pairs={{8,0},{10,2},{12,4},{14,6},{16,8},{18,10},{20,12},{22,14},{24,16},... | collective-permute-start | bytes 786440 | tf_op jit(solution)/shard_map/ppermute | solution.py:720
  145.1 1.0 copy-start.9
  146.1 6.9 %copy-start.5 = (bf16[1024,256]{1,0:T(8,128)(2,1)S(1)}, bf16[1024,256]{1,0:T(8,128)(2,1)}, u32[]{:S(2)}) copy-start(bf16[1024,256]{1,0:T(8,128)(2,1)} %pad_maximum_fusion.7.refs_5_) | copy-start | bytes 1572868
  146.1 6.9 %copy-start.6 = (bf16[1024,256]{1,0:T(8,128)(2,1)S(1)}, bf16[1024,256]{1,0:T(8,128)(2,1)}, u32[]{:S(2)}) copy-start(bf16[1024,256]{1,0:T(8,128)(2,1)} %pad_maximum_fusion.10.refs_8_) | copy-start | bytes 1572868
  146.1 6.9 %copy-start.7 = (bf16[1024,256]{1,0:T(8,128)(2,1)S(1)}, bf16[1024,256]{1,0:T(8,128)(2,1)}, u32[]{:S(2)}) copy-start(bf16[1024,256]{1,0:T(8,128)(2,1)} %pad_maximum_fusion.9.refs_7_) | copy-start | bytes 1572868
  157.6 5.5 %copy-start.4 = (bf16[2,2,128,2048]{3,2,1,0:T(8,128)(2,1)}, bf16[2,2,128,2048]{3,2,1,0:T(8,128)(2,1)S(1)}, u32[]{:S(2)}) copy-start(bf16[2,2,128,2048]{3,2,1,0:T(8,128)(2,1)S(1)} %get-tuple-element.39) | copy-start | bytes 6291460
  157.6 4.2 %collective-permute-start.24 = (bf16[2,2,128,2048]{3,2,1,0:T(8,128)(2,1)S(1)}, bf16[2,2,128,2048]{3,2,1,0:T(8,128)(2,1)S(1)}, u32[]{:S(2)}, u32[]{:S(2)}) collective-permute-start(bf16[2,2,128,2048]{3,2,1,0:T(8,128)(2,1)S(1)} %get-tuple-element.40), channel_id=1, source_target_pairs={{0,2},{2,0},{4,6},{6,4},{8,10},{10,8},{12,14},{14,12},{16,18},{18,... | collective-permute-start | bytes 6291464 | tf_op jit(solution)/shard_map/ppermute | solution.py:608
  161.8 2.3 %copy-start.14 = (bf16[2,2,128,2048]{3,2,1,0:T(8,128)(2,1)}, bf16[2,2,128,2048]{3,2,1,0:T(8,128)(2,1)S(1)}, u32[]{:S(2)}) copy-start(bf16[2,2,128,2048]{3,2,1,0:T(8,128)(2,1)S(1)} %collective-permute-done.24) | copy-start | bytes 6291460
  163.0 15.1 %collective-permute-start.25 = (bf16[2,128,1024]{2,1,0:T(8,128)(2,1)}, bf16[2,128,1024]{2,1,0:T(8,128)(2,1)}, u32[]{:S(2)}, u32[]{:S(2)}) collective-permute-start(bf16[2,128,1024]{2,1,0:T(8,128)(2,1)} %fusion.9), channel_id=1, source_target_pairs={{0,4},{2,6},{4,0},{6,2},{8,12},{10,14},{12,8},{14,10},{16,20},{18,... | collective-permute-start | bytes 1572872 | tf_op jit(solution)/shard_map/ppermute | solution.py:608
  164.1 14.2 %collective-permute-start.27 = (bf16[2,128,1024]{2,1,0:T(8,128)(2,1)}, bf16[2,128,1024]{2,1,0:T(8,128)(2,1)}, u32[]{:S(2)}, u32[]{:S(2)}) collective-permute-start(bf16[2,128,1024]{2,1,0:T(8,128)(2,1)} %fusion.10), channel_id=1, source_target_pairs={{0,1},{1,0},{2,3},{3,2},{4,5},{5,4},{6,7},{7,6},{8,9},{9,8},{10,11... | collective-permute-start | bytes 1572872 | tf_op jit(solution)/shard_map/ppermute | solution.py:611
  165.6 17.7 %copy-start.3 = (bf16[512,1024]{1,0:T(8,128)(2,1)S(1)}, bf16[512,1024]{1,0:T(8,128)(2,1)}, u32[]{:S(2)}) copy-start(bf16[512,1024]{1,0:T(8,128)(2,1)} %copy-done.2) | copy-start | bytes 3145732
  165.6 17.7 %collective-permute-start.32 = (bf16[512,128]{1,0:T(8,128)(2,1)S(1)}, bf16[512,128]{1,0:T(8,128)(2,1)S(1)}, u32[]{:S(2)}, u32[]{:S(2)}) collective-permute-start(bf16[512,128]{1,0:T(8,128)(2,1)S(1)} %get-tuple-element.41.refs_4_), channel_id=1, source_target_pairs={{0,6},{2,4},{4,2},{6,0},{8,14},{10,12},{12,10},{14,8},{16,22},{18,... | collective-permute-start | bytes 393224 | tf_op jit(solution)/shard_map/ppermute | solution.py:608
  166.9 16.4 %collective-permute-start.31 = (bf16[512,128]{1,0:T(8,128)(2,1)S(1)}, bf16[512,128]{1,0:T(8,128)(2,1)S(1)}, u32[]{:S(2)}, u32[]{:S(2)}) collective-permute-start(bf16[512,128]{1,0:T(8,128)(2,1)S(1)} %get-tuple-element.41.refs_4_), channel_id=1, source_target_pairs={{0,4},{2,6},{4,0},{6,2},{8,12},{10,14},{12,8},{14,10},{16,20},{18,... | collective-permute-start | bytes 393224 | tf_op jit(solution)/shard_map/ppermute | solution.py:608
  167.8 15.5 %collective-permute-start.30 = (bf16[512,128]{1,0:T(8,128)(2,1)S(1)}, bf16[512,128]{1,0:T(8,128)(2,1)S(1)}, u32[]{:S(2)}, u32[]{:S(2)}) collective-permute-start(bf16[512,128]{1,0:T(8,128)(2,1)S(1)} %get-tuple-element.41.refs_4_), channel_id=1, source_target_pairs={{0,2},{2,0},{4,6},{6,4},{8,10},{10,8},{12,14},{14,12},{16,18},{18,... | collective-permute-start | bytes 393224 | tf_op jit(solution)/shard_map/ppermute | solution.py:608
  180.8 8.8 %collective-permute-start.28 = (bf16[128,1024]{1,0:T(8,128)(2,1)S(1)}, bf16[128,1024]{1,0:T(8,128)(2,1)S(1)}, u32[]{:S(2)}, u32[]{:S(2)}) collective-permute-start(bf16[128,1024]{1,0:T(8,128)(2,1)S(1)} %fusion.14), channel_id=1, source_target_pairs={{0,4},{2,6},{4,0},{6,2},{8,12},{10,14},{12,8},{14,10},{16,20},{18,... | collective-permute-start | bytes 786440 | tf_op jit(solution)/shard_map/ppermute | solution.py:608
  182.6 7.1 %collective-permute-start.26 = (bf16[128,1024]{1,0:T(8,128)(2,1)S(1)}, bf16[128,1024]{1,0:T(8,128)(2,1)S(1)}, u32[]{:S(2)}, u32[]{:S(2)}) collective-permute-start(bf16[128,1024]{1,0:T(8,128)(2,1)S(1)} %fusion.13), channel_id=1, source_target_pairs={{0,1},{1,0},{2,3},{3,2},{4,5},{5,4},{6,7},{7,6},{8,9},{9,8},{10,11... | collective-permute-start | bytes 786440 | tf_op jit(solution)/shard_map/ppermute | solution.py:611
  185.0 4.8 %copy-start.13 = (bf16[128,2048]{1,0:T(8,128)(2,1)S(1)}, bf16[128,2048]{1,0:T(8,128)(2,1)}, u32[]{:S(2)}) copy-start(bf16[128,2048]{1,0:T(8,128)(2,1)} %param.8) | copy-start | bytes 1572868
  185.0 8.1 %collective-permute-start.33 = (bf16[256,512]{1,0:T(8,128)(2,1)S(1)}, bf16[256,512]{1,0:T(8,128)(2,1)S(1)}, u32[]{:S(2)}, u32[]{:S(2)}) collective-permute-start(bf16[256,512]{1,0:T(8,128)(2,1)S(1)} %get-tuple-element.43), channel_id=1, source_target_pairs={{0,24},{2,26},{4,28},{6,30},{8,0},{10,2},{12,4},{14,6},{16,8},{18,... | collective-permute-start | bytes 786440 | tf_op jit(solution)/shard_map/ppermute | solution.py:615
  186.3 23.7 %collective-permute-start.34 = (bf16[256,512]{1,0:T(8,128)(2,1)S(1)}, bf16[256,512]{1,0:T(8,128)(2,1)S(1)}, u32[]{:S(2)}, u32[]{:S(2)}) collective-permute-start(bf16[256,512]{1,0:T(8,128)(2,1)S(1)} %get-tuple-element.44), channel_id=1, source_target_pairs={{0,16},{2,18},{4,20},{6,22},{8,24},{10,26},{12,28},{14,30},{16,0},... | collective-permute-start | bytes 786440 | tf_op jit(solution)/shard_map/ppermute | solution.py:615
  188.2 21.8 %collective-permute-start.35 = (bf16[256,512]{1,0:T(8,128)(2,1)S(1)}, bf16[256,512]{1,0:T(8,128)(2,1)S(1)}, u32[]{:S(2)}, u32[]{:S(2)}) collective-permute-start(bf16[256,512]{1,0:T(8,128)(2,1)S(1)} %get-tuple-element.45), channel_id=1, source_target_pairs={{0,8},{2,10},{4,12},{6,14},{8,16},{10,18},{12,20},{14,22},{16,24},... | collective-permute-start | bytes 786440 | tf_op jit(solution)/shard_map/ppermute | solution.py:615
  189.8 22.4 %copy-start.1 = (f32[16,2048]{1,0:T(8,128)S(1)}, f32[16,2048]{1,0:T(8,128)}, u32[]{:S(2)}) copy-start(f32[16,2048]{1,0:T(8,128)} %param.14) | copy-start | bytes 393220
  190.0 20.9 %collective-permute-start.29 = (f32[1,128]{1,0:T(1,128)S(1)}, f32[1,128]{1,0:T(1,128)S(1)}, u32[]{:S(2)}, u32[]{:S(2)}) collective-permute-start(f32[1,128]{1,0:T(1,128)S(1)} %bitcast.85), channel_id=1, source_target_pairs={{0,1},{1,0},{2,3},{3,2},{4,5},{5,4},{6,7},{7,6},{8,9},{9,8},{10,11... | collective-permute-start | bytes 1544 | tf_op jit(solution)/shard_map/ppermute | solution.py:611

commit v5 on v4

--- a/solution.py
+++ b/solution.py
@@ -281,7 +281,7 @@
         ),
         out_shape=[jax.ShapeDtypeStruct((tokens, width), jnp.bfloat16)] * ring_size
         + [jax.ShapeDtypeStruct((tokens, 128), jnp.float32)],
-        compiler_params=pltpu.CompilerParams(vmem_limit_bytes=24 << 20),
+        compiler_params=pltpu.CompilerParams(vmem_limit_bytes=14 << 20),
         cost_estimate=pl.CostEstimate(
             flops=8 * tokens * 2 * half, bytes_accessed=8 * tokens * half, transcendentals=tokens
         ),
@@ -460,7 +460,7 @@
             ],
         ),
         out_shape=jax.ShapeDtypeStruct((ring_size, tokens, width), jnp.float32),
-        compiler_params=pltpu.CompilerParams(vmem_limit_bytes=24 << 20),
+        compiler_params=pltpu.CompilerParams(vmem_limit_bytes=14 << 20),
         cost_estimate=pl.CostEstimate(
             flops=2 * tokens * width * ring_size * depth,
             bytes_accessed=4 * tokens * width * ring_size,
@@ -538,7 +538,7 @@
         ),
         out_shape=[jax.ShapeDtypeStruct((tokens, HD), jnp.bfloat16)]
         + [jax.ShapeDtypeStruct(shape, jnp.bfloat16)] * 2,
-        compiler_params=pltpu.CompilerParams(vmem_limit_bytes=28 << 20),
+        compiler_params=pltpu.CompilerParams(vmem_limit_bytes=14 << 20),
         cost_estimate=pl.CostEstimate(
             flops=4 * tokens * width * ring_size * HD,
             bytes_accessed=4 * tokens * width * ring_size,
@@ -565,7 +565,7 @@
         ).astype(out_ref.dtype)
 
 
-def key_weights(where, normed, grads, rows):
+def key_weights(where, normed, grads, rows, dtype):
     tokens, members = grads[0].shape[0], len(grads)
     width = members * grads[0].shape[1]
     shape = (rows, width)
@@ -579,9 +579,8 @@
             out_specs=[pl.BlockSpec(shape, lambda i, w: (0, 0))] * len(normed),
             scratch_shapes=[pltpu.VMEM((tokens, width), jnp.bfloat16)],
         ),
-        out_shape=[jax.ShapeDtypeStruct(shape, jnp.float32)]
-        + [jax.ShapeDtypeStruct(shape, jnp.bfloat16)] * (len(normed) - 1),
-        compiler_params=pltpu.CompilerParams(vmem_limit_bytes=16 << 20),
+        out_shape=[jax.ShapeDtypeStruct(shape, dtype)] * len(normed),
+        compiler_params=pltpu.CompilerParams(vmem_limit_bytes=10 << 20),
         cost_estimate=pl.CostEstimate(
             flops=2 * tokens * width * rows * len(normed),
             bytes_accessed=2 * tokens * (width + rows * len(normed)),
@@ -731,7 +730,8 @@
     )
 
     key_dones = [key_done] + [to_partner(key_done, d) for d in range(1, members)]
-    grad_wkey, *others = key_weights(where, normed, key_dones, weight_rows)
+    others = key_weights(where, normed[1:], key_dones, weight_rows, jnp.bfloat16)
+    (grad_wkey,) = key_weights(where, normed[:1], key_dones, weight_rows, jnp.float32)
     for s in range(1, ring_size):
         term = along(others[s - 1], -s)
         grad_wkey = grad_wkey + term.astype(jnp.float32)
@@ -746,10 +746,13 @@
     right_half = narrow(both(every, 1, every, high_cut))
     left_half = to_partner(left_half, 2)
     right_half = to_side(right_half)
-    left = both(0, every, every, low_cut) + wide(left_half)
-    right = both(every, 0, every, high_cut) + wide(right_half)
-    left_sum = left[0] + wide(to_side(narrow(left[1])))
-    right_sum = right[0] + wide(to_partner(narrow(right[1]), 2))
+    left_next = narrow(both(0, 1, every, low_cut) + wide(left_half[1]))
+    right_next = narrow(both(1, 0, every, high_cut) + wide(right_half[1]))
+    left_next, right_next = lax.optimization_barrier((left_next, right_next))
+    right_next = to_partner(right_next, 2)
+    left_next = to_side(left_next)
+    left_sum = both(0, 0, every, low_cut) + wide(left_half[0]) + wide(left_next)
+    right_sum = both(0, 0, every, high_cut) + wide(right_half[0]) + wide(right_next)
     normed_grad = jnp.concatenate([left_sum, right_sum], axis=1)
     own_hidden = wide(hidden)
     own_gain = lax.dynamic_slice_in_dim(norm_gain, tensor * half, half, 0)

time: 213 us -> 223 us (1.047)
  waiting for transfers between devices: 108 us -> 117 us
  Pallas kernels: 27.3 us -> 30.1 us
    ppermute x14, waiting for transfers between devices: 27.1 us -> 39.4 us  [to_partner(): return lax.ppermute(block, 'dp', [(i, i ^ d) for i in range(devices)])]
    ppermute x15, waiting for transfers between devices: 61.7 us -> 57.6 us  [along(): return lax.ppermute(block, 'dp', route)]
    pallas_call x1 -> x2, Pallas kernels: 1.6 us -> 4.32 us  [key_weights(): pl.pallas_call(partial(key_weights_kernel, len(normed)), grid_spec=pltpu....]
  transfers between devices with their start and end apart: 36 -> 36, of which waited for: 18 -> 19; matrix products, arithmetic and copies ran while one was open for 16% -> 14% of each run, Pallas kernels for 7% -> 8%
where the time goes in v5:
time: 223 us; the launch traced here: 222 us
  waiting for transfers between devices  117 us (52%)
  starting transfers between devices  35.6 us (16%)
  Pallas kernels  30.1 us (13%)
  other arithmetic  16.6 us (7%)
  local copies, waits for them, and re-layouts  12.3 us (6%)
  matrix products  8.86 us (4%)
    ppermute x15, waiting for transfers between devices, along(): return lax.ppermute(block, 'dp', route)  57.6 us
    ppermute x14, waiting for transfers between devices, to_partner(): return lax.ppermute(block, 'dp', [(i, i ^ d) for i in range(devices)])  39.4 us
    ppermute x15, starting transfers between devices, along(): return lax.ppermute(block, 'dp', route)  18.3 us
    pallas_call x2, Pallas kernels, attend(): pl.pallas_call(partial(attend_kernel, heads, rows, len(normed), before is...  13.6 us
    ppermute x5, waiting for transfers between devices, to_side(): return lax.ppermute(block, 'tensor', [(i, i ^ 1) for i in range(tensors)])  12.3 us
    ppermute x14, starting transfers between devices, to_partner(): return lax.ppermute(block, 'dp', [(i, i ^ d) for i in range(devices)])  8.31 us
    dot_general x10, matrix products, project(): term = jnp.dot(normed[s], piece, preferred_element_type=jnp.float32)  8.2 us
    ppermute x5, starting transfers between devices, to_side(): return lax.ppermute(block, 'tensor', [(i, i ^ 1) for i in range(tensors)])  6.35 us
  transfers between devices with their start and end apart: 36, of which 19 were waited for; matrix products, arithmetic and copies ran while one was open for 14% of the time, Pallas kernels for 8%

profile of v5, /device:TPU:0, one launch (start us, length us, event | category | flops | bytes accessed | tf_op | source)
XLA Modules:
  0.0 222.0 jit_solution(4831802977747675478)
XLA Ops:
  0.7 3.1 %collective-permute-start = (bf16[128,2048]{1,0:T(8,128)(2,1)}, bf16[128,2048]{1,0:T(8,128)(2,1)}, u32[]{:S(2)}, u32[]{:S(2)}) collective-permute-start(bf16[128,2048]{1,0:T(8,128)(2,1)} %param.8), channel_id=1, source_target_pairs={{0,1},{1,0},{2,3},{3,2},{4,5},{5,4},{6,7},{7,6},{8,9},{9,8},{10,11... | collective-permute-start | bytes 1572872 | tf_op jit(solution)/shard_map/ppermute | solution.py:610
  3.7 1.5 collective-permute-start.1
  5.2 1.6 collective-permute-start.10
  6.8 1.6 collective-permute-start.11
  8.4 1.2 dynamic-slice_bitcast_fusion.4
  9.6 1.3 constant_dynamic-slice_fusion.38
  14.5 2.0 collective-permute-done.10
  16.5 1.0 constant_dynamic-slice_fusion.5
  17.5 2.9 %collective-permute-done.11 = bf16[256,512]{1,0:T(8,128)(2,1)S(1)} collective-permute-done((bf16[256,512]{1,0:T(8,128)(2,1)}, bf16[256,512]{1,0:T(8,128)(2,1)S(1)}, u32[]{:S(2)}, u32[]{:S(2)}) %collective-permute-start.11) | collective-permute-done | bytes 262176 | tf_op jit(solution)/shard_map/ppermute | solution.py:614
  20.5 6.7 %collective-permute-done.5 = bf16[384,512]{1,0:T(8,128)(2,1)} collective-permute-done((bf16[384,512]{1,0:T(8,128)(2,1)S(1)}, bf16[384,512]{1,0:T(8,128)(2,1)}, u32[]{:S(2)}, u32[]{:S(2)}) %collective-permute-start.5) | collective-permute-done | bytes 393248 | tf_op jit(solution)/shard_map/ppermute | solution.py:607
  27.3 1.6 collective-permute-start.12
  28.8 1.0 slice.186
  29.8 3.4 %collective-permute-done.6 = bf16[384,512]{1,0:T(8,128)(2,1)S(1)} collective-permute-done((bf16[384,512]{1,0:T(8,128)(2,1)S(1)}, bf16[384,512]{1,0:T(8,128)(2,1)S(1)}, u32[]{:S(2)}, u32[]{:S(2)}) %collective-permute-start.6) | collective-permute-done | bytes 393248 | tf_op jit(solution)/shard_map/ppermute | solution.py:607
  33.2 1.6 collective-permute-start.13
  35.0 1.6 collective-permute-start.20
  36.6 0.9 slice_bitcast_fusion.6
  38.2 1.6 collective-permute-start.7
  39.9 12.0 %collective-permute-done.2 = bf16[128,2048]{1,0:T(8,128)(2,1)S(1)} collective-permute-done((bf16[128,2048]{1,0:T(8,128)(2,1)}, bf16[128,2048]{1,0:T(8,128)(2,1)S(1)}, u32[]{:S(2)}, u32[]{:S(2)}) %collective-permute-start.2) | collective-permute-done | bytes 524320 | tf_op jit(solution)/shard_map/ppermute | solution.py:610
  51.9 1.5 pad_maximum_fusion
  54.2 1.6 collective-permute-start.14
  56.7 15.4 %collective-permute-done.14 = bf16[256,512]{1,0:T(8,128)(2,1)S(1)} collective-permute-done((bf16[256,512]{1,0:T(8,128)(2,1)S(1)}, bf16[256,512]{1,0:T(8,128)(2,1)S(1)}, u32[]{:S(2)}, u32[]{:S(2)}) %collective-permute-start.14) | collective-permute-done | bytes 262176 | tf_op jit(solution)/shard_map/ppermute | solution.py:614
  72.2 5.6 %collective-permute-done.15 = bf16[256,512]{1,0:T(8,128)(2,1)S(1)} collective-permute-done((bf16[256,512]{1,0:T(8,128)(2,1)S(1)}, bf16[256,512]{1,0:T(8,128)(2,1)S(1)}, u32[]{:S(2)}, u32[]{:S(2)}) %collective-permute-start.15) | collective-permute-done | bytes 262176 | tf_op jit(solution)/shard_map/ppermute | solution.py:614
  78.6 0.9 collective-permute-start.18
  79.5 0.9 fusion.28
  81.3 14.7 %collective-permute-done.8.refs_4_ = bf16[1024,256]{1,0:T(8,128)(2,1)} collective-permute-done((bf16[1024,256]{1,0:T(8,128)(2,1)S(1)}, bf16[1024,256]{1,0:T(8,128)(2,1)}, u32[]{:S(2)}, u32[]{:S(2)}) %collective-permute-start.8) | collective-permute-done | bytes 524320 | tf_op jit(solution)/shard_map/ppermute | solution.py:614
  96.0 2.7 %shard_map.95 = (bf16[512,1024]{1,0:T(8,128)(2,1)S(1)}, bf16[512,1024]{1,0:T(8,128)(2,1)S(1)}, bf16[512,1024]{1,0:T(8,128)(2,1)S(1)}, bf16[512,1024]{1,0:T(8,128)(2,1)S(1)}, f32[512,128]{1,0:T(8,128)S(1)}) custom-call(s32[7]{0:T(128)S(1)} %stack.58.where, bf16[2,2,128,2048]{3,2,1,0:T(8,128)(2,1)S(1)} %bitcast.88, ...), custom_call_target="tpu_custom_call" | custom-call | flops 16777216 | bytes 8388608 | tf_op jit(solution)/shard_map/pallas_call | solution.py:273
  98.7 3.6 %collective-permute-done.18 = bf16[1024,256]{1,0:T(8,128)(2,1)S(1)} collective-permute-done((bf16[1024,256]{1,0:T(8,128)(2,1)S(1)}, bf16[1024,256]{1,0:T(8,128)(2,1)S(1)}, u32[]{:S(2)}, u32[]{:S(2)}) %collective-permute-start.18) | collective-permute-done | bytes 524320 | tf_op jit(solution)/shard_map/ppermute | solution.py:607
  105.9 1.9 fusion.16
  107.8 1.4 collective-permute-start.19
  110.1 2.3 %convolution_add_fusion.3.q_ref = f32[512,256]{1,0:T(8,128)} fusion(f32[512,256]{1,0:T(8,128)S(1)} %convolution_add_fusion.4, bf16[512,1024]{1,0:T(8,128)(2,1)S(1)} %get-tuple-element.28.refs_1_, bf16[1024,256]{1,0:T(8,128)(2,1)} %collective-permute-done.8.refs_4_), kind=kOutput, calls=%fused_computation.9 | convolution fusion | flops 268566528 | bytes 2621440 | tf_op jit(solution)/shard_map/dot_general | solution.py:665
  112.6 2.3 %convolution_add_fusion.q_ref = f32[512,256]{1,0:T(8,128)} fusion(f32[512,256]{1,0:T(8,128)S(1)} %convolution_add_fusion.1, bf16[512,1024]{1,0:T(8,128)(2,1)S(1)} %get-tuple-element.28.refs_1_, bf16[1024,256]{1,0:T(8,128)(2,1)} %collective-permute-done.21.refs_8_), kind=kOutput, calls=%fused_computation.6 | convolution fusion | flops 268566528 | bytes 2621440 | tf_op jit(solution)/shard_map/dot_general | solution.py:665
  115.8 0.8 pad_maximum_fusion.10.refs_8_
  116.6 2.0 collective-permute-start.22
  119.4 5.7 %collective-permute-done.19 = bf16[512,256]{1,0:T(8,128)(2,1)S(1)} collective-permute-done((bf16[512,256]{1,0:T(8,128)(2,1)S(1)}, bf16[512,256]{1,0:T(8,128)(2,1)S(1)}, u32[]{:S(2)}, u32[]{:S(2)}) %collective-permute-start.19) | collective-permute-done | bytes 262176 | tf_op jit(solution)/shard_map/ppermute | solution.py:704
  125.2 0.9 fusion.29
  126.1 0.8 copy.33.refs_4_
  126.9 6.7 %shard_map.96 = (bf16[512,256]{1,0:T(8,128)(2,1)}, f32[512,256]{1,0:T(8,128)}, f32[512,256]{1,0:T(8,128)}) custom-call(f32[512,256]{1,0:T(8,128)} %convolution_add_fusion.3.q_ref, bf16[512,1024]{1,0:T(8,128)(2,1)} %copy-done.2, bf16[1024,256]{1,0:T(8,128)(2,1)} %collective-permute-done.9.refs_1_.refs_5_, bf16[512,256]{1,0:T(8,128)(2,1)} %get-tuple-element.65.refs_2_, ...), custom_call_target="tpu_custom_call" | custom-call | flops 838860800 | bytes 1572864 | tf_op jit(solution)/shard_map/pallas_call | solution.py:378
  133.7 1.9 collective-permute-done.22.refs_1_.refs_9_
  135.6 6.9 %shard_map.97 = (bf16[512,256]{1,0:T(8,128)(2,1)}, bf16[512,256]{1,0:T(8,128)(2,1)}, f32[512,256]{1,0:T(8,128)}) custom-call(f32[512,256]{1,0:T(8,128)} %convolution_add_fusion.q_ref, bf16[512,1024]{1,0:T(8,128)(2,1)} %copy-done.2, bf16[1024,256]{1,0:T(8,128)(2,1)} %collective-permute-done.22.refs_1_.refs_9_, bf16[512,256]{1,0:T(8,128)(2,1)} %get-tuple-element.64.refs_2_, ...), custom_call_target="tpu_custom_call" | custom-call | flops 838860800 | bytes 1572864 | tf_op jit(solution)/shard_map/pallas_call | solution.py:378
  142.4 1.3 collective-permute-start.23
  143.7 1.1 pad_maximum_fusion.8.refs_6_
  144.9 0.9 copy-done.9
  145.9 4.8 %shard_map.98.so_far = f32[4,512,1024]{2,1,0:T(8,128)S(1)} custom-call(s32[7]{0:T(128)S(1)} %stack.58.where, bf16[512,256]{1,0:T(8,128)(2,1)S(1)} %copy-done.8, bf16[512,256]{1,0:T(8,128)(2,1)S(1)} %copy-done.9, bf16[1024,256]{1,0:T(8,128)(2,1)} %copy-done.18, bf16[1024,256]{1,0:T(8,128)(2,1)} %copy-done.20, ...), custom_call_target="tpu_custom_call" | custom-call | flops 2147483648 | bytes 8388608 | tf_op jit(solution)/shard_map/pallas_call | solution.py:448
  150.7 2.1 collective-permute-done.23.refs_2_
  152.8 4.7 %shard_map.99 = (bf16[512,128]{1,0:T(8,128)(2,1)S(1)}, bf16[2,2,128,2048]{3,2,1,0:T(8,128)(2,1)S(1)}, bf16[2,2,128,2048]{3,2,1,0:T(8,128)(2,1)S(1)}) custom-call(s32[7]{0:T(128)S(1)} %stack.58.where, f32[4,512,1024]{2,1,0:T(8,128)S(1)} %shard_map.98.so_far, f32[512,256]{1,0:T(8,128)} %get-tuple-element.37.refs_0_, f32[512,256]{1,0:T(8,128)} %get-tuple-element.38.refs_1_, ...), custom_call_target="tpu_custom_call" | custom-call | flops 1073741824 | bytes 8388608 | tf_op jit(solution)/shard_map/pallas_call | solution.py:527
  157.6 4.1 %collective-permute-done.24 = bf16[2,2,128,2048]{3,2,1,0:T(8,128)(2,1)S(1)} collective-permute-done((bf16[2,2,128,2048]{3,2,1,0:T(8,128)(2,1)S(1)}, bf16[2,2,128,2048]{3,2,1,0:T(8,128)(2,1)S(1)}, u32[]{:S(2)}, u32[]{:S(2)}) %collective-permute-start.24) | collective-permute-done | bytes 2097184 | tf_op jit(solution)/shard_map/ppermute | solution.py:607
  162.9 13.0 %collective-permute-done.25 = bf16[2,128,1024]{2,1,0:T(8,128)(2,1)S(1)} collective-permute-done((bf16[2,128,1024]{2,1,0:T(8,128)(2,1)S(1)}, bf16[2,128,1024]{2,1,0:T(8,128)(2,1)S(1)}, u32[]{:S(2)}, u32[]{:S(2)}) %collective-permute-start.25) | collective-permute-done | bytes 524320 | tf_op jit(solution)/shard_map/ppermute | solution.py:607
  176.2 1.1 fusion.12
  177.9 1.7 collective-permute-start.28
  180.0 1.6 collective-permute-start.30
  181.5 0.9 dynamic-slice_reduce_fusion
  182.5 6.1 %collective-permute-done.32.refs_4_.refs_6_ = bf16[512,128]{1,0:T(8,128)(2,1)S(1)} collective-permute-done((bf16[512,128]{1,0:T(8,128)(2,1)S(1)}, bf16[512,128]{1,0:T(8,128)(2,1)S(1)}, u32[]{:S(2)}, u32[]{:S(2)}) %collective-permute-start.32) | collective-permute-done | bytes 131104 | tf_op jit(solution)/shard_map/ppermute | solution.py:607
  188.5 2.4 %collective-permute-done.31.refs_3_.refs_5_ = bf16[512,128]{1,0:T(8,128)(2,1)S(1)} collective-permute-done((bf16[512,128]{1,0:T(8,128)(2,1)S(1)}, bf16[512,128]{1,0:T(8,128)(2,1)S(1)}, u32[]{:S(2)}, u32[]{:S(2)}) %collective-permute-start.31) | collective-permute-done | bytes 131104 | tf_op jit(solution)/shard_map/ppermute | solution.py:607
  191.0 1.2 copy-done.3
  192.8 2.3 %shard_map.101 = (bf16[256,512]{1,0:T(8,128)(2,1)S(1)}, bf16[256,512]{1,0:T(8,128)(2,1)S(1)}, bf16[256,512]{1,0:T(8,128)(2,1)S(1)}) custom-call(s32[7]{0:T(128)S(1)} %copy-done.12, bf16[512,1024]{1,0:T(8,128)(2,1)S(1)} %get-tuple-element.27.refs_0_, bf16[512,1024]{1,0:T(8,128)(2,1)S(1)} %get-tuple-element.28.refs_1_, bf16[512,1024]{1,0:T(8,128)(2,1)S(1)} %copy-done.3, ...), custom_call_target="tpu_custom_call" | custom-call | flops 402653184 | bytes 1310720 | tf_op jit(solution)/shard_map/pallas_call | solution.py:572
  195.1 1.5 collective-permute-start.33
  196.7 1.7 collective-permute-start.34
  198.4 1.2 collective-permute-start.35
  199.6 2.0 shard_map.100
  201.6 1.7 fusion.14
  203.6 1.4 collective-permute-start.29
  205.0 14.8 %collective-permute-done.34 = bf16[256,512]{1,0:T(8,128)(2,1)S(1)} collective-permute-done((bf16[256,512]{1,0:T(8,128)(2,1)S(1)}, bf16[256,512]{1,0:T(8,128)(2,1)S(1)}, u32[]{:S(2)}, u32[]{:S(2)}) %collective-permute-start.34) | collective-permute-done | bytes 262176 | tf_op jit(solution)/shard_map/ppermute | solution.py:614
  219.9 0.9 convert_add_fusion.4
  220.8 1.2 fusion.7
  (170 shorter events, 17.6 us)
Async XLA Ops:
  0.6 52.9 %copy-start = (f32[16,2048]{1,0:T(8,128)S(1)}, f32[16,2048]{1,0:T(8,128)}, u32[]{:S(2)}) copy-start(f32[16,2048]{1,0:T(8,128)} %param.14) | copy-start | bytes 393220
  0.6 10.8 %copy-start.31 = (bf16[256,512]{1,0:T(8,128)(2,1)S(1)}, bf16[256,512]{1,0:T(8,128)(2,1)}, u32[]{:S(2)}) copy-start(bf16[256,512]{1,0:T(8,128)(2,1)} %param.11) | copy-start | bytes 786436
  0.7 37.6 %collective-permute-start = (bf16[128,2048]{1,0:T(8,128)(2,1)}, bf16[128,2048]{1,0:T(8,128)(2,1)}, u32[]{:S(2)}, u32[]{:S(2)}) collective-permute-start(bf16[128,2048]{1,0:T(8,128)(2,1)} %param.8), channel_id=1, source_target_pairs={{0,1},{1,0},{2,3},{3,2},{4,5},{5,4},{6,7},{7,6},{8,9},{9,8},{10,11... | collective-permute-start | bytes 1572872 | tf_op jit(solution)/shard_map/ppermute | solution.py:610
  3.7 33.8 %collective-permute-start.1 = (bf16[128,2048]{1,0:T(8,128)(2,1)}, bf16[128,2048]{1,0:T(8,128)(2,1)}, u32[]{:S(2)}, u32[]{:S(2)}) collective-permute-start(bf16[128,2048]{1,0:T(8,128)(2,1)} %param.8), channel_id=1, source_target_pairs={{0,4},{2,6},{4,0},{6,2},{8,12},{10,14},{12,8},{14,10},{16,20},{18,... | collective-permute-start | bytes 1572872 | tf_op jit(solution)/shard_map/ppermute | solution.py:607
  5.2 11.3 %collective-permute-start.10 = (bf16[256,512]{1,0:T(8,128)(2,1)}, bf16[256,512]{1,0:T(8,128)(2,1)}, u32[]{:S(2)}, u32[]{:S(2)}) collective-permute-start(bf16[256,512]{1,0:T(8,128)(2,1)} %param.11), channel_id=1, source_target_pairs={{0,8},{2,10},{4,12},{6,14},{8,16},{10,18},{12,20},{14,22},{16,24},... | collective-permute-start | bytes 786440 | tf_op jit(solution)/shard_map/ppermute | solution.py:614
  6.8 13.6 %collective-permute-start.11 = (bf16[256,512]{1,0:T(8,128)(2,1)}, bf16[256,512]{1,0:T(8,128)(2,1)S(1)}, u32[]{:S(2)}, u32[]{:S(2)}) collective-permute-start(bf16[256,512]{1,0:T(8,128)(2,1)} %param.12), channel_id=1, source_target_pairs={{0,8},{2,10},{4,12},{6,14},{8,16},{10,18},{12,20},{14,22},{16,24},... | collective-permute-start | bytes 786440 | tf_op jit(solution)/shard_map/ppermute | solution.py:614
  8.4 3.2 %copy-start.32 = (bf16[256,512]{1,0:T(8,128)(2,1)S(1)}, bf16[256,512]{1,0:T(8,128)(2,1)}, u32[]{:S(2)}) copy-start(bf16[256,512]{1,0:T(8,128)(2,1)} %param.12) | copy-start | bytes 786436
  9.5 2.1 copy-start.33
  10.9 16.4 %collective-permute-start.5 = (bf16[384,512]{1,0:T(8,128)(2,1)S(1)}, bf16[384,512]{1,0:T(8,128)(2,1)}, u32[]{:S(2)}, u32[]{:S(2)}) collective-permute-start(bf16[384,512]{1,0:T(8,128)(2,1)S(1)} %pad_maximum_fusion.12), channel_id=1, source_target_pairs={{0,4},{2,6},{4,0},{6,2},{8,12},{10,14},{12,8},{14,10},{16,20},{18,... | collective-permute-start | bytes 1179656 | tf_op jit(solution)/shard_map/ppermute | solution.py:607
  14.4 138.3 %copy-start.11 = (s32[7]{0:T(128)}, s32[7]{0:T(128)S(1)}, u32[]{:S(2)}) copy-start(s32[7]{0:T(128)S(1)} %stack.58.where) | copy-start | bytes 88
  16.5 16.7 %collective-permute-start.6 = (bf16[384,512]{1,0:T(8,128)(2,1)S(1)}, bf16[384,512]{1,0:T(8,128)(2,1)S(1)}, u32[]{:S(2)}, u32[]{:S(2)}) collective-permute-start(bf16[384,512]{1,0:T(8,128)(2,1)S(1)} %pad_maximum_fusion.13), channel_id=1, source_target_pairs={{0,6},{2,4},{4,2},{6,0},{8,14},{10,12},{12,10},{14,8},{16,22},{18,... | collective-permute-start | bytes 1179656 | tf_op jit(solution)/shard_map/ppermute | solution.py:607
  20.4 14.4 %collective-permute-start.4 = (bf16[384,512]{1,0:T(8,128)(2,1)S(1)}, bf16[384,512]{1,0:T(8,128)(2,1)S(1)}, u32[]{:S(2)}, u32[]{:S(2)}) collective-permute-start(bf16[384,512]{1,0:T(8,128)(2,1)S(1)} %pad_maximum_fusion.11), channel_id=1, source_target_pairs={{0,2},{2,0},{4,6},{6,4},{8,10},{10,8},{12,14},{14,12},{16,18},{18,... | collective-permute-start | bytes 1179656 | tf_op jit(solution)/shard_map/ppermute | solution.py:607
  20.5 82.9 %copy-start.27 = (bf16[256,256]{1,0:T(8,128)(2,1)}, bf16[256,256]{1,0:T(8,128)(2,1)S(1)}, u32[]{:S(2)}) copy-start(bf16[256,256]{1,0:T(8,128)(2,1)S(1)} %pad_maximum_fusion.29) | copy-start | bytes 393220
  27.3 27.0 %collective-permute-start.12 = (bf16[256,512]{1,0:T(8,128)(2,1)}, bf16[256,512]{1,0:T(8,128)(2,1)S(1)}, u32[]{:S(2)}, u32[]{:S(2)}) collective-permute-start(bf16[256,512]{1,0:T(8,128)(2,1)} %collective-permute-done.10), channel_id=1, source_target_pairs={{0,8},{2,10},{4,12},{6,14},{8,16},{10,18},{12,20},{14,22},{16,24},... | collective-permute-start | bytes 786440 | tf_op jit(solution)/shard_map/ppermute | solution.py:614
  33.2 22.7 %collective-permute-start.13 = (bf16[256,512]{1,0:T(8,128)(2,1)S(1)}, bf16[256,512]{1,0:T(8,128)(2,1)S(1)}, u32[]{:S(2)}, u32[]{:S(2)}) collective-permute-start(bf16[256,512]{1,0:T(8,128)(2,1)S(1)} %collective-permute-done.11), channel_id=1, source_target_pairs={{0,8},{2,10},{4,12},{6,14},{8,16},{10,18},{12,20},{14,22},{16,24},... | collective-permute-start | bytes 786440 | tf_op jit(solution)/shard_map/ppermute | solution.py:614
  34.9 17.0 %copy-start.14 = (bf16[128,2048]{1,0:T(8,128)(2,1)S(1)}, bf16[128,2048]{1,0:T(8,128)(2,1)}, u32[]{:S(2)}) copy-start(bf16[128,2048]{1,0:T(8,128)(2,1)} %param.8) | copy-start | bytes 1572868
  35.0 18.4 %copy-start.17 = (bf16[1024,256]{1,0:T(8,128)(2,1)}, bf16[1024,256]{1,0:T(8,128)(2,1)S(1)}, u32[]{:S(2)}) copy-start(bf16[1024,256]{1,0:T(8,128)(2,1)S(1)} %get-tuple-element.58.refs_6_) | copy-start | bytes 1572868
  35.0 18.4 %copy-start.18 = (bf16[1024,256]{1,0:T(8,128)(2,1)}, bf16[1024,256]{1,0:T(8,128)(2,1)S(1)}, u32[]{:S(2)}) copy-start(bf16[1024,256]{1,0:T(8,128)(2,1)S(1)} %get-tuple-element.59.refs_2_) | copy-start | bytes 1572868
  35.0 45.5 %collective-permute-start.20 = (bf16[1024,256]{1,0:T(8,128)(2,1)S(1)}, bf16[1024,256]{1,0:T(8,128)(2,1)S(1)}, u32[]{:S(2)}, u32[]{:S(2)}) collective-permute-start(bf16[1024,256]{1,0:T(8,128)(2,1)S(1)} %get-tuple-element.58.refs_6_), channel_id=1, source_target_pairs={{0,8},{2,10},{4,12},{6,14},{8,16},{10,18},{12,20},{14,22},{16,24},... | collective-permute-start | bytes 1572872 | tf_op jit(solution)/shard_map/ppermute | solution.py:614
  37.6 14.4 %collective-permute-start.2 = (bf16[128,2048]{1,0:T(8,128)(2,1)}, bf16[128,2048]{1,0:T(8,128)(2,1)S(1)}, u32[]{:S(2)}, u32[]{:S(2)}) collective-permute-start(bf16[128,2048]{1,0:T(8,128)(2,1)} %collective-permute-done.1), channel_id=1, source_target_pairs={{0,1},{1,0},{2,3},{3,2},{4,5},{5,4},{6,7},{7,6},{8,9},{9,8},{10,11... | collective-permute-start | bytes 1572872 | tf_op jit(solution)/shard_map/ppermute | solution.py:610
  38.2 41.3 %collective-permute-start.7 = (bf16[1024,256]{1,0:T(8,128)(2,1)S(1)}, bf16[1024,256]{1,0:T(8,128)(2,1)S(1)}, u32[]{:S(2)}, u32[]{:S(2)}) collective-permute-start(bf16[1024,256]{1,0:T(8,128)(2,1)S(1)} %get-tuple-element.59.refs_2_), channel_id=1, source_target_pairs={{0,8},{2,10},{4,12},{6,14},{8,16},{10,18},{12,20},{14,22},{16,24},... | collective-permute-start | bytes 1572872 | tf_op jit(solution)/shard_map/ppermute | solution.py:614
  53.4 42.6 %collective-permute-start.3 = (bf16[2,2,128,2048]{3,2,1,0:T(8,128)(2,1)S(1)}, bf16[2,2,128,2048]{3,2,1,0:T(8,128)(2,1)S(1)}, u32[]{:S(2)}, u32[]{:S(2)}) collective-permute-start(bf16[2,2,128,2048]{3,2,1,0:T(8,128)(2,1)S(1)} %bitcast.87), channel_id=1, source_target_pairs={{0,2},{2,0},{4,6},{6,4},{8,10},{10,8},{12,14},{14,12},{16,18},{18,... | collective-permute-start | bytes 6291464 | tf_op jit(solution)/shard_map/ppermute | solution.py:607
  54.2 17.9 %collective-permute-start.14 = (bf16[256,512]{1,0:T(8,128)(2,1)S(1)}, bf16[256,512]{1,0:T(8,128)(2,1)S(1)}, u32[]{:S(2)}, u32[]{:S(2)}) collective-permute-start(bf16[256,512]{1,0:T(8,128)(2,1)S(1)} %collective-permute-done.12), channel_id=1, source_target_pairs={{0,8},{2,10},{4,12},{6,14},{8,16},{10,18},{12,20},{14,22},{16,24},... | collective-permute-start | bytes 786440 | tf_op jit(solution)/shard_map/ppermute | solution.py:614
  56.0 21.7 %collective-permute-start.15 = (bf16[256,512]{1,0:T(8,128)(2,1)S(1)}, bf16[256,512]{1,0:T(8,128)(2,1)S(1)}, u32[]{:S(2)}, u32[]{:S(2)}) collective-permute-start(bf16[256,512]{1,0:T(8,128)(2,1)S(1)} %collective-permute-done.13), channel_id=1, source_target_pairs={{0,8},{2,10},{4,12},{6,14},{8,16},{10,18},{12,20},{14,22},{16,24},... | collective-permute-start | bytes 786440 | tf_op jit(solution)/shard_map/ppermute | solution.py:614
  77.9 18.1 %copy-start.10 = (f32[4096]{0:T(1024)S(1)}, f32[4096]{0:T(1024)}, u32[]{:S(2)}) copy-start(f32[4096]{0:T(1024)} %param.9) | copy-start | bytes 49156
  77.9 24.4 %collective-permute-start.17 = (bf16[1024,256]{1,0:T(8,128)(2,1)S(1)}, bf16[1024,256]{1,0:T(8,128)(2,1)S(1)}, u32[]{:S(2)}, u32[]{:S(2)}) collective-permute-start(bf16[1024,256]{1,0:T(8,128)(2,1)S(1)} %pad_maximum_fusion.5), channel_id=1, source_target_pairs={{0,4},{2,6},{4,0},{6,2},{8,12},{10,14},{12,8},{14,10},{16,20},{18,... | collective-permute-start | bytes 1572872 | tf_op jit(solution)/shard_map/ppermute | solution.py:607
  78.6 23.6 %collective-permute-start.18 = (bf16[1024,256]{1,0:T(8,128)(2,1)S(1)}, bf16[1024,256]{1,0:T(8,128)(2,1)S(1)}, u32[]{:S(2)}, u32[]{:S(2)}) collective-permute-start(bf16[1024,256]{1,0:T(8,128)(2,1)S(1)} %pad_maximum_fusion.6), channel_id=1, source_target_pairs={{0,6},{2,4},{4,2},{6,0},{8,14},{10,12},{12,10},{14,8},{16,22},{18,... | collective-permute-start | bytes 1572872 | tf_op jit(solution)/shard_map/ppermute | solution.py:607
  79.5 29.6 %copy-start.20 = (bf16[1024,256]{1,0:T(8,128)(2,1)}, bf16[1024,256]{1,0:T(8,128)(2,1)S(1)}, u32[]{:S(2)}) copy-start(bf16[1024,256]{1,0:T(8,128)(2,1)S(1)} %collective-permute-done.7.refs_3_) | copy-start | bytes 1572868
  79.5 16.4 %collective-permute-start.8 = (bf16[1024,256]{1,0:T(8,128)(2,1)S(1)}, bf16[1024,256]{1,0:T(8,128)(2,1)}, u32[]{:S(2)}, u32[]{:S(2)}) collective-permute-start(bf16[1024,256]{1,0:T(8,128)(2,1)S(1)} %collective-permute-done.7.refs_3_), channel_id=1, source_target_pairs={{0,8},{2,10},{4,12},{6,14},{8,16},{10,18},{12,20},{14,22},{16,24},... | collective-permute-start | bytes 1572872 | tf_op jit(solution)/shard_map/ppermute | solution.py:614
  80.5 24.4 %copy-start.19 = (bf16[1024,256]{1,0:T(8,128)(2,1)}, bf16[1024,256]{1,0:T(8,128)(2,1)S(1)}, u32[]{:S(2)}) copy-start(bf16[1024,256]{1,0:T(8,128)(2,1)S(1)} %collective-permute-done.20.refs_7_) | copy-start | bytes 1572868
  80.5 21.9 %collective-permute-start.16 = (bf16[1024,256]{1,0:T(8,128)(2,1)S(1)}, bf16[1024,256]{1,0:T(8,128)(2,1)S(1)}, u32[]{:S(2)}, u32[]{:S(2)}) collective-permute-start(bf16[1024,256]{1,0:T(8,128)(2,1)S(1)} %pad_maximum_fusion.4), channel_id=1, source_target_pairs={{0,2},{2,0},{4,6},{6,4},{8,10},{10,8},{12,14},{14,12},{16,18},{18,... | collective-permute-start | bytes 1572872 | tf_op jit(solution)/shard_map/ppermute | solution.py:607
  95.9 16.7 %collective-permute-start.21 = (bf16[1024,256]{1,0:T(8,128)(2,1)S(1)}, bf16[1024,256]{1,0:T(8,128)(2,1)}, u32[]{:S(2)}, u32[]{:S(2)}) collective-permute-start(bf16[1024,256]{1,0:T(8,128)(2,1)S(1)} %collective-permute-done.20.refs_7_), channel_id=1, source_target_pairs={{0,8},{2,10},{4,12},{6,14},{8,16},{10,18},{12,20},{14,22},{16,24},... | collective-permute-start | bytes 1572872 | tf_op jit(solution)/shard_map/ppermute | solution.py:614
  96.0 31.0 %collective-permute-start.9 = (bf16[1024,256]{1,0:T(8,128)(2,1)}, bf16[1024,256]{1,0:T(8,128)(2,1)}, u32[]{:S(2)}, u32[]{:S(2)}) collective-permute-start(bf16[1024,256]{1,0:T(8,128)(2,1)} %collective-permute-done.8.refs_4_), channel_id=1, source_target_pairs={{0,8},{2,10},{4,12},{6,14},{8,16},{10,18},{12,20},{14,22},{16,24},... | collective-permute-start | bytes 1572872 | tf_op jit(solution)/shard_map/ppermute | solution.py:614
  98.7 4.2 %copy-start.2 = (bf16[512,1024]{1,0:T(8,128)(2,1)}, bf16[512,1024]{1,0:T(8,128)(2,1)S(1)}, u32[]{:S(2)}) copy-start(bf16[512,1024]{1,0:T(8,128)(2,1)S(1)} %get-tuple-element.29.refs_0_.refs_2_) | copy-start | bytes 3145732
  98.7 5.2 %copy-start.13 = (f32[512,128]{1,0:T(8,128)}, f32[512,128]{1,0:T(8,128)S(1)}, u32[]{:S(2)}) copy-start(f32[512,128]{1,0:T(8,128)S(1)} %get-tuple-element.25) | copy-start | bytes 786436
  102.3 2.4 %copy-start.28 = (bf16[256,256]{1,0:T(8,128)(2,1)}, bf16[256,256]{1,0:T(8,128)(2,1)S(1)}, u32[]{:S(2)}) copy-start(bf16[256,256]{1,0:T(8,128)(2,1)S(1)} %get-tuple-element.82) | copy-start | bytes 393220
  102.4 2.4 %copy-start.29 = (bf16[256,256]{1,0:T(8,128)(2,1)}, bf16[256,256]{1,0:T(8,128)(2,1)S(1)}, u32[]{:S(2)}) copy-start(bf16[256,256]{1,0:T(8,128)(2,1)S(1)} %get-tuple-element.78) | copy-start | bytes 393220
  107.8 17.3 %collective-permute-start.19 = (bf16[512,256]{1,0:T(8,128)(2,1)S(1)}, bf16[512,256]{1,0:T(8,128)(2,1)S(1)}, u32[]{:S(2)}, u32[]{:S(2)}) collective-permute-start(bf16[512,256]{1,0:T(8,128)(2,1)S(1)} %pad_maximum_fusion.15), channel_id=1, source_target_pairs={{0,8},{2,10},{4,12},{6,14},{8,16},{10,18},{12,20},{14,22},{16,24},... | collective-permute-start | bytes 786440 | tf_op jit(solution)/shard_map/ppermute | solution.py:704
  116.6 19.0 %collective-permute-start.22 = (bf16[1024,256]{1,0:T(8,128)(2,1)}, bf16[1024,256]{1,0:T(8,128)(2,1)}, u32[]{:S(2)}, u32[]{:S(2)}) collective-permute-start(bf16[1024,256]{1,0:T(8,128)(2,1)} %collective-permute-done.21.refs_8_), channel_id=1, source_target_pairs={{0,8},{2,10},{4,12},{6,14},{8,16},{10,18},{12,20},{14,22},{16,24},... | collective-permute-start | bytes 1572872 | tf_op jit(solution)/shard_map/ppermute | solution.py:614
  135.6 9.3 %copy-start.8 = (bf16[512,256]{1,0:T(8,128)(2,1)S(1)}, bf16[512,256]{1,0:T(8,128)(2,1)}, u32[]{:S(2)}) copy-start(bf16[512,256]{1,0:T(8,128)(2,1)} %get-tuple-element.33.refs_0_) | copy-start | bytes 786436
  142.4 10.3 %collective-permute-start.23 = (bf16[512,256]{1,0:T(8,128)(2,1)}, bf16[512,256]{1,0:T(8,128)(2,1)S(1)}, u32[]{:S(2)}, u32[]{:S(2)}) collective-permute-start(bf16[512,256]{1,0:T(8,128)(2,1)} %get-tuple-element.39), channel_id=1, source_target_pairs={{8,0},{10,2},{12,4},{14,6},{16,8},{18,10},{20,12},{22,14},{24,16},... | collective-permute-start | bytes 786440 | tf_op jit(solution)/shard_map/ppermute | solution.py:719
  145.8 6.9 %copy-start.4 = (bf16[1024,256]{1,0:T(8,128)(2,1)S(1)}, bf16[1024,256]{1,0:T(8,128)(2,1)}, u32[]{:S(2)}) copy-start(bf16[1024,256]{1,0:T(8,128)(2,1)} %pad_maximum_fusion.7.refs_5_) | copy-start | bytes 1572868
  145.8 6.9 %copy-start.5 = (bf16[1024,256]{1,0:T(8,128)(2,1)S(1)}, bf16[1024,256]{1,0:T(8,128)(2,1)}, u32[]{:S(2)}) copy-start(bf16[1024,256]{1,0:T(8,128)(2,1)} %pad_maximum_fusion.10.refs_8_) | copy-start | bytes 1572868
  145.8 6.9 %copy-start.6 = (bf16[1024,256]{1,0:T(8,128)(2,1)S(1)}, bf16[1024,256]{1,0:T(8,128)(2,1)}, u32[]{:S(2)}) copy-start(bf16[1024,256]{1,0:T(8,128)(2,1)} %pad_maximum_fusion.9.refs_7_) | copy-start | bytes 1572868
  157.5 19.8 %copy-start.7 = (bf16[2,2,128,2048]{3,2,1,0:T(8,128)(2,1)}, bf16[2,2,128,2048]{3,2,1,0:T(8,128)(2,1)S(1)}, u32[]{:S(2)}) copy-start(bf16[2,2,128,2048]{3,2,1,0:T(8,128)(2,1)S(1)} %get-tuple-element.40) | copy-start | bytes 6291460
  157.5 4.2 %collective-permute-start.24 = (bf16[2,2,128,2048]{3,2,1,0:T(8,128)(2,1)S(1)}, bf16[2,2,128,2048]{3,2,1,0:T(8,128)(2,1)S(1)}, u32[]{:S(2)}, u32[]{:S(2)}) collective-permute-start(bf16[2,2,128,2048]{3,2,1,0:T(8,128)(2,1)S(1)} %get-tuple-element.41), channel_id=1, source_target_pairs={{0,2},{2,0},{4,6},{6,4},{8,10},{10,8},{12,14},{14,12},{16,18},{18,... | collective-permute-start | bytes 6291464 | tf_op jit(solution)/shard_map/ppermute | solution.py:607
  161.7 15.6 %copy-start.16 = (bf16[2,2,128,2048]{3,2,1,0:T(8,128)(2,1)}, bf16[2,2,128,2048]{3,2,1,0:T(8,128)(2,1)S(1)}, u32[]{:S(2)}) copy-start(bf16[2,2,128,2048]{3,2,1,0:T(8,128)(2,1)S(1)} %collective-permute-done.24) | copy-start | bytes 6291460
  161.9 14.0 %collective-permute-start.25 = (bf16[2,128,1024]{2,1,0:T(8,128)(2,1)S(1)}, bf16[2,128,1024]{2,1,0:T(8,128)(2,1)S(1)}, u32[]{:S(2)}, u32[]{:S(2)}) collective-permute-start(bf16[2,128,1024]{2,1,0:T(8,128)(2,1)S(1)} %fusion.9), channel_id=1, source_target_pairs={{0,4},{2,6},{4,0},{6,2},{8,12},{10,14},{12,8},{14,10},{16,20},{18,... | collective-permute-start | bytes 1572872 | tf_op jit(solution)/shard_map/ppermute | solution.py:607
  162.2 14.0 %collective-permute-start.26 = (bf16[2,128,1024]{2,1,0:T(8,128)(2,1)S(1)}, bf16[2,128,1024]{2,1,0:T(8,128)(2,1)S(1)}, u32[]{:S(2)}, u32[]{:S(2)}) collective-permute-start(bf16[2,128,1024]{2,1,0:T(8,128)(2,1)S(1)} %fusion.10), channel_id=1, source_target_pairs={{0,1},{1,0},{2,3},{3,2},{4,5},{5,4},{6,7},{7,6},{8,9},{9,8},{10,11... | collective-permute-start | bytes 1572872 | tf_op jit(solution)/shard_map/ppermute | solution.py:610
  175.9 3.7 %copy-start.22 = (bf16[2,128,1024]{2,1,0:T(8,128)(2,1)}, bf16[2,128,1024]{2,1,0:T(8,128)(2,1)S(1)}, u32[]{:S(2)}) copy-start(bf16[2,128,1024]{2,1,0:T(8,128)(2,1)S(1)} %collective-permute-done.25) | copy-start | bytes 1572868
  176.2 3.8 %copy-start.24 = (bf16[2,128,1024]{2,1,0:T(8,128)(2,1)}, bf16[2,128,1024]{2,1,0:T(8,128)(2,1)S(1)}, u32[]{:S(2)}) copy-start(bf16[2,128,1024]{2,1,0:T(8,128)(2,1)S(1)} %collective-permute-done.26) | copy-start | bytes 1572868
  177.3 24.3 %collective-permute-start.27 = (bf16[128,1024]{1,0:T(8,128)(2,1)}, bf16[128,1024]{1,0:T(8,128)(2,1)}, u32[]{:S(2)}, u32[]{:S(2)}) collective-permute-start(bf16[128,1024]{1,0:T(8,128)(2,1)} %get-tuple-element.42), channel_id=1, source_target_pairs={{0,1},{1,0},{2,3},{3,2},{4,5},{5,4},{6,7},{7,6},{8,9},{9,8},{10,11... | collective-permute-start | bytes 786440 | tf_op jit(solution)/shard_map/ppermute | solution.py:610
  177.9 23.7 %collective-permute-start.28 = (bf16[128,1024]{1,0:T(8,128)(2,1)}, bf16[128,1024]{1,0:T(8,128)(2,1)}, u32[]{:S(2)}, u32[]{:S(2)}) collective-permute-start(bf16[128,1024]{1,0:T(8,128)(2,1)} %get-tuple-element.43), channel_id=1, source_target_pairs={{0,4},{2,6},{4,0},{6,2},{8,12},{10,14},{12,8},{14,10},{16,20},{18,... | collective-permute-start | bytes 786440 | tf_op jit(solution)/shard_map/ppermute | solution.py:607
  179.7 8.9 %collective-permute-start.32 = (bf16[512,128]{1,0:T(8,128)(2,1)S(1)}, bf16[512,128]{1,0:T(8,128)(2,1)S(1)}, u32[]{:S(2)}, u32[]{:S(2)}) collective-permute-start(bf16[512,128]{1,0:T(8,128)(2,1)S(1)} %get-tuple-element.44.refs_1_.refs_3_), channel_id=1, source_target_pairs={{0,6},{2,4},{4,2},{6,0},{8,14},{10,12},{12,10},{14,8},{16,22},{18,... | collective-permute-start | bytes 393224 | tf_op jit(solution)/shard_map/ppermute | solution.py:607
  179.7 11.3 %collective-permute-start.31 = (bf16[512,128]{1,0:T(8,128)(2,1)S(1)}, bf16[512,128]{1,0:T(8,128)(2,1)S(1)}, u32[]{:S(2)}, u32[]{:S(2)}) collective-permute-start(bf16[512,128]{1,0:T(8,128)(2,1)S(1)} %get-tuple-element.44.refs_1_.refs_3_), channel_id=1, source_target_pairs={{0,4},{2,6},{4,0},{6,2},{8,12},{10,14},{12,8},{14,10},{16,20},{18,... | collective-permute-start | bytes 393224 | tf_op jit(solution)/shard_map/ppermute | solution.py:607
  180.0 11.0 %collective-permute-start.30 = (bf16[512,128]{1,0:T(8,128)(2,1)S(1)}, bf16[512,128]{1,0:T(8,128)(2,1)}, u32[]{:S(2)}, u32[]{:S(2)}) collective-permute-start(bf16[512,128]{1,0:T(8,128)(2,1)S(1)} %get-tuple-element.44.refs_1_.refs_3_), channel_id=1, source_target_pairs={{0,2},{2,0},{4,6},{6,4},{8,10},{10,8},{12,14},{14,12},{16,18},{18,... | collective-permute-start | bytes 393224 | tf_op jit(solution)/shard_map/ppermute | solution.py:607
  192.8 8.8 %copy-start.23 = (bf16[2,128,1024]{2,1,0:T(8,128)(2,1)S(1)}, bf16[2,128,1024]{2,1,0:T(8,128)(2,1)}, u32[]{:S(2)}) copy-start(bf16[2,128,1024]{2,1,0:T(8,128)(2,1)} %copy-done.22) | copy-start | bytes 1572868
  192.8 8.8 %copy-start.25 = (bf16[2,128,1024]{2,1,0:T(8,128)(2,1)S(1)}, bf16[2,128,1024]{2,1,0:T(8,128)(2,1)}, u32[]{:S(2)}) copy-start(bf16[2,128,1024]{2,1,0:T(8,128)(2,1)} %copy-done.24) | copy-start | bytes 1572868
  195.1 9.9 %collective-permute-start.33 = (bf16[256,512]{1,0:T(8,128)(2,1)S(1)}, bf16[256,512]{1,0:T(8,128)(2,1)S(1)}, u32[]{:S(2)}, u32[]{:S(2)}) collective-permute-start(bf16[256,512]{1,0:T(8,128)(2,1)S(1)} %get-tuple-element.45), channel_id=1, source_target_pairs={{0,24},{2,26},{4,28},{6,30},{8,0},{10,2},{12,4},{14,6},{16,8},{18,... | collective-permute-start | bytes 786440 | tf_op jit(solution)/shard_map/ppermute | solution.py:614
  196.7 23.2 %collective-permute-start.34 = (bf16[256,512]{1,0:T(8,128)(2,1)S(1)}, bf16[256,512]{1,0:T(8,128)(2,1)S(1)}, u32[]{:S(2)}, u32[]{:S(2)}) collective-permute-start(bf16[256,512]{1,0:T(8,128)(2,1)S(1)} %get-tuple-element.46), channel_id=1, source_target_pairs={{0,16},{2,18},{4,20},{6,22},{8,24},{10,26},{12,28},{14,30},{16,0},... | collective-permute-start | bytes 786440 | tf_op jit(solution)/shard_map/ppermute | solution.py:614
  198.4 21.5 %collective-permute-start.35 = (bf16[256,512]{1,0:T(8,128)(2,1)S(1)}, bf16[256,512]{1,0:T(8,128)(2,1)S(1)}, u32[]{:S(2)}, u32[]{:S(2)}) collective-permute-start(bf16[256,512]{1,0:T(8,128)(2,1)S(1)} %get-tuple-element.47), channel_id=1, source_target_pairs={{0,8},{2,10},{4,12},{6,14},{8,16},{10,18},{12,20},{14,22},{16,24},... | collective-permute-start | bytes 786440 | tf_op jit(solution)/shard_map/ppermute | solution.py:614
  201.6 1.8 copy-start.15
  203.4 18.7 %copy-start.1 = (f32[16,2048]{1,0:T(8,128)S(1)}, f32[16,2048]{1,0:T(8,128)}, u32[]{:S(2)}) copy-start(f32[16,2048]{1,0:T(8,128)} %param.14) | copy-start | bytes 393220
  203.6 17.2 %collective-permute-start.29 = (f32[1,128]{1,0:T(1,128)S(1)}, f32[1,128]{1,0:T(1,128)S(1)}, u32[]{:S(2)}, u32[]{:S(2)}) collective-permute-start(f32[1,128]{1,0:T(1,128)S(1)} %bitcast.95), channel_id=1, source_target_pairs={{0,1},{1,0},{2,3},{3,2},{4,5},{5,4},{6,7},{7,6},{8,9},{9,8},{10,11... | collective-permute-start | bytes 1544 | tf_op jit(solution)/shard_map/ppermute | solution.py:610
  (6 other events, 5.6 us)

commit v6 on v5

--- a/solution.py
+++ b/solution.py
@@ -375,6 +375,8 @@
     by_rows = lambda w: pl.BlockSpec((step, w), lambda i: (i, 0))
     fixed = lambda n, w: pl.BlockSpec((n, w), lambda i: (0, 0))
     extra = [] if before is None else [before]
+    operands = [q_proj, *normed, *weights, grads, keys, keys_turned, values, cosine, sine, low]
+    operands = [pltpu.with_memory_space_constraint(a, pltpu.HBM) for a in operands + extra]
     return pl.pallas_call(
         partial(attend_kernel, heads, rows, len(normed), before is None),
         grid=(tokens // step,),
@@ -391,11 +393,12 @@
                    ),
                    jax.ShapeDtypeStruct((tokens, 2 * HD), jnp.float32)],
         scratch_shapes=[pltpu.VMEM((total, 2 * HD), jnp.float32)],
+        compiler_params=pltpu.CompilerParams(vmem_limit_bytes=24 << 20),
         cost_estimate=pl.CostEstimate(
             flops=10 * tokens * window * width, bytes_accessed=12 * tokens * width,
             transcendentals=tokens * window * heads,
         ),
-    )(q_proj, *normed, *weights, grads, keys, keys_turned, values, cosine, sine, low, *extra)
+    )(*operands)
 
 
 def spread_blocks(where, wide, grads, rows):

time: 223 us -> 222 us (level)
  local copies, waits for them, and re-layouts: 12.3 us -> 14.6 us
  transfers between devices with their start and end apart: 36 -> 36, of which waited for: 19 -> 19; matrix products, arithmetic and copies ran while one was open for 14% -> 15% of each run, Pallas kernels for 8% -> 8%
where the time goes in v6:
time: 222 us; the launch traced here: 221 us
  waiting for transfers between devices  118 us (53%)
  starting transfers between devices  34.1 us (15%)
  Pallas kernels  28.2 us (13%)
  other arithmetic  15.4 us (7%)
  local copies, waits for them, and re-layouts  14.6 us (7%)
  matrix products  8.85 us (4%)
    ppermute x15, waiting for transfers between devices, along(): return lax.ppermute(block, 'dp', route)  57.9 us
    ppermute x14, waiting for transfers between devices, to_partner(): return lax.ppermute(block, 'dp', [(i, i ^ d) for i in range(devices)])  38.4 us
    ppermute x15, starting transfers between devices, along(): return lax.ppermute(block, 'dp', route)  16.8 us
    ppermute x5, waiting for transfers between devices, to_side(): return lax.ppermute(block, 'tensor', [(i, i ^ 1) for i in range(tensors)])  12.3 us
    pallas_call x2, Pallas kernels, attend(): pl.pallas_call(partial(attend_kernel, heads, rows, len(normed), before is...  11.7 us
    ppermute x14, starting transfers between devices, to_partner(): return lax.ppermute(block, 'dp', [(i, i ^ d) for i in range(devices)])  8.32 us
    dot_general x10, matrix products, project(): term = jnp.dot(normed[s], piece, preferred_element_type=jnp.float32)  8.2 us
    ppermute x5, starting transfers between devices, to_side(): return lax.ppermute(block, 'tensor', [(i, i ^ 1) for i in range(tensors)])  6.3 us
  transfers between devices with their start and end apart: 36, of which 19 were waited for; matrix products, arithmetic and copies ran while one was open for 15% of the time, Pallas kernels for 8%

profile of v6, /device:TPU:0, one launch (start us, length us, event | category | flops | bytes accessed | tf_op | source)
XLA Modules:
  0.0 221.2 jit_solution(18058644862635164354)
XLA Ops:
  0.7 3.1 %collective-permute-start = (bf16[128,2048]{1,0:T(8,128)(2,1)}, bf16[128,2048]{1,0:T(8,128)(2,1)}, u32[]{:S(2)}, u32[]{:S(2)}) collective-permute-start(bf16[128,2048]{1,0:T(8,128)(2,1)} %param.8), channel_id=1, source_target_pairs={{0,1},{1,0},{2,3},{3,2},{4,5},{5,4},{6,7},{7,6},{8,9},{9,8},{10,11... | collective-permute-start | bytes 1572872 | tf_op jit(solution)/shard_map/ppermute | solution.py:613
  3.7 1.5 collective-permute-start.1
  5.2 1.6 collective-permute-start.10
  6.8 1.6 collective-permute-start.11
  8.4 1.2 dynamic-slice_bitcast_fusion.4
  9.6 1.3 constant_dynamic-slice_fusion.38
  12.7 0.8 broadcast_multiply_fusion
  14.3 2.2 %collective-permute-done.10 = bf16[256,512]{1,0:T(8,128)(2,1)} collective-permute-done((bf16[256,512]{1,0:T(8,128)(2,1)}, bf16[256,512]{1,0:T(8,128)(2,1)}, u32[]{:S(2)}, u32[]{:S(2)}) %collective-permute-start.10) | collective-permute-done | bytes 262176 | tf_op jit(solution)/shard_map/ppermute | solution.py:617
  16.5 1.0 constant_dynamic-slice_fusion.5
  17.5 3.0 %collective-permute-done.11 = bf16[256,512]{1,0:T(8,128)(2,1)} collective-permute-done((bf16[256,512]{1,0:T(8,128)(2,1)}, bf16[256,512]{1,0:T(8,128)(2,1)}, u32[]{:S(2)}, u32[]{:S(2)}) %collective-permute-start.11) | collective-permute-done | bytes 262176 | tf_op jit(solution)/shard_map/ppermute | solution.py:617
  20.5 1.0 constant_dynamic-slice_fusion.4
  21.6 5.7 %collective-permute-done.5 = bf16[384,512]{1,0:T(8,128)(2,1)} collective-permute-done((bf16[384,512]{1,0:T(8,128)(2,1)S(1)}, bf16[384,512]{1,0:T(8,128)(2,1)}, u32[]{:S(2)}, u32[]{:S(2)}) %collective-permute-start.5) | collective-permute-done | bytes 393248 | tf_op jit(solution)/shard_map/ppermute | solution.py:610
  27.3 1.6 collective-permute-start.12
  28.8 1.0 slice.186
  29.8 3.4 %collective-permute-done.6 = bf16[384,512]{1,0:T(8,128)(2,1)S(1)} collective-permute-done((bf16[384,512]{1,0:T(8,128)(2,1)S(1)}, bf16[384,512]{1,0:T(8,128)(2,1)S(1)}, u32[]{:S(2)}, u32[]{:S(2)}) %collective-permute-start.6) | collective-permute-done | bytes 393248 | tf_op jit(solution)/shard_map/ppermute | solution.py:610
  33.2 1.6 collective-permute-start.13
  35.0 1.6 collective-permute-start.20
  36.6 0.9 slice_bitcast_fusion.6
  38.2 1.6 collective-permute-start.7
  39.9 12.0 %collective-permute-done.2 = bf16[128,2048]{1,0:T(8,128)(2,1)S(1)} collective-permute-done((bf16[128,2048]{1,0:T(8,128)(2,1)}, bf16[128,2048]{1,0:T(8,128)(2,1)S(1)}, u32[]{:S(2)}, u32[]{:S(2)}) %collective-permute-start.2) | collective-permute-done | bytes 524320 | tf_op jit(solution)/shard_map/ppermute | solution.py:613
  51.9 1.5 pad_maximum_fusion
  54.2 1.6 collective-permute-start.14
  56.7 15.6 %collective-permute-done.14 = bf16[256,512]{1,0:T(8,128)(2,1)S(1)} collective-permute-done((bf16[256,512]{1,0:T(8,128)(2,1)S(1)}, bf16[256,512]{1,0:T(8,128)(2,1)S(1)}, u32[]{:S(2)}, u32[]{:S(2)}) %collective-permute-start.14) | collective-permute-done | bytes 262176 | tf_op jit(solution)/shard_map/ppermute | solution.py:617
  72.4 5.6 %collective-permute-done.15 = bf16[256,512]{1,0:T(8,128)(2,1)S(1)} collective-permute-done((bf16[256,512]{1,0:T(8,128)(2,1)S(1)}, bf16[256,512]{1,0:T(8,128)(2,1)S(1)}, u32[]{:S(2)}, u32[]{:S(2)}) %collective-permute-start.15) | collective-permute-done | bytes 262176 | tf_op jit(solution)/shard_map/ppermute | solution.py:617
  78.8 0.9 collective-permute-start.18
  79.8 1.0 fusion.28
  81.6 14.6 %collective-permute-done.8.refs_4_ = bf16[1024,256]{1,0:T(8,128)(2,1)} collective-permute-done((bf16[1024,256]{1,0:T(8,128)(2,1)S(1)}, bf16[1024,256]{1,0:T(8,128)(2,1)}, u32[]{:S(2)}, u32[]{:S(2)}) %collective-permute-start.8) | collective-permute-done | bytes 524320 | tf_op jit(solution)/shard_map/ppermute | solution.py:617
  96.2 2.7 %shard_map.95 = (bf16[512,1024]{1,0:T(8,128)(2,1)S(1)}, bf16[512,1024]{1,0:T(8,128)(2,1)S(1)}, bf16[512,1024]{1,0:T(8,128)(2,1)S(1)}, bf16[512,1024]{1,0:T(8,128)(2,1)S(1)}, f32[512,128]{1,0:T(8,128)S(1)}) custom-call(s32[7]{0:T(128)S(1)} %stack.58.where, bf16[2,2,128,2048]{3,2,1,0:T(8,128)(2,1)S(1)} %bitcast.88, ...), custom_call_target="tpu_custom_call" | custom-call | flops 16777216 | bytes 8388608 | tf_op jit(solution)/shard_map/pallas_call | solution.py:273
  98.9 3.6 %collective-permute-done.18 = bf16[1024,256]{1,0:T(8,128)(2,1)S(1)} collective-permute-done((bf16[1024,256]{1,0:T(8,128)(2,1)S(1)}, bf16[1024,256]{1,0:T(8,128)(2,1)S(1)}, u32[]{:S(2)}, u32[]{:S(2)}) %collective-permute-start.18) | collective-permute-done | bytes 524320 | tf_op jit(solution)/shard_map/ppermute | solution.py:610
  105.7 1.9 fusion.16
  107.7 1.4 collective-permute-start.19
  110.0 2.3 %convolution_add_fusion.3.q_ref = f32[512,256]{1,0:T(8,128)} fusion(f32[512,256]{1,0:T(8,128)S(1)} %convolution_add_fusion.4, bf16[512,1024]{1,0:T(8,128)(2,1)S(1)} %get-tuple-element.28.refs_1_, bf16[1024,256]{1,0:T(8,128)(2,1)} %collective-permute-done.8.refs_4_), kind=kOutput, calls=%fused_computation.9 | convolution fusion | flops 268566528 | bytes 2621440 | tf_op jit(solution)/shard_map/dot_general | solution.py:668
  112.9 2.3 %convolution_add_fusion.q_ref = f32[512,256]{1,0:T(8,128)} fusion(f32[512,256]{1,0:T(8,128)S(1)} %convolution_add_fusion.1, bf16[512,1024]{1,0:T(8,128)(2,1)S(1)} %get-tuple-element.28.refs_1_, bf16[1024,256]{1,0:T(8,128)(2,1)} %collective-permute-done.21.refs_8_), kind=kOutput, calls=%fused_computation.6 | convolution fusion | flops 268566528 | bytes 2621440 | tf_op jit(solution)/shard_map/dot_general | solution.py:668
  115.1 0.8 pad_maximum_fusion.7.refs_5_
  116.0 0.8 pad_maximum_fusion.10.refs_8_
  116.8 1.7 collective-permute-start.22
  118.5 0.8 pad_maximum_fusion.9.refs_7_
  119.3 6.0 %collective-permute-done.19 = bf16[512,256]{1,0:T(8,128)(2,1)S(1)} collective-permute-done((bf16[512,256]{1,0:T(8,128)(2,1)S(1)}, bf16[512,256]{1,0:T(8,128)(2,1)S(1)}, u32[]{:S(2)}, u32[]{:S(2)}) %collective-permute-start.19) | collective-permute-done | bytes 262176 | tf_op jit(solution)/shard_map/ppermute | solution.py:707
  125.4 1.0 fusion.29
  126.4 1.8 copy.33.refs_4_
  128.2 5.7 %shard_map.96 = (bf16[512,256]{1,0:T(8,128)(2,1)S(1)}, f32[512,256]{1,0:T(8,128)S(1)}, f32[512,256]{1,0:T(8,128)S(1)}) custom-call(f32[512,256]{1,0:T(8,128)} %convolution_add_fusion.3.q_ref, bf16[512,1024]{1,0:T(8,128)(2,1)} %copy-done.2, bf16[1024,256]{1,0:T(8,128)(2,1)} %collective-permute-done.9.refs_1_.refs_5_, ...), custom_call_target="tpu_custom_call" | custom-call | flops 838860800 | bytes 1572864 | tf_op jit(solution)/shard_map/pallas_call | solution.py:380
  133.9 0.8 copy-done.8
  135.8 6.0 %shard_map.97 = (bf16[512,256]{1,0:T(8,128)(2,1)S(1)}, bf16[512,256]{1,0:T(8,128)(2,1)S(1)}, f32[512,256]{1,0:T(8,128)S(1)}) custom-call(f32[512,256]{1,0:T(8,128)} %convolution_add_fusion.q_ref, bf16[512,1024]{1,0:T(8,128)(2,1)} %copy-done.2, bf16[1024,256]{1,0:T(8,128)(2,1)} %collective-permute-done.22.refs_1_.refs_9_, ...), custom_call_target="tpu_custom_call" | custom-call | flops 838860800 | bytes 1572864 | tf_op jit(solution)/shard_map/pallas_call | solution.py:380
  141.8 1.3 collective-permute-start.23
  143.2 4.8 %shard_map.98.so_far = f32[4,512,1024]{2,1,0:T(8,128)S(1)} custom-call(s32[7]{0:T(128)S(1)} %stack.58.where, bf16[512,256]{1,0:T(8,128)(2,1)S(1)} %get-tuple-element.33.refs_0_, bf16[512,256]{1,0:T(8,128)(2,1)S(1)} %get-tuple-element.36.refs_1_, bf16[1024,256]{1,0:T(8,128)(2,1)} %copy-done.19, bf16[1024,256]{1,0:T(8,128)(2,1)} %copy-done.21, ...), custom_call_target="tpu_custom_call" | custom-call | flops 2147483648 | bytes 8388608 | tf_op jit(solution)/shard_map/pallas_call | solution.py:451
  148.1 3.8 %collective-permute-done.23.refs_2_ = bf16[512,256]{1,0:T(8,128)(2,1)S(1)} collective-permute-done((bf16[512,256]{1,0:T(8,128)(2,1)S(1)}, bf16[512,256]{1,0:T(8,128)(2,1)S(1)}, u32[]{:S(2)}, u32[]{:S(2)}) %collective-permute-start.23) | collective-permute-done | bytes 262176 | tf_op jit(solution)/shard_map/ppermute | solution.py:722
  151.9 4.7 %shard_map.99 = (bf16[512,128]{1,0:T(8,128)(2,1)S(1)}, bf16[2,2,128,2048]{3,2,1,0:T(8,128)(2,1)S(1)}, bf16[2,2,128,2048]{3,2,1,0:T(8,128)(2,1)S(1)}) custom-call(s32[7]{0:T(128)S(1)} %stack.58.where, f32[4,512,1024]{2,1,0:T(8,128)S(1)} %shard_map.98.so_far, f32[512,256]{1,0:T(8,128)} %copy-done.8, f32[512,256]{1,0:T(8,128)} %copy-done.9, ...), custom_call_target="tpu_custom_call" | custom-call | flops 1073741824 | bytes 8388608 | tf_op jit(solution)/shard_map/pallas_call | solution.py:530
  156.7 4.1 %collective-permute-done.24 = bf16[2,2,128,2048]{3,2,1,0:T(8,128)(2,1)S(1)} collective-permute-done((bf16[2,2,128,2048]{3,2,1,0:T(8,128)(2,1)S(1)}, bf16[2,2,128,2048]{3,2,1,0:T(8,128)(2,1)S(1)}, u32[]{:S(2)}, u32[]{:S(2)}) %collective-permute-start.24) | collective-permute-done | bytes 2097184 | tf_op jit(solution)/shard_map/ppermute | solution.py:610
  162.0 13.0 %collective-permute-done.25 = bf16[2,128,1024]{2,1,0:T(8,128)(2,1)S(1)} collective-permute-done((bf16[2,128,1024]{2,1,0:T(8,128)(2,1)S(1)}, bf16[2,128,1024]{2,1,0:T(8,128)(2,1)S(1)}, u32[]{:S(2)}, u32[]{:S(2)}) %collective-permute-start.25) | collective-permute-done | bytes 524320 | tf_op jit(solution)/shard_map/ppermute | solution.py:610
  175.4 1.1 fusion.12
  177.1 1.7 collective-permute-start.28
  179.1 1.6 collective-permute-start.30
  180.7 0.9 dynamic-slice_reduce_fusion
  181.6 6.1 %collective-permute-done.32.refs_4_.refs_6_ = bf16[512,128]{1,0:T(8,128)(2,1)S(1)} collective-permute-done((bf16[512,128]{1,0:T(8,128)(2,1)S(1)}, bf16[512,128]{1,0:T(8,128)(2,1)S(1)}, u32[]{:S(2)}, u32[]{:S(2)}) %collective-permute-start.32) | collective-permute-done | bytes 131104 | tf_op jit(solution)/shard_map/ppermute | solution.py:610
  187.7 2.4 %collective-permute-done.31.refs_3_.refs_5_ = bf16[512,128]{1,0:T(8,128)(2,1)S(1)} collective-permute-done((bf16[512,128]{1,0:T(8,128)(2,1)S(1)}, bf16[512,128]{1,0:T(8,128)(2,1)S(1)}, u32[]{:S(2)}, u32[]{:S(2)}) %collective-permute-start.31) | collective-permute-done | bytes 131104 | tf_op jit(solution)/shard_map/ppermute | solution.py:610
  190.1 1.2 copy-done.3
  192.0 2.3 %shard_map.101 = (bf16[256,512]{1,0:T(8,128)(2,1)S(1)}, bf16[256,512]{1,0:T(8,128)(2,1)S(1)}, bf16[256,512]{1,0:T(8,128)(2,1)S(1)}) custom-call(s32[7]{0:T(128)S(1)} %copy-done.13, bf16[512,1024]{1,0:T(8,128)(2,1)S(1)} %get-tuple-element.27.refs_0_, bf16[512,1024]{1,0:T(8,128)(2,1)S(1)} %get-tuple-element.28.refs_1_, bf16[512,1024]{1,0:T(8,128)(2,1)S(1)} %copy-done.3, ...), custom_call_target="tpu_custom_call" | custom-call | flops 402653184 | bytes 1310720 | tf_op jit(solution)/shard_map/pallas_call | solution.py:575
  194.4 3.2 %collective-permute-start.34 = (bf16[256,512]{1,0:T(8,128)(2,1)S(1)}, bf16[256,512]{1,0:T(8,128)(2,1)S(1)}, u32[]{:S(2)}, u32[]{:S(2)}) collective-permute-start(bf16[256,512]{1,0:T(8,128)(2,1)S(1)} %get-tuple-element.46), channel_id=1, source_target_pairs={{0,16},{2,18},{4,20},{6,22},{8,24},{10,26},{12,28},{14,30},{16,0},... | collective-permute-start | bytes 786440 | tf_op jit(solution)/shard_map/ppermute | solution.py:617
  197.6 2.0 shard_map.100
  199.7 1.7 fusion.14
  201.6 1.4 collective-permute-start.29
  203.0 16.1 %collective-permute-done.34 = bf16[256,512]{1,0:T(8,128)(2,1)S(1)} collective-permute-done((bf16[256,512]{1,0:T(8,128)(2,1)S(1)}, bf16[256,512]{1,0:T(8,128)(2,1)S(1)}, u32[]{:S(2)}, u32[]{:S(2)}) %collective-permute-start.34) | collective-permute-done | bytes 262176 | tf_op jit(solution)/shard_map/ppermute | solution.py:617
  219.1 0.9 convert_add_fusion.4
  220.0 1.2 fusion.7
  (184 shorter events, 16.0 us)
Async XLA Ops:
  0.6 52.9 %copy-start = (f32[16,2048]{1,0:T(8,128)S(1)}, f32[16,2048]{1,0:T(8,128)}, u32[]{:S(2)}) copy-start(f32[16,2048]{1,0:T(8,128)} %param.14) | copy-start | bytes 393220
  0.6 10.8 %copy-start.37 = (bf16[256,512]{1,0:T(8,128)(2,1)S(1)}, bf16[256,512]{1,0:T(8,128)(2,1)}, u32[]{:S(2)}) copy-start(bf16[256,512]{1,0:T(8,128)(2,1)} %param.11) | copy-start | bytes 786436
  0.7 37.6 %collective-permute-start = (bf16[128,2048]{1,0:T(8,128)(2,1)}, bf16[128,2048]{1,0:T(8,128)(2,1)}, u32[]{:S(2)}, u32[]{:S(2)}) collective-permute-start(bf16[128,2048]{1,0:T(8,128)(2,1)} %param.8), channel_id=1, source_target_pairs={{0,1},{1,0},{2,3},{3,2},{4,5},{5,4},{6,7},{7,6},{8,9},{9,8},{10,11... | collective-permute-start | bytes 1572872 | tf_op jit(solution)/shard_map/ppermute | solution.py:613
  3.7 33.8 %collective-permute-start.1 = (bf16[128,2048]{1,0:T(8,128)(2,1)}, bf16[128,2048]{1,0:T(8,128)(2,1)}, u32[]{:S(2)}, u32[]{:S(2)}) collective-permute-start(bf16[128,2048]{1,0:T(8,128)(2,1)} %param.8), channel_id=1, source_target_pairs={{0,4},{2,6},{4,0},{6,2},{8,12},{10,14},{12,8},{14,10},{16,20},{18,... | collective-permute-start | bytes 1572872 | tf_op jit(solution)/shard_map/ppermute | solution.py:610
  5.2 11.3 %collective-permute-start.10 = (bf16[256,512]{1,0:T(8,128)(2,1)}, bf16[256,512]{1,0:T(8,128)(2,1)}, u32[]{:S(2)}, u32[]{:S(2)}) collective-permute-start(bf16[256,512]{1,0:T(8,128)(2,1)} %param.11), channel_id=1, source_target_pairs={{0,8},{2,10},{4,12},{6,14},{8,16},{10,18},{12,20},{14,22},{16,24},... | collective-permute-start | bytes 786440 | tf_op jit(solution)/shard_map/ppermute | solution.py:617
  6.8 13.7 %collective-permute-start.11 = (bf16[256,512]{1,0:T(8,128)(2,1)}, bf16[256,512]{1,0:T(8,128)(2,1)}, u32[]{:S(2)}, u32[]{:S(2)}) collective-permute-start(bf16[256,512]{1,0:T(8,128)(2,1)} %param.12), channel_id=1, source_target_pairs={{0,8},{2,10},{4,12},{6,14},{8,16},{10,18},{12,20},{14,22},{16,24},... | collective-permute-start | bytes 786440 | tf_op jit(solution)/shard_map/ppermute | solution.py:617
  10.9 16.4 %collective-permute-start.5 = (bf16[384,512]{1,0:T(8,128)(2,1)S(1)}, bf16[384,512]{1,0:T(8,128)(2,1)}, u32[]{:S(2)}, u32[]{:S(2)}) collective-permute-start(bf16[384,512]{1,0:T(8,128)(2,1)S(1)} %pad_maximum_fusion.12), channel_id=1, source_target_pairs={{0,4},{2,6},{4,0},{6,2},{8,12},{10,14},{12,8},{14,10},{16,20},{18,... | collective-permute-start | bytes 1179656 | tf_op jit(solution)/shard_map/ppermute | solution.py:610
  13.5 90.6 %copy-start.27 = (bf16[256,256]{1,0:T(8,128)(2,1)}, bf16[256,256]{1,0:T(8,128)(2,1)S(1)}, u32[]{:S(2)}) copy-start(bf16[256,256]{1,0:T(8,128)(2,1)S(1)} %pad_maximum_fusion.16) | copy-start | bytes 393220
  14.2 137.7 %copy-start.12 = (s32[7]{0:T(128)}, s32[7]{0:T(128)S(1)}, u32[]{:S(2)}) copy-start(s32[7]{0:T(128)S(1)} %stack.58.where) | copy-start | bytes 88
  16.5 16.7 %collective-permute-start.6 = (bf16[384,512]{1,0:T(8,128)(2,1)S(1)}, bf16[384,512]{1,0:T(8,128)(2,1)S(1)}, u32[]{:S(2)}, u32[]{:S(2)}) collective-permute-start(bf16[384,512]{1,0:T(8,128)(2,1)S(1)} %pad_maximum_fusion.13), channel_id=1, source_target_pairs={{0,6},{2,4},{4,2},{6,0},{8,14},{10,12},{12,10},{14,8},{16,22},{18,... | collective-permute-start | bytes 1179656 | tf_op jit(solution)/shard_map/ppermute | solution.py:610
  20.5 14.3 %collective-permute-start.4 = (bf16[384,512]{1,0:T(8,128)(2,1)S(1)}, bf16[384,512]{1,0:T(8,128)(2,1)S(1)}, u32[]{:S(2)}, u32[]{:S(2)}) collective-permute-start(bf16[384,512]{1,0:T(8,128)(2,1)S(1)} %pad_maximum_fusion.11), channel_id=1, source_target_pairs={{0,2},{2,0},{4,6},{6,4},{8,10},{10,8},{12,14},{14,12},{16,18},{18,... | collective-permute-start | bytes 1179656 | tf_op jit(solution)/shard_map/ppermute | solution.py:610
  21.5 82.1 %copy-start.29 = (bf16[256,256]{1,0:T(8,128)(2,1)}, bf16[256,256]{1,0:T(8,128)(2,1)S(1)}, u32[]{:S(2)}) copy-start(bf16[256,256]{1,0:T(8,128)(2,1)S(1)} %pad_maximum_fusion.29) | copy-start | bytes 393220
  27.3 27.0 %collective-permute-start.12 = (bf16[256,512]{1,0:T(8,128)(2,1)}, bf16[256,512]{1,0:T(8,128)(2,1)S(1)}, u32[]{:S(2)}, u32[]{:S(2)}) collective-permute-start(bf16[256,512]{1,0:T(8,128)(2,1)} %collective-permute-done.10), channel_id=1, source_target_pairs={{0,8},{2,10},{4,12},{6,14},{8,16},{10,18},{12,20},{14,22},{16,24},... | collective-permute-start | bytes 786440 | tf_op jit(solution)/shard_map/ppermute | solution.py:617
  33.2 22.7 %collective-permute-start.13 = (bf16[256,512]{1,0:T(8,128)(2,1)}, bf16[256,512]{1,0:T(8,128)(2,1)S(1)}, u32[]{:S(2)}, u32[]{:S(2)}) collective-permute-start(bf16[256,512]{1,0:T(8,128)(2,1)} %collective-permute-done.11), channel_id=1, source_target_pairs={{0,8},{2,10},{4,12},{6,14},{8,16},{10,18},{12,20},{14,22},{16,24},... | collective-permute-start | bytes 786440 | tf_op jit(solution)/shard_map/ppermute | solution.py:617
  34.9 17.0 %copy-start.15 = (bf16[128,2048]{1,0:T(8,128)(2,1)S(1)}, bf16[128,2048]{1,0:T(8,128)(2,1)}, u32[]{:S(2)}) copy-start(bf16[128,2048]{1,0:T(8,128)(2,1)} %param.8) | copy-start | bytes 1572868
  35.0 18.4 %copy-start.18 = (bf16[1024,256]{1,0:T(8,128)(2,1)}, bf16[1024,256]{1,0:T(8,128)(2,1)S(1)}, u32[]{:S(2)}) copy-start(bf16[1024,256]{1,0:T(8,128)(2,1)S(1)} %get-tuple-element.58.refs_6_) | copy-start | bytes 1572868
  35.0 18.4 %copy-start.19 = (bf16[1024,256]{1,0:T(8,128)(2,1)}, bf16[1024,256]{1,0:T(8,128)(2,1)S(1)}, u32[]{:S(2)}) copy-start(bf16[1024,256]{1,0:T(8,128)(2,1)S(1)} %get-tuple-element.59.refs_2_) | copy-start | bytes 1572868
  35.0 45.8 %collective-permute-start.20 = (bf16[1024,256]{1,0:T(8,128)(2,1)S(1)}, bf16[1024,256]{1,0:T(8,128)(2,1)S(1)}, u32[]{:S(2)}, u32[]{:S(2)}) collective-permute-start(bf16[1024,256]{1,0:T(8,128)(2,1)S(1)} %get-tuple-element.58.refs_6_), channel_id=1, source_target_pairs={{0,8},{2,10},{4,12},{6,14},{8,16},{10,18},{12,20},{14,22},{16,24},... | collective-permute-start | bytes 1572872 | tf_op jit(solution)/shard_map/ppermute | solution.py:617
  37.6 14.4 %collective-permute-start.2 = (bf16[128,2048]{1,0:T(8,128)(2,1)}, bf16[128,2048]{1,0:T(8,128)(2,1)S(1)}, u32[]{:S(2)}, u32[]{:S(2)}) collective-permute-start(bf16[128,2048]{1,0:T(8,128)(2,1)} %collective-permute-done.1), channel_id=1, source_target_pairs={{0,1},{1,0},{2,3},{3,2},{4,5},{5,4},{6,7},{7,6},{8,9},{9,8},{10,11... | collective-permute-start | bytes 1572872 | tf_op jit(solution)/shard_map/ppermute | solution.py:613
  38.2 41.5 %collective-permute-start.7 = (bf16[1024,256]{1,0:T(8,128)(2,1)S(1)}, bf16[1024,256]{1,0:T(8,128)(2,1)S(1)}, u32[]{:S(2)}, u32[]{:S(2)}) collective-permute-start(bf16[1024,256]{1,0:T(8,128)(2,1)S(1)} %get-tuple-element.59.refs_2_), channel_id=1, source_target_pairs={{0,8},{2,10},{4,12},{6,14},{8,16},{10,18},{12,20},{14,22},{16,24},... | collective-permute-start | bytes 1572872 | tf_op jit(solution)/shard_map/ppermute | solution.py:617
  53.4 42.8 %collective-permute-start.3 = (bf16[2,2,128,2048]{3,2,1,0:T(8,128)(2,1)S(1)}, bf16[2,2,128,2048]{3,2,1,0:T(8,128)(2,1)S(1)}, u32[]{:S(2)}, u32[]{:S(2)}) collective-permute-start(bf16[2,2,128,2048]{3,2,1,0:T(8,128)(2,1)S(1)} %bitcast.87), channel_id=1, source_target_pairs={{0,2},{2,0},{4,6},{6,4},{8,10},{10,8},{12,14},{14,12},{16,18},{18,... | collective-permute-start | bytes 6291464 | tf_op jit(solution)/shard_map/ppermute | solution.py:610
  54.2 18.1 %collective-permute-start.14 = (bf16[256,512]{1,0:T(8,128)(2,1)S(1)}, bf16[256,512]{1,0:T(8,128)(2,1)S(1)}, u32[]{:S(2)}, u32[]{:S(2)}) collective-permute-start(bf16[256,512]{1,0:T(8,128)(2,1)S(1)} %collective-permute-done.12), channel_id=1, source_target_pairs={{0,8},{2,10},{4,12},{6,14},{8,16},{10,18},{12,20},{14,22},{16,24},... | collective-permute-start | bytes 786440 | tf_op jit(solution)/shard_map/ppermute | solution.py:617
  56.0 22.0 %collective-permute-start.15 = (bf16[256,512]{1,0:T(8,128)(2,1)S(1)}, bf16[256,512]{1,0:T(8,128)(2,1)S(1)}, u32[]{:S(2)}, u32[]{:S(2)}) collective-permute-start(bf16[256,512]{1,0:T(8,128)(2,1)S(1)} %collective-permute-done.13), channel_id=1, source_target_pairs={{0,8},{2,10},{4,12},{6,14},{8,16},{10,18},{12,20},{14,22},{16,24},... | collective-permute-start | bytes 786440 | tf_op jit(solution)/shard_map/ppermute | solution.py:617
  78.1 18.1 %copy-start.11 = (f32[4096]{0:T(1024)S(1)}, f32[4096]{0:T(1024)}, u32[]{:S(2)}) copy-start(f32[4096]{0:T(1024)} %param.9) | copy-start | bytes 49156
  78.1 24.4 %collective-permute-start.17 = (bf16[1024,256]{1,0:T(8,128)(2,1)S(1)}, bf16[1024,256]{1,0:T(8,128)(2,1)S(1)}, u32[]{:S(2)}, u32[]{:S(2)}) collective-permute-start(bf16[1024,256]{1,0:T(8,128)(2,1)S(1)} %pad_maximum_fusion.5), channel_id=1, source_target_pairs={{0,4},{2,6},{4,0},{6,2},{8,12},{10,14},{12,8},{14,10},{16,20},{18,... | collective-permute-start | bytes 1572872 | tf_op jit(solution)/shard_map/ppermute | solution.py:610
  78.8 23.6 %collective-permute-start.18 = (bf16[1024,256]{1,0:T(8,128)(2,1)S(1)}, bf16[1024,256]{1,0:T(8,128)(2,1)S(1)}, u32[]{:S(2)}, u32[]{:S(2)}) collective-permute-start(bf16[1024,256]{1,0:T(8,128)(2,1)S(1)} %pad_maximum_fusion.6), channel_id=1, source_target_pairs={{0,6},{2,4},{4,2},{6,0},{8,14},{10,12},{12,10},{14,8},{16,22},{18,... | collective-permute-start | bytes 1572872 | tf_op jit(solution)/shard_map/ppermute | solution.py:610
  79.7 29.3 %copy-start.21 = (bf16[1024,256]{1,0:T(8,128)(2,1)}, bf16[1024,256]{1,0:T(8,128)(2,1)S(1)}, u32[]{:S(2)}) copy-start(bf16[1024,256]{1,0:T(8,128)(2,1)S(1)} %collective-permute-done.7.refs_3_) | copy-start | bytes 1572868
  79.7 16.4 %collective-permute-start.8 = (bf16[1024,256]{1,0:T(8,128)(2,1)S(1)}, bf16[1024,256]{1,0:T(8,128)(2,1)}, u32[]{:S(2)}, u32[]{:S(2)}) collective-permute-start(bf16[1024,256]{1,0:T(8,128)(2,1)S(1)} %collective-permute-done.7.refs_3_), channel_id=1, source_target_pairs={{0,8},{2,10},{4,12},{6,14},{8,16},{10,18},{12,20},{14,22},{16,24},... | collective-permute-start | bytes 1572872 | tf_op jit(solution)/shard_map/ppermute | solution.py:617
  80.8 24.0 %copy-start.20 = (bf16[1024,256]{1,0:T(8,128)(2,1)}, bf16[1024,256]{1,0:T(8,128)(2,1)S(1)}, u32[]{:S(2)}) copy-start(bf16[1024,256]{1,0:T(8,128)(2,1)S(1)} %collective-permute-done.20.refs_7_) | copy-start | bytes 1572868
  80.8 21.8 %collective-permute-start.16 = (bf16[1024,256]{1,0:T(8,128)(2,1)S(1)}, bf16[1024,256]{1,0:T(8,128)(2,1)S(1)}, u32[]{:S(2)}, u32[]{:S(2)}) collective-permute-start(bf16[1024,256]{1,0:T(8,128)(2,1)S(1)} %pad_maximum_fusion.4), channel_id=1, source_target_pairs={{0,2},{2,0},{4,6},{6,4},{8,10},{10,8},{12,14},{14,12},{16,18},{18,... | collective-permute-start | bytes 1572872 | tf_op jit(solution)/shard_map/ppermute | solution.py:610
  96.2 16.7 %collective-permute-start.21 = (bf16[1024,256]{1,0:T(8,128)(2,1)S(1)}, bf16[1024,256]{1,0:T(8,128)(2,1)}, u32[]{:S(2)}, u32[]{:S(2)}) collective-permute-start(bf16[1024,256]{1,0:T(8,128)(2,1)S(1)} %collective-permute-done.20.refs_7_), channel_id=1, source_target_pairs={{0,8},{2,10},{4,12},{6,14},{8,16},{10,18},{12,20},{14,22},{16,24},... | collective-permute-start | bytes 1572872 | tf_op jit(solution)/shard_map/ppermute | solution.py:617
  96.2 32.0 %collective-permute-start.9 = (bf16[1024,256]{1,0:T(8,128)(2,1)}, bf16[1024,256]{1,0:T(8,128)(2,1)}, u32[]{:S(2)}, u32[]{:S(2)}) collective-permute-start(bf16[1024,256]{1,0:T(8,128)(2,1)} %collective-permute-done.8.refs_4_), channel_id=1, source_target_pairs={{0,8},{2,10},{4,12},{6,14},{8,16},{10,18},{12,20},{14,22},{16,24},... | collective-permute-start | bytes 1572872 | tf_op jit(solution)/shard_map/ppermute | solution.py:617
  98.9 4.2 %copy-start.2 = (bf16[512,1024]{1,0:T(8,128)(2,1)}, bf16[512,1024]{1,0:T(8,128)(2,1)S(1)}, u32[]{:S(2)}) copy-start(bf16[512,1024]{1,0:T(8,128)(2,1)S(1)} %get-tuple-element.29.refs_0_.refs_2_) | copy-start | bytes 3145732
  98.9 5.2 %copy-start.14 = (f32[512,128]{1,0:T(8,128)}, f32[512,128]{1,0:T(8,128)S(1)}, u32[]{:S(2)}) copy-start(f32[512,128]{1,0:T(8,128)S(1)} %get-tuple-element.25) | copy-start | bytes 786436
  107.7 17.6 %collective-permute-start.19 = (bf16[512,256]{1,0:T(8,128)(2,1)S(1)}, bf16[512,256]{1,0:T(8,128)(2,1)S(1)}, u32[]{:S(2)}, u32[]{:S(2)}) collective-permute-start(bf16[512,256]{1,0:T(8,128)(2,1)S(1)} %pad_maximum_fusion.15), channel_id=1, source_target_pairs={{0,8},{2,10},{4,12},{6,14},{8,16},{10,18},{12,20},{14,22},{16,24},... | collective-permute-start | bytes 786440 | tf_op jit(solution)/shard_map/ppermute | solution.py:707
  110.0 5.2 %copy-start.28 = (bf16[256,256]{1,0:T(8,128)(2,1)S(1)}, bf16[256,256]{1,0:T(8,128)(2,1)}, u32[]{:S(2)}) copy-start(bf16[256,256]{1,0:T(8,128)(2,1)} %copy-done.27) | copy-start | bytes 393220
  116.8 19.0 %collective-permute-start.22 = (bf16[1024,256]{1,0:T(8,128)(2,1)}, bf16[1024,256]{1,0:T(8,128)(2,1)}, u32[]{:S(2)}, u32[]{:S(2)}) collective-permute-start(bf16[1024,256]{1,0:T(8,128)(2,1)} %collective-permute-done.21.refs_8_), channel_id=1, source_target_pairs={{0,8},{2,10},{4,12},{6,14},{8,16},{10,18},{12,20},{14,22},{16,24},... | collective-permute-start | bytes 1572872 | tf_op jit(solution)/shard_map/ppermute | solution.py:617
  135.8 7.3 %copy-start.30 = (bf16[256,256]{1,0:T(8,128)(2,1)S(1)}, bf16[256,256]{1,0:T(8,128)(2,1)}, u32[]{:S(2)}) copy-start(bf16[256,256]{1,0:T(8,128)(2,1)} %copy-done.29) | copy-start | bytes 393220
  135.8 7.3 %copy-start.32 = (bf16[256,256]{1,0:T(8,128)(2,1)S(1)}, bf16[256,256]{1,0:T(8,128)(2,1)}, u32[]{:S(2)}) copy-start(bf16[256,256]{1,0:T(8,128)(2,1)} %copy-done.31) | copy-start | bytes 393220
  135.8 7.3 %copy-start.34 = (bf16[256,256]{1,0:T(8,128)(2,1)S(1)}, bf16[256,256]{1,0:T(8,128)(2,1)}, u32[]{:S(2)}) copy-start(bf16[256,256]{1,0:T(8,128)(2,1)} %copy-done.33) | copy-start | bytes 393220
  135.8 7.3 %copy-start.36 = (bf16[256,256]{1,0:T(8,128)(2,1)S(1)}, bf16[256,256]{1,0:T(8,128)(2,1)}, u32[]{:S(2)}) copy-start(bf16[256,256]{1,0:T(8,128)(2,1)} %copy-done.35) | copy-start | bytes 393220
  141.8 6.3 %copy-start.9 = (f32[512,256]{1,0:T(8,128)}, f32[512,256]{1,0:T(8,128)S(1)}, u32[]{:S(2)}) copy-start(f32[512,256]{1,0:T(8,128)S(1)} %get-tuple-element.38.refs_1_) | copy-start | bytes 1572868
  141.8 10.1 %collective-permute-start.23 = (bf16[512,256]{1,0:T(8,128)(2,1)S(1)}, bf16[512,256]{1,0:T(8,128)(2,1)S(1)}, u32[]{:S(2)}, u32[]{:S(2)}) collective-permute-start(bf16[512,256]{1,0:T(8,128)(2,1)S(1)} %get-tuple-element.39), channel_id=1, source_target_pairs={{8,0},{10,2},{12,4},{14,6},{16,8},{18,10},{20,12},{22,14},{24,16},... | collective-permute-start | bytes 786440 | tf_op jit(solution)/shard_map/ppermute | solution.py:722
  143.2 8.7 %copy-start.4 = (bf16[1024,256]{1,0:T(8,128)(2,1)S(1)}, bf16[1024,256]{1,0:T(8,128)(2,1)}, u32[]{:S(2)}) copy-start(bf16[1024,256]{1,0:T(8,128)(2,1)} %pad_maximum_fusion.7.refs_5_) | copy-start | bytes 1572868
  143.2 8.7 %copy-start.5 = (bf16[1024,256]{1,0:T(8,128)(2,1)S(1)}, bf16[1024,256]{1,0:T(8,128)(2,1)}, u32[]{:S(2)}) copy-start(bf16[1024,256]{1,0:T(8,128)(2,1)} %pad_maximum_fusion.10.refs_8_) | copy-start | bytes 1572868
  143.2 8.7 %copy-start.6 = (bf16[1024,256]{1,0:T(8,128)(2,1)S(1)}, bf16[1024,256]{1,0:T(8,128)(2,1)}, u32[]{:S(2)}) copy-start(bf16[1024,256]{1,0:T(8,128)(2,1)} %pad_maximum_fusion.9.refs_7_) | copy-start | bytes 1572868
  156.6 19.8 %copy-start.7 = (bf16[2,2,128,2048]{3,2,1,0:T(8,128)(2,1)}, bf16[2,2,128,2048]{3,2,1,0:T(8,128)(2,1)S(1)}, u32[]{:S(2)}) copy-start(bf16[2,2,128,2048]{3,2,1,0:T(8,128)(2,1)S(1)} %get-tuple-element.40) | copy-start | bytes 6291460
  156.6 4.2 %collective-permute-start.24 = (bf16[2,2,128,2048]{3,2,1,0:T(8,128)(2,1)S(1)}, bf16[2,2,128,2048]{3,2,1,0:T(8,128)(2,1)S(1)}, u32[]{:S(2)}, u32[]{:S(2)}) collective-permute-start(bf16[2,2,128,2048]{3,2,1,0:T(8,128)(2,1)S(1)} %get-tuple-element.41), channel_id=1, source_target_pairs={{0,2},{2,0},{4,6},{6,4},{8,10},{10,8},{12,14},{14,12},{16,18},{18,... | collective-permute-start | bytes 6291464 | tf_op jit(solution)/shard_map/ppermute | solution.py:610
  160.8 15.6 %copy-start.17 = (bf16[2,2,128,2048]{3,2,1,0:T(8,128)(2,1)}, bf16[2,2,128,2048]{3,2,1,0:T(8,128)(2,1)S(1)}, u32[]{:S(2)}) copy-start(bf16[2,2,128,2048]{3,2,1,0:T(8,128)(2,1)S(1)} %collective-permute-done.24) | copy-start | bytes 6291460
  161.0 14.0 %collective-permute-start.25 = (bf16[2,128,1024]{2,1,0:T(8,128)(2,1)S(1)}, bf16[2,128,1024]{2,1,0:T(8,128)(2,1)S(1)}, u32[]{:S(2)}, u32[]{:S(2)}) collective-permute-start(bf16[2,128,1024]{2,1,0:T(8,128)(2,1)S(1)} %fusion.9), channel_id=1, source_target_pairs={{0,4},{2,6},{4,0},{6,2},{8,12},{10,14},{12,8},{14,10},{16,20},{18,... | collective-permute-start | bytes 1572872 | tf_op jit(solution)/shard_map/ppermute | solution.py:610
  161.4 14.0 %collective-permute-start.26 = (bf16[2,128,1024]{2,1,0:T(8,128)(2,1)S(1)}, bf16[2,128,1024]{2,1,0:T(8,128)(2,1)S(1)}, u32[]{:S(2)}, u32[]{:S(2)}) collective-permute-start(bf16[2,128,1024]{2,1,0:T(8,128)(2,1)S(1)} %fusion.10), channel_id=1, source_target_pairs={{0,1},{1,0},{2,3},{3,2},{4,5},{5,4},{6,7},{7,6},{8,9},{9,8},{10,11... | collective-permute-start | bytes 1572872 | tf_op jit(solution)/shard_map/ppermute | solution.py:613
  175.4 3.8 %copy-start.25 = (bf16[2,128,1024]{2,1,0:T(8,128)(2,1)}, bf16[2,128,1024]{2,1,0:T(8,128)(2,1)S(1)}, u32[]{:S(2)}) copy-start(bf16[2,128,1024]{2,1,0:T(8,128)(2,1)S(1)} %collective-permute-done.26) | copy-start | bytes 1572868
  176.4 23.2 %collective-permute-start.27 = (bf16[128,1024]{1,0:T(8,128)(2,1)}, bf16[128,1024]{1,0:T(8,128)(2,1)}, u32[]{:S(2)}, u32[]{:S(2)}) collective-permute-start(bf16[128,1024]{1,0:T(8,128)(2,1)} %get-tuple-element.42), channel_id=1, source_target_pairs={{0,1},{1,0},{2,3},{3,2},{4,5},{5,4},{6,7},{7,6},{8,9},{9,8},{10,11... | collective-permute-start | bytes 786440 | tf_op jit(solution)/shard_map/ppermute | solution.py:613
  177.1 22.5 %collective-permute-start.28 = (bf16[128,1024]{1,0:T(8,128)(2,1)}, bf16[128,1024]{1,0:T(8,128)(2,1)}, u32[]{:S(2)}, u32[]{:S(2)}) collective-permute-start(bf16[128,1024]{1,0:T(8,128)(2,1)} %get-tuple-element.43), channel_id=1, source_target_pairs={{0,4},{2,6},{4,0},{6,2},{8,12},{10,14},{12,8},{14,10},{16,20},{18,... | collective-permute-start | bytes 786440 | tf_op jit(solution)/shard_map/ppermute | solution.py:610
  178.8 8.9 %collective-permute-start.32 = (bf16[512,128]{1,0:T(8,128)(2,1)S(1)}, bf16[512,128]{1,0:T(8,128)(2,1)S(1)}, u32[]{:S(2)}, u32[]{:S(2)}) collective-permute-start(bf16[512,128]{1,0:T(8,128)(2,1)S(1)} %get-tuple-element.44.refs_1_.refs_3_), channel_id=1, source_target_pairs={{0,6},{2,4},{4,2},{6,0},{8,14},{10,12},{12,10},{14,8},{16,22},{18,... | collective-permute-start | bytes 393224 | tf_op jit(solution)/shard_map/ppermute | solution.py:610
  178.8 11.3 %collective-permute-start.31 = (bf16[512,128]{1,0:T(8,128)(2,1)S(1)}, bf16[512,128]{1,0:T(8,128)(2,1)S(1)}, u32[]{:S(2)}, u32[]{:S(2)}) collective-permute-start(bf16[512,128]{1,0:T(8,128)(2,1)S(1)} %get-tuple-element.44.refs_1_.refs_3_), channel_id=1, source_target_pairs={{0,4},{2,6},{4,0},{6,2},{8,12},{10,14},{12,8},{14,10},{16,20},{18,... | collective-permute-start | bytes 393224 | tf_op jit(solution)/shard_map/ppermute | solution.py:610
  179.1 11.0 %collective-permute-start.30 = (bf16[512,128]{1,0:T(8,128)(2,1)S(1)}, bf16[512,128]{1,0:T(8,128)(2,1)}, u32[]{:S(2)}, u32[]{:S(2)}) collective-permute-start(bf16[512,128]{1,0:T(8,128)(2,1)S(1)} %get-tuple-element.44.refs_1_.refs_3_), channel_id=1, source_target_pairs={{0,2},{2,0},{4,6},{6,4},{8,10},{10,8},{12,14},{14,12},{16,18},{18,... | collective-permute-start | bytes 393224 | tf_op jit(solution)/shard_map/ppermute | solution.py:610
  192.0 7.6 %copy-start.24 = (bf16[2,128,1024]{2,1,0:T(8,128)(2,1)S(1)}, bf16[2,128,1024]{2,1,0:T(8,128)(2,1)}, u32[]{:S(2)}) copy-start(bf16[2,128,1024]{2,1,0:T(8,128)(2,1)} %copy-done.23) | copy-start | bytes 1572868
  192.0 7.6 %copy-start.26 = (bf16[2,128,1024]{2,1,0:T(8,128)(2,1)S(1)}, bf16[2,128,1024]{2,1,0:T(8,128)(2,1)}, u32[]{:S(2)}) copy-start(bf16[2,128,1024]{2,1,0:T(8,128)(2,1)} %copy-done.25) | copy-start | bytes 1572868
  194.4 8.6 %collective-permute-start.33 = (bf16[256,512]{1,0:T(8,128)(2,1)S(1)}, bf16[256,512]{1,0:T(8,128)(2,1)S(1)}, u32[]{:S(2)}, u32[]{:S(2)}) collective-permute-start(bf16[256,512]{1,0:T(8,128)(2,1)S(1)} %get-tuple-element.45), channel_id=1, source_target_pairs={{0,24},{2,26},{4,28},{6,30},{8,0},{10,2},{12,4},{14,6},{16,8},{18,... | collective-permute-start | bytes 786440 | tf_op jit(solution)/shard_map/ppermute | solution.py:617
  194.4 24.6 %collective-permute-start.34 = (bf16[256,512]{1,0:T(8,128)(2,1)S(1)}, bf16[256,512]{1,0:T(8,128)(2,1)S(1)}, u32[]{:S(2)}, u32[]{:S(2)}) collective-permute-start(bf16[256,512]{1,0:T(8,128)(2,1)S(1)} %get-tuple-element.46), channel_id=1, source_target_pairs={{0,16},{2,18},{4,20},{6,22},{8,24},{10,26},{12,28},{14,30},{16,0},... | collective-permute-start | bytes 786440 | tf_op jit(solution)/shard_map/ppermute | solution.py:617
  197.6 21.5 %collective-permute-start.35 = (bf16[256,512]{1,0:T(8,128)(2,1)S(1)}, bf16[256,512]{1,0:T(8,128)(2,1)S(1)}, u32[]{:S(2)}, u32[]{:S(2)}) collective-permute-start(bf16[256,512]{1,0:T(8,128)(2,1)S(1)} %get-tuple-element.47), channel_id=1, source_target_pairs={{0,8},{2,10},{4,12},{6,14},{8,16},{10,18},{12,20},{14,22},{16,24},... | collective-permute-start | bytes 786440 | tf_op jit(solution)/shard_map/ppermute | solution.py:617
  201.4 19.8 %copy-start.1 = (f32[16,2048]{1,0:T(8,128)S(1)}, f32[16,2048]{1,0:T(8,128)}, u32[]{:S(2)}) copy-start(f32[16,2048]{1,0:T(8,128)} %param.14) | copy-start | bytes 393220
  201.6 18.4 %collective-permute-start.29 = (f32[1,128]{1,0:T(1,128)S(1)}, f32[1,128]{1,0:T(1,128)S(1)}, u32[]{:S(2)}, u32[]{:S(2)}) collective-permute-start(f32[1,128]{1,0:T(1,128)S(1)} %bitcast.95), channel_id=1, source_target_pairs={{0,1},{1,0},{2,3},{3,2},{4,5},{5,4},{6,7},{7,6},{8,9},{9,8},{10,11... | collective-permute-start | bytes 1544 | tf_op jit(solution)/shard_map/ppermute | solution.py:613
  (13 other events, 19.3 us)

commit v7 on v6

--- a/solution.py
+++ b/solution.py
@@ -727,9 +727,10 @@
         for piece in pieces
     ]
     so_far = spread_first(where, query_dones, weights, ring_size)
-    in_hbm = [pltpu.with_memory_space_constraint(a, pltpu.HBM) for a in (*owns, cosine, sine)]
+    own_sum = lax.optimization_barrier(sum(owns[1:], owns[0]))
+    in_hbm = [pltpu.with_memory_space_constraint(a, pltpu.HBM) for a in (cosine, sine)]
     key_done, keep, send = spread_last(
-        where, so_far, in_hbm[:-2], back, *in_hbm[-2:], kv_pieces, ring_size
+        where, so_far, [own_sum], back, *in_hbm, kv_pieces, ring_size
     )
 
     key_dones = [key_done] + [to_partner(key_done, d) for d in range(1, members)]

time: 222 us -> 222 us (level)
  no operation moved by 1% of the time
where the time goes in v7:
time: 222 us; the launch traced here: 221 us
  waiting for transfers between devices  119 us (54%)
  starting transfers between devices  34 us (15%)
  Pallas kernels  27.9 us (13%)
  other arithmetic  15.5 us (7%)
  local copies, waits for them, and re-layouts  13.6 us (6%)
  matrix products  8.85 us (4%)
    ppermute x15, waiting for transfers between devices, along(): return lax.ppermute(block, 'dp', route)  58.8 us
    ppermute x14, waiting for transfers between devices, to_partner(): return lax.ppermute(block, 'dp', [(i, i ^ d) for i in range(devices)])  38.4 us
    ppermute x15, starting transfers between devices, along(): return lax.ppermute(block, 'dp', route)  16.8 us
    ppermute x5, waiting for transfers between devices, to_side(): return lax.ppermute(block, 'tensor', [(i, i ^ 1) for i in range(tensors)])  12.3 us
    pallas_call x2, Pallas kernels, attend(): pl.pallas_call(partial(attend_kernel, heads, rows, len(normed), before is...  11.7 us
    ppermute x14, starting transfers between devices, to_partner(): return lax.ppermute(block, 'dp', [(i, i ^ d) for i in range(devices)])  8.32 us
    dot_general x10, matrix products, project(): term = jnp.dot(normed[s], piece, preferred_element_type=jnp.float32)  8.19 us
    ppermute x5, starting transfers between devices, to_side(): return lax.ppermute(block, 'tensor', [(i, i ^ 1) for i in range(tensors)])  6.28 us
  transfers between devices with their start and end apart: 36, of which 19 were waited for; matrix products, arithmetic and copies ran while one was open for 15% of the time, Pallas kernels for 8%

profile of v7, /device:TPU:0, one launch (start us, length us, event | category | flops | bytes accessed | tf_op | source)
XLA Modules:
  0.0 220.8 jit_solution(5926899720466209192)
XLA Ops:
  0.7 3.1 %collective-permute-start = (bf16[128,2048]{1,0:T(8,128)(2,1)}, bf16[128,2048]{1,0:T(8,128)(2,1)}, u32[]{:S(2)}, u32[]{:S(2)}) collective-permute-start(bf16[128,2048]{1,0:T(8,128)(2,1)} %param.8), channel_id=1, source_target_pairs={{0,1},{1,0},{2,3},{3,2},{4,5},{5,4},{6,7},{7,6},{8,9},{9,8},{10,11... | collective-permute-start | bytes 1572872 | tf_op jit(solution)/shard_map/ppermute | solution.py:613
  3.7 1.5 collective-permute-start.1
  5.2 1.6 collective-permute-start.10
  6.8 1.6 collective-permute-start.11
  8.4 1.2 dynamic-slice_bitcast_fusion.4
  9.6 1.3 constant_dynamic-slice_fusion.38
  12.7 0.8 broadcast_multiply_fusion
  14.3 2.2 collective-permute-done.10
  16.5 1.0 constant_dynamic-slice_fusion.5
  17.5 3.0 %collective-permute-done.11 = bf16[256,512]{1,0:T(8,128)(2,1)} collective-permute-done((bf16[256,512]{1,0:T(8,128)(2,1)}, bf16[256,512]{1,0:T(8,128)(2,1)}, u32[]{:S(2)}, u32[]{:S(2)}) %collective-permute-start.11) | collective-permute-done | bytes 262176 | tf_op jit(solution)/shard_map/ppermute | solution.py:617
  20.5 1.0 constant_dynamic-slice_fusion.4
  21.6 5.7 %collective-permute-done.5 = bf16[384,512]{1,0:T(8,128)(2,1)} collective-permute-done((bf16[384,512]{1,0:T(8,128)(2,1)S(1)}, bf16[384,512]{1,0:T(8,128)(2,1)}, u32[]{:S(2)}, u32[]{:S(2)}) %collective-permute-start.5) | collective-permute-done | bytes 393248 | tf_op jit(solution)/shard_map/ppermute | solution.py:610
  27.3 1.6 collective-permute-start.12
  28.8 1.0 slice.186
  29.8 3.4 %collective-permute-done.6 = bf16[384,512]{1,0:T(8,128)(2,1)S(1)} collective-permute-done((bf16[384,512]{1,0:T(8,128)(2,1)S(1)}, bf16[384,512]{1,0:T(8,128)(2,1)S(1)}, u32[]{:S(2)}, u32[]{:S(2)}) %collective-permute-start.6) | collective-permute-done | bytes 393248 | tf_op jit(solution)/shard_map/ppermute | solution.py:610
  33.2 1.6 collective-permute-start.13
  35.0 1.6 collective-permute-start.20
  36.6 0.9 slice_bitcast_fusion.6
  38.2 1.6 collective-permute-start.7
  39.9 12.0 %collective-permute-done.2 = bf16[128,2048]{1,0:T(8,128)(2,1)S(1)} collective-permute-done((bf16[128,2048]{1,0:T(8,128)(2,1)}, bf16[128,2048]{1,0:T(8,128)(2,1)S(1)}, u32[]{:S(2)}, u32[]{:S(2)}) %collective-permute-start.2) | collective-permute-done | bytes 524320 | tf_op jit(solution)/shard_map/ppermute | solution.py:613
  51.9 1.5 pad_maximum_fusion
  54.2 1.6 collective-permute-start.14
  56.7 15.6 %collective-permute-done.14 = bf16[256,512]{1,0:T(8,128)(2,1)S(1)} collective-permute-done((bf16[256,512]{1,0:T(8,128)(2,1)S(1)}, bf16[256,512]{1,0:T(8,128)(2,1)S(1)}, u32[]{:S(2)}, u32[]{:S(2)}) %collective-permute-start.14) | collective-permute-done | bytes 262176 | tf_op jit(solution)/shard_map/ppermute | solution.py:617
  72.4 5.6 %collective-permute-done.15 = bf16[256,512]{1,0:T(8,128)(2,1)S(1)} collective-permute-done((bf16[256,512]{1,0:T(8,128)(2,1)S(1)}, bf16[256,512]{1,0:T(8,128)(2,1)S(1)}, u32[]{:S(2)}, u32[]{:S(2)}) %collective-permute-start.15) | collective-permute-done | bytes 262176 | tf_op jit(solution)/shard_map/ppermute | solution.py:617
  78.8 0.9 collective-permute-start.18
  79.8 0.9 fusion.28
  81.5 14.6 %collective-permute-done.8.refs_4_ = bf16[1024,256]{1,0:T(8,128)(2,1)} collective-permute-done((bf16[1024,256]{1,0:T(8,128)(2,1)S(1)}, bf16[1024,256]{1,0:T(8,128)(2,1)}, u32[]{:S(2)}, u32[]{:S(2)}) %collective-permute-start.8) | collective-permute-done | bytes 524320 | tf_op jit(solution)/shard_map/ppermute | solution.py:617
  96.2 2.7 %shard_map.95 = (bf16[512,1024]{1,0:T(8,128)(2,1)S(1)}, bf16[512,1024]{1,0:T(8,128)(2,1)S(1)}, bf16[512,1024]{1,0:T(8,128)(2,1)S(1)}, bf16[512,1024]{1,0:T(8,128)(2,1)S(1)}, f32[512,128]{1,0:T(8,128)S(1)}) custom-call(s32[7]{0:T(128)S(1)} %stack.58.where, bf16[2,2,128,2048]{3,2,1,0:T(8,128)(2,1)S(1)} %bitcast.88, ...), custom_call_target="tpu_custom_call" | custom-call | flops 16777216 | bytes 8388608 | tf_op jit(solution)/shard_map/pallas_call | solution.py:273
  98.9 3.6 %collective-permute-done.18 = bf16[1024,256]{1,0:T(8,128)(2,1)S(1)} collective-permute-done((bf16[1024,256]{1,0:T(8,128)(2,1)S(1)}, bf16[1024,256]{1,0:T(8,128)(2,1)S(1)}, u32[]{:S(2)}, u32[]{:S(2)}) %collective-permute-start.18) | collective-permute-done | bytes 524320 | tf_op jit(solution)/shard_map/ppermute | solution.py:610
  105.7 1.9 fusion.16
  107.6 1.4 collective-permute-start.19
  109.9 2.3 %convolution_add_fusion.3.q_ref = f32[512,256]{1,0:T(8,128)} fusion(f32[512,256]{1,0:T(8,128)S(1)} %convolution_add_fusion.4, bf16[512,1024]{1,0:T(8,128)(2,1)S(1)} %get-tuple-element.28.refs_1_, bf16[1024,256]{1,0:T(8,128)(2,1)} %collective-permute-done.8.refs_4_), kind=kOutput, calls=%fused_computation.9 | convolution fusion | flops 268566528 | bytes 2621440 | tf_op jit(solution)/shard_map/dot_general | solution.py:668
  112.9 2.3 %convolution_add_fusion.q_ref = f32[512,256]{1,0:T(8,128)} fusion(f32[512,256]{1,0:T(8,128)S(1)} %convolution_add_fusion.1, bf16[512,1024]{1,0:T(8,128)(2,1)S(1)} %get-tuple-element.28.refs_1_, bf16[1024,256]{1,0:T(8,128)(2,1)} %collective-permute-done.21.refs_8_), kind=kOutput, calls=%fused_computation.6 | convolution fusion | flops 268566528 | bytes 2621440 | tf_op jit(solution)/shard_map/dot_general | solution.py:668
  115.1 0.8 pad_maximum_fusion.7.refs_4_
  116.0 0.8 pad_maximum_fusion.10.refs_7_
  116.8 1.6 collective-permute-start.22
  118.4 0.8 pad_maximum_fusion.9.refs_6_
  119.3 6.0 %collective-permute-done.19 = bf16[512,256]{1,0:T(8,128)(2,1)S(1)} collective-permute-done((bf16[512,256]{1,0:T(8,128)(2,1)S(1)}, bf16[512,256]{1,0:T(8,128)(2,1)S(1)}, u32[]{:S(2)}, u32[]{:S(2)}) %collective-permute-start.19) | collective-permute-done | bytes 262176 | tf_op jit(solution)/shard_map/ppermute | solution.py:707
  125.4 0.9 fusion.29
  126.3 1.8 copy.33.refs_4_
  128.1 5.7 %shard_map.96 = (bf16[512,256]{1,0:T(8,128)(2,1)S(1)}, f32[512,256]{1,0:T(8,128)S(1)}, f32[512,256]{1,0:T(8,128)S(1)}) custom-call(f32[512,256]{1,0:T(8,128)} %convolution_add_fusion.3.q_ref, bf16[512,1024]{1,0:T(8,128)(2,1)} %copy-done.2, bf16[1024,256]{1,0:T(8,128)(2,1)} %collective-permute-done.9.refs_1_.refs_5_, ...), custom_call_target="tpu_custom_call" | custom-call | flops 838860800 | bytes 1572864 | tf_op jit(solution)/shard_map/pallas_call | solution.py:380
  134.7 1.1 collective-permute-done.22.refs_1_.refs_9_
  135.8 6.0 %shard_map.97 = (bf16[512,256]{1,0:T(8,128)(2,1)S(1)}, bf16[512,256]{1,0:T(8,128)(2,1)S(1)}, f32[512,256]{1,0:T(8,128)S(1)}) custom-call(f32[512,256]{1,0:T(8,128)} %convolution_add_fusion.q_ref, bf16[512,1024]{1,0:T(8,128)(2,1)} %copy-done.2, bf16[1024,256]{1,0:T(8,128)(2,1)} %collective-permute-done.22.refs_1_.refs_9_, ...), custom_call_target="tpu_custom_call" | custom-call | flops 838860800 | bytes 1572864 | tf_op jit(solution)/shard_map/pallas_call | solution.py:380
  141.8 1.3 collective-permute-start.23
  143.3 4.8 %shard_map.98.so_far = f32[4,512,1024]{2,1,0:T(8,128)S(1)} custom-call(s32[7]{0:T(128)S(1)} %stack.58.where, bf16[512,256]{1,0:T(8,128)(2,1)S(1)} %get-tuple-element.33.refs_0_, bf16[512,256]{1,0:T(8,128)(2,1)S(1)} %get-tuple-element.36.refs_1_, bf16[1024,256]{1,0:T(8,128)(2,1)} %copy-done.17, bf16[1024,256]{1,0:T(8,128)(2,1)} %copy-done.19, ...), custom_call_target="tpu_custom_call" | custom-call | flops 2147483648 | bytes 8388608 | tf_op jit(solution)/shard_map/pallas_call | solution.py:451
  148.1 3.8 %collective-permute-done.23.refs_1_ = bf16[512,256]{1,0:T(8,128)(2,1)S(1)} collective-permute-done((bf16[512,256]{1,0:T(8,128)(2,1)S(1)}, bf16[512,256]{1,0:T(8,128)(2,1)S(1)}, u32[]{:S(2)}, u32[]{:S(2)}) %collective-permute-start.23) | collective-permute-done | bytes 262176 | tf_op jit(solution)/shard_map/ppermute | solution.py:722
  151.9 4.3 %shard_map.99 = (bf16[512,128]{1,0:T(8,128)(2,1)S(1)}, bf16[2,2,128,2048]{3,2,1,0:T(8,128)(2,1)S(1)}, bf16[2,2,128,2048]{3,2,1,0:T(8,128)(2,1)S(1)}) custom-call(s32[7]{0:T(128)S(1)} %stack.58.where, f32[4,512,1024]{2,1,0:T(8,128)S(1)} %shard_map.98.so_far, f32[512,256]{1,0:T(8,128)S(1)} %add.255.refs_0_, ...), custom_call_target="tpu_custom_call" | custom-call | flops 1073741824 | bytes 8388608 | tf_op jit(solution)/shard_map/pallas_call | solution.py:530
  156.3 4.1 %collective-permute-done.24 = bf16[2,2,128,2048]{3,2,1,0:T(8,128)(2,1)S(1)} collective-permute-done((bf16[2,2,128,2048]{3,2,1,0:T(8,128)(2,1)S(1)}, bf16[2,2,128,2048]{3,2,1,0:T(8,128)(2,1)S(1)}, u32[]{:S(2)}, u32[]{:S(2)}) %collective-permute-start.24) | collective-permute-done | bytes 2097184 | tf_op jit(solution)/shard_map/ppermute | solution.py:610
  161.7 13.0 %collective-permute-done.25 = bf16[2,128,1024]{2,1,0:T(8,128)(2,1)S(1)} collective-permute-done((bf16[2,128,1024]{2,1,0:T(8,128)(2,1)S(1)}, bf16[2,128,1024]{2,1,0:T(8,128)(2,1)S(1)}, u32[]{:S(2)}, u32[]{:S(2)}) %collective-permute-start.25) | collective-permute-done | bytes 524320 | tf_op jit(solution)/shard_map/ppermute | solution.py:610
  175.0 1.1 fusion.12
  176.7 1.7 collective-permute-start.28
  178.8 1.6 collective-permute-start.30
  180.3 0.9 dynamic-slice_reduce_fusion
  181.3 6.1 %collective-permute-done.32.refs_4_.refs_6_ = bf16[512,128]{1,0:T(8,128)(2,1)S(1)} collective-permute-done((bf16[512,128]{1,0:T(8,128)(2,1)S(1)}, bf16[512,128]{1,0:T(8,128)(2,1)S(1)}, u32[]{:S(2)}, u32[]{:S(2)}) %collective-permute-start.32) | collective-permute-done | bytes 131104 | tf_op jit(solution)/shard_map/ppermute | solution.py:610
  187.3 2.4 %collective-permute-done.31.refs_3_.refs_5_ = bf16[512,128]{1,0:T(8,128)(2,1)S(1)} collective-permute-done((bf16[512,128]{1,0:T(8,128)(2,1)S(1)}, bf16[512,128]{1,0:T(8,128)(2,1)S(1)}, u32[]{:S(2)}, u32[]{:S(2)}) %collective-permute-start.31) | collective-permute-done | bytes 131104 | tf_op jit(solution)/shard_map/ppermute | solution.py:610
  189.8 1.2 copy-done.3
  191.6 2.3 %shard_map.101 = (bf16[256,512]{1,0:T(8,128)(2,1)S(1)}, bf16[256,512]{1,0:T(8,128)(2,1)S(1)}, bf16[256,512]{1,0:T(8,128)(2,1)S(1)}) custom-call(s32[7]{0:T(128)S(1)} %copy-done.11, bf16[512,1024]{1,0:T(8,128)(2,1)S(1)} %get-tuple-element.27.refs_0_, bf16[512,1024]{1,0:T(8,128)(2,1)S(1)} %get-tuple-element.28.refs_1_, bf16[512,1024]{1,0:T(8,128)(2,1)S(1)} %copy-done.3, ...), custom_call_target="tpu_custom_call" | custom-call | flops 402653184 | bytes 1310720 | tf_op jit(solution)/shard_map/pallas_call | solution.py:575
  194.0 3.2 %collective-permute-start.34 = (bf16[256,512]{1,0:T(8,128)(2,1)S(1)}, bf16[256,512]{1,0:T(8,128)(2,1)S(1)}, u32[]{:S(2)}, u32[]{:S(2)}) collective-permute-start(bf16[256,512]{1,0:T(8,128)(2,1)S(1)} %get-tuple-element.46), channel_id=1, source_target_pairs={{0,16},{2,18},{4,20},{6,22},{8,24},{10,26},{12,28},{14,30},{16,0},... | collective-permute-start | bytes 786440 | tf_op jit(solution)/shard_map/ppermute | solution.py:617
  197.2 2.0 shard_map.100
  199.3 1.7 fusion.14
  201.2 1.3 collective-permute-start.29
  202.6 16.1 %collective-permute-done.34 = bf16[256,512]{1,0:T(8,128)(2,1)S(1)} collective-permute-done((bf16[256,512]{1,0:T(8,128)(2,1)S(1)}, bf16[256,512]{1,0:T(8,128)(2,1)S(1)}, u32[]{:S(2)}, u32[]{:S(2)}) %collective-permute-start.34) | collective-permute-done | bytes 262176 | tf_op jit(solution)/shard_map/ppermute | solution.py:617
  218.7 0.9 convert_add_fusion.4
  219.6 1.2 fusion.7
  (181 shorter events, 15.9 us)
Async XLA Ops:
  0.6 52.9 %copy-start = (f32[16,2048]{1,0:T(8,128)S(1)}, f32[16,2048]{1,0:T(8,128)}, u32[]{:S(2)}) copy-start(f32[16,2048]{1,0:T(8,128)} %param.14) | copy-start | bytes 393220
  0.6 10.8 %copy-start.35 = (bf16[256,512]{1,0:T(8,128)(2,1)S(1)}, bf16[256,512]{1,0:T(8,128)(2,1)}, u32[]{:S(2)}) copy-start(bf16[256,512]{1,0:T(8,128)(2,1)} %param.11) | copy-start | bytes 786436
  0.7 37.6 %collective-permute-start = (bf16[128,2048]{1,0:T(8,128)(2,1)}, bf16[128,2048]{1,0:T(8,128)(2,1)}, u32[]{:S(2)}, u32[]{:S(2)}) collective-permute-start(bf16[128,2048]{1,0:T(8,128)(2,1)} %param.8), channel_id=1, source_target_pairs={{0,1},{1,0},{2,3},{3,2},{4,5},{5,4},{6,7},{7,6},{8,9},{9,8},{10,11... | collective-permute-start | bytes 1572872 | tf_op jit(solution)/shard_map/ppermute | solution.py:613
  3.7 33.8 %collective-permute-start.1 = (bf16[128,2048]{1,0:T(8,128)(2,1)}, bf16[128,2048]{1,0:T(8,128)(2,1)}, u32[]{:S(2)}, u32[]{:S(2)}) collective-permute-start(bf16[128,2048]{1,0:T(8,128)(2,1)} %param.8), channel_id=1, source_target_pairs={{0,4},{2,6},{4,0},{6,2},{8,12},{10,14},{12,8},{14,10},{16,20},{18,... | collective-permute-start | bytes 1572872 | tf_op jit(solution)/shard_map/ppermute | solution.py:610
  5.2 11.3 %collective-permute-start.10 = (bf16[256,512]{1,0:T(8,128)(2,1)}, bf16[256,512]{1,0:T(8,128)(2,1)}, u32[]{:S(2)}, u32[]{:S(2)}) collective-permute-start(bf16[256,512]{1,0:T(8,128)(2,1)} %param.11), channel_id=1, source_target_pairs={{0,8},{2,10},{4,12},{6,14},{8,16},{10,18},{12,20},{14,22},{16,24},... | collective-permute-start | bytes 786440 | tf_op jit(solution)/shard_map/ppermute | solution.py:617
  6.8 13.7 %collective-permute-start.11 = (bf16[256,512]{1,0:T(8,128)(2,1)}, bf16[256,512]{1,0:T(8,128)(2,1)}, u32[]{:S(2)}, u32[]{:S(2)}) collective-permute-start(bf16[256,512]{1,0:T(8,128)(2,1)} %param.12), channel_id=1, source_target_pairs={{0,8},{2,10},{4,12},{6,14},{8,16},{10,18},{12,20},{14,22},{16,24},... | collective-permute-start | bytes 786440 | tf_op jit(solution)/shard_map/ppermute | solution.py:617
  10.9 16.4 %collective-permute-start.5 = (bf16[384,512]{1,0:T(8,128)(2,1)S(1)}, bf16[384,512]{1,0:T(8,128)(2,1)}, u32[]{:S(2)}, u32[]{:S(2)}) collective-permute-start(bf16[384,512]{1,0:T(8,128)(2,1)S(1)} %pad_maximum_fusion.12), channel_id=1, source_target_pairs={{0,4},{2,6},{4,0},{6,2},{8,12},{10,14},{12,8},{14,10},{16,20},{18,... | collective-permute-start | bytes 1179656 | tf_op jit(solution)/shard_map/ppermute | solution.py:610
  13.5 90.6 %copy-start.25 = (bf16[256,256]{1,0:T(8,128)(2,1)}, bf16[256,256]{1,0:T(8,128)(2,1)S(1)}, u32[]{:S(2)}) copy-start(bf16[256,256]{1,0:T(8,128)(2,1)S(1)} %pad_maximum_fusion.16) | copy-start | bytes 393220
  14.3 137.6 %copy-start.10 = (s32[7]{0:T(128)}, s32[7]{0:T(128)S(1)}, u32[]{:S(2)}) copy-start(s32[7]{0:T(128)S(1)} %stack.58.where) | copy-start | bytes 88
  16.5 16.7 %collective-permute-start.6 = (bf16[384,512]{1,0:T(8,128)(2,1)S(1)}, bf16[384,512]{1,0:T(8,128)(2,1)S(1)}, u32[]{:S(2)}, u32[]{:S(2)}) collective-permute-start(bf16[384,512]{1,0:T(8,128)(2,1)S(1)} %pad_maximum_fusion.13), channel_id=1, source_target_pairs={{0,6},{2,4},{4,2},{6,0},{8,14},{10,12},{12,10},{14,8},{16,22},{18,... | collective-permute-start | bytes 1179656 | tf_op jit(solution)/shard_map/ppermute | solution.py:610
  20.5 14.3 %collective-permute-start.4 = (bf16[384,512]{1,0:T(8,128)(2,1)S(1)}, bf16[384,512]{1,0:T(8,128)(2,1)S(1)}, u32[]{:S(2)}, u32[]{:S(2)}) collective-permute-start(bf16[384,512]{1,0:T(8,128)(2,1)S(1)} %pad_maximum_fusion.11), channel_id=1, source_target_pairs={{0,2},{2,0},{4,6},{6,4},{8,10},{10,8},{12,14},{14,12},{16,18},{18,... | collective-permute-start | bytes 1179656 | tf_op jit(solution)/shard_map/ppermute | solution.py:610
  21.5 82.1 %copy-start.27 = (bf16[256,256]{1,0:T(8,128)(2,1)}, bf16[256,256]{1,0:T(8,128)(2,1)S(1)}, u32[]{:S(2)}) copy-start(bf16[256,256]{1,0:T(8,128)(2,1)S(1)} %pad_maximum_fusion.29) | copy-start | bytes 393220
  27.3 27.0 %collective-permute-start.12 = (bf16[256,512]{1,0:T(8,128)(2,1)}, bf16[256,512]{1,0:T(8,128)(2,1)S(1)}, u32[]{:S(2)}, u32[]{:S(2)}) collective-permute-start(bf16[256,512]{1,0:T(8,128)(2,1)} %collective-permute-done.10), channel_id=1, source_target_pairs={{0,8},{2,10},{4,12},{6,14},{8,16},{10,18},{12,20},{14,22},{16,24},... | collective-permute-start | bytes 786440 | tf_op jit(solution)/shard_map/ppermute | solution.py:617
  33.2 22.7 %collective-permute-start.13 = (bf16[256,512]{1,0:T(8,128)(2,1)}, bf16[256,512]{1,0:T(8,128)(2,1)S(1)}, u32[]{:S(2)}, u32[]{:S(2)}) collective-permute-start(bf16[256,512]{1,0:T(8,128)(2,1)} %collective-permute-done.11), channel_id=1, source_target_pairs={{0,8},{2,10},{4,12},{6,14},{8,16},{10,18},{12,20},{14,22},{16,24},... | collective-permute-start | bytes 786440 | tf_op jit(solution)/shard_map/ppermute | solution.py:617
  34.9 17.0 %copy-start.13 = (bf16[128,2048]{1,0:T(8,128)(2,1)S(1)}, bf16[128,2048]{1,0:T(8,128)(2,1)}, u32[]{:S(2)}) copy-start(bf16[128,2048]{1,0:T(8,128)(2,1)} %param.8) | copy-start | bytes 1572868
  35.0 18.4 %copy-start.16 = (bf16[1024,256]{1,0:T(8,128)(2,1)}, bf16[1024,256]{1,0:T(8,128)(2,1)S(1)}, u32[]{:S(2)}) copy-start(bf16[1024,256]{1,0:T(8,128)(2,1)S(1)} %get-tuple-element.58.refs_6_) | copy-start | bytes 1572868
  35.0 18.4 %copy-start.17 = (bf16[1024,256]{1,0:T(8,128)(2,1)}, bf16[1024,256]{1,0:T(8,128)(2,1)S(1)}, u32[]{:S(2)}) copy-start(bf16[1024,256]{1,0:T(8,128)(2,1)S(1)} %get-tuple-element.59.refs_2_) | copy-start | bytes 1572868
  35.0 45.8 %collective-permute-start.20 = (bf16[1024,256]{1,0:T(8,128)(2,1)S(1)}, bf16[1024,256]{1,0:T(8,128)(2,1)S(1)}, u32[]{:S(2)}, u32[]{:S(2)}) collective-permute-start(bf16[1024,256]{1,0:T(8,128)(2,1)S(1)} %get-tuple-element.58.refs_6_), channel_id=1, source_target_pairs={{0,8},{2,10},{4,12},{6,14},{8,16},{10,18},{12,20},{14,22},{16,24},... | collective-permute-start | bytes 1572872 | tf_op jit(solution)/shard_map/ppermute | solution.py:617
  37.6 14.4 %collective-permute-start.2 = (bf16[128,2048]{1,0:T(8,128)(2,1)}, bf16[128,2048]{1,0:T(8,128)(2,1)S(1)}, u32[]{:S(2)}, u32[]{:S(2)}) collective-permute-start(bf16[128,2048]{1,0:T(8,128)(2,1)} %collective-permute-done.1), channel_id=1, source_target_pairs={{0,1},{1,0},{2,3},{3,2},{4,5},{5,4},{6,7},{7,6},{8,9},{9,8},{10,11... | collective-permute-start | bytes 1572872 | tf_op jit(solution)/shard_map/ppermute | solution.py:613
  38.2 41.5 %collective-permute-start.7 = (bf16[1024,256]{1,0:T(8,128)(2,1)S(1)}, bf16[1024,256]{1,0:T(8,128)(2,1)S(1)}, u32[]{:S(2)}, u32[]{:S(2)}) collective-permute-start(bf16[1024,256]{1,0:T(8,128)(2,1)S(1)} %get-tuple-element.59.refs_2_), channel_id=1, source_target_pairs={{0,8},{2,10},{4,12},{6,14},{8,16},{10,18},{12,20},{14,22},{16,24},... | collective-permute-start | bytes 1572872 | tf_op jit(solution)/shard_map/ppermute | solution.py:617
  53.4 42.8 %collective-permute-start.3 = (bf16[2,2,128,2048]{3,2,1,0:T(8,128)(2,1)S(1)}, bf16[2,2,128,2048]{3,2,1,0:T(8,128)(2,1)S(1)}, u32[]{:S(2)}, u32[]{:S(2)}) collective-permute-start(bf16[2,2,128,2048]{3,2,1,0:T(8,128)(2,1)S(1)} %bitcast.87), channel_id=1, source_target_pairs={{0,2},{2,0},{4,6},{6,4},{8,10},{10,8},{12,14},{14,12},{16,18},{18,... | collective-permute-start | bytes 6291464 | tf_op jit(solution)/shard_map/ppermute | solution.py:610
  54.2 18.1 %collective-permute-start.14 = (bf16[256,512]{1,0:T(8,128)(2,1)S(1)}, bf16[256,512]{1,0:T(8,128)(2,1)S(1)}, u32[]{:S(2)}, u32[]{:S(2)}) collective-permute-start(bf16[256,512]{1,0:T(8,128)(2,1)S(1)} %collective-permute-done.12), channel_id=1, source_target_pairs={{0,8},{2,10},{4,12},{6,14},{8,16},{10,18},{12,20},{14,22},{16,24},... | collective-permute-start | bytes 786440 | tf_op jit(solution)/shard_map/ppermute | solution.py:617
  56.0 22.0 %collective-permute-start.15 = (bf16[256,512]{1,0:T(8,128)(2,1)S(1)}, bf16[256,512]{1,0:T(8,128)(2,1)S(1)}, u32[]{:S(2)}, u32[]{:S(2)}) collective-permute-start(bf16[256,512]{1,0:T(8,128)(2,1)S(1)} %collective-permute-done.13), channel_id=1, source_target_pairs={{0,8},{2,10},{4,12},{6,14},{8,16},{10,18},{12,20},{14,22},{16,24},... | collective-permute-start | bytes 786440 | tf_op jit(solution)/shard_map/ppermute | solution.py:617
  78.1 18.1 %copy-start.9 = (f32[4096]{0:T(1024)S(1)}, f32[4096]{0:T(1024)}, u32[]{:S(2)}) copy-start(f32[4096]{0:T(1024)} %param.9) | copy-start | bytes 49156
  78.1 24.4 %collective-permute-start.17 = (bf16[1024,256]{1,0:T(8,128)(2,1)S(1)}, bf16[1024,256]{1,0:T(8,128)(2,1)S(1)}, u32[]{:S(2)}, u32[]{:S(2)}) collective-permute-start(bf16[1024,256]{1,0:T(8,128)(2,1)S(1)} %pad_maximum_fusion.5), channel_id=1, source_target_pairs={{0,4},{2,6},{4,0},{6,2},{8,12},{10,14},{12,8},{14,10},{16,20},{18,... | collective-permute-start | bytes 1572872 | tf_op jit(solution)/shard_map/ppermute | solution.py:610
  78.8 23.6 %collective-permute-start.18 = (bf16[1024,256]{1,0:T(8,128)(2,1)S(1)}, bf16[1024,256]{1,0:T(8,128)(2,1)S(1)}, u32[]{:S(2)}, u32[]{:S(2)}) collective-permute-start(bf16[1024,256]{1,0:T(8,128)(2,1)S(1)} %pad_maximum_fusion.6), channel_id=1, source_target_pairs={{0,6},{2,4},{4,2},{6,0},{8,14},{10,12},{12,10},{14,8},{16,22},{18,... | collective-permute-start | bytes 1572872 | tf_op jit(solution)/shard_map/ppermute | solution.py:610
  79.7 29.3 %copy-start.19 = (bf16[1024,256]{1,0:T(8,128)(2,1)}, bf16[1024,256]{1,0:T(8,128)(2,1)S(1)}, u32[]{:S(2)}) copy-start(bf16[1024,256]{1,0:T(8,128)(2,1)S(1)} %collective-permute-done.7.refs_3_) | copy-start | bytes 1572868
  79.7 16.4 %collective-permute-start.8 = (bf16[1024,256]{1,0:T(8,128)(2,1)S(1)}, bf16[1024,256]{1,0:T(8,128)(2,1)}, u32[]{:S(2)}, u32[]{:S(2)}) collective-permute-start(bf16[1024,256]{1,0:T(8,128)(2,1)S(1)} %collective-permute-done.7.refs_3_), channel_id=1, source_target_pairs={{0,8},{2,10},{4,12},{6,14},{8,16},{10,18},{12,20},{14,22},{16,24},... | collective-permute-start | bytes 1572872 | tf_op jit(solution)/shard_map/ppermute | solution.py:617
  80.8 24.0 %copy-start.18 = (bf16[1024,256]{1,0:T(8,128)(2,1)}, bf16[1024,256]{1,0:T(8,128)(2,1)S(1)}, u32[]{:S(2)}) copy-start(bf16[1024,256]{1,0:T(8,128)(2,1)S(1)} %collective-permute-done.20.refs_7_) | copy-start | bytes 1572868
  80.8 21.8 %collective-permute-start.16 = (bf16[1024,256]{1,0:T(8,128)(2,1)S(1)}, bf16[1024,256]{1,0:T(8,128)(2,1)S(1)}, u32[]{:S(2)}, u32[]{:S(2)}) collective-permute-start(bf16[1024,256]{1,0:T(8,128)(2,1)S(1)} %pad_maximum_fusion.4), channel_id=1, source_target_pairs={{0,2},{2,0},{4,6},{6,4},{8,10},{10,8},{12,14},{14,12},{16,18},{18,... | collective-permute-start | bytes 1572872 | tf_op jit(solution)/shard_map/ppermute | solution.py:610
  96.2 16.7 %collective-permute-start.21 = (bf16[1024,256]{1,0:T(8,128)(2,1)S(1)}, bf16[1024,256]{1,0:T(8,128)(2,1)}, u32[]{:S(2)}, u32[]{:S(2)}) collective-permute-start(bf16[1024,256]{1,0:T(8,128)(2,1)S(1)} %collective-permute-done.20.refs_7_), channel_id=1, source_target_pairs={{0,8},{2,10},{4,12},{6,14},{8,16},{10,18},{12,20},{14,22},{16,24},... | collective-permute-start | bytes 1572872 | tf_op jit(solution)/shard_map/ppermute | solution.py:617
  96.2 32.0 %collective-permute-start.9 = (bf16[1024,256]{1,0:T(8,128)(2,1)}, bf16[1024,256]{1,0:T(8,128)(2,1)}, u32[]{:S(2)}, u32[]{:S(2)}) collective-permute-start(bf16[1024,256]{1,0:T(8,128)(2,1)} %collective-permute-done.8.refs_4_), channel_id=1, source_target_pairs={{0,8},{2,10},{4,12},{6,14},{8,16},{10,18},{12,20},{14,22},{16,24},... | collective-permute-start | bytes 1572872 | tf_op jit(solution)/shard_map/ppermute | solution.py:617
  98.9 4.2 %copy-start.2 = (bf16[512,1024]{1,0:T(8,128)(2,1)}, bf16[512,1024]{1,0:T(8,128)(2,1)S(1)}, u32[]{:S(2)}) copy-start(bf16[512,1024]{1,0:T(8,128)(2,1)S(1)} %get-tuple-element.29.refs_0_.refs_2_) | copy-start | bytes 3145732
  98.9 5.2 %copy-start.12 = (f32[512,128]{1,0:T(8,128)}, f32[512,128]{1,0:T(8,128)S(1)}, u32[]{:S(2)}) copy-start(f32[512,128]{1,0:T(8,128)S(1)} %get-tuple-element.25) | copy-start | bytes 786436
  107.6 17.7 %collective-permute-start.19 = (bf16[512,256]{1,0:T(8,128)(2,1)S(1)}, bf16[512,256]{1,0:T(8,128)(2,1)S(1)}, u32[]{:S(2)}, u32[]{:S(2)}) collective-permute-start(bf16[512,256]{1,0:T(8,128)(2,1)S(1)} %pad_maximum_fusion.15), channel_id=1, source_target_pairs={{0,8},{2,10},{4,12},{6,14},{8,16},{10,18},{12,20},{14,22},{16,24},... | collective-permute-start | bytes 786440 | tf_op jit(solution)/shard_map/ppermute | solution.py:707
  109.9 5.2 %copy-start.26 = (bf16[256,256]{1,0:T(8,128)(2,1)S(1)}, bf16[256,256]{1,0:T(8,128)(2,1)}, u32[]{:S(2)}) copy-start(bf16[256,256]{1,0:T(8,128)(2,1)} %copy-done.25) | copy-start | bytes 393220
  116.8 19.0 %collective-permute-start.22 = (bf16[1024,256]{1,0:T(8,128)(2,1)}, bf16[1024,256]{1,0:T(8,128)(2,1)}, u32[]{:S(2)}, u32[]{:S(2)}) collective-permute-start(bf16[1024,256]{1,0:T(8,128)(2,1)} %collective-permute-done.21.refs_8_), channel_id=1, source_target_pairs={{0,8},{2,10},{4,12},{6,14},{8,16},{10,18},{12,20},{14,22},{16,24},... | collective-permute-start | bytes 1572872 | tf_op jit(solution)/shard_map/ppermute | solution.py:617
  135.8 7.3 %copy-start.28 = (bf16[256,256]{1,0:T(8,128)(2,1)S(1)}, bf16[256,256]{1,0:T(8,128)(2,1)}, u32[]{:S(2)}) copy-start(bf16[256,256]{1,0:T(8,128)(2,1)} %copy-done.27) | copy-start | bytes 393220
  135.8 7.3 %copy-start.30 = (bf16[256,256]{1,0:T(8,128)(2,1)S(1)}, bf16[256,256]{1,0:T(8,128)(2,1)}, u32[]{:S(2)}) copy-start(bf16[256,256]{1,0:T(8,128)(2,1)} %copy-done.29) | copy-start | bytes 393220
  135.8 7.3 %copy-start.32 = (bf16[256,256]{1,0:T(8,128)(2,1)S(1)}, bf16[256,256]{1,0:T(8,128)(2,1)}, u32[]{:S(2)}) copy-start(bf16[256,256]{1,0:T(8,128)(2,1)} %copy-done.31) | copy-start | bytes 393220
  135.8 7.3 %copy-start.34 = (bf16[256,256]{1,0:T(8,128)(2,1)S(1)}, bf16[256,256]{1,0:T(8,128)(2,1)}, u32[]{:S(2)}) copy-start(bf16[256,256]{1,0:T(8,128)(2,1)} %copy-done.33) | copy-start | bytes 393220
  141.8 10.1 %collective-permute-start.23 = (bf16[512,256]{1,0:T(8,128)(2,1)S(1)}, bf16[512,256]{1,0:T(8,128)(2,1)S(1)}, u32[]{:S(2)}, u32[]{:S(2)}) collective-permute-start(bf16[512,256]{1,0:T(8,128)(2,1)S(1)} %get-tuple-element.39), channel_id=1, source_target_pairs={{8,0},{10,2},{12,4},{14,6},{16,8},{18,10},{20,12},{22,14},{24,16},... | collective-permute-start | bytes 786440 | tf_op jit(solution)/shard_map/ppermute | solution.py:722
  143.2 8.6 %copy-start.4 = (bf16[1024,256]{1,0:T(8,128)(2,1)S(1)}, bf16[1024,256]{1,0:T(8,128)(2,1)}, u32[]{:S(2)}) copy-start(bf16[1024,256]{1,0:T(8,128)(2,1)} %pad_maximum_fusion.7.refs_4_) | copy-start | bytes 1572868
  143.3 8.6 %copy-start.5 = (bf16[1024,256]{1,0:T(8,128)(2,1)S(1)}, bf16[1024,256]{1,0:T(8,128)(2,1)}, u32[]{:S(2)}) copy-start(bf16[1024,256]{1,0:T(8,128)(2,1)} %pad_maximum_fusion.10.refs_7_) | copy-start | bytes 1572868
  143.3 8.6 %copy-start.6 = (bf16[1024,256]{1,0:T(8,128)(2,1)S(1)}, bf16[1024,256]{1,0:T(8,128)(2,1)}, u32[]{:S(2)}) copy-start(bf16[1024,256]{1,0:T(8,128)(2,1)} %pad_maximum_fusion.9.refs_6_) | copy-start | bytes 1572868
  156.2 19.8 %copy-start.7 = (bf16[2,2,128,2048]{3,2,1,0:T(8,128)(2,1)}, bf16[2,2,128,2048]{3,2,1,0:T(8,128)(2,1)S(1)}, u32[]{:S(2)}) copy-start(bf16[2,2,128,2048]{3,2,1,0:T(8,128)(2,1)S(1)} %get-tuple-element.40) | copy-start | bytes 6291460
  156.2 4.2 %collective-permute-start.24 = (bf16[2,2,128,2048]{3,2,1,0:T(8,128)(2,1)S(1)}, bf16[2,2,128,2048]{3,2,1,0:T(8,128)(2,1)S(1)}, u32[]{:S(2)}, u32[]{:S(2)}) collective-permute-start(bf16[2,2,128,2048]{3,2,1,0:T(8,128)(2,1)S(1)} %get-tuple-element.41), channel_id=1, source_target_pairs={{0,2},{2,0},{4,6},{6,4},{8,10},{10,8},{12,14},{14,12},{16,18},{18,... | collective-permute-start | bytes 6291464 | tf_op jit(solution)/shard_map/ppermute | solution.py:610
  160.5 15.6 %copy-start.15 = (bf16[2,2,128,2048]{3,2,1,0:T(8,128)(2,1)}, bf16[2,2,128,2048]{3,2,1,0:T(8,128)(2,1)S(1)}, u32[]{:S(2)}) copy-start(bf16[2,2,128,2048]{3,2,1,0:T(8,128)(2,1)S(1)} %collective-permute-done.24) | copy-start | bytes 6291460
  160.7 14.0 %collective-permute-start.25 = (bf16[2,128,1024]{2,1,0:T(8,128)(2,1)S(1)}, bf16[2,128,1024]{2,1,0:T(8,128)(2,1)S(1)}, u32[]{:S(2)}, u32[]{:S(2)}) collective-permute-start(bf16[2,128,1024]{2,1,0:T(8,128)(2,1)S(1)} %fusion.9), channel_id=1, source_target_pairs={{0,4},{2,6},{4,0},{6,2},{8,12},{10,14},{12,8},{14,10},{16,20},{18,... | collective-permute-start | bytes 1572872 | tf_op jit(solution)/shard_map/ppermute | solution.py:610
  161.0 14.0 %collective-permute-start.26 = (bf16[2,128,1024]{2,1,0:T(8,128)(2,1)S(1)}, bf16[2,128,1024]{2,1,0:T(8,128)(2,1)S(1)}, u32[]{:S(2)}, u32[]{:S(2)}) collective-permute-start(bf16[2,128,1024]{2,1,0:T(8,128)(2,1)S(1)} %fusion.10), channel_id=1, source_target_pairs={{0,1},{1,0},{2,3},{3,2},{4,5},{5,4},{6,7},{7,6},{8,9},{9,8},{10,11... | collective-permute-start | bytes 1572872 | tf_op jit(solution)/shard_map/ppermute | solution.py:613
  174.7 3.8 %copy-start.21 = (bf16[2,128,1024]{2,1,0:T(8,128)(2,1)}, bf16[2,128,1024]{2,1,0:T(8,128)(2,1)S(1)}, u32[]{:S(2)}) copy-start(bf16[2,128,1024]{2,1,0:T(8,128)(2,1)S(1)} %collective-permute-done.25) | copy-start | bytes 1572868
  175.0 3.8 %copy-start.23 = (bf16[2,128,1024]{2,1,0:T(8,128)(2,1)}, bf16[2,128,1024]{2,1,0:T(8,128)(2,1)S(1)}, u32[]{:S(2)}) copy-start(bf16[2,128,1024]{2,1,0:T(8,128)(2,1)S(1)} %collective-permute-done.26) | copy-start | bytes 1572868
  176.1 23.2 %collective-permute-start.27 = (bf16[128,1024]{1,0:T(8,128)(2,1)}, bf16[128,1024]{1,0:T(8,128)(2,1)}, u32[]{:S(2)}, u32[]{:S(2)}) collective-permute-start(bf16[128,1024]{1,0:T(8,128)(2,1)} %get-tuple-element.42), channel_id=1, source_target_pairs={{0,1},{1,0},{2,3},{3,2},{4,5},{5,4},{6,7},{7,6},{8,9},{9,8},{10,11... | collective-permute-start | bytes 786440 | tf_op jit(solution)/shard_map/ppermute | solution.py:613
  176.7 22.5 %collective-permute-start.28 = (bf16[128,1024]{1,0:T(8,128)(2,1)}, bf16[128,1024]{1,0:T(8,128)(2,1)}, u32[]{:S(2)}, u32[]{:S(2)}) collective-permute-start(bf16[128,1024]{1,0:T(8,128)(2,1)} %get-tuple-element.43), channel_id=1, source_target_pairs={{0,4},{2,6},{4,0},{6,2},{8,12},{10,14},{12,8},{14,10},{16,20},{18,... | collective-permute-start | bytes 786440 | tf_op jit(solution)/shard_map/ppermute | solution.py:610
  178.4 8.9 %collective-permute-start.32 = (bf16[512,128]{1,0:T(8,128)(2,1)S(1)}, bf16[512,128]{1,0:T(8,128)(2,1)S(1)}, u32[]{:S(2)}, u32[]{:S(2)}) collective-permute-start(bf16[512,128]{1,0:T(8,128)(2,1)S(1)} %get-tuple-element.44.refs_1_.refs_3_), channel_id=1, source_target_pairs={{0,6},{2,4},{4,2},{6,0},{8,14},{10,12},{12,10},{14,8},{16,22},{18,... | collective-permute-start | bytes 393224 | tf_op jit(solution)/shard_map/ppermute | solution.py:610
  178.5 11.3 %collective-permute-start.31 = (bf16[512,128]{1,0:T(8,128)(2,1)S(1)}, bf16[512,128]{1,0:T(8,128)(2,1)S(1)}, u32[]{:S(2)}, u32[]{:S(2)}) collective-permute-start(bf16[512,128]{1,0:T(8,128)(2,1)S(1)} %get-tuple-element.44.refs_1_.refs_3_), channel_id=1, source_target_pairs={{0,4},{2,6},{4,0},{6,2},{8,12},{10,14},{12,8},{14,10},{16,20},{18,... | collective-permute-start | bytes 393224 | tf_op jit(solution)/shard_map/ppermute | solution.py:610
  178.8 11.0 %collective-permute-start.30 = (bf16[512,128]{1,0:T(8,128)(2,1)S(1)}, bf16[512,128]{1,0:T(8,128)(2,1)}, u32[]{:S(2)}, u32[]{:S(2)}) collective-permute-start(bf16[512,128]{1,0:T(8,128)(2,1)S(1)} %get-tuple-element.44.refs_1_.refs_3_), channel_id=1, source_target_pairs={{0,2},{2,0},{4,6},{6,4},{8,10},{10,8},{12,14},{14,12},{16,18},{18,... | collective-permute-start | bytes 393224 | tf_op jit(solution)/shard_map/ppermute | solution.py:610
  191.6 7.6 %copy-start.22 = (bf16[2,128,1024]{2,1,0:T(8,128)(2,1)S(1)}, bf16[2,128,1024]{2,1,0:T(8,128)(2,1)}, u32[]{:S(2)}) copy-start(bf16[2,128,1024]{2,1,0:T(8,128)(2,1)} %copy-done.21) | copy-start | bytes 1572868
  191.6 7.6 %copy-start.24 = (bf16[2,128,1024]{2,1,0:T(8,128)(2,1)S(1)}, bf16[2,128,1024]{2,1,0:T(8,128)(2,1)}, u32[]{:S(2)}) copy-start(bf16[2,128,1024]{2,1,0:T(8,128)(2,1)} %copy-done.23) | copy-start | bytes 1572868
  194.0 8.6 %collective-permute-start.33 = (bf16[256,512]{1,0:T(8,128)(2,1)S(1)}, bf16[256,512]{1,0:T(8,128)(2,1)S(1)}, u32[]{:S(2)}, u32[]{:S(2)}) collective-permute-start(bf16[256,512]{1,0:T(8,128)(2,1)S(1)} %get-tuple-element.45), channel_id=1, source_target_pairs={{0,24},{2,26},{4,28},{6,30},{8,0},{10,2},{12,4},{14,6},{16,8},{18,... | collective-permute-start | bytes 786440 | tf_op jit(solution)/shard_map/ppermute | solution.py:617
  194.0 24.6 %collective-permute-start.34 = (bf16[256,512]{1,0:T(8,128)(2,1)S(1)}, bf16[256,512]{1,0:T(8,128)(2,1)S(1)}, u32[]{:S(2)}, u32[]{:S(2)}) collective-permute-start(bf16[256,512]{1,0:T(8,128)(2,1)S(1)} %get-tuple-element.46), channel_id=1, source_target_pairs={{0,16},{2,18},{4,20},{6,22},{8,24},{10,26},{12,28},{14,30},{16,0},... | collective-permute-start | bytes 786440 | tf_op jit(solution)/shard_map/ppermute | solution.py:617
  197.2 21.5 %collective-permute-start.35 = (bf16[256,512]{1,0:T(8,128)(2,1)S(1)}, bf16[256,512]{1,0:T(8,128)(2,1)S(1)}, u32[]{:S(2)}, u32[]{:S(2)}) collective-permute-start(bf16[256,512]{1,0:T(8,128)(2,1)S(1)} %get-tuple-element.47), channel_id=1, source_target_pairs={{0,8},{2,10},{4,12},{6,14},{8,16},{10,18},{12,20},{14,22},{16,24},... | collective-permute-start | bytes 786440 | tf_op jit(solution)/shard_map/ppermute | solution.py:617
  201.0 19.8 %copy-start.1 = (f32[16,2048]{1,0:T(8,128)S(1)}, f32[16,2048]{1,0:T(8,128)}, u32[]{:S(2)}) copy-start(f32[16,2048]{1,0:T(8,128)} %param.14) | copy-start | bytes 393220
  201.2 18.4 %collective-permute-start.29 = (f32[1,128]{1,0:T(1,128)S(1)}, f32[1,128]{1,0:T(1,128)S(1)}, u32[]{:S(2)}, u32[]{:S(2)}) collective-permute-start(f32[1,128]{1,0:T(1,128)S(1)} %bitcast.95), channel_id=1, source_target_pairs={{0,1},{1,0},{2,3},{3,2},{4,5},{5,4},{6,7},{7,6},{8,9},{9,8},{10,11... | collective-permute-start | bytes 1544 | tf_op jit(solution)/shard_map/ppermute | solution.py:613
  (11 other events, 14.7 us)
